TPU v7x, 32 devices: a whole 2x2x4 slice. The times are simulated.
32 devices in a mesh: ens: 2 (over y), lon: 4 (over x, core), lat: 4 (over z).
Axes of the slice: x: 2, y: 2, z: 4, core: 2. Of those that a mesh axis runs over, the one named last changes fastest.
Arguments:
- noise: float32 [64, 64, 512], P('ens', 'lat', 'lon'), parts along dimension 0, may hold values from -6 to 6
- kappa2: float32 [32, 64, 512], P(None, 'lat', 'lon'), may hold values from 0.03 to 0.3
- conduct: float32 [3, 32, 64, 512], P(None, None, 'lat', 'lon'), may hold values from 0.3 to 3
- land: int32 [32, 64, 512], P(None, 'lat', 'lon'), may hold values 0 or 1
Outputs:
- solution_field: float32 [64, 64, 512], P('ens', 'lat', 'lon'), parts along dimension 0
- residual: float32 [64, 64, 512], P('ens', 'lat', 'lon'), parts along dimension 0
There are 2 independent parts, one for each index of `ens`. A program takes and returns all parts, laid end to end along the dimension named above; an argument that names none is the same for every part. Nothing has to cross between parts.
Inputs may be any that keep to these rules, and one draw needn't show every extreme that they name: 1 marks an ocean cell, 0 a land cell.
All inputs are finite; a program needn't handle non-finite values. No bound on the sum of `land` on one device may be relied on, other than what follows from the above.
Results may differ from a plain program's by a relative error of at most 0.00035.
Values sent between devices are 32-bit elements; how exact they have to be, the bound alone decides.
No kernel may reach another device: no remote copies, remote signals or barrier semaphores. Data moves between devices by JAX's collectives and lax.ppermute only.
A program may use at most 64 MiB of HBM per device.

v0:
```python
import math

import jax
import jax.numpy as jnp
from jax import lax
from jax.sharding import PartitionSpec as P

ITERS = 2


base_kappa = 0.001
base_conduct = 1.0


def padded_2(x, sides, width, wrap):
    for axis, dim in sides:
        size, length = (lax.axis_size(axis), x.shape[dim])
        up = [(i, (i + 1) % size) for i in range(size if wrap else size - 1)]
        down = [(j, i) for i, j in up]
        last = lax.slice_in_dim(x, length - width, length, axis=dim)
        initial = lax.slice_in_dim(x, 0, width, axis=dim)
        before = lax.ppermute(last, axis, up)
        after = lax.ppermute(initial, axis, down)
        x = jnp.concatenate([before, x, after], axis=dim)
    return x


def shifted(x, axis, by):
    size = lax.axis_size(axis)
    return lax.ppermute(x, axis, [(i, (i + by) % size) for i in range(size)])


def shifted_2(x, axis, by):
    size = lax.axis_size(axis)
    pairs = [(i, i + by) for i in range(size) if 0 <= i + by < size]
    return lax.ppermute(x, axis, pairs)


def cut_cycle(padded, width, extend):
    margin = width - extend
    return padded[:, :, margin : padded.shape[2] - margin, margin : padded.shape[3] - margin]


def divergence_form(padded, statics, width, extend):
    cycle = cut_cycle(statics, width, extend + 1)
    kappa_cells = cycle[0][:, 1:-1, 1:-1]
    east_face = cycle[2][:, 1:-1, 1:-1]
    west_face = cycle[2][:, 1:-1, :-2]
    north_face = cycle[3][:, 1:-1, 1:-1]
    south_face = cycle[3][:, :-2, 1:-1]
    upper_face = cycle[4][:, 1:-1, 1:-1]
    center = padded[:, 1:-1, 1:-1]
    zero_level = jnp.zeros_like(center[:1])
    lower_face = jnp.concatenate([zero_level, upper_face[:-1]], axis=0)
    upper_value = jnp.concatenate([center[1:], zero_level], axis=0)
    lower_value = jnp.concatenate([zero_level, center[:-1]], axis=0)
    return (
        kappa_cells * center
        + east_face * (center - padded[:, 1:-1, 2:])
        + west_face * (center - padded[:, 1:-1, :-2])
        + north_face * (center - padded[:, 2:, 1:-1])
        + south_face * (center - padded[:, :-2, 1:-1])
        + upper_face * (center - upper_value)
        + lower_face * (center - lower_value)
    )


def pad_each(field):
    across = padded_2(field, (("lon", 2),), 1, True)
    return padded_2(across, (("lat", 1),), 1, False)


def operator(field, statics, width):
    ocean = cut_cycle(statics, width, 0)[1]
    first = divergence_form(pad_each(ocean * field), statics, width, 0)
    second = divergence_form(pad_each(ocean * first), statics, width, 0)
    return ocean * second + (1.0 - ocean) * field


def spectral(block, width):
    length = block.shape[2]
    count_a = length // width
    lead = block.shape[:2]
    shaped = block.reshape(lead + (count_a, width))
    index_a = jnp.arange(count_a, dtype=jnp.int32)
    index_b = jnp.arange(width, dtype=jnp.int32)
    angle_a = (
        2.0
        * math.pi
        / count_a
        * (index_a[:, None] * index_a[None, :] % count_a).astype(jnp.float32)
    )
    angle_b = (
        2.0 * math.pi / width * (index_b[:, None] * index_b[None, :] % width).astype(jnp.float32)
    )
    angle_t = (
        2.0 * math.pi / length * (index_a[:, None] * index_b[None, :] % length).astype(jnp.float32)
    )
    cos_a, sin_a = (jnp.cos(angle_a), jnp.sin(angle_a))
    cos_b, sin_b = (jnp.cos(angle_b), jnp.sin(angle_b))
    cos_t, sin_t = (jnp.cos(angle_t), jnp.sin(angle_t))
    wave = (index_a[:, None] + count_a * index_b[None, :]).astype(jnp.float32)
    symbol = base_kappa + base_conduct * (2.0 - 2.0 * jnp.cos(2.0 * math.pi * wave / length))
    factor = 1.0 / (symbol * symbol)
    highest = lax.Precision.HIGHEST
    section_real = jnp.einsum("pqab,ak->pqkb", shaped, cos_a, precision=highest)
    section_imag = -jnp.einsum("pqab,ak->pqkb", shaped, sin_a, precision=highest)
    twist_real = section_real * cos_t + section_imag * sin_t
    twist_imag = section_imag * cos_t - section_real * sin_t
    freq_real = (
        jnp.einsum("pqkb,bm->pqkm", twist_real, cos_b, precision=highest)
        + jnp.einsum("pqkb,bm->pqkm", twist_imag, sin_b, precision=highest)
    ) * factor
    freq_imag = (
        jnp.einsum("pqkb,bm->pqkm", twist_imag, cos_b, precision=highest)
        - jnp.einsum("pqkb,bm->pqkm", twist_real, sin_b, precision=highest)
    ) * factor
    back_real = jnp.einsum("pqkm,bm->pqkb", freq_real, cos_b, precision=highest) - jnp.einsum(
        "pqkm,bm->pqkb", freq_imag, sin_b, precision=highest
    )
    back_imag = jnp.einsum("pqkm,bm->pqkb", freq_imag, cos_b, precision=highest) + jnp.einsum(
        "pqkm,bm->pqkb", freq_real, sin_b, precision=highest
    )
    turn_real = back_real * cos_t - back_imag * sin_t
    turn_imag = back_imag * cos_t + back_real * sin_t
    result = jnp.einsum("pqkb,ak->pqab", turn_real, cos_a, precision=highest) - jnp.einsum(
        "pqkb,ak->pqab", turn_imag, sin_a, precision=highest
    )
    return (result / length).reshape(block.shape)


def precondition(residual):
    width = residual.shape[2]
    turned = spectral(
        lax.all_to_all(residual, "lon", split_axis=0, concat_axis=2, tiled=True), width
    )
    return lax.all_to_all(turned, "lon", split_axis=2, concat_axis=0, tiled=True)


def paired_sums(residual, precond, image):
    return lax.psum((jnp.sum(residual * precond), jnp.sum(image * precond)), ("lon", "lat"))


def body(noise, kappa2, conduct, land):
    levels, rows, columns = noise.shape
    width = 1
    ocean = land.astype(jnp.float32)
    row_global = lax.axis_index("lat") * rows + lax.broadcasted_iota(jnp.int32, (1, rows, 1), 1)
    total_rows = rows * lax.axis_size("lat")
    north_face = jnp.where(row_global < total_rows - 1, conduct[1], 0.0)
    level_index = lax.broadcasted_iota(jnp.int32, (levels, 1, 1), 0)
    upper_face = jnp.where(level_index < levels - 1, conduct[2], 0.0)
    statics = jnp.stack([kappa2, ocean, conduct[0], north_face, upper_face])
    west_column = shifted(conduct[0][:, :, columns - 1 :], "lon", 1)
    zero_column = jnp.zeros((5, levels, rows, 1), jnp.float32)
    low_column = zero_column.at[2].set(west_column)
    statics = jnp.concatenate([low_column, statics, zero_column], axis=3)
    south_row = shifted_2(statics[3][:, rows - 1 :, :], "lat", 1)
    zero_row = jnp.zeros((5, levels, 1, columns + 2), jnp.float32)
    low_row = zero_row.at[3].set(south_row)
    statics = jnp.concatenate([low_row, statics, zero_row], axis=2)
    solution = jnp.zeros_like(noise)
    residual = noise
    precond = precondition(residual)
    image = operator(precond, statics, width)
    energy, curvature = paired_sums(residual, precond, image)
    alpha = energy / curvature
    direction, along = (precond, image)
    for iteration in range(ITERS):
        solution = solution + alpha * direction
        residual = residual - alpha * along
        if iteration < ITERS - 1:
            precond = precondition(residual)
            image = operator(precond, statics, width)
            renewed, curvature = paired_sums(residual, precond, image)
            ratio = renewed / energy
            alpha = renewed / (curvature - ratio * renewed / alpha)
            direction = precond + ratio * direction
            along = image + ratio * along
            energy = renewed
    return (solution, residual)


def solution(mesh):
    return jax.shard_map(
        body,
        mesh=mesh,
        in_specs=(
            P("ens", "lat", "lon"),
            P(None, "lat", "lon"),
            P(None, None, "lat", "lon"),
            P(None, "lat", "lon"),
        ),
        out_specs=(P("ens", "lat", "lon"), P("ens", "lat", "lon")),
        check_vma=False,
    )
```

profile of v0, /device:TPU:0, one launch (start us, length us, event | category | flops | bytes accessed | tf_op | source)
XLA Modules:
  0.0 230.5 jit_solution(14411306132536024307)
XLA Ops:
  0.6 4.4 %all-to-all-start = ((f32[32,16,128]{2,1,0:T(8,128)}), f32[32,16,128]{2,1,0:T(8,128)S(1)}, u32[]{:S(2)}, u32[]{:S(2)}) async-start(f32[32,16,128]{2,1,0:T(8,128)} %param.8), calls=%async_computation | async-start | bytes 524288 | tf_op jit(solution)/shard_map/all_to_all | solution.py:135
  5.0 1.0 bitcast_dynamic-update-slice_fusion.1
  6.0 1.0 bitcast_dynamic-update-slice_fusion
  8.1 5.7 %collective-permute-done = f32[32,16,1]{2,1,0:T(8,128)S(1)} collective-permute-done((f32[32,16,1]{2,1,0:T(8,128)S(1)}, f32[32,16,1]{2,1,0:T(8,128)S(1)}, u32[]{:S(2)}, u32[]{:S(2)}) %collective-permute-start) | collective-permute-done | bytes 2080 | tf_op jit(solution)/shard_map/ppermute | solution.py:30
  14.5 1.1 copy-done.2
  15.9 4.1 %collective-permute-start.1 = (f32[32,1,130]{2,1,0:T(1,128)S(1)}, f32[32,1,130]{2,1,0:T(1,128)S(1)}, u32[]{:S(2)}, u32[]{:S(2)}) collective-permute-start(f32[32,1,130]{2,1,0:T(1,128)S(1)} %slice.336), channel_id=1, source_target_pairs={{0,1},{1,2},{2,3},{4,5},{5,6},{6,7},{8,9},{9,10},{10,11},{12,13},{... | collective-permute-start | bytes 49928 | tf_op jit(solution)/shard_map/ppermute | solution.py:36
  20.0 0.8 convolution_negate_fusion.1
  20.8 0.9 add_bitcast_fusion.1
  26.1 0.7 multiply_add_fusion.1
  26.8 0.6 fusion.88
  27.4 0.7 fusion.8
  28.1 2.0 copy.133
  30.1 2.9 %reshape.184 = f32[4,1,16384]{2,1,0:T(1,128)} reshape(f32[512,8,16]{2,1,0:T(8,128)} %bitcast.172) | data formatting | bytes 524288
  33.0 3.6 %all-to-all-start.1 = ((f32[4,1,16384]{2,1,0:T(1,128)}), f32[4,1,16384]{2,1,0:T(1,128)S(1)}, u32[]{:S(2)}, u32[]{:S(2)}) async-start(f32[4,1,16384]{2,1,0:T(1,128)} %reshape.184), calls=%async_computation.1 | async-start | bytes 524288 | tf_op jit(solution)/shard_map/all_to_all | solution.py:137
  36.6 4.8 %fusion = f32[5,32,18,130]{3,2,1,0:T(8,128)} fusion(f32[1,32,1,130]{3,2,1,0:T(1,128)S(1)} %bitcast.182, f32[5,32,16,1]{3,2,1,0:T(8,128)S(1)} %broadcast_in_dim.29, f32[5,32,16,128]{3,2,1,0:T(8,128)} %copy-done.1, f32[5,32,16,1]{3,2,1,0:T(8,128)S(1)} %scatter.6, f32[18]{0:T(128)S(1)} %pad.79.clone), kind=kLoop, calls=%fused_computation.1 | loop fusion | flops 2246400 | bytes 2845512 | tf_op jit(solution)/shard_map/concatenate | solution.py:161
  41.4 1.0 all-to-all-done.1
  42.9 1.4 reduce.4
  44.2 0.7 reshape.185
  44.9 0.7 copy.134
  46.1 1.7 collective-permute-start.2
  47.8 2.2 slice_bitcast_fusion.3
  50.1 3.4 %collective-permute-done.3 = f32[32,16,1]{2,1,0:T(8,128)S(1)} collective-permute-done((f32[32,16,1]{2,1,0:T(8,128)S(1)}, f32[32,16,1]{2,1,0:T(8,128)S(1)}, u32[]{:S(2)}, u32[]{:S(2)}) %collective-permute-start.3) | collective-permute-done | bytes 2080 | tf_op jit(solution)/shard_map/ppermute | solution.py:22
  53.8 1.3 collective-permute-start.4
  55.1 4.5 %collective-permute-start.5 = (f32[32,1,130]{2,1,0:T(1,128)S(1)}, f32[32,1,130]{2,1,0:T(1,128)S(1)}, u32[]{:S(2)}, u32[]{:S(2)}) collective-permute-start(f32[32,1,130]{2,1,0:T(1,128)S(1)} %get-tuple-element.51), channel_id=1, source_target_pairs={{0,1},{1,2},{2,3},{4,5},{5,6},{6,7},{8,9},{9,10},{10,11},{12,13},{... | collective-permute-start | bytes 49928 | tf_op jit(solution)/shard_map/ppermute | solution.py:22
  60.0 1.3 collective-permute-done.5
  61.3 0.8 fusion.62
  62.3 1.7 collective-permute-start.6
  64.1 5.8 %collective-permute-done.7 = f32[32,16,1]{2,1,0:T(8,128)S(1)} collective-permute-done((f32[32,16,1]{2,1,0:T(8,128)S(1)}, f32[32,16,1]{2,1,0:T(8,128)S(1)}, u32[]{:S(2)}, u32[]{:S(2)}) %collective-permute-start.7) | collective-permute-done | bytes 2080 | tf_op jit(solution)/shard_map/ppermute | solution.py:22
  70.2 1.3 collective-permute-start.8
  71.5 4.8 %collective-permute-start.9 = (f32[32,1,130]{2,1,0:T(1,128)S(1)}, f32[32,1,130]{2,1,0:T(1,128)S(1)}, u32[]{:S(2)}, u32[]{:S(2)}) collective-permute-start(f32[32,1,130]{2,1,0:T(1,128)S(1)} %get-tuple-element.47), channel_id=1, source_target_pairs={{0,1},{1,2},{2,3},{4,5},{5,6},{6,7},{8,9},{9,10},{10,11},{12,13},{... | collective-permute-start | bytes 49928 | tf_op jit(solution)/shard_map/ppermute | solution.py:22
  76.3 1.7 collective-permute-done.9
  78.0 1.5 fusion.80
  79.5 34.8 %all-reduce.12 = (f32[]{:T(128)}, f32[]{:T(128)}) all-reduce(f32[]{:T(128)} %get-tuple-element.31, f32[]{:T(128)} %get-tuple-element.30), channel_id=1, replica_groups=mesh['ens'=2,'lon'=4,'lat'=4] {'lon','lat'}, use_global_device_ids=true, to_apply=%region_1.2 | all-reduce | flops 2 | bytes 16 | tf_op jit(solution)/shard_map/psum | solution.py:141
  115.7 1.0 multiply_subtract_fusion.2
  116.7 0.7 copy-done.5
  117.4 8.4 %all_to_all.66 = f32[32,16,128]{2,1,0:T(8,128)S(1)} all-to-all(f32[32,16,128]{2,1,0:T(8,128)S(1)} %multiply_subtract_fusion.2), channel_id=1, replica_groups=mesh['ens'=2,'lon'=4,'lat'=4] {'lon'}, dimensions={0} | all-to-all | bytes 524288 | tf_op jit(solution)/shard_map/all_to_all | solution.py:135
  125.8 0.9 convolution_negate_fusion
  126.6 0.9 add_bitcast_fusion
  128.8 0.6 fusion.2
  131.9 0.6 multiply_add_fusion
  132.6 0.6 fusion.85
  133.2 0.7 fusion.6
  133.9 2.0 copy.137
  135.8 2.3 reshape.186
  138.1 9.1 %all_to_all.67 = f32[4,1,16384]{2,1,0:T(1,128)} all-to-all(f32[4,1,16384]{2,1,0:T(1,128)S(1)} %reshape.186), channel_id=1, replica_groups=mesh['ens'=2,'lon'=4,'lat'=4] {'lon'}, dimensions={0} | all-to-all | bytes 524288 | tf_op jit(solution)/shard_map/all_to_all | solution.py:137
  147.2 2.3 reduce.5
  149.5 2.0 reshape.187
  151.5 2.9 %copy.138 = f32[8,16,4,128]{3,2,1,0:T(4,128)} copy(f32[8,16,4,128]{1,0,3,2:T(8,128)} %bitcast.175) | data formatting | bytes 524288 | tf_op jit(solution)/shard_map/all_to_all | solution.py:137
  154.4 1.0 copy.122
  155.6 1.7 collective-permute-start.10
  157.3 6.2 %collective-permute-done.11 = f32[32,16,1]{2,1,0:T(8,128)S(1)} collective-permute-done((f32[32,16,1]{2,1,0:T(8,128)S(1)}, f32[32,16,1]{2,1,0:T(8,128)S(1)}, u32[]{:S(2)}, u32[]{:S(2)}) %collective-permute-start.11) | collective-permute-done | bytes 2080 | tf_op jit(solution)/shard_map/ppermute | solution.py:22
  163.8 1.3 collective-permute-start.12
  165.1 4.5 %collective-permute-start.13 = (f32[32,1,130]{2,1,0:T(1,128)S(1)}, f32[32,1,130]{2,1,0:T(1,128)S(1)}, u32[]{:S(2)}, u32[]{:S(2)}) collective-permute-start(f32[32,1,130]{2,1,0:T(1,128)S(1)} %get-tuple-element.45), channel_id=1, source_target_pairs={{0,1},{1,2},{2,3},{4,5},{5,6},{6,7},{8,9},{9,10},{10,11},{12,13},{... | collective-permute-start | bytes 49928 | tf_op jit(solution)/shard_map/ppermute | solution.py:22
  169.7 1.5 collective-permute-done.13
  171.2 0.8 fusion.31
  172.3 1.7 collective-permute-start.14
  174.0 6.3 %collective-permute-done.15 = f32[32,16,1]{2,1,0:T(8,128)S(1)} collective-permute-done((f32[32,16,1]{2,1,0:T(8,128)S(1)}, f32[32,16,1]{2,1,0:T(8,128)S(1)}, u32[]{:S(2)}, u32[]{:S(2)}) %collective-permute-start.15) | collective-permute-done | bytes 2080 | tf_op jit(solution)/shard_map/ppermute | solution.py:22
  180.6 1.3 collective-permute-start.16
  181.9 4.9 %collective-permute-start.17 = (f32[32,1,130]{2,1,0:T(1,128)S(1)}, f32[32,1,130]{2,1,0:T(1,128)S(1)}, u32[]{:S(2)}, u32[]{:S(2)}) collective-permute-start(f32[32,1,130]{2,1,0:T(1,128)S(1)} %get-tuple-element.43), channel_id=1, source_target_pairs={{0,1},{1,2},{2,3},{4,5},{5,6},{6,7},{8,9},{9,10},{10,11},{12,13},{... | collective-permute-start | bytes 49928 | tf_op jit(solution)/shard_map/ppermute | solution.py:22
  186.8 1.5 collective-permute-done.17
  188.4 2.3 fusion.73
  190.6 32.7 %all-reduce.11 = (f32[]{:T(128)}, f32[]{:T(128)}) all-reduce(f32[]{:T(128)} %get-tuple-element.29, f32[]{:T(128)} %get-tuple-element.28), channel_id=1, replica_groups=mesh['ens'=2,'lon'=4,'lat'=4] {'lon','lat'}, use_global_device_ids=true, to_apply=%region_5.6 | all-reduce | flops 2 | bytes 16 | tf_op jit(solution)/shard_map/psum | solution.py:141
  227.9 0.8 fusion.75
  228.7 1.9 multiply_subtract_fusion
  (79 shorter events, 13.2 us)
Async XLA Ops:
  0.6 6.3 %copy-start.9 = (f32[3,32,16,128]{3,2,1,0:T(8,128)S(1)}, f32[3,32,16,128]{3,2,1,0:T(8,128)}, u32[]{:S(2)}) copy-start(f32[3,32,16,128]{3,2,1,0:T(8,128)} %param.10) | copy-start | bytes 2359300
  0.6 19.3 %all-to-all-start = ((f32[32,16,128]{2,1,0:T(8,128)}), f32[32,16,128]{2,1,0:T(8,128)S(1)}, u32[]{:S(2)}, u32[]{:S(2)}) async-start(f32[32,16,128]{2,1,0:T(8,128)} %param.8), calls=%async_computation | async-start | bytes 524288 | tf_op jit(solution)/shard_map/all_to_all | solution.py:135
  7.2 6.7 %collective-permute-start = (f32[32,16,1]{2,1,0:T(8,128)S(1)}, f32[32,16,1]{2,1,0:T(8,128)S(1)}, u32[]{:S(2)}, u32[]{:S(2)}) collective-permute-start(f32[32,16,1]{2,1,0:T(8,128)S(1)} %slice.335), channel_id=1, source_target_pairs={{0,4},{4,8},{8,12},{12,0},{1,5},{5,9},{9,13},{13,1},{2,6},{6,10},{... | collective-permute-start | bytes 6152 | tf_op jit(solution)/shard_map/ppermute | solution.py:30
  8.0 6.0 %copy-start.1 = (f32[5,32,16,128]{3,2,1,0:T(8,128)}, f32[5,32,16,128]{3,2,1,0:T(8,128)S(1)}, u32[]{:S(2)}) copy-start(f32[5,32,16,128]{3,2,1,0:T(8,128)S(1)} %select_dynamic-update-slice_fusion) | copy-start | bytes 3932164
  14.2 1.3 copy-start.2
  15.9 20.7 %collective-permute-start.1 = (f32[32,1,130]{2,1,0:T(1,128)S(1)}, f32[32,1,130]{2,1,0:T(1,128)S(1)}, u32[]{:S(2)}, u32[]{:S(2)}) collective-permute-start(f32[32,1,130]{2,1,0:T(1,128)S(1)} %slice.336), channel_id=1, source_target_pairs={{0,1},{1,2},{2,3},{4,5},{5,6},{6,7},{8,9},{9,10},{10,11},{12,13},{... | collective-permute-start | bytes 49928 | tf_op jit(solution)/shard_map/ppermute | solution.py:36
  33.0 9.4 %all-to-all-start.1 = ((f32[4,1,16384]{2,1,0:T(1,128)}), f32[4,1,16384]{2,1,0:T(1,128)S(1)}, u32[]{:S(2)}, u32[]{:S(2)}) async-start(f32[4,1,16384]{2,1,0:T(1,128)} %reshape.184), calls=%async_computation.1 | async-start | bytes 524288 | tf_op jit(solution)/shard_map/all_to_all | solution.py:137
  44.9 1.0 copy-start
  46.0 7.5 %collective-permute-start.3 = (f32[32,16,1]{2,1,0:T(8,128)S(1)}, f32[32,16,1]{2,1,0:T(8,128)S(1)}, u32[]{:S(2)}, u32[]{:S(2)}) collective-permute-start(f32[32,16,1]{2,1,0:T(8,128)S(1)} %get-tuple-element.74), channel_id=1, source_target_pairs={{0,4},{4,8},{8,12},{12,0},{1,5},{5,9},{9,13},{13,1},{2,6},{6,10},{... | collective-permute-start | bytes 6152 | tf_op jit(solution)/shard_map/ppermute | solution.py:22
  46.1 7.4 %collective-permute-start.2 = (f32[32,16,1]{2,1,0:T(8,128)S(1)}, f32[32,16,1]{2,1,0:T(8,128)S(1)}, u32[]{:S(2)}, u32[]{:S(2)}) collective-permute-start(f32[32,16,1]{2,1,0:T(8,128)S(1)} %get-tuple-element.75), channel_id=1, source_target_pairs={{4,0},{8,4},{12,8},{0,12},{5,1},{9,5},{13,9},{1,13},{6,2},{10,6},{... | collective-permute-start | bytes 6152 | tf_op jit(solution)/shard_map/ppermute | solution.py:23
  50.0 28.0 %copy-start.3 = (f32[32,18,130]{2,1,0:T(8,128)}, f32[32,18,130]{2,1,0:T(8,128)S(1)}, u32[]{:S(2)}) copy-start(f32[32,18,130]{2,1,0:T(8,128)S(1)} %get-tuple-element.38) | copy-start | bytes 898564
  53.8 6.2 %collective-permute-start.4 = (f32[32,1,130]{2,1,0:T(1,128)S(1)}, f32[32,1,130]{2,1,0:T(1,128)S(1)}, u32[]{:S(2)}, u32[]{:S(2)}) collective-permute-start(f32[32,1,130]{2,1,0:T(1,128)S(1)} %get-tuple-element.50), channel_id=1, source_target_pairs={{1,0},{2,1},{3,2},{5,4},{6,5},{7,6},{9,8},{10,9},{11,10},{13,12},{... | collective-permute-start | bytes 49928 | tf_op jit(solution)/shard_map/ppermute | solution.py:23
  55.1 6.1 %collective-permute-start.5 = (f32[32,1,130]{2,1,0:T(1,128)S(1)}, f32[32,1,130]{2,1,0:T(1,128)S(1)}, u32[]{:S(2)}, u32[]{:S(2)}) collective-permute-start(f32[32,1,130]{2,1,0:T(1,128)S(1)} %get-tuple-element.51), channel_id=1, source_target_pairs={{0,1},{1,2},{2,3},{4,5},{5,6},{6,7},{8,9},{9,10},{10,11},{12,13},{... | collective-permute-start | bytes 49928 | tf_op jit(solution)/shard_map/ppermute | solution.py:22
  62.1 15.9 %copy-start.8 = (f32[32,16,128]{2,1,0:T(8,128)S(1)}, f32[32,16,128]{2,1,0:T(8,128)}, u32[]{:S(2)}) copy-start(f32[32,16,128]{2,1,0:T(8,128)} %param.8) | copy-start | bytes 786436
  62.3 7.6 %collective-permute-start.7 = (f32[32,16,1]{2,1,0:T(8,128)S(1)}, f32[32,16,1]{2,1,0:T(8,128)S(1)}, u32[]{:S(2)}, u32[]{:S(2)}) collective-permute-start(f32[32,16,1]{2,1,0:T(8,128)S(1)} %get-tuple-element.68), channel_id=1, source_target_pairs={{0,4},{4,8},{8,12},{12,0},{1,5},{5,9},{9,13},{13,1},{2,6},{6,10},{... | collective-permute-start | bytes 6152 | tf_op jit(solution)/shard_map/ppermute | solution.py:22
  62.3 7.6 %collective-permute-start.6 = (f32[32,16,1]{2,1,0:T(8,128)S(1)}, f32[32,16,1]{2,1,0:T(8,128)S(1)}, u32[]{:S(2)}, u32[]{:S(2)}) collective-permute-start(f32[32,16,1]{2,1,0:T(8,128)S(1)} %get-tuple-element.69), channel_id=1, source_target_pairs={{4,0},{8,4},{12,8},{0,12},{5,1},{9,5},{13,9},{1,13},{6,2},{10,6},{... | collective-permute-start | bytes 6152 | tf_op jit(solution)/shard_map/ppermute | solution.py:23
  70.2 6.2 %collective-permute-start.8 = (f32[32,1,130]{2,1,0:T(1,128)S(1)}, f32[32,1,130]{2,1,0:T(1,128)S(1)}, u32[]{:S(2)}, u32[]{:S(2)}) collective-permute-start(f32[32,1,130]{2,1,0:T(1,128)S(1)} %get-tuple-element.46), channel_id=1, source_target_pairs={{1,0},{2,1},{3,2},{5,4},{6,5},{7,6},{9,8},{10,9},{11,10},{13,12},{... | collective-permute-start | bytes 49928 | tf_op jit(solution)/shard_map/ppermute | solution.py:23
  71.5 6.6 %collective-permute-start.9 = (f32[32,1,130]{2,1,0:T(1,128)S(1)}, f32[32,1,130]{2,1,0:T(1,128)S(1)}, u32[]{:S(2)}, u32[]{:S(2)}) collective-permute-start(f32[32,1,130]{2,1,0:T(1,128)S(1)} %get-tuple-element.47), channel_id=1, source_target_pairs={{0,1},{1,2},{2,3},{4,5},{5,6},{6,7},{8,9},{9,10},{10,11},{12,13},{... | collective-permute-start | bytes 49928 | tf_op jit(solution)/shard_map/ppermute | solution.py:22
  79.5 48.0 %copy-start.7 = (f32[32,16,128]{2,1,0:T(8,128)}, f32[32,16,128]{2,1,0:T(8,128)S(1)}, u32[]{:S(2)}) copy-start(f32[32,16,128]{2,1,0:T(8,128)S(1)} %get-tuple-element.37) | copy-start | bytes 786436
  116.7 0.7 copy-start.5
  155.4 15.8 %copy-start.4 = (f32[32,18,130]{2,1,0:T(8,128)S(1)}, f32[32,18,130]{2,1,0:T(8,128)}, u32[]{:S(2)}) copy-start(f32[32,18,130]{2,1,0:T(8,128)} %copy-done.3) | copy-start | bytes 898564
  155.5 8.0 %collective-permute-start.11 = (f32[32,16,1]{2,1,0:T(8,128)S(1)}, f32[32,16,1]{2,1,0:T(8,128)S(1)}, u32[]{:S(2)}, u32[]{:S(2)}) collective-permute-start(f32[32,16,1]{2,1,0:T(8,128)S(1)} %get-tuple-element.66), channel_id=1, source_target_pairs={{0,4},{4,8},{8,12},{12,0},{1,5},{5,9},{9,13},{13,1},{2,6},{6,10},{... | collective-permute-start | bytes 6152 | tf_op jit(solution)/shard_map/ppermute | solution.py:22
  155.6 7.9 %collective-permute-start.10 = (f32[32,16,1]{2,1,0:T(8,128)S(1)}, f32[32,16,1]{2,1,0:T(8,128)S(1)}, u32[]{:S(2)}, u32[]{:S(2)}) collective-permute-start(f32[32,16,1]{2,1,0:T(8,128)S(1)} %get-tuple-element.67), channel_id=1, source_target_pairs={{4,0},{8,4},{12,8},{0,12},{5,1},{9,5},{13,9},{1,13},{6,2},{10,6},{... | collective-permute-start | bytes 6152 | tf_op jit(solution)/shard_map/ppermute | solution.py:23
  163.8 5.9 %collective-permute-start.12 = (f32[32,1,130]{2,1,0:T(1,128)S(1)}, f32[32,1,130]{2,1,0:T(1,128)S(1)}, u32[]{:S(2)}, u32[]{:S(2)}) collective-permute-start(f32[32,1,130]{2,1,0:T(1,128)S(1)} %get-tuple-element.44), channel_id=1, source_target_pairs={{1,0},{2,1},{3,2},{5,4},{6,5},{7,6},{9,8},{10,9},{11,10},{13,12},{... | collective-permute-start | bytes 49928 | tf_op jit(solution)/shard_map/ppermute | solution.py:23
  165.1 6.1 %collective-permute-start.13 = (f32[32,1,130]{2,1,0:T(1,128)S(1)}, f32[32,1,130]{2,1,0:T(1,128)S(1)}, u32[]{:S(2)}, u32[]{:S(2)}) collective-permute-start(f32[32,1,130]{2,1,0:T(1,128)S(1)} %get-tuple-element.45), channel_id=1, source_target_pairs={{0,1},{1,2},{2,3},{4,5},{5,6},{6,7},{8,9},{9,10},{10,11},{12,13},{... | collective-permute-start | bytes 49928 | tf_op jit(solution)/shard_map/ppermute | solution.py:22
  172.1 16.3 %copy-start.6 = (f32[32,16,128]{2,1,0:T(8,128)S(1)}, f32[32,16,128]{2,1,0:T(8,128)}, u32[]{:S(2)}) copy-start(f32[32,16,128]{2,1,0:T(8,128)} %copy-done.5) | copy-start | bytes 786436
  172.2 8.1 %collective-permute-start.15 = (f32[32,16,1]{2,1,0:T(8,128)S(1)}, f32[32,16,1]{2,1,0:T(8,128)S(1)}, u32[]{:S(2)}, u32[]{:S(2)}) collective-permute-start(f32[32,16,1]{2,1,0:T(8,128)S(1)} %get-tuple-element.60), channel_id=1, source_target_pairs={{0,4},{4,8},{8,12},{12,0},{1,5},{5,9},{9,13},{13,1},{2,6},{6,10},{... | collective-permute-start | bytes 6152 | tf_op jit(solution)/shard_map/ppermute | solution.py:22
  172.3 8.1 %collective-permute-start.14 = (f32[32,16,1]{2,1,0:T(8,128)S(1)}, f32[32,16,1]{2,1,0:T(8,128)S(1)}, u32[]{:S(2)}, u32[]{:S(2)}) collective-permute-start(f32[32,16,1]{2,1,0:T(8,128)S(1)} %get-tuple-element.61), channel_id=1, source_target_pairs={{4,0},{8,4},{12,8},{0,12},{5,1},{9,5},{13,9},{1,13},{6,2},{10,6},{... | collective-permute-start | bytes 6152 | tf_op jit(solution)/shard_map/ppermute | solution.py:23
  180.6 6.2 %collective-permute-start.16 = (f32[32,1,130]{2,1,0:T(1,128)S(1)}, f32[32,1,130]{2,1,0:T(1,128)S(1)}, u32[]{:S(2)}, u32[]{:S(2)}) collective-permute-start(f32[32,1,130]{2,1,0:T(1,128)S(1)} %get-tuple-element.42), channel_id=1, source_target_pairs={{1,0},{2,1},{3,2},{5,4},{6,5},{7,6},{9,8},{10,9},{11,10},{13,12},{... | collective-permute-start | bytes 49928 | tf_op jit(solution)/shard_map/ppermute | solution.py:23
  181.9 6.4 %collective-permute-start.17 = (f32[32,1,130]{2,1,0:T(1,128)S(1)}, f32[32,1,130]{2,1,0:T(1,128)S(1)}, u32[]{:S(2)}, u32[]{:S(2)}) collective-permute-start(f32[32,1,130]{2,1,0:T(1,128)S(1)} %get-tuple-element.43), channel_id=1, source_target_pairs={{0,1},{1,2},{2,3},{4,5},{5,6},{6,7},{8,9},{9,10},{10,11},{12,13},{... | collective-permute-start | bytes 49928 | tf_op jit(solution)/shard_map/ppermute | solution.py:22
where the time goes:
time: 232 us; the launch traced here: 231 us
  blocking collectives  84.9 us (37%)
  starting transfers between devices  43.7 us (19%)
  waiting for transfers between devices  34.7 us (15%)
  local copies, waits for them, and re-layouts  23.7 us (10%)
  other arithmetic  20.2 us (9%)
  matrix products  16 us (7%)
  between operations  7.26 us (3%)
    psum x2, blocking collectives, paired_sums(): lax.psum((jnp.sum(residual * precond), jnp.sum(image * precond)), ('lon',...  67.5 us
    ppermute x8, waiting for transfers between devices, padded_2(): before = lax.ppermute(last, axis, up)  27.8 us
    ppermute x8, starting transfers between devices, padded_2(): before = lax.ppermute(last, axis, up)  19 us
    ppermute x8, starting transfers between devices, padded_2(): after = lax.ppermute(initial, axis, down)  12.1 us
    unnamed x25, local copies, waits for them, and re-layouts  10.9 us
    all_to_all x1, blocking collectives, precondition(): lax.all_to_all(turned, 'lon', split_axis=2, concat_axis=0, tiled=True)  9.07 us
    all_to_all x1, blocking collectives, precondition(): lax.all_to_all(residual, 'lon', split_axis=0, concat_axis=2, tiled=True)  8.38 us
    ppermute x1, waiting for transfers between devices, shifted(): return lax.ppermute(x, axis, [(i, (i + by) % size) for i in range(size)])  5.71 us
  transfers between devices with their start and end apart: 20, of which 11 were waited for; matrix products, arithmetic and copies ran while one was open for 10% of the time, Pallas kernels for 0%

commit v1 on v0

v1 whole, which is shorter than its diff:
```python
import functools
import math

import jax
import jax.numpy as jnp
import numpy as np
from jax import lax
from jax.experimental import pallas as pl
from jax.experimental.pallas import tpu as pltpu
from jax.sharding import PartitionSpec as P

base_kappa = 0.001
base_conduct = 1.0

SCALE = 2.0**-31
REACH = 4
EDGE = 8

HIGHEST = lax.Precision.HIGHEST


def dot(a, b):
    return jnp.dot(a, b, precision=HIGHEST, preferred_element_type=jnp.float32)


def circle_kernel(total):
    middle = 2.0 + base_kappa / base_conduct
    rho = (middle - math.sqrt(middle * middle - 4.0)) / 2.0
    height = 1.0 / (1.0 / rho - rho) / base_conduct
    wrap = rho**total
    shift = (1.0 + rho * rho) / (1.0 - rho * rho) + total * wrap / (1.0 - wrap)
    front = height * height / (1.0 - wrap)
    return rho, front, shift


def circle_matrices(count, columns):
    total = count * columns
    rho, front, shift = circle_kernel(total)

    def one_side(n):
        return front * rho**n * (n + shift)

    def both_sides(n):
        return one_side(n) + one_side(total - n)

    place = np.arange(columns)
    rows = columns + 2 * EDGE
    x = np.arange(rows) - EDGE
    used = (x >= -2) & (x < columns + 2)
    near = both_sides(np.abs(x[:, None] - place[None, :])) * used[:, None]
    back = columns - 1 - place
    moments = np.zeros((8, columns))
    moments[0] = rho**place
    moments[1] = place * rho**place
    moments[2] = rho**back
    moments[3] = back * rho**back

    def block(offset):
        a = columns * offset - x
        b = total - columns * offset + x - (columns - 1)
        out = np.zeros((rows, 8))
        out[:, 0] = front * rho**a * (a + shift)
        out[:, 1] = front * rho**a
        out[:, 2] = front * rho**b * (b + shift)
        out[:, 3] = front * rho**b
        amend = both_sides(1) - both_sides(-1)
        if offset == 1:
            out[EDGE + columns + 1, 4] = amend
        if offset == count - 1:
            out[EDGE - 2, 4] += amend
        return out * used[:, None]

    others = [block(count - d) for d in range(2, count - 1)]
    far = np.stack(
        [
            np.concatenate([block(1), block(count - 1)] + others, axis=1),
            np.concatenate([block(count - 1), block(1)] + others, axis=1),
        ]
    )
    as_f32 = lambda m: np.asarray(m, np.float32)
    return as_f32(near), as_f32(moments), as_f32(far)


def pair_perms(count, wrap):
    first = [(i, i + 1) for i in range(0, count - 1, 2)]
    second = [(i, i + 1) for i in range(1, count - 1, 2)]
    if wrap:
        second.append((count - 1, 0))
    both = lambda pairs: pairs + [(j, i) for i, j in pairs]
    return both(first), both(second)


def whole(n):
    return [pl.BlockSpec(memory_space=pltpu.VMEM)] * n


def call(kernel, outs, *args, scratch=()):
    return pl.pallas_call(
        kernel,
        out_shape=[jax.ShapeDtypeStruct(s, jnp.float32) for s in outs],
        in_specs=whole(len(args)),
        out_specs=whole(len(outs)),
        scratch_shapes=[pltpu.VMEM(s, jnp.float32) for s in scratch],
    )(*args)


KINDS = 6


def band_kernel(rows, levels, noise, kappa2, conduct, land, first, second):
    odd = lax.axis_index("lat") % 2
    top = rows - REACH
    for out, start in ((first, (1 - odd) * top), (second, odd * top)):
        for kind in range(KINDS):
            for j in range(REACH):
                at = pl.ds(start + j, levels, stride=rows)
                if kind == 0:
                    plane = noise[at, :]
                elif kind == 1:
                    plane = land[at, :].astype(jnp.float32)
                elif kind == 2:
                    plane = conduct[1, at, :]
                elif kind == 3:
                    plane = kappa2[at, :]
                elif kind == 4:
                    plane = conduct[0, at, :]
                else:
                    plane = conduct[2, at, :]
                out[kind * REACH + j] = plane


def prepare_kernel(
    rows, levels, columns,
    noise, kappa2, conduct, land, got_first, got_second, weights,
    field, statics, to_first, to_second,
):
    lat_odd = lax.axis_index("lat") % 2
    last_band = lax.axis_index("lat") == lax.axis_size("lat") - 1
    lon_odd = lax.axis_index("lon") % 2
    lanes = (rows + 2 * REACH) * levels
    group = REACH * levels

    def ghost(kind, north):
        a = got_first[pl.ds(kind * REACH, REACH)].reshape(group, columns)
        b = got_second[pl.ds(kind * REACH, REACH)].reshape(group, columns)
        from_first = (lat_odd == 0) if north else (lat_odd == 1)
        return jnp.where(from_first, a, b)

    def turned(kind, load):
        blocks = [ghost(kind, False)]
        for j in range(0, rows, REACH):
            blocks.append(jnp.concatenate([load(pl.ds(j + i, levels, stride=rows)) for i in range(REACH)], axis=0))
        blocks.append(ghost(kind, True))
        return jnp.concatenate([b.T for b in blocks], axis=1)

    r = turned(0, lambda at: noise[at, :])
    field[...] = r
    ocean = turned(1, lambda at: land[at, :].astype(jnp.float32))
    north = turned(2, lambda at: conduct[1, at, :])
    kappa = turned(3, lambda at: kappa2[at, :])
    east = turned(4, lambda at: conduct[0, at, :])
    upper = turned(5, lambda at: conduct[2, at, :])
    lane = lax.broadcasted_iota(jnp.int32, (1, lanes), 1)
    top = (rows + REACH - 1) * levels
    ends = last_band & (lane >= top) & (lane < top + levels)
    north = jnp.where(ends, 0.0, north)
    upper = jnp.where(lane % levels == levels - 1, 0.0, upper)
    row = lax.broadcasted_iota(jnp.int32, (columns, 1), 0)
    west = jnp.where(row == 0, 0.0, pltpu.roll(east, 1, 0))
    ocean_east = jnp.where(row == columns - 1, 1.0, pltpu.roll(ocean, columns - 1, 0))
    diagonal = ocean * (
        kappa + east + west + north + pltpu.roll(north, levels, 1) + upper + pltpu.roll(upper, 1, 1)
    )
    to_east = east * ocean * ocean_east
    to_north = north * ocean * pltpu.roll(ocean, lanes - levels, 1)
    to_upper = upper * ocean * pltpu.roll(ocean, lanes - 1, 1)
    statics[0] = diagonal
    statics[1] = to_east
    statics[2] = to_north
    statics[3] = to_upper
    statics[4] = ocean
    statics[5] = east
    m = dot(weights[...], r)[:4]
    end = columns - 1
    blank = jnp.zeros((5, lanes), jnp.float32)
    for_east = [m, r[end:], diagonal[end:], to_east[end - 1 : end], east[end:], ocean[end:], to_north[end:], to_upper[end:], blank]
    for_west = [m, r[:1], diagonal[:1], to_east[:1], east[:1], ocean[:1], to_north[:1], to_upper[:1], blank]
    for_east = jnp.concatenate(for_east, axis=0)
    for_west = jnp.concatenate(for_west, axis=0)
    to_first[...] = jnp.where(lon_odd == 0, for_east, for_west)
    to_second[...] = jnp.where(lon_odd == 0, for_west, for_east)


def circle(near, far, own, received):
    lon_odd = lax.axis_index("lon") % 2
    told = jnp.concatenate([t[0:8] for t in received], axis=0)
    return dot(near[...], own) + dot(far[lon_odd], told)


def stencil(v, east_v, west_v, d, e, w, n, u, levels):
    lanes = v.shape[1]
    return (
        d * v
        - e * east_v
        - w * west_v
        - n * pltpu.roll(v, lanes - levels, 1)
        - pltpu.roll(n * v, levels, 1)
        - u * pltpu.roll(v, lanes - 1, 1)
        - pltpu.roll(u * v, 1, 1)
    )


def apply_twice(levels, columns, v, f, diagonal, to_east, north, upper, ocean, rim):
    own = pl.ds(EDGE, columns)
    after = pl.ds(EDGE + 1, columns)
    before = pl.ds(EDGE - 1, columns)
    end = EDGE + columns
    e, w = to_east[own], to_east[before]
    f[own] = stencil(v[own], v[after], v[before], diagonal[...], e, w, north, upper, levels)
    pick = lambda a, b: jnp.concatenate([v[a : a + 1], v[b : b + 1], jnp.zeros((6, v.shape[1]), jnp.float32)], axis=0)
    g = stencil(
        pick(EDGE - 1, end), pick(EDGE, end + 1), pick(EDGE - 2, end - 1),
        rim[0], rim[1], rim[2], rim[3], rim[4], levels,
    )
    f[EDGE - 1 : EDGE] = g[0:1]
    f[end : end + 1] = g[1:2]
    second = stencil(f[own], f[after], f[before], diagonal[...], e, w, north, upper, levels)
    return jnp.where(ocean > 0.5, second, v[own])


def first_kernel(
    levels, columns, others,
    field, statics, near, far, weights, mine_first, mine_second, *rest,
):
    received = rest[: 2 + others]
    precond, image, diagonal, to_east, rim, to_first, to_second, v, f = rest[2 + others :]
    lon_odd = lax.axis_index("lon") % 2
    even = lon_odd == 0
    a, b = received[0][...], received[1][...]
    east_list = jnp.where(even, a, b)
    west_list = jnp.where(even, b, a)
    v[...] = circle(near, far, field[...], received)
    ocean = statics[4]
    end = columns - 1
    row = lax.broadcasted_iota(jnp.int32, (columns, 1), 0)
    full_east = jnp.where(row == end, statics[1] * east_list[8:9], statics[1])
    to_east[pl.ds(EDGE, columns)] = full_east
    face_west = west_list[7:8] * west_list[8:9] * ocean[0:1]
    to_east[EDGE - 1 : EDGE] = face_west
    diagonal[...] = statics[0] + jnp.where(row == 0, ocean * west_list[7:8], 0.0)
    blank = jnp.zeros((6, ocean.shape[1]), jnp.float32)
    stack = lambda p, q: jnp.concatenate([p, q, blank], axis=0)
    rim[0] = stack(west_list[5:6], east_list[5:6] + east_list[8:9] * statics[5, end:])
    rim[1] = stack(face_west, east_list[6:7])
    rim[2] = stack(west_list[6:7], full_east[end:])
    rim[3] = stack(west_list[9:10], east_list[9:10])
    rim[4] = stack(west_list[10:11], east_list[10:11])
    w0 = apply_twice(levels, columns, v, f, diagonal, to_east, statics[2], statics[3], ocean, rim)
    precond[...] = v[pl.ds(EDGE, columns)]
    image[...] = w0
    scaled = w0 * SCALE
    m = dot(weights[...], scaled)[:4]
    pad = jnp.zeros((3, m.shape[1]), jnp.float32)
    for_east = jnp.concatenate([m, scaled[end:], pad], axis=0)
    for_west = jnp.concatenate([m, scaled[:1], pad], axis=0)
    to_first[...] = jnp.where(even, for_east, for_west)
    to_second[...] = jnp.where(even, for_west, for_east)


def second_kernel(
    levels, columns, rows, others,
    field, precond, image, statics, near, far, diagonal, to_east, rim, *rest,
):
    received = rest[: 2 + others]
    again, along, sums, v, f = rest[2 + others :]
    v[...] = circle(near, far, image[...] * SCALE, received)
    out = apply_twice(levels, columns, v, f, diagonal, to_east, statics[2], statics[3], statics[4], rim)
    own = slice(REACH * levels, (REACH + rows) * levels)
    again[...] = v[pl.ds(EDGE, columns)][:, own]
    along[...] = out[:, own]
    r, p, w = field[:, own], precond[:, own], image[:, own]
    q, z = again[...], along[...]

    def part(x):
        s = jnp.sum(x, axis=0, keepdims=True)
        return sum(s[:, k : k + 128] for k in range(0, s.shape[1], 128))

    parts = [part(r * p), part(p * w), part(w * q), part(q * z), jnp.zeros((4, 128), jnp.float32)]
    sums[...] = jnp.concatenate(parts, axis=0)


def combine_kernel(rows, levels, sums, noise, precond, image, again, along, answer, left):
    total = jnp.sum(sums[...], axis=1, keepdims=True)
    energy, curve, mixed, last = total[0:1], total[1:2], total[2:3], total[3:4]
    alpha = energy / curve
    beta = alpha / SCALE
    growth = alpha * beta * mixed / energy
    step = energy * (growth - 1.0) / (beta * beta * last - growth * growth * curve)
    keep = alpha + step * growth
    back = step * beta
    own = slice(REACH * levels, (REACH + rows) * levels)
    x = keep * precond[:, own] - back * again[...]
    y = keep * image[:, own] - back * along[...]
    group = REACH * levels
    for j in range(0, rows, REACH):
        at = slice(j * levels, j * levels + group)
        xt, yt = x[:, at].T, y[:, at].T
        for i in range(REACH):
            part = slice(i * levels, (i + 1) * levels)
            to = pl.ds(j + i, levels, stride=rows)
            answer[to, :] = xt[part]
            left[to, :] = noise[to, :] - yt[part]


def summed(x, axis):
    count = lax.axis_size(axis)
    step = 1
    while step < count:
        x = x + lax.ppermute(x, axis, [(i, i ^ step) for i in range(count)])
        step *= 2
    return x


def body(near, weights, far, noise, kappa2, conduct, land):
    levels, rows, columns = noise.shape
    count = lax.axis_size("lon")
    others = count - 3
    flat = levels * rows
    lanes = (rows + 2 * REACH) * levels
    tall = columns + 2 * EDGE
    noise = noise.reshape(flat, columns)
    kappa2 = kappa2.reshape(flat, columns)
    land = land.reshape(flat, columns)
    conduct = conduct.reshape(3, flat, columns)

    planes = (KINDS * REACH, levels, columns)
    first, second = call(functools.partial(band_kernel, rows, levels), [planes, planes], noise, kappa2, conduct, land)
    perm_a, perm_b = pair_perms(lax.axis_size("lat"), False)
    got_first = lax.ppermute(first, "lat", perm_a)
    got_second = lax.ppermute(second, "lat", perm_b)

    field, statics, to_first, to_second = call(
        functools.partial(prepare_kernel, rows, levels, columns),
        [(columns, lanes), (6, columns, lanes), (16, lanes), (16, lanes)],
        noise, kappa2, conduct, land, got_first, got_second, weights,
    )
    lon_a, lon_b = pair_perms(count, True)

    def exchange(one, two):
        got = [lax.ppermute(one, "lon", lon_a), lax.ppermute(two, "lon", lon_b)]
        for d in range(2, count - 1):
            got.append(lax.ppermute(one[:8], "lon", [(i, (i + d) % count) for i in range(count)]))
        return got

    told = exchange(to_first, to_second)
    precond, image, diagonal, to_east, rim, to_first2, to_second2 = call(
        functools.partial(first_kernel, levels, columns, others),
        [(columns, lanes), (columns, lanes), (columns, lanes), (tall, lanes), (5, 8, lanes), (8, lanes), (8, lanes)],
        field, statics, near, far, weights, to_first, to_second, *told,
        scratch=[(tall, lanes), (tall, lanes)],
    )
    told = exchange(to_first2, to_second2)
    again, along, sums = call(
        functools.partial(second_kernel, levels, columns, rows, others),
        [(columns, flat), (columns, flat), (8, 128)],
        field, precond, image, statics, near, far, diagonal, to_east, rim, *told,
        scratch=[(tall, lanes), (tall, lanes)],
    )
    sums = summed(summed(sums, "lon"), "lat")
    answer, left = call(
        functools.partial(combine_kernel, rows, levels),
        [(flat, columns), (flat, columns)],
        sums, noise, precond, image, again, along,
    )
    return answer.reshape(levels, rows, columns), left.reshape(levels, rows, columns)


def solution(mesh):
    def run(noise, kappa2, conduct, land):
        count = mesh.shape["lon"]
        near, weights, far = circle_matrices(count, noise.shape[2] // count)
        return jax.shard_map(
            functools.partial(body, near, weights, far),
            mesh=mesh,
            in_specs=(
                P("ens", "lat", "lon"),
                P(None, "lat", "lon"),
                P(None, None, "lat", "lon"),
                P(None, "lat", "lon"),
            ),
            out_specs=(P("ens", "lat", "lon"), P("ens", "lat", "lon")),
            check_vma=False,
        )(noise, kappa2, conduct, land)

    return run
```

time: 232 us -> 61.4 us (0.26)
  blocking collectives: 84.9 us -> 0 us
  starting transfers between devices: 43.7 us -> 15.3 us
  local copies, waits for them, and re-layouts: 23.7 us -> 3.51 us
  other arithmetic: 20.2 us -> 1.27 us
  Pallas kernels: 0 us -> 18.4 us
  matrix products: 16 us -> 0 us
  waiting for transfers between devices: 34.7 us -> 21.9 us
  between operations: 7.26 us -> 0.68 us
    psum x2 -> x0, blocking collectives: 67.5 us -> none  [paired_sums(): lax.psum((jnp.sum(residual * precond), jnp.sum(image * precond)), ('lon',...]
    ppermute x18 -> x12, starting transfers between devices: 35.7 us -> 15.3 us  [the longest x4 7.61 us: summed(): x = x + lax.ppermute(x, axis, [(i, i ^ step) for i in range(count)])]
    pallas_call x0 -> x5, Pallas kernels: none -> 18.4 us  [call(): pl.pallas_call(kernel, out_shape=[jax.ShapeDtypeStruct(s, jnp.float32) fo...]
    all_to_all x2 -> x0, blocking collectives: 17.4 us -> none  [the longest x1 9.07 us: precondition(): lax.all_to_all(turned, 'lon', split_axis=2, concat_axis=0, tiled=True)]
    dot_general x24 -> x0, matrix products: 16 us -> none  [the longest x2 1.85 us: spectral(): section_real = jnp.einsum('pqab,ak->pqkb', shaped, cos_a, precision=highest)]
    ppermute x18 -> x12, waiting for transfers between devices: 33.8 us -> 21.9 us  [the longest x1 8.64 us: body(): got_first = lax.ppermute(first, 'lat', perm_a)]
    unnamed x25 -> x16, local copies, waits for them, and re-layouts: 10.9 us -> 2.77 us
    all_to_all x2 -> x0, starting transfers between devices: 7.97 us -> none  [the longest x1 4.38 us: precondition(): lax.all_to_all(residual, 'lon', split_axis=0, concat_axis=2, tiled=True)]
  transfers between devices with their start and end apart: 20 -> 12, of which waited for: 11 -> 8; matrix products, arithmetic and copies ran while one was open for 10% -> 1% of each run, Pallas kernels for 0% -> 0%
where the time goes in v1:
time: 61.4 us; the launch traced here: 61.1 us
  waiting for transfers between devices  21.9 us (36%)
  Pallas kernels  18.4 us (30%)
  starting transfers between devices  15.3 us (25%)
  local copies, waits for them, and re-layouts  3.51 us (6%)
  other arithmetic  1.27 us (2%)
  between operations  0.68 us (1%)
    pallas_call x5, Pallas kernels, call(): pl.pallas_call(kernel, out_shape=[jax.ShapeDtypeStruct(s, jnp.float32) fo...  18.4 us
    ppermute x1, waiting for transfers between devices, body(): got_first = lax.ppermute(first, 'lat', perm_a)  8.64 us
    ppermute x4, starting transfers between devices, summed(): x = x + lax.ppermute(x, axis, [(i, i ^ step) for i in range(count)])  7.61 us
    ppermute x4, waiting for transfers between devices, summed(): x = x + lax.ppermute(x, axis, [(i, i ^ step) for i in range(count)])  7.56 us
    ppermute x2, waiting for transfers between devices, exchange(): lax.ppermute(one[:8], 'lon', [(i, (i + d) % count) for i in range(count)])  4.09 us
    ppermute x4, starting transfers between devices, exchange(): got = [lax.ppermute(one, 'lon', lon_a), lax.ppermute(two, 'lon', lon_b)]  3.15 us
    ppermute x1, starting transfers between devices, body(): got_first = lax.ppermute(first, 'lat', perm_a)  3.05 us
    unnamed x16, local copies, waits for them, and re-layouts  2.77 us
  transfers between devices with their start and end apart: 12, of which 8 were waited for; matrix products, arithmetic and copies ran while one was open for 1% of the time, Pallas kernels for 0%

profile of v1, /device:TPU:0, one launch (start us, length us, event | category | flops | bytes accessed | tf_op | source)
XLA Modules:
  0.0 61.1 jit_solution(7829029039729037295)
XLA Ops:
  0.6 2.5 %shard_map.86 = (f32[24,32,128]{2,1,0:T(8,128)}, f32[24,32,128]{2,1,0:T(8,128)}) custom-call(f32[512,128]{1,0:T(8,128)} %bitcast.8, f32[512,128]{1,0:T(8,128)} %bitcast.11, f32[3,512,128]{2,1,0:T(8,128)} %bitcast.6, s32[512,128]{1,0:T(8,128)} %bitcast.13), custom_call_target="tpu_custom_call" | custom-call | tf_op jit(solution)/shard_map/pallas_call | solution.py:98
  3.1 3.1 %collective-permute-start = (f32[24,32,128]{2,1,0:T(8,128)}, f32[24,32,128]{2,1,0:T(8,128)S(1)}, u32[]{:S(2)}, u32[]{:S(2)}) collective-permute-start(f32[24,32,128]{2,1,0:T(8,128)} %get-tuple-element.20), channel_id=1, source_target_pairs={{0,1},{2,3},{1,0},{3,2},{4,5},{6,7},{5,4},{7,6},{8,9},{10,11},{9,8... | collective-permute-start | bytes 1179656 | tf_op jit(solution)/shard_map/ppermute | solution.py:339
  6.2 0.7 %collective-permute-start.1 = (f32[24,32,128]{2,1,0:T(8,128)}, f32[24,32,128]{2,1,0:T(8,128)S(1)}, u32[]{:S(2)}, u32[]{:S(2)}) collective-permute-start(f32[24,32,128]{2,1,0:T(8,128)} %get-tuple-element.21), channel_id=1, source_target_pairs={{1,2},{2,1},{5,6},{6,5},{9,10},{10,9},{13,14},{14,13},{17,18},{18,... | collective-permute-start | bytes 1179656 | tf_op jit(solution)/shard_map/ppermute | solution.py:340
  6.8 8.6 %collective-permute-done.got_first = f32[24,32,128]{2,1,0:T(8,128)S(1)} collective-permute-done((f32[24,32,128]{2,1,0:T(8,128)}, f32[24,32,128]{2,1,0:T(8,128)S(1)}, u32[]{:S(2)}, u32[]{:S(2)}) %collective-permute-start) | collective-permute-done | bytes 393248 | tf_op jit(solution)/shard_map/ppermute | solution.py:339
  15.5 0.0 copy-start
  15.5 0.0 collective-permute-done.1.got_second
  15.5 0.8 %copy-done = f32[24,32,128]{2,1,0:T(8,128)} copy-done((f32[24,32,128]{2,1,0:T(8,128)}, f32[24,32,128]{2,1,0:T(8,128)S(1)}, u32[]{:S(2)}) %copy-start) | copy-done | bytes 393240
  16.3 0.0 copy-start.1
  16.3 0.7 %copy-done.1 = f32[24,32,128]{2,1,0:T(8,128)} copy-done((f32[24,32,128]{2,1,0:T(8,128)}, f32[24,32,128]{2,1,0:T(8,128)S(1)}, u32[]{:S(2)}) %copy-start.1) | copy-done | bytes 393240
  17.0 4.3 %shard_map.87 = (f32[128,768]{1,0:T(8,128)}, f32[6,128,768]{2,1,0:T(8,128)}, f32[16,768]{1,0:T(8,128)}, f32[16,768]{1,0:T(8,128)}) custom-call(f32[512,128]{1,0:T(8,128)} %bitcast.9, f32[512,128]{1,0:T(8,128)} %bitcast.12, f32[3,512,128]{2,1,0:T(8,128)} %bitcast.7, s32[512,128]{1,0:T(8,128)} %bitcast.14, f32[24,32,128]{2,1,0:T(8,128)} %copy-done, ...), custom_call_target="tpu_custom_call" | custom-call | tf_op jit(solution)/shard_map/pallas_call | solution.py:98
  21.3 0.2 collective-permute-start.3
  21.5 1.5 %collective-permute-start.2 = (f32[16,768]{1,0:T(8,128)}, f32[16,768]{1,0:T(8,128)S(1)}, u32[]{:S(2)}, u32[]{:S(2)}) collective-permute-start(f32[16,768]{1,0:T(8,128)} %get-tuple-element.24.mine_first), channel_id=1, source_target_pairs={{0,4},{8,12},{4,0},{12,8},{1,5},{9,13},{5,1},{13,9},{2,6},{10,14},... | collective-permute-start | bytes 147464 | tf_op jit(solution)/shard_map/ppermute | solution.py:350
  23.1 0.7 %slice.3 = f32[8,768]{1,0:T(8,128)S(1)} slice(f32[16,768]{1,0:T(8,128)} %get-tuple-element.24.mine_first), slice={[0:8], [0:768]} | slice | bytes 49152 | tf_op jit(solution)/shard_map/slice | solution.py:352
  23.8 0.4 collective-permute-start.4
  24.2 3.5 %collective-permute-done.4.rest_2_ = f32[8,768]{1,0:T(8,128)S(1)} collective-permute-done((f32[8,768]{1,0:T(8,128)S(1)}, f32[8,768]{1,0:T(8,128)S(1)}, u32[]{:S(2)}, u32[]{:S(2)}) %collective-permute-start.4) | collective-permute-done | bytes 24608 | tf_op jit(solution)/shard_map/ppermute | solution.py:352
  27.6 0.0 copy-start.7
  27.6 0.0 collective-permute-done.3.rest_1_
  27.6 0.0 copy-start.2
  27.6 0.0 collective-permute-done.2.rest_0_
  27.7 0.0 copy-start.3
  27.7 0.6 copy-done.7
  28.3 0.0 copy-done.2
  28.3 0.0 copy-done.3
  28.3 4.4 %shard_map.88 = (f32[128,768]{1,0:T(8,128)}, f32[128,768]{1,0:T(8,128)}, f32[128,768]{1,0:T(8,128)}, f32[144,768]{1,0:T(8,128)}, f32[5,8,768]{2,1,0:T(8,128)}, /*index=5*/f32[8,768]{1,0:T(8,128)}, f32[8,768]{1,0:T(8,128)}) custom-call(f32[128,768]{1,0:T(8,128)} %get-tuple-element.22.field, f32[6,128,768]{2,1,0:T(8,128)} %get-tuple-element.23.statics, ...), custom_call_target="tpu_custom_call" | custom-call | tf_op jit(solution)/shard_map/pallas_call | solution.py:98
  32.8 0.0 collective-permute-start.6
  32.8 0.5 collective-permute-start.7
  33.2 1.4 %collective-permute-start.5 = (f32[8,768]{1,0:T(8,128)}, f32[8,768]{1,0:T(8,128)S(1)}, u32[]{:S(2)}, u32[]{:S(2)}) collective-permute-start(f32[8,768]{1,0:T(8,128)} %get-tuple-element.31), channel_id=1, source_target_pairs={{0,4},{8,12},{4,0},{12,8},{1,5},{9,13},{5,1},{13,9},{2,6},{10,14},... | collective-permute-start | bytes 73736 | tf_op jit(solution)/shard_map/ppermute | solution.py:350
  34.6 1.6 %collective-permute-done.6.rest_1_ = f32[8,768]{1,0:T(8,128)S(1)} collective-permute-done((f32[8,768]{1,0:T(8,128)}, f32[8,768]{1,0:T(8,128)S(1)}, u32[]{:S(2)}, u32[]{:S(2)}) %collective-permute-start.6) | collective-permute-done | bytes 24608 | tf_op jit(solution)/shard_map/ppermute | solution.py:350
  36.2 0.0 copy-start.4
  36.2 0.6 %collective-permute-done.7.rest_2_ = f32[8,768]{1,0:T(8,128)S(1)} collective-permute-done((f32[8,768]{1,0:T(8,128)}, f32[8,768]{1,0:T(8,128)S(1)}, u32[]{:S(2)}, u32[]{:S(2)}) %collective-permute-start.7) | collective-permute-done | bytes 24608 | tf_op jit(solution)/shard_map/ppermute | solution.py:352
  36.9 0.0 copy-start.5
  36.9 0.0 collective-permute-done.5.rest_0_
  36.9 0.0 copy-start.6
  36.9 0.0 copy-done.4
  36.9 0.6 copy-done.5
  37.5 0.0 copy-done.6
  37.5 4.6 %shard_map.89 = (f32[128,512]{1,0:T(8,128)}, f32[128,512]{1,0:T(8,128)}, f32[8,128]{1,0:T(8,128)}) custom-call(f32[128,768]{1,0:T(8,128)} %get-tuple-element.22.field, f32[128,768]{1,0:T(8,128)} %get-tuple-element.26.precond, f32[128,768]{1,0:T(8,128)} %get-tuple-element.27.image, f32[6,128,768]{2,1,0:T(8,128)} %get-tuple-element.23.statics, ...), custom_call_target="tpu_custom_call" | custom-call | tf_op jit(solution)/shard_map/pallas_call | solution.py:98
  42.1 0.0 collective-permute-start.8
  42.1 1.4 %collective-permute-done.8 = f32[8,128]{1,0:T(8,128)S(1)} collective-permute-done((f32[8,128]{1,0:T(8,128)}, f32[8,128]{1,0:T(8,128)S(1)}, u32[]{:S(2)}, u32[]{:S(2)}) %collective-permute-start.8) | collective-permute-done | bytes 4128 | tf_op jit(solution)/shard_map/ppermute | solution.py:319
  43.4 0.7 %add.12 = f32[8,128]{1,0:T(8,128)S(1)} add(f32[8,128]{1,0:T(8,128)} %get-tuple-element.33, f32[8,128]{1,0:T(8,128)S(1)} %collective-permute-done.8) | non-fusion elementwise | flops 1024 | bytes 12288 | tf_op jit(solution)/shard_map/add | solution.py:319
  44.1 0.6 collective-permute-start.9
  44.7 3.0 %collective-permute-done.9 = f32[8,128]{1,0:T(8,128)S(1)} collective-permute-done((f32[8,128]{1,0:T(8,128)S(1)}, f32[8,128]{1,0:T(8,128)S(1)}, u32[]{:S(2)}, u32[]{:S(2)}) %collective-permute-start.9) | collective-permute-done | bytes 4128 | tf_op jit(solution)/shard_map/ppermute | solution.py:319
  47.7 3.8 %collective-permute-start.10 = (f32[8,128]{1,0:T(8,128)S(1)}, f32[8,128]{1,0:T(8,128)S(1)}, u32[]{:S(2)}, u32[]{:S(2)}) collective-permute-start(f32[8,128]{1,0:T(8,128)S(1)} %add.13), channel_id=1, source_target_pairs={{0,1},{1,0},{2,3},{3,2},{4,5},{5,4},{6,7},{7,6},{8,9},{9,8},{10,11... | collective-permute-start | bytes 12296 | tf_op jit(solution)/shard_map/ppermute | solution.py:319
  51.5 1.6 %collective-permute-done.10 = f32[8,128]{1,0:T(8,128)S(1)} collective-permute-done((f32[8,128]{1,0:T(8,128)S(1)}, f32[8,128]{1,0:T(8,128)S(1)}, u32[]{:S(2)}, u32[]{:S(2)}) %collective-permute-start.10) | collective-permute-done | bytes 4128 | tf_op jit(solution)/shard_map/ppermute | solution.py:319
  53.1 3.2 %collective-permute-start.11 = (f32[8,128]{1,0:T(8,128)S(1)}, f32[8,128]{1,0:T(8,128)S(1)}, u32[]{:S(2)}, u32[]{:S(2)}) collective-permute-start(f32[8,128]{1,0:T(8,128)S(1)} %add.14), channel_id=1, source_target_pairs={{0,2},{1,3},{2,0},{3,1},{4,6},{5,7},{6,4},{7,5},{8,10},{9,11},{10,... | collective-permute-start | bytes 12296 | tf_op jit(solution)/shard_map/ppermute | solution.py:319
  56.3 1.6 %collective-permute-done.11 = f32[8,128]{1,0:T(8,128)S(1)} collective-permute-done((f32[8,128]{1,0:T(8,128)S(1)}, f32[8,128]{1,0:T(8,128)S(1)}, u32[]{:S(2)}, u32[]{:S(2)}) %collective-permute-start.11) | collective-permute-done | bytes 4128 | tf_op jit(solution)/shard_map/ppermute | solution.py:319
  57.9 0.6 add.15.sums
  58.5 2.6 %shard_map.90 = (f32[512,128]{1,0:T(8,128)}, f32[512,128]{1,0:T(8,128)}) custom-call(f32[8,128]{1,0:T(8,128)} %add.15.sums, f32[512,128]{1,0:T(8,128)} %bitcast.10, f32[128,768]{1,0:T(8,128)} %get-tuple-element.26.precond, f32[128,768]{1,0:T(8,128)} %get-tuple-element.27.image, f32[128,512]{1,0:T(8,128)} %get-tuple-element.34.again, ...), custom_call_target="tpu_custom_call" | custom-call | tf_op jit(solution)/shard_map/pallas_call | solution.py:98
  (2 shorter events, 0.0 us)
Async XLA Ops:
  3.1 12.4 %collective-permute-start = (f32[24,32,128]{2,1,0:T(8,128)}, f32[24,32,128]{2,1,0:T(8,128)S(1)}, u32[]{:S(2)}, u32[]{:S(2)}) collective-permute-start(f32[24,32,128]{2,1,0:T(8,128)} %get-tuple-element.20), channel_id=1, source_target_pairs={{0,1},{2,3},{1,0},{3,2},{4,5},{6,7},{5,4},{7,6},{8,9},{10,11},{9,8... | collective-permute-start | bytes 1179656 | tf_op jit(solution)/shard_map/ppermute | solution.py:339
  6.2 9.3 %collective-permute-start.1 = (f32[24,32,128]{2,1,0:T(8,128)}, f32[24,32,128]{2,1,0:T(8,128)S(1)}, u32[]{:S(2)}, u32[]{:S(2)}) collective-permute-start(f32[24,32,128]{2,1,0:T(8,128)} %get-tuple-element.21), channel_id=1, source_target_pairs={{1,2},{2,1},{5,6},{6,5},{9,10},{10,9},{13,14},{14,13},{17,18},{18,... | collective-permute-start | bytes 1179656 | tf_op jit(solution)/shard_map/ppermute | solution.py:340
  15.5 0.8 %copy-start = (f32[24,32,128]{2,1,0:T(8,128)}, f32[24,32,128]{2,1,0:T(8,128)S(1)}, u32[]{:S(2)}) copy-start(f32[24,32,128]{2,1,0:T(8,128)S(1)} %collective-permute-done.got_first) | copy-start | bytes 1179652
  16.3 0.7 %copy-start.1 = (f32[24,32,128]{2,1,0:T(8,128)}, f32[24,32,128]{2,1,0:T(8,128)S(1)}, u32[]{:S(2)}) copy-start(f32[24,32,128]{2,1,0:T(8,128)S(1)} %collective-permute-done.1.got_second) | copy-start | bytes 1179652
  21.3 6.3 %collective-permute-start.3 = (f32[16,768]{1,0:T(8,128)}, f32[16,768]{1,0:T(8,128)S(1)}, u32[]{:S(2)}, u32[]{:S(2)}) collective-permute-start(f32[16,768]{1,0:T(8,128)} %get-tuple-element.25.mine_second), channel_id=1, source_target_pairs={{4,8},{12,0},{8,4},{0,12},{5,9},{13,1},{9,5},{1,13},{6,10},{14,2},... | collective-permute-start | bytes 147464 | tf_op jit(solution)/shard_map/ppermute | solution.py:350
  21.5 6.1 %collective-permute-start.2 = (f32[16,768]{1,0:T(8,128)}, f32[16,768]{1,0:T(8,128)S(1)}, u32[]{:S(2)}, u32[]{:S(2)}) collective-permute-start(f32[16,768]{1,0:T(8,128)} %get-tuple-element.24.mine_first), channel_id=1, source_target_pairs={{0,4},{8,12},{4,0},{12,8},{1,5},{9,13},{5,1},{13,9},{2,6},{10,14},... | collective-permute-start | bytes 147464 | tf_op jit(solution)/shard_map/ppermute | solution.py:350
  23.8 3.8 %collective-permute-start.4 = (f32[8,768]{1,0:T(8,128)S(1)}, f32[8,768]{1,0:T(8,128)S(1)}, u32[]{:S(2)}, u32[]{:S(2)}) collective-permute-start(f32[8,768]{1,0:T(8,128)S(1)} %slice.3), channel_id=1, source_target_pairs={{0,8},{4,12},{8,0},{12,4},{1,9},{5,13},{9,1},{13,5},{2,10},{6,14},... | collective-permute-start | bytes 73736 | tf_op jit(solution)/shard_map/ppermute | solution.py:352
  27.6 0.6 %copy-start.7 = (f32[8,768]{1,0:T(8,128)}, f32[8,768]{1,0:T(8,128)S(1)}, u32[]{:S(2)}) copy-start(f32[8,768]{1,0:T(8,128)S(1)} %collective-permute-done.4.rest_2_) | copy-start | bytes 73732
  27.6 0.7 %copy-start.2 = (f32[16,768]{1,0:T(8,128)}, f32[16,768]{1,0:T(8,128)S(1)}, u32[]{:S(2)}) copy-start(f32[16,768]{1,0:T(8,128)S(1)} %collective-permute-done.3.rest_1_) | copy-start | bytes 147460
  27.7 0.7 %copy-start.3 = (f32[16,768]{1,0:T(8,128)}, f32[16,768]{1,0:T(8,128)S(1)}, u32[]{:S(2)}) copy-start(f32[16,768]{1,0:T(8,128)S(1)} %collective-permute-done.2.rest_0_) | copy-start | bytes 147460
  32.8 3.5 %collective-permute-start.6 = (f32[8,768]{1,0:T(8,128)}, f32[8,768]{1,0:T(8,128)S(1)}, u32[]{:S(2)}, u32[]{:S(2)}) collective-permute-start(f32[8,768]{1,0:T(8,128)} %get-tuple-element.32), channel_id=1, source_target_pairs={{4,8},{12,0},{8,4},{0,12},{5,9},{13,1},{9,5},{1,13},{6,10},{14,2},... | collective-permute-start | bytes 73736 | tf_op jit(solution)/shard_map/ppermute | solution.py:350
  32.8 4.1 %collective-permute-start.7 = (f32[8,768]{1,0:T(8,128)}, f32[8,768]{1,0:T(8,128)S(1)}, u32[]{:S(2)}, u32[]{:S(2)}) collective-permute-start(f32[8,768]{1,0:T(8,128)} %get-tuple-element.31), channel_id=1, source_target_pairs={{0,8},{4,12},{8,0},{12,4},{1,9},{5,13},{9,1},{13,5},{2,10},{6,14},... | collective-permute-start | bytes 73736 | tf_op jit(solution)/shard_map/ppermute | solution.py:352
  33.2 3.6 %collective-permute-start.5 = (f32[8,768]{1,0:T(8,128)}, f32[8,768]{1,0:T(8,128)S(1)}, u32[]{:S(2)}, u32[]{:S(2)}) collective-permute-start(f32[8,768]{1,0:T(8,128)} %get-tuple-element.31), channel_id=1, source_target_pairs={{0,4},{8,12},{4,0},{12,8},{1,5},{9,13},{5,1},{13,9},{2,6},{10,14},... | collective-permute-start | bytes 73736 | tf_op jit(solution)/shard_map/ppermute | solution.py:350
  36.2 0.6 %copy-start.4 = (f32[8,768]{1,0:T(8,128)}, f32[8,768]{1,0:T(8,128)S(1)}, u32[]{:S(2)}) copy-start(f32[8,768]{1,0:T(8,128)S(1)} %collective-permute-done.6.rest_1_) | copy-start | bytes 73732
  36.9 0.6 copy-start.5
  36.9 0.6 copy-start.6
  42.1 1.4 %collective-permute-start.8 = (f32[8,128]{1,0:T(8,128)}, f32[8,128]{1,0:T(8,128)S(1)}, u32[]{:S(2)}, u32[]{:S(2)}) collective-permute-start(f32[8,128]{1,0:T(8,128)} %get-tuple-element.33), channel_id=1, source_target_pairs={{0,4},{4,0},{8,12},{12,8},{1,5},{5,1},{9,13},{13,9},{2,6},{6,2},{1... | collective-permute-start | bytes 12296 | tf_op jit(solution)/shard_map/ppermute | solution.py:319
  44.1 3.6 %collective-permute-start.9 = (f32[8,128]{1,0:T(8,128)S(1)}, f32[8,128]{1,0:T(8,128)S(1)}, u32[]{:S(2)}, u32[]{:S(2)}) collective-permute-start(f32[8,128]{1,0:T(8,128)S(1)} %add.12), channel_id=1, source_target_pairs={{0,8},{4,12},{8,0},{12,4},{1,9},{5,13},{9,1},{13,5},{2,10},{6,14},... | collective-permute-start | bytes 12296 | tf_op jit(solution)/shard_map/ppermute | solution.py:319
  47.7 5.4 %collective-permute-start.10 = (f32[8,128]{1,0:T(8,128)S(1)}, f32[8,128]{1,0:T(8,128)S(1)}, u32[]{:S(2)}, u32[]{:S(2)}) collective-permute-start(f32[8,128]{1,0:T(8,128)S(1)} %add.13), channel_id=1, source_target_pairs={{0,1},{1,0},{2,3},{3,2},{4,5},{5,4},{6,7},{7,6},{8,9},{9,8},{10,11... | collective-permute-start | bytes 12296 | tf_op jit(solution)/shard_map/ppermute | solution.py:319
  53.1 4.8 %collective-permute-start.11 = (f32[8,128]{1,0:T(8,128)S(1)}, f32[8,128]{1,0:T(8,128)S(1)}, u32[]{:S(2)}, u32[]{:S(2)}) collective-permute-start(f32[8,128]{1,0:T(8,128)S(1)} %add.14), channel_id=1, source_target_pairs={{0,2},{1,3},{2,0},{3,1},{4,6},{5,7},{6,4},{7,5},{8,10},{9,11},{10,... | collective-permute-start | bytes 12296 | tf_op jit(solution)/shard_map/ppermute | solution.py:319

commit v2 on v1

--- a/solution.py
+++ b/solution.py
@@ -94,13 +94,16 @@
     return [pl.BlockSpec(memory_space=pltpu.VMEM)] * n
 
 
-def call(kernel, outs, *args, scratch=()):
+def call(kernel, outs, *args, near_memory=(), scratch=(), last=False):
+    args = [pltpu.with_memory_space_constraint(a, pltpu.VMEM) if k in near_memory else a for k, a in enumerate(args)]
+    kind = jax.ShapeDtypeStruct if last else pltpu.VMEM
     return pl.pallas_call(
         kernel,
-        out_shape=[jax.ShapeDtypeStruct(s, jnp.float32) for s in outs],
+        out_shape=[kind(s, jnp.float32) for s in outs],
         in_specs=whole(len(args)),
         out_specs=whole(len(outs)),
         scratch_shapes=[pltpu.VMEM(s, jnp.float32) for s in scratch],
+        compiler_params=pltpu.CompilerParams(vmem_limit_bytes=24 << 20),
     )(*args)
 
 
@@ -132,7 +135,7 @@
 def prepare_kernel(
     rows, levels, columns,
     noise, kappa2, conduct, land, got_first, got_second, weights,
-    field, statics, to_first, to_second,
+    field, statics, to_first, to_second, to_others,
 ):
     lat_odd = lax.axis_index("lat") % 2
     last_band = lax.axis_index("lat") == lax.axis_size("lat") - 1
@@ -180,7 +183,9 @@
     statics[3] = to_upper
     statics[4] = ocean
     statics[5] = east
-    m = dot(weights[...], r)[:4]
+    m = dot(weights[...], r)
+    to_others[...] = m
+    m = m[:4]
     end = columns - 1
     blank = jnp.zeros((5, lanes), jnp.float32)
     for_east = [m, r[end:], diagonal[end:], to_east[end - 1 : end], east[end:], ocean[end:], to_north[end:], to_upper[end:], blank]
@@ -339,38 +344,39 @@
     got_first = lax.ppermute(first, "lat", perm_a)
     got_second = lax.ppermute(second, "lat", perm_b)
 
-    field, statics, to_first, to_second = call(
+    field, statics, to_first, to_second, to_others = call(
         functools.partial(prepare_kernel, rows, levels, columns),
-        [(columns, lanes), (6, columns, lanes), (16, lanes), (16, lanes)],
-        noise, kappa2, conduct, land, got_first, got_second, weights,
+        [(columns, lanes), (6, columns, lanes), (16, lanes), (16, lanes), (8, lanes)],
+        noise, kappa2, conduct, land, got_first, got_second, weights, near_memory=(4, 5),
     )
     lon_a, lon_b = pair_perms(count, True)
 
-    def exchange(one, two):
+    def exchange(one, two, rest):
         got = [lax.ppermute(one, "lon", lon_a), lax.ppermute(two, "lon", lon_b)]
         for d in range(2, count - 1):
-            got.append(lax.ppermute(one[:8], "lon", [(i, (i + d) % count) for i in range(count)]))
+            got.append(lax.ppermute(rest, "lon", [(i, (i + d) % count) for i in range(count)]))
         return got
 
-    told = exchange(to_first, to_second)
+    told = exchange(to_first, to_second, to_others)
     precond, image, diagonal, to_east, rim, to_first2, to_second2 = call(
         functools.partial(first_kernel, levels, columns, others),
         [(columns, lanes), (columns, lanes), (columns, lanes), (tall, lanes), (5, 8, lanes), (8, lanes), (8, lanes)],
-        field, statics, near, far, weights, to_first, to_second, *told,
+        field, statics, near, far, weights, to_first, to_second, *told, near_memory=(0, 1, 5, 6, *range(7, 9 + others)),
         scratch=[(tall, lanes), (tall, lanes)],
     )
-    told = exchange(to_first2, to_second2)
+    told = exchange(to_first2, to_second2, to_first2)
     again, along, sums = call(
         functools.partial(second_kernel, levels, columns, rows, others),
         [(columns, flat), (columns, flat), (8, 128)],
         field, precond, image, statics, near, far, diagonal, to_east, rim, *told,
+        near_memory=(0, 1, 2, 3, 6, 7, 8, *range(9, 11 + others)),
         scratch=[(tall, lanes), (tall, lanes)],
     )
     sums = summed(summed(sums, "lon"), "lat")
     answer, left = call(
         functools.partial(combine_kernel, rows, levels),
         [(flat, columns), (flat, columns)],
-        sums, noise, precond, image, again, along,
+        sums, noise, precond, image, again, along, near_memory=(0, 2, 3, 4, 5), last=True,
     )
     return answer.reshape(levels, rows, columns), left.reshape(levels, rows, columns)
 

time: 61.4 us -> 50.2 us (0.82)
  Pallas kernels: 18.4 us -> 6.84 us
  other arithmetic: 1.27 us -> 0.01 us
  local copies, waits for them, and re-layouts: 3.51 us -> 4.69 us
  starting transfers between devices: 15.3 us -> 16.3 us
    pallas_call x5, Pallas kernels: 18.4 us -> 6.84 us  [call(): pl.pallas_call(kernel, out_shape=[kind(s, jnp.float32) for s in outs], in...]
    unnamed x16 -> x18, local copies, waits for them, and re-layouts: 2.77 us -> 4.69 us
    add x4, other arithmetic: 1.27 us -> 0.01 us  [summed(): x = x + lax.ppermute(x, axis, [(i, i ^ step) for i in range(count)])]
    ppermute x4, starting transfers between devices: 7.61 us -> 8.49 us  [summed(): x = x + lax.ppermute(x, axis, [(i, i ^ step) for i in range(count)])]
    slice x1 -> x0, local copies, waits for them, and re-layouts: 0.74 us -> none  [exchange(): one[:8]]
  transfers between devices with their start and end apart: 12 -> 12, of which waited for: 8 -> 8; matrix products, arithmetic and copies ran while one was open for 1% -> 0% of each run, Pallas kernels for 0% -> 0%
where the time goes in v2:
time: 50.2 us; the launch traced here: 49.9 us
  waiting for transfers between devices  21.3 us (42%)
  starting transfers between devices  16.3 us (32%)
  Pallas kernels  6.84 us (14%)
  local copies, waits for them, and re-layouts  4.69 us (9%)
  between operations  0.72 us (1%)
    ppermute x4, starting transfers between devices, summed(): x = x + lax.ppermute(x, axis, [(i, i ^ step) for i in range(count)])  8.49 us
    ppermute x1, waiting for transfers between devices, body(): got_first = lax.ppermute(first, 'lat', perm_a)  8.43 us
    ppermute x4, waiting for transfers between devices, summed(): x = x + lax.ppermute(x, axis, [(i, i ^ step) for i in range(count)])  7.3 us
    pallas_call x5, Pallas kernels, call(): pl.pallas_call(kernel, out_shape=[kind(s, jnp.float32) for s in outs], in...  6.84 us
    unnamed x18, local copies, waits for them, and re-layouts  4.69 us
    ppermute x2, waiting for transfers between devices, exchange(): lax.ppermute(rest, 'lon', [(i, (i + d) % count) for i in range(count)])  4.15 us
    ppermute x1, starting transfers between devices, body(): got_first = lax.ppermute(first, 'lat', perm_a)  3.12 us
    ppermute x4, starting transfers between devices, exchange(): got = [lax.ppermute(one, 'lon', lon_a), lax.ppermute(two, 'lon', lon_b)]  2.95 us
  transfers between devices with their start and end apart: 12, of which 8 were waited for; matrix products, arithmetic and copies ran while one was open for 0% of the time, Pallas kernels for 0%

profile of v2, /device:TPU:0, one launch (start us, length us, event | category | flops | bytes accessed | tf_op | source)
XLA Modules:
  0.0 49.9 jit_solution(17158041103141970660)
XLA Ops:
  0.6 0.0 copy-start.8
  0.6 0.0 copy-start
  0.7 1.1 %copy-done = f32[3,32,16,128]{3,2,1,0:T(8,128)S(1)} copy-done((f32[3,32,16,128]{3,2,1,0:T(8,128)S(1)}, f32[3,32,16,128]{3,2,1,0:T(8,128)}, u32[]{:S(2)}) %copy-start) | copy-done | bytes 786456
  1.8 0.0 copy-start.1
  1.8 0.9 %copy-done.1 = f32[32,16,128]{2,1,0:T(8,128)S(1)} copy-done((f32[32,16,128]{2,1,0:T(8,128)S(1)}, f32[32,16,128]{2,1,0:T(8,128)}, u32[]{:S(2)}) %copy-start.1) | copy-done | bytes 262168
  2.7 0.0 copy-start.3
  2.7 0.9 %copy-done.3 = f32[32,16,128]{2,1,0:T(8,128)S(1)} copy-done((f32[32,16,128]{2,1,0:T(8,128)S(1)}, f32[32,16,128]{2,1,0:T(8,128)}, u32[]{:S(2)}) %copy-start.3) | copy-done | bytes 262168
  3.7 0.0 copy-start.4
  3.7 0.9 %copy-done.4 = s32[32,16,128]{2,1,0:T(8,128)S(1)} copy-done((s32[32,16,128]{2,1,0:T(8,128)S(1)}, s32[32,16,128]{2,1,0:T(8,128)}, u32[]{:S(2)}) %copy-start.4) | copy-done | bytes 262168
  4.6 0.0 copy-start.5
  4.6 0.0 copy-start.6
  4.6 0.2 shard_map.86
  4.9 3.1 %collective-permute-start = (f32[24,32,128]{2,1,0:T(8,128)S(1)}, f32[24,32,128]{2,1,0:T(8,128)S(1)}, u32[]{:S(2)}, u32[]{:S(2)}) collective-permute-start(f32[24,32,128]{2,1,0:T(8,128)S(1)} %get-tuple-element.21), channel_id=1, source_target_pairs={{0,1},{2,3},{1,0},{3,2},{4,5},{6,7},{5,4},{7,6},{8,9},{10,11},{9,8... | collective-permute-start | bytes 1179656 | tf_op jit(solution)/shard_map/ppermute | solution.py:344
  8.0 0.7 %collective-permute-start.1 = (f32[24,32,128]{2,1,0:T(8,128)S(1)}, f32[24,32,128]{2,1,0:T(8,128)S(1)}, u32[]{:S(2)}, u32[]{:S(2)}) collective-permute-start(f32[24,32,128]{2,1,0:T(8,128)S(1)} %get-tuple-element.22), channel_id=1, source_target_pairs={{1,2},{2,1},{5,6},{6,5},{9,10},{10,9},{13,14},{14,13},{17,18},{18,... | collective-permute-start | bytes 1179656 | tf_op jit(solution)/shard_map/ppermute | solution.py:345
  8.7 8.4 %collective-permute-done.got_first = f32[24,32,128]{2,1,0:T(8,128)S(1)} collective-permute-done((f32[24,32,128]{2,1,0:T(8,128)S(1)}, f32[24,32,128]{2,1,0:T(8,128)S(1)}, u32[]{:S(2)}, u32[]{:S(2)}) %collective-permute-start) | collective-permute-done | bytes 393248 | tf_op jit(solution)/shard_map/ppermute | solution.py:344
  17.1 0.0 collective-permute-done.1.got_second
  17.1 0.0 copy-start.7
  17.1 0.7 %copy-done.7 = f32[8,128]{1,0:T(8,128)S(1)} copy-done((f32[8,128]{1,0:T(8,128)S(1)}, f32[8,128]{1,0:T(8,128)}, u32[]{:S(2)}) %copy-start.7) | copy-done | bytes 4120
  17.8 1.4 %shard_map.87 = (f32[128,768]{1,0:T(8,128)S(1)}, f32[6,128,768]{2,1,0:T(8,128)S(1)}, f32[16,768]{1,0:T(8,128)S(1)}, f32[16,768]{1,0:T(8,128)S(1)}, f32[8,768]{1,0:T(8,128)S(1)}) custom-call(f32[512,128]{1,0:T(8,128)S(1)} %bitcast.9, f32[512,128]{1,0:T(8,128)S(1)} %bitcast.12, f32[3,512,128]{2,1,0:T(8,128)S(1)} %bitcast.7, s32[512,128]{1,0:T(8,128)S(1)} %bitcast.14, ...), custom_call_target="tpu_custom_call" | custom-call | tf_op jit(solution)/shard_map/pallas_call | solution.py:100
  19.3 0.1 collective-permute-start.2
  19.3 1.8 %collective-permute-start.3 = (f32[16,768]{1,0:T(8,128)S(1)}, f32[16,768]{1,0:T(8,128)S(1)}, u32[]{:S(2)}, u32[]{:S(2)}) collective-permute-start(f32[16,768]{1,0:T(8,128)S(1)} %get-tuple-element.26.mine_second), channel_id=1, source_target_pairs={{4,8},{12,0},{8,4},{0,12},{5,9},{13,1},{9,5},{1,13},{6,10},{14,2},... | collective-permute-start | bytes 147464 | tf_op jit(solution)/shard_map/ppermute | solution.py:355
  21.1 0.4 collective-permute-start.4
  21.5 3.5 %collective-permute-done.4.rest_2_ = f32[8,768]{1,0:T(8,128)S(1)} collective-permute-done((f32[8,768]{1,0:T(8,128)S(1)}, f32[8,768]{1,0:T(8,128)S(1)}, u32[]{:S(2)}, u32[]{:S(2)}) %collective-permute-start.4) | collective-permute-done | bytes 24608 | tf_op jit(solution)/shard_map/ppermute | solution.py:357
  24.9 0.0 collective-permute-done.2.rest_0_
  24.9 0.0 collective-permute-done.3.rest_1_
  24.9 0.0 copy-done.8
  24.9 0.0 copy-done.5
  24.9 0.0 copy-done.6
  24.9 2.2 %shard_map.88 = (f32[128,768]{1,0:T(8,128)S(1)}, f32[128,768]{1,0:T(8,128)S(1)}, f32[128,768]{1,0:T(8,128)S(1)}, f32[144,768]{1,0:T(8,128)S(1)}, f32[5,8,768]{2,...) custom-call(f32[128,768]{1,0:T(8,128)S(1)} %get-tuple-element.23.field, ...), custom_call_target="tpu_custom_call" | custom-call | tf_op jit(solution)/shard_map/pallas_call | solution.py:100
  27.1 0.0 collective-permute-start.6
  27.1 0.8 %collective-permute-start.7 = (f32[8,768]{1,0:T(8,128)S(1)}, f32[8,768]{1,0:T(8,128)S(1)}, u32[]{:S(2)}, u32[]{:S(2)}) collective-permute-start(f32[8,768]{1,0:T(8,128)S(1)} %get-tuple-element.33), channel_id=1, source_target_pairs={{0,8},{4,12},{8,0},{12,4},{1,9},{5,13},{9,1},{13,5},{2,10},{6,14},... | collective-permute-start | bytes 73736 | tf_op jit(solution)/shard_map/ppermute | solution.py:357
  27.9 1.1 %collective-permute-start.5 = (f32[8,768]{1,0:T(8,128)S(1)}, f32[8,768]{1,0:T(8,128)S(1)}, u32[]{:S(2)}, u32[]{:S(2)}) collective-permute-start(f32[8,768]{1,0:T(8,128)S(1)} %get-tuple-element.33), channel_id=1, source_target_pairs={{0,4},{8,12},{4,0},{12,8},{1,5},{9,13},{5,1},{13,9},{2,6},{10,14},... | collective-permute-start | bytes 73736 | tf_op jit(solution)/shard_map/ppermute | solution.py:355
  29.0 1.4 %collective-permute-done.6.rest_1_ = f32[8,768]{1,0:T(8,128)S(1)} collective-permute-done((f32[8,768]{1,0:T(8,128)S(1)}, f32[8,768]{1,0:T(8,128)S(1)}, u32[]{:S(2)}, u32[]{:S(2)}) %collective-permute-start.6) | collective-permute-done | bytes 24608 | tf_op jit(solution)/shard_map/ppermute | solution.py:355
  30.4 0.7 %collective-permute-done.7.rest_2_ = f32[8,768]{1,0:T(8,128)S(1)} collective-permute-done((f32[8,768]{1,0:T(8,128)S(1)}, f32[8,768]{1,0:T(8,128)S(1)}, u32[]{:S(2)}, u32[]{:S(2)}) %collective-permute-start.7) | collective-permute-done | bytes 24608 | tf_op jit(solution)/shard_map/ppermute | solution.py:357
  31.1 0.0 collective-permute-done.5.rest_0_
  31.1 0.0 copy-start.2
  31.1 1.7 %shard_map.89 = (f32[128,512]{1,0:T(8,128)S(1)}, f32[128,512]{1,0:T(8,128)S(1)}, f32[8,128]{1,0:T(8,128)S(1)}) custom-call(f32[128,768]{1,0:T(8,128)S(1)} %get-tuple-element.23.field, f32[128,768]{1,0:T(8,128)S(1)} %get-tuple-element.28.precond, f32[128,768]{1,0:T(8,128)S(1)} %get-tuple-element.29.image, f32[6,128,768]{2,1,0:T(8,128)S(1)} %get-tuple-element.24.statics, ...), custom_call_target="tpu_custom_call" | custom-call | tf_op jit(solution)/shard_map/pallas_call | solution.py:100
  32.8 0.1 collective-permute-start.8
  32.9 1.2 %collective-permute-done.8 = f32[8,128]{1,0:T(8,128)S(1)} collective-permute-done((f32[8,128]{1,0:T(8,128)S(1)}, f32[8,128]{1,0:T(8,128)S(1)}, u32[]{:S(2)}, u32[]{:S(2)}) %collective-permute-start.8) | collective-permute-done | bytes 4128 | tf_op jit(solution)/shard_map/ppermute | solution.py:324
  34.0 0.6 %collective-permute-start.9 = (f32[8,128]{1,0:T(8,128)S(1)}, f32[8,128]{1,0:T(8,128)S(1)}, u32[]{:S(2)}, u32[]{:S(2)}) collective-permute-start(f32[8,128]{1,0:T(8,128)S(1)} %add.12), channel_id=1, source_target_pairs={{0,8},{4,12},{8,0},{12,4},{1,9},{5,13},{9,1},{13,5},{2,10},{6,14},... | collective-permute-start | bytes 12296 | tf_op jit(solution)/shard_map/ppermute | solution.py:324
  34.7 3.0 %collective-permute-done.9 = f32[8,128]{1,0:T(8,128)S(1)} collective-permute-done((f32[8,128]{1,0:T(8,128)S(1)}, f32[8,128]{1,0:T(8,128)S(1)}, u32[]{:S(2)}, u32[]{:S(2)}) %collective-permute-start.9) | collective-permute-done | bytes 4128 | tf_op jit(solution)/shard_map/ppermute | solution.py:324
  37.6 4.6 %collective-permute-start.10 = (f32[8,128]{1,0:T(8,128)S(1)}, f32[8,128]{1,0:T(8,128)S(1)}, u32[]{:S(2)}, u32[]{:S(2)}) collective-permute-start(f32[8,128]{1,0:T(8,128)S(1)} %add.13), channel_id=1, source_target_pairs={{0,1},{1,0},{2,3},{3,2},{4,5},{5,4},{6,7},{7,6},{8,9},{9,8},{10,11... | collective-permute-start | bytes 12296 | tf_op jit(solution)/shard_map/ppermute | solution.py:324
  42.2 1.6 %collective-permute-done.10 = f32[8,128]{1,0:T(8,128)S(1)} collective-permute-done((f32[8,128]{1,0:T(8,128)S(1)}, f32[8,128]{1,0:T(8,128)S(1)}, u32[]{:S(2)}, u32[]{:S(2)}) %collective-permute-start.10) | collective-permute-done | bytes 4128 | tf_op jit(solution)/shard_map/ppermute | solution.py:324
  43.8 3.2 %collective-permute-start.11 = (f32[8,128]{1,0:T(8,128)S(1)}, f32[8,128]{1,0:T(8,128)S(1)}, u32[]{:S(2)}, u32[]{:S(2)}) collective-permute-start(f32[8,128]{1,0:T(8,128)S(1)} %add.14), channel_id=1, source_target_pairs={{0,2},{1,3},{2,0},{3,1},{4,6},{5,7},{6,4},{7,5},{8,10},{9,11},{10,... | collective-permute-start | bytes 12296 | tf_op jit(solution)/shard_map/ppermute | solution.py:324
  47.0 1.6 %collective-permute-done.11 = f32[8,128]{1,0:T(8,128)S(1)} collective-permute-done((f32[8,128]{1,0:T(8,128)S(1)}, f32[8,128]{1,0:T(8,128)S(1)}, u32[]{:S(2)}, u32[]{:S(2)}) %collective-permute-start.11) | collective-permute-done | bytes 4128 | tf_op jit(solution)/shard_map/ppermute | solution.py:324
  48.6 0.0 copy-done.2
  48.6 1.3 %shard_map.90 = (f32[512,128]{1,0:T(8,128)}, f32[512,128]{1,0:T(8,128)}) custom-call(f32[8,128]{1,0:T(8,128)S(1)} %add.15.sums, f32[512,128]{1,0:T(8,128)S(1)} %bitcast.10, f32[128,768]{1,0:T(8,128)S(1)} %get-tuple-element.28.precond, f32[128,768]{1,0:T(8,128)S(1)} %get-tuple-element.29.image, f32[128,512]{1,0:T(8,128)S(1)} %get-tuple-element.36.again, ...), custom_call_target="tpu_custom_call" | custom-call | tf_op jit(solution)/shard_map/pallas_call | solution.py:100
  (4 shorter events, 0.0 us)
Async XLA Ops:
  0.6 24.3 %copy-start.8 = (f32[8,128]{1,0:T(8,128)S(1)}, f32[8,128]{1,0:T(8,128)}, u32[]{:S(2)}) copy-start(f32[8,128]{1,0:T(8,128)} %constant.6.clone.weights) | copy-start | bytes 12292
  0.6 1.1 %copy-start = (f32[3,32,16,128]{3,2,1,0:T(8,128)S(1)}, f32[3,32,16,128]{3,2,1,0:T(8,128)}, u32[]{:S(2)}) copy-start(f32[3,32,16,128]{3,2,1,0:T(8,128)} %param.9) | copy-start | bytes 2359300
  1.8 0.9 %copy-start.1 = (f32[32,16,128]{2,1,0:T(8,128)S(1)}, f32[32,16,128]{2,1,0:T(8,128)}, u32[]{:S(2)}) copy-start(f32[32,16,128]{2,1,0:T(8,128)} %param.7) | copy-start | bytes 786436
  2.7 0.9 %copy-start.3 = (f32[32,16,128]{2,1,0:T(8,128)S(1)}, f32[32,16,128]{2,1,0:T(8,128)}, u32[]{:S(2)}) copy-start(f32[32,16,128]{2,1,0:T(8,128)} %param.8) | copy-start | bytes 786436
  3.7 0.9 %copy-start.4 = (s32[32,16,128]{2,1,0:T(8,128)S(1)}, s32[32,16,128]{2,1,0:T(8,128)}, u32[]{:S(2)}) copy-start(s32[32,16,128]{2,1,0:T(8,128)} %param.10) | copy-start | bytes 786436
  4.6 20.3 %copy-start.5 = (f32[2,144,24]{2,1,0:T(8,128)S(1)}, f32[2,144,24]{2,1,0:T(8,128)}, u32[]{:S(2)}) copy-start(f32[2,144,24]{2,1,0:T(8,128)} %constant.8.clone.far) | copy-start | bytes 82948
  4.6 20.3 %copy-start.6 = (f32[144,128]{1,0:T(8,128)S(1)}, f32[144,128]{1,0:T(8,128)}, u32[]{:S(2)}) copy-start(f32[144,128]{1,0:T(8,128)} %constant.7.clone.near) | copy-start | bytes 221188
  4.9 12.2 %collective-permute-start = (f32[24,32,128]{2,1,0:T(8,128)S(1)}, f32[24,32,128]{2,1,0:T(8,128)S(1)}, u32[]{:S(2)}, u32[]{:S(2)}) collective-permute-start(f32[24,32,128]{2,1,0:T(8,128)S(1)} %get-tuple-element.21), channel_id=1, source_target_pairs={{0,1},{2,3},{1,0},{3,2},{4,5},{6,7},{5,4},{7,6},{8,9},{10,11},{9,8... | collective-permute-start | bytes 1179656 | tf_op jit(solution)/shard_map/ppermute | solution.py:344
  8.0 9.1 %collective-permute-start.1 = (f32[24,32,128]{2,1,0:T(8,128)S(1)}, f32[24,32,128]{2,1,0:T(8,128)S(1)}, u32[]{:S(2)}, u32[]{:S(2)}) collective-permute-start(f32[24,32,128]{2,1,0:T(8,128)S(1)} %get-tuple-element.22), channel_id=1, source_target_pairs={{1,2},{2,1},{5,6},{6,5},{9,10},{10,9},{13,14},{14,13},{17,18},{18,... | collective-permute-start | bytes 1179656 | tf_op jit(solution)/shard_map/ppermute | solution.py:345
  17.1 0.7 %copy-start.7 = (f32[8,128]{1,0:T(8,128)S(1)}, f32[8,128]{1,0:T(8,128)}, u32[]{:S(2)}) copy-start(f32[8,128]{1,0:T(8,128)} %constant.6.clone.weights) | copy-start | bytes 12292
  19.3 5.7 %collective-permute-start.2 = (f32[16,768]{1,0:T(8,128)S(1)}, f32[16,768]{1,0:T(8,128)S(1)}, u32[]{:S(2)}, u32[]{:S(2)}) collective-permute-start(f32[16,768]{1,0:T(8,128)S(1)} %get-tuple-element.25.mine_first), channel_id=1, source_target_pairs={{0,4},{8,12},{4,0},{12,8},{1,5},{9,13},{5,1},{13,9},{2,6},{10,14},... | collective-permute-start | bytes 147464 | tf_op jit(solution)/shard_map/ppermute | solution.py:355
  19.3 5.6 %collective-permute-start.3 = (f32[16,768]{1,0:T(8,128)S(1)}, f32[16,768]{1,0:T(8,128)S(1)}, u32[]{:S(2)}, u32[]{:S(2)}) collective-permute-start(f32[16,768]{1,0:T(8,128)S(1)} %get-tuple-element.26.mine_second), channel_id=1, source_target_pairs={{4,8},{12,0},{8,4},{0,12},{5,9},{13,1},{9,5},{1,13},{6,10},{14,2},... | collective-permute-start | bytes 147464 | tf_op jit(solution)/shard_map/ppermute | solution.py:355
  21.1 3.8 %collective-permute-start.4 = (f32[8,768]{1,0:T(8,128)S(1)}, f32[8,768]{1,0:T(8,128)S(1)}, u32[]{:S(2)}, u32[]{:S(2)}) collective-permute-start(f32[8,768]{1,0:T(8,128)S(1)} %get-tuple-element.27), channel_id=1, source_target_pairs={{0,8},{4,12},{8,0},{12,4},{1,9},{5,13},{9,1},{13,5},{2,10},{6,14},... | collective-permute-start | bytes 73736 | tf_op jit(solution)/shard_map/ppermute | solution.py:357
  27.1 3.3 %collective-permute-start.6 = (f32[8,768]{1,0:T(8,128)S(1)}, f32[8,768]{1,0:T(8,128)S(1)}, u32[]{:S(2)}, u32[]{:S(2)}) collective-permute-start(f32[8,768]{1,0:T(8,128)S(1)} %get-tuple-element.34), channel_id=1, source_target_pairs={{4,8},{12,0},{8,4},{0,12},{5,9},{13,1},{9,5},{1,13},{6,10},{14,2},... | collective-permute-start | bytes 73736 | tf_op jit(solution)/shard_map/ppermute | solution.py:355
  27.1 4.0 %collective-permute-start.7 = (f32[8,768]{1,0:T(8,128)S(1)}, f32[8,768]{1,0:T(8,128)S(1)}, u32[]{:S(2)}, u32[]{:S(2)}) collective-permute-start(f32[8,768]{1,0:T(8,128)S(1)} %get-tuple-element.33), channel_id=1, source_target_pairs={{0,8},{4,12},{8,0},{12,4},{1,9},{5,13},{9,1},{13,5},{2,10},{6,14},... | collective-permute-start | bytes 73736 | tf_op jit(solution)/shard_map/ppermute | solution.py:357
  27.9 3.2 %collective-permute-start.5 = (f32[8,768]{1,0:T(8,128)S(1)}, f32[8,768]{1,0:T(8,128)S(1)}, u32[]{:S(2)}, u32[]{:S(2)}) collective-permute-start(f32[8,768]{1,0:T(8,128)S(1)} %get-tuple-element.33), channel_id=1, source_target_pairs={{0,4},{8,12},{4,0},{12,8},{1,5},{9,13},{5,1},{13,9},{2,6},{10,14},... | collective-permute-start | bytes 73736 | tf_op jit(solution)/shard_map/ppermute | solution.py:355
  31.1 17.5 %copy-start.2 = (f32[32,16,128]{2,1,0:T(8,128)S(1)}, f32[32,16,128]{2,1,0:T(8,128)}, u32[]{:S(2)}) copy-start(f32[32,16,128]{2,1,0:T(8,128)} %param.7) | copy-start | bytes 786436
  32.8 1.2 %collective-permute-start.8 = (f32[8,128]{1,0:T(8,128)S(1)}, f32[8,128]{1,0:T(8,128)S(1)}, u32[]{:S(2)}, u32[]{:S(2)}) collective-permute-start(f32[8,128]{1,0:T(8,128)S(1)} %get-tuple-element.35), channel_id=1, source_target_pairs={{0,4},{4,0},{8,12},{12,8},{1,5},{5,1},{9,13},{13,9},{2,6},{6,2},{1... | collective-permute-start | bytes 12296 | tf_op jit(solution)/shard_map/ppermute | solution.py:324
  34.0 3.6 %collective-permute-start.9 = (f32[8,128]{1,0:T(8,128)S(1)}, f32[8,128]{1,0:T(8,128)S(1)}, u32[]{:S(2)}, u32[]{:S(2)}) collective-permute-start(f32[8,128]{1,0:T(8,128)S(1)} %add.12), channel_id=1, source_target_pairs={{0,8},{4,12},{8,0},{12,4},{1,9},{5,13},{9,1},{13,5},{2,10},{6,14},... | collective-permute-start | bytes 12296 | tf_op jit(solution)/shard_map/ppermute | solution.py:324
  37.6 6.2 %collective-permute-start.10 = (f32[8,128]{1,0:T(8,128)S(1)}, f32[8,128]{1,0:T(8,128)S(1)}, u32[]{:S(2)}, u32[]{:S(2)}) collective-permute-start(f32[8,128]{1,0:T(8,128)S(1)} %add.13), channel_id=1, source_target_pairs={{0,1},{1,0},{2,3},{3,2},{4,5},{5,4},{6,7},{7,6},{8,9},{9,8},{10,11... | collective-permute-start | bytes 12296 | tf_op jit(solution)/shard_map/ppermute | solution.py:324
  43.8 4.8 %collective-permute-start.11 = (f32[8,128]{1,0:T(8,128)S(1)}, f32[8,128]{1,0:T(8,128)S(1)}, u32[]{:S(2)}, u32[]{:S(2)}) collective-permute-start(f32[8,128]{1,0:T(8,128)S(1)} %add.14), channel_id=1, source_target_pairs={{0,2},{1,3},{2,0},{3,1},{4,6},{5,7},{6,4},{7,5},{8,10},{9,11},{10,... | collective-permute-start | bytes 12296 | tf_op jit(solution)/shard_map/ppermute | solution.py:324

commit v3 on v2

--- a/solution.py
+++ b/solution.py
@@ -107,34 +107,41 @@
     )(*args)
 
 
-KINDS = 6
-
-
-def band_kernel(rows, levels, noise, kappa2, conduct, land, first, second):
+FULL, PART = REACH, REACH - 1
+PLANES = 3 * FULL + 3 * PART
+
+
+def band_kernel(rows, levels, *refs):
+    sources, (second, first), copies, sems = refs[:7], refs[7:9], refs[9:16], refs[16]
+    moves = [pltpu.make_async_copy(x, y, sems.at[k]) for k, (x, y) in enumerate(zip(sources, copies))]
+    for move in moves:
+        move.start()
+    for move in moves:
+        move.wait()
+    noise, kappa2, conduct, land = copies[:4]
     odd = lax.axis_index("lat") % 2
     top = rows - REACH
-    for out, start in ((first, (1 - odd) * top), (second, odd * top)):
-        for kind in range(KINDS):
-            for j in range(REACH):
-                at = pl.ds(start + j, levels, stride=rows)
-                if kind == 0:
-                    plane = noise[at, :]
-                elif kind == 1:
-                    plane = land[at, :].astype(jnp.float32)
-                elif kind == 2:
-                    plane = conduct[1, at, :]
-                elif kind == 3:
-                    plane = kappa2[at, :]
-                elif kind == 4:
-                    plane = conduct[0, at, :]
-                else:
-                    plane = conduct[2, at, :]
-                out[kind * REACH + j] = plane
+    loads = (
+        lambda at: noise[at, :],
+        lambda at: land[at, :].astype(jnp.float32),
+        lambda at: conduct[1, at, :],
+        lambda at: kappa2[at, :],
+        lambda at: conduct[0, at, :],
+        lambda at: conduct[2, at, :],
+    )
+    for out, side in ((first, odd), (second, 1 - odd)):
+        k = 0
+        for kind, load in enumerate(loads):
+            count = FULL if kind < 3 else PART
+            start = (1 - side) * (rows - count)
+            for j in range(count):
+                out[k] = load(pl.ds(start + j, levels, stride=rows))
+                k += 1
 
 
 def prepare_kernel(
     rows, levels, columns,
-    noise, kappa2, conduct, land, got_first, got_second, weights,
+    noise, kappa2, conduct, land, got_second, got_first, weights,
     field, statics, to_first, to_second, to_others,
 ):
     lat_odd = lax.axis_index("lat") % 2
@@ -144,10 +151,16 @@
     group = REACH * levels
 
     def ghost(kind, north):
-        a = got_first[pl.ds(kind * REACH, REACH)].reshape(group, columns)
-        b = got_second[pl.ds(kind * REACH, REACH)].reshape(group, columns)
+        count = FULL if kind < 3 else PART
+        k = kind * FULL if kind < 3 else 3 * FULL + (kind - 3) * PART
+        a = got_first[pl.ds(k, count)].reshape(count * levels, columns)
+        b = got_second[pl.ds(k, count)].reshape(count * levels, columns)
         from_first = (lat_odd == 0) if north else (lat_odd == 1)
-        return jnp.where(from_first, a, b)
+        planes = jnp.where(from_first, a, b)
+        if count == REACH:
+            return planes
+        blank = jnp.zeros((group - count * levels, columns), jnp.float32)
+        return jnp.concatenate([planes, blank] if north else [blank, planes], axis=0)
 
     def turned(kind, load):
         blocks = [ghost(kind, False)]
@@ -338,16 +351,24 @@
     land = land.reshape(flat, columns)
     conduct = conduct.reshape(3, flat, columns)
 
-    planes = (KINDS * REACH, levels, columns)
-    first, second = call(functools.partial(band_kernel, rows, levels), [planes, planes], noise, kappa2, conduct, land)
+    sources = (noise, kappa2, conduct, land, near, far, weights)
+    planes = (PLANES, levels, columns)
+    second, first, noise, kappa2, conduct, land, near, far, weights = pl.pallas_call(
+        functools.partial(band_kernel, rows, levels),
+        out_shape=[pltpu.VMEM(planes, jnp.float32)] * 2 + [pltpu.VMEM(x.shape, x.dtype) for x in sources],
+        in_specs=[pl.BlockSpec(memory_space=pltpu.HBM)] * len(sources),
+        out_specs=whole(2 + len(sources)),
+        scratch_shapes=[pltpu.SemaphoreType.DMA((len(sources),))],
+        compiler_params=pltpu.CompilerParams(vmem_limit_bytes=8 << 20),
+    )(*[pltpu.with_memory_space_constraint(x, pltpu.HBM) for x in sources])
     perm_a, perm_b = pair_perms(lax.axis_size("lat"), False)
+    got_second = lax.ppermute(second, "lat", perm_b)
     got_first = lax.ppermute(first, "lat", perm_a)
-    got_second = lax.ppermute(second, "lat", perm_b)
 
     field, statics, to_first, to_second, to_others = call(
         functools.partial(prepare_kernel, rows, levels, columns),
         [(columns, lanes), (6, columns, lanes), (16, lanes), (16, lanes), (8, lanes)],
-        noise, kappa2, conduct, land, got_first, got_second, weights, near_memory=(4, 5),
+        noise, kappa2, conduct, land, got_second, got_first, weights, near_memory=range(7),
     )
     lon_a, lon_b = pair_perms(count, True)
 
@@ -361,7 +382,7 @@
     precond, image, diagonal, to_east, rim, to_first2, to_second2 = call(
         functools.partial(first_kernel, levels, columns, others),
         [(columns, lanes), (columns, lanes), (columns, lanes), (tall, lanes), (5, 8, lanes), (8, lanes), (8, lanes)],
-        field, statics, near, far, weights, to_first, to_second, *told, near_memory=(0, 1, 5, 6, *range(7, 9 + others)),
+        field, statics, near, far, weights, to_first, to_second, *told, near_memory=range(9 + others),
         scratch=[(tall, lanes), (tall, lanes)],
     )
     told = exchange(to_first2, to_second2, to_first2)
@@ -369,14 +390,14 @@
         functools.partial(second_kernel, levels, columns, rows, others),
         [(columns, flat), (columns, flat), (8, 128)],
         field, precond, image, statics, near, far, diagonal, to_east, rim, *told,
-        near_memory=(0, 1, 2, 3, 6, 7, 8, *range(9, 11 + others)),
+        near_memory=range(11 + others),
         scratch=[(tall, lanes), (tall, lanes)],
     )
     sums = summed(summed(sums, "lon"), "lat")
     answer, left = call(
         functools.partial(combine_kernel, rows, levels),
         [(flat, columns), (flat, columns)],
-        sums, noise, precond, image, again, along, near_memory=(0, 2, 3, 4, 5), last=True,
+        sums, noise, precond, image, again, along, near_memory=range(6), last=True,
     )
     return answer.reshape(levels, rows, columns), left.reshape(levels, rows, columns)
 

time: 50.2 us -> 45.8 us (0.912)
  local copies, waits for them, and re-layouts: 4.69 us -> 0 us
  starting transfers between devices: 16.3 us -> 14.7 us
  Pallas kernels: 6.84 us -> 8.19 us
  waiting for transfers between devices: 21.3 us -> 22 us
    unnamed x18 -> x0, local copies, waits for them, and re-layouts: 4.69 us -> none
    ppermute x4, starting transfers between devices: 8.49 us -> 4.07 us  [summed(): x = x + lax.ppermute(x, axis, [(i, i ^ step) for i in range(count)])]
    ppermute x1, starting transfers between devices: 3.12 us -> 5.92 us  [body(): got_first = lax.ppermute(first, 'lat', perm_a)]
    pallas_call x0 -> x1, Pallas kernels: none -> 1.69 us  [body(): pl.pallas_call(functools.partial(band_kernel, rows, levels), out_shape=[p...]
    ppermute x4, waiting for transfers between devices: 7.3 us -> 8.87 us  [summed(): x = x + lax.ppermute(x, axis, [(i, i ^ step) for i in range(count)])]
    ppermute x1, waiting for transfers between devices: 8.43 us -> 7.78 us  [body(): got_first = lax.ppermute(first, 'lat', perm_a)]
    pallas_call x5 -> x4, Pallas kernels: 6.84 us -> 6.5 us  [call(): pl.pallas_call(kernel, out_shape=[kind(s, jnp.float32) for s in outs], in...]
where the time goes in v3:
time: 45.8 us; the launch traced here: 45.7 us
  waiting for transfers between devices  22 us (48%)
  starting transfers between devices  14.7 us (32%)
  Pallas kernels  8.19 us (18%)
  between operations  0.69 us (2%)
    ppermute x4, waiting for transfers between devices, summed(): x = x + lax.ppermute(x, axis, [(i, i ^ step) for i in range(count)])  8.87 us
    ppermute x1, waiting for transfers between devices, body(): got_first = lax.ppermute(first, 'lat', perm_a)  7.78 us
    pallas_call x4, Pallas kernels, call(): pl.pallas_call(kernel, out_shape=[kind(s, jnp.float32) for s in outs], in...  6.5 us
    ppermute x1, starting transfers between devices, body(): got_first = lax.ppermute(first, 'lat', perm_a)  5.92 us
    ppermute x4, starting transfers between devices, summed(): x = x + lax.ppermute(x, axis, [(i, i ^ step) for i in range(count)])  4.07 us
    ppermute x2, waiting for transfers between devices, exchange(): lax.ppermute(rest, 'lon', [(i, (i + d) % count) for i in range(count)])  3.98 us
    ppermute x4, starting transfers between devices, exchange(): got = [lax.ppermute(one, 'lon', lon_a), lax.ppermute(two, 'lon', lon_b)]  2.79 us
    pallas_call x1, Pallas kernels, body(): pl.pallas_call(functools.partial(band_kernel, rows, levels), out_shape=[p...  1.69 us
  transfers between devices with their start and end apart: 12, of which 8 were waited for; matrix products, arithmetic and copies ran while one was open for 0% of the time, Pallas kernels for 0%

profile of v3, /device:TPU:0, one launch (start us, length us, event | category | flops | bytes accessed | tf_op | source)
XLA Modules:
  0.0 45.7 jit_solution(1331315584178872246)
XLA Ops:
  0.6 1.7 %shard_map.86 = (f32[21,32,128]{2,1,0:T(8,128)S(1)}, f32[21,32,128]{2,1,0:T(8,128)S(1)}, f32[512,128]{1,0:T(8,128)S(1)}, f32[512,128]{1,0:T(8,128)S(1)}, f32[3,5...) custom-call(f32[512,128]{1,0:T(8,128)} %bitcast.7, ...), custom_call_target="tpu_custom_call" | custom-call | tf_op jit(solution)/shard_map/pallas_call | solution.py:356
  2.3 0.7 %collective-permute-start = (f32[21,32,128]{2,1,0:T(8,128)S(1)}, f32[21,32,128]{2,1,0:T(8,128)S(1)}, u32[]{:S(2)}, u32[]{:S(2)}) collective-permute-start(f32[21,32,128]{2,1,0:T(8,128)S(1)} %get-tuple-element.32), channel_id=1, source_target_pairs={{1,2},{2,1},{5,6},{6,5},{9,10},{10,9},{13,14},{14,13},{17,18},{18,... | collective-permute-start | bytes 1032200 | tf_op jit(solution)/shard_map/ppermute | solution.py:365
  3.0 5.9 %collective-permute-start.1 = (f32[21,32,128]{2,1,0:T(8,128)S(1)}, f32[21,32,128]{2,1,0:T(8,128)S(1)}, u32[]{:S(2)}, u32[]{:S(2)}) collective-permute-start(f32[21,32,128]{2,1,0:T(8,128)S(1)} %get-tuple-element.33), channel_id=1, source_target_pairs={{0,1},{2,3},{1,0},{3,2},{4,5},{6,7},{5,4},{7,6},{8,9},{10,11},{9,8... | collective-permute-start | bytes 1032200 | tf_op jit(solution)/shard_map/ppermute | solution.py:366
  8.9 0.0 collective-permute-done.got_second
  8.9 7.8 %collective-permute-done.1.got_first = f32[21,32,128]{2,1,0:T(8,128)S(1)} collective-permute-done((f32[21,32,128]{2,1,0:T(8,128)S(1)}, f32[21,32,128]{2,1,0:T(8,128)S(1)}, u32[]{:S(2)}, u32[]{:S(2)}) %collective-permute-start.1) | collective-permute-done | bytes 344096 | tf_op jit(solution)/shard_map/ppermute | solution.py:366
  16.7 1.4 %shard_map.87 = (f32[128,768]{1,0:T(8,128)S(1)}, f32[6,128,768]{2,1,0:T(8,128)S(1)}, f32[16,768]{1,0:T(8,128)S(1)}, f32[16,768]{1,0:T(8,128)S(1)}, f32[8,768]{1,0:T(8,128)S(1)}) custom-call(f32[512,128]{1,0:T(8,128)S(1)} %get-tuple-element.28.noise, f32[512,128]{1,0:T(8,128)S(1)} %get-tuple-element.29.kappa2, f32[3,512,128]{2,1,0:T(8,128)S(1)} %get-tuple-element.30.conduct, ...), custom_call_target="tpu_custom_call" | custom-call | tf_op jit(solution)/shard_map/pallas_call | solution.py:100
  18.1 0.1 collective-permute-start.2
  18.2 1.6 %collective-permute-start.3 = (f32[16,768]{1,0:T(8,128)S(1)}, f32[16,768]{1,0:T(8,128)S(1)}, u32[]{:S(2)}, u32[]{:S(2)}) collective-permute-start(f32[16,768]{1,0:T(8,128)S(1)} %get-tuple-element.40.mine_second), channel_id=1, source_target_pairs={{4,8},{12,0},{8,4},{0,12},{5,9},{13,1},{9,5},{1,13},{6,10},{14,2},... | collective-permute-start | bytes 147464 | tf_op jit(solution)/shard_map/ppermute | solution.py:376
  19.8 0.5 %collective-permute-start.4 = (f32[8,768]{1,0:T(8,128)S(1)}, f32[8,768]{1,0:T(8,128)S(1)}, u32[]{:S(2)}, u32[]{:S(2)}) collective-permute-start(f32[8,768]{1,0:T(8,128)S(1)} %get-tuple-element.41), channel_id=1, source_target_pairs={{0,8},{4,12},{8,0},{12,4},{1,9},{5,13},{9,1},{13,5},{2,10},{6,14},... | collective-permute-start | bytes 73736 | tf_op jit(solution)/shard_map/ppermute | solution.py:378
  20.4 3.3 %collective-permute-done.4.rest_2_ = f32[8,768]{1,0:T(8,128)S(1)} collective-permute-done((f32[8,768]{1,0:T(8,128)S(1)}, f32[8,768]{1,0:T(8,128)S(1)}, u32[]{:S(2)}, u32[]{:S(2)}) %collective-permute-start.4) | collective-permute-done | bytes 24608 | tf_op jit(solution)/shard_map/ppermute | solution.py:378
  23.6 0.0 collective-permute-done.2.rest_0_
  23.7 0.0 collective-permute-done.3.rest_1_
  23.7 2.1 %shard_map.88 = (f32[128,768]{1,0:T(8,128)S(1)}, f32[128,768]{1,0:T(8,128)S(1)}, f32[128,768]{1,0:T(8,128)S(1)}, f32[144,768]{1,0:T(8,128)S(1)}, f32[5,8,768]{2,...) custom-call(f32[128,768]{1,0:T(8,128)S(1)} %get-tuple-element.35.field, ...), custom_call_target="tpu_custom_call" | custom-call | tf_op jit(solution)/shard_map/pallas_call | solution.py:100
  25.8 0.0 collective-permute-start.6
  25.8 0.7 %collective-permute-start.7 = (f32[8,768]{1,0:T(8,128)S(1)}, f32[8,768]{1,0:T(8,128)S(1)}, u32[]{:S(2)}, u32[]{:S(2)}) collective-permute-start(f32[8,768]{1,0:T(8,128)S(1)} %get-tuple-element.47), channel_id=1, source_target_pairs={{0,8},{4,12},{8,0},{12,4},{1,9},{5,13},{9,1},{13,5},{2,10},{6,14},... | collective-permute-start | bytes 73736 | tf_op jit(solution)/shard_map/ppermute | solution.py:378
  26.5 1.1 %collective-permute-start.5 = (f32[8,768]{1,0:T(8,128)S(1)}, f32[8,768]{1,0:T(8,128)S(1)}, u32[]{:S(2)}, u32[]{:S(2)}) collective-permute-start(f32[8,768]{1,0:T(8,128)S(1)} %get-tuple-element.47), channel_id=1, source_target_pairs={{0,4},{8,12},{4,0},{12,8},{1,5},{9,13},{5,1},{13,9},{2,6},{10,14},... | collective-permute-start | bytes 73736 | tf_op jit(solution)/shard_map/ppermute | solution.py:376
  27.7 1.4 %collective-permute-done.6.rest_1_ = f32[8,768]{1,0:T(8,128)S(1)} collective-permute-done((f32[8,768]{1,0:T(8,128)S(1)}, f32[8,768]{1,0:T(8,128)S(1)}, u32[]{:S(2)}, u32[]{:S(2)}) %collective-permute-start.6) | collective-permute-done | bytes 24608 | tf_op jit(solution)/shard_map/ppermute | solution.py:376
  29.0 0.7 %collective-permute-done.7.rest_2_ = f32[8,768]{1,0:T(8,128)S(1)} collective-permute-done((f32[8,768]{1,0:T(8,128)S(1)}, f32[8,768]{1,0:T(8,128)S(1)}, u32[]{:S(2)}, u32[]{:S(2)}) %collective-permute-start.7) | collective-permute-done | bytes 24608 | tf_op jit(solution)/shard_map/ppermute | solution.py:378
  29.7 0.0 collective-permute-done.5.rest_0_
  29.7 1.7 %shard_map.89 = (f32[128,512]{1,0:T(8,128)S(1)}, f32[128,512]{1,0:T(8,128)S(1)}, f32[8,128]{1,0:T(8,128)S(1)}) custom-call(f32[128,768]{1,0:T(8,128)S(1)} %get-tuple-element.35.field, f32[128,768]{1,0:T(8,128)S(1)} %get-tuple-element.42.precond, f32[128,768]{1,0:T(8,128)S(1)} %get-tuple-element.43.image, f32[6,128,768]{2,1,0:T(8,128)S(1)} %get-tuple-element.36.statics, ...), custom_call_target="tpu_custom_call" | custom-call | tf_op jit(solution)/shard_map/pallas_call | solution.py:100
  31.4 0.1 collective-permute-start.8
  31.5 1.2 %collective-permute-done.8 = f32[8,128]{1,0:T(8,128)S(1)} collective-permute-done((f32[8,128]{1,0:T(8,128)S(1)}, f32[8,128]{1,0:T(8,128)S(1)}, u32[]{:S(2)}, u32[]{:S(2)}) %collective-permute-start.8) | collective-permute-done | bytes 4128 | tf_op jit(solution)/shard_map/ppermute | solution.py:337
  32.6 0.6 %collective-permute-start.9 = (f32[8,128]{1,0:T(8,128)S(1)}, f32[8,128]{1,0:T(8,128)S(1)}, u32[]{:S(2)}, u32[]{:S(2)}) collective-permute-start(f32[8,128]{1,0:T(8,128)S(1)} %add.12), channel_id=1, source_target_pairs={{0,8},{4,12},{8,0},{12,4},{1,9},{5,13},{9,1},{13,5},{2,10},{6,14},... | collective-permute-start | bytes 12296 | tf_op jit(solution)/shard_map/ppermute | solution.py:337
  33.3 3.0 %collective-permute-done.9 = f32[8,128]{1,0:T(8,128)S(1)} collective-permute-done((f32[8,128]{1,0:T(8,128)S(1)}, f32[8,128]{1,0:T(8,128)S(1)}, u32[]{:S(2)}, u32[]{:S(2)}) %collective-permute-start.9) | collective-permute-done | bytes 4128 | tf_op jit(solution)/shard_map/ppermute | solution.py:337
  36.3 1.7 %collective-permute-start.10 = (f32[8,128]{1,0:T(8,128)S(1)}, f32[8,128]{1,0:T(8,128)S(1)}, u32[]{:S(2)}, u32[]{:S(2)}) collective-permute-start(f32[8,128]{1,0:T(8,128)S(1)} %add.13), channel_id=1, source_target_pairs={{0,1},{1,0},{2,3},{3,2},{4,5},{5,4},{6,7},{7,6},{8,9},{9,8},{10,11... | collective-permute-start | bytes 12296 | tf_op jit(solution)/shard_map/ppermute | solution.py:337
  38.0 1.9 %collective-permute-done.10 = f32[8,128]{1,0:T(8,128)S(1)} collective-permute-done((f32[8,128]{1,0:T(8,128)S(1)}, f32[8,128]{1,0:T(8,128)S(1)}, u32[]{:S(2)}, u32[]{:S(2)}) %collective-permute-start.10) | collective-permute-done | bytes 4128 | tf_op jit(solution)/shard_map/ppermute | solution.py:337
  39.9 1.6 %collective-permute-start.11 = (f32[8,128]{1,0:T(8,128)S(1)}, f32[8,128]{1,0:T(8,128)S(1)}, u32[]{:S(2)}, u32[]{:S(2)}) collective-permute-start(f32[8,128]{1,0:T(8,128)S(1)} %add.14), channel_id=1, source_target_pairs={{0,2},{1,3},{2,0},{3,1},{4,6},{5,7},{6,4},{7,5},{8,10},{9,11},{10,... | collective-permute-start | bytes 12296 | tf_op jit(solution)/shard_map/ppermute | solution.py:337
  41.5 2.9 %collective-permute-done.11 = f32[8,128]{1,0:T(8,128)S(1)} collective-permute-done((f32[8,128]{1,0:T(8,128)S(1)}, f32[8,128]{1,0:T(8,128)S(1)}, u32[]{:S(2)}, u32[]{:S(2)}) %collective-permute-start.11) | collective-permute-done | bytes 4128 | tf_op jit(solution)/shard_map/ppermute | solution.py:337
  44.4 1.3 %shard_map.90 = (f32[512,128]{1,0:T(8,128)}, f32[512,128]{1,0:T(8,128)}) custom-call(f32[8,128]{1,0:T(8,128)S(1)} %add.15.sums, f32[512,128]{1,0:T(8,128)S(1)} %get-tuple-element.28.noise, f32[128,768]{1,0:T(8,128)S(1)} %get-tuple-element.42.precond, f32[128,768]{1,0:T(8,128)S(1)} %get-tuple-element.43.image, f32[128,512]{1,0:T(8,128)S(1)} %get-tuple-element.50.again, ...), custom_call_target="tpu_custom_call" | custom-call | tf_op jit(solution)/shard_map/pallas_call | solution.py:100
  (4 shorter events, 0.0 us)
Async XLA Ops:
  2.3 6.6 %collective-permute-start = (f32[21,32,128]{2,1,0:T(8,128)S(1)}, f32[21,32,128]{2,1,0:T(8,128)S(1)}, u32[]{:S(2)}, u32[]{:S(2)}) collective-permute-start(f32[21,32,128]{2,1,0:T(8,128)S(1)} %get-tuple-element.32), channel_id=1, source_target_pairs={{1,2},{2,1},{5,6},{6,5},{9,10},{10,9},{13,14},{14,13},{17,18},{18,... | collective-permute-start | bytes 1032200 | tf_op jit(solution)/shard_map/ppermute | solution.py:365
  3.0 13.7 %collective-permute-start.1 = (f32[21,32,128]{2,1,0:T(8,128)S(1)}, f32[21,32,128]{2,1,0:T(8,128)S(1)}, u32[]{:S(2)}, u32[]{:S(2)}) collective-permute-start(f32[21,32,128]{2,1,0:T(8,128)S(1)} %get-tuple-element.33), channel_id=1, source_target_pairs={{0,1},{2,3},{1,0},{3,2},{4,5},{6,7},{5,4},{7,6},{8,9},{10,11},{9,8... | collective-permute-start | bytes 1032200 | tf_op jit(solution)/shard_map/ppermute | solution.py:366
  18.1 5.5 %collective-permute-start.2 = (f32[16,768]{1,0:T(8,128)S(1)}, f32[16,768]{1,0:T(8,128)S(1)}, u32[]{:S(2)}, u32[]{:S(2)}) collective-permute-start(f32[16,768]{1,0:T(8,128)S(1)} %get-tuple-element.39.mine_first), channel_id=1, source_target_pairs={{0,4},{8,12},{4,0},{12,8},{1,5},{9,13},{5,1},{13,9},{2,6},{10,14},... | collective-permute-start | bytes 147464 | tf_op jit(solution)/shard_map/ppermute | solution.py:376
  18.2 5.4 %collective-permute-start.3 = (f32[16,768]{1,0:T(8,128)S(1)}, f32[16,768]{1,0:T(8,128)S(1)}, u32[]{:S(2)}, u32[]{:S(2)}) collective-permute-start(f32[16,768]{1,0:T(8,128)S(1)} %get-tuple-element.40.mine_second), channel_id=1, source_target_pairs={{4,8},{12,0},{8,4},{0,12},{5,9},{13,1},{9,5},{1,13},{6,10},{14,2},... | collective-permute-start | bytes 147464 | tf_op jit(solution)/shard_map/ppermute | solution.py:376
  19.8 3.8 %collective-permute-start.4 = (f32[8,768]{1,0:T(8,128)S(1)}, f32[8,768]{1,0:T(8,128)S(1)}, u32[]{:S(2)}, u32[]{:S(2)}) collective-permute-start(f32[8,768]{1,0:T(8,128)S(1)} %get-tuple-element.41), channel_id=1, source_target_pairs={{0,8},{4,12},{8,0},{12,4},{1,9},{5,13},{9,1},{13,5},{2,10},{6,14},... | collective-permute-start | bytes 73736 | tf_op jit(solution)/shard_map/ppermute | solution.py:378
  25.8 3.3 %collective-permute-start.6 = (f32[8,768]{1,0:T(8,128)S(1)}, f32[8,768]{1,0:T(8,128)S(1)}, u32[]{:S(2)}, u32[]{:S(2)}) collective-permute-start(f32[8,768]{1,0:T(8,128)S(1)} %get-tuple-element.48), channel_id=1, source_target_pairs={{4,8},{12,0},{8,4},{0,12},{5,9},{13,1},{9,5},{1,13},{6,10},{14,2},... | collective-permute-start | bytes 73736 | tf_op jit(solution)/shard_map/ppermute | solution.py:376
  25.8 3.9 %collective-permute-start.7 = (f32[8,768]{1,0:T(8,128)S(1)}, f32[8,768]{1,0:T(8,128)S(1)}, u32[]{:S(2)}, u32[]{:S(2)}) collective-permute-start(f32[8,768]{1,0:T(8,128)S(1)} %get-tuple-element.47), channel_id=1, source_target_pairs={{0,8},{4,12},{8,0},{12,4},{1,9},{5,13},{9,1},{13,5},{2,10},{6,14},... | collective-permute-start | bytes 73736 | tf_op jit(solution)/shard_map/ppermute | solution.py:378
  26.5 3.2 %collective-permute-start.5 = (f32[8,768]{1,0:T(8,128)S(1)}, f32[8,768]{1,0:T(8,128)S(1)}, u32[]{:S(2)}, u32[]{:S(2)}) collective-permute-start(f32[8,768]{1,0:T(8,128)S(1)} %get-tuple-element.47), channel_id=1, source_target_pairs={{0,4},{8,12},{4,0},{12,8},{1,5},{9,13},{5,1},{13,9},{2,6},{10,14},... | collective-permute-start | bytes 73736 | tf_op jit(solution)/shard_map/ppermute | solution.py:376
  31.4 1.2 %collective-permute-start.8 = (f32[8,128]{1,0:T(8,128)S(1)}, f32[8,128]{1,0:T(8,128)S(1)}, u32[]{:S(2)}, u32[]{:S(2)}) collective-permute-start(f32[8,128]{1,0:T(8,128)S(1)} %get-tuple-element.49), channel_id=1, source_target_pairs={{0,4},{4,0},{8,12},{12,8},{1,5},{5,1},{9,13},{13,9},{2,6},{6,2},{1... | collective-permute-start | bytes 12296 | tf_op jit(solution)/shard_map/ppermute | solution.py:337
  32.6 3.6 %collective-permute-start.9 = (f32[8,128]{1,0:T(8,128)S(1)}, f32[8,128]{1,0:T(8,128)S(1)}, u32[]{:S(2)}, u32[]{:S(2)}) collective-permute-start(f32[8,128]{1,0:T(8,128)S(1)} %add.12), channel_id=1, source_target_pairs={{0,8},{4,12},{8,0},{12,4},{1,9},{5,13},{9,1},{13,5},{2,10},{6,14},... | collective-permute-start | bytes 12296 | tf_op jit(solution)/shard_map/ppermute | solution.py:337
  36.3 3.6 %collective-permute-start.10 = (f32[8,128]{1,0:T(8,128)S(1)}, f32[8,128]{1,0:T(8,128)S(1)}, u32[]{:S(2)}, u32[]{:S(2)}) collective-permute-start(f32[8,128]{1,0:T(8,128)S(1)} %add.13), channel_id=1, source_target_pairs={{0,1},{1,0},{2,3},{3,2},{4,5},{5,4},{6,7},{7,6},{8,9},{9,8},{10,11... | collective-permute-start | bytes 12296 | tf_op jit(solution)/shard_map/ppermute | solution.py:337
  39.9 4.5 %collective-permute-start.11 = (f32[8,128]{1,0:T(8,128)S(1)}, f32[8,128]{1,0:T(8,128)S(1)}, u32[]{:S(2)}, u32[]{:S(2)}) collective-permute-start(f32[8,128]{1,0:T(8,128)S(1)} %add.14), channel_id=1, source_target_pairs={{0,2},{1,3},{2,0},{3,1},{4,6},{5,7},{6,4},{7,5},{8,10},{9,11},{10,... | collective-permute-start | bytes 12296 | tf_op jit(solution)/shard_map/ppermute | solution.py:337

commit v4 on v3

--- a/solution.py
+++ b/solution.py
@@ -94,8 +94,8 @@
     return [pl.BlockSpec(memory_space=pltpu.VMEM)] * n
 
 
-def call(kernel, outs, *args, near_memory=(), scratch=(), last=False):
-    args = [pltpu.with_memory_space_constraint(a, pltpu.VMEM) if k in near_memory else a for k, a in enumerate(args)]
+def call(kernel, outs, *args, scratch=(), last=False):
+    args = [pltpu.with_memory_space_constraint(a, pltpu.VMEM) for a in args]
     kind = jax.ShapeDtypeStruct if last else pltpu.VMEM
     return pl.pallas_call(
         kernel,
@@ -139,15 +139,67 @@
                 k += 1
 
 
-def prepare_kernel(
+def turned(planes, rows_of_planes):
+    blocks = [jnp.concatenate(planes[j : j + REACH], axis=0) for j in range(0, rows_of_planes, REACH)]
+    return jnp.concatenate([b.T for b in blocks], axis=1)
+
+
+def coefficients(levels, band, kappa, east, north, upper, ocean):
+    columns, lanes = kappa.shape
+    lane = lax.broadcasted_iota(jnp.int32, (1, lanes), 1)
+    row = lax.broadcasted_iota(jnp.int32, (columns, 1), 0)
+    upper = jnp.where(lane % levels == levels - 1, 0.0, upper)
+    south = jnp.where(lane % band < levels, 0.0, pltpu.roll(north, levels, 1))
+    west = jnp.where(row == 0, 0.0, pltpu.roll(east, 1, 0))
+    ocean_east = jnp.where(row == columns - 1, 1.0, pltpu.roll(ocean, columns - 1, 0))
+    diagonal = ocean * (kappa + east + west + north + south + upper + pltpu.roll(upper, 1, 1))
+    return diagonal, east * ocean * ocean_east, upper * ocean * pltpu.roll(ocean, lanes - 1, 1)
+
+
+def store(statics, edge, diagonal, to_east, north, to_upper, ocean, east):
+    for k, x in enumerate((diagonal, to_east, north, to_upper, ocean)):
+        statics[k] = x
+    edge[0:1] = east[east.shape[0] - 1 :]
+
+
+def own_kernel(
     rows, levels, columns,
-    noise, kappa2, conduct, land, got_second, got_first, weights,
-    field, statics, to_first, to_second, to_others,
+    noise, kappa2, conduct, land, weights,
+    field, statics, edge, to_first, to_second, to_others,
 ):
-    lat_odd = lax.axis_index("lat") % 2
     last_band = lax.axis_index("lat") == lax.axis_size("lat") - 1
     lon_odd = lax.axis_index("lon") % 2
-    lanes = (rows + 2 * REACH) * levels
+    lanes = rows * levels
+
+    def own(load):
+        return turned([load(pl.ds(j, levels, stride=rows)) for j in range(rows)], rows)
+
+    r = own(lambda at: noise[at, :])
+    field[...] = r
+    ocean = own(lambda at: land[at, :].astype(jnp.float32))
+    north = own(lambda at: conduct[1, at, :])
+    kappa = own(lambda at: kappa2[at, :])
+    east = own(lambda at: conduct[0, at, :])
+    upper = own(lambda at: conduct[2, at, :])
+    lane = lax.broadcasted_iota(jnp.int32, (1, lanes), 1)
+    north = jnp.where(last_band & (lane >= lanes - levels), 0.0, north)
+    diagonal, to_east, to_upper = coefficients(levels, lanes, kappa, east, north, upper, ocean)
+    store(statics, edge, diagonal, to_east, north, to_upper, ocean, east)
+    m = dot(weights[...], r)
+    to_others[...] = m
+    m = m[:4]
+    end = columns - 1
+    blank = jnp.zeros((5, lanes), jnp.float32)
+    for_east = [m, r[end:], diagonal[end:], to_east[end - 1 : end], east[end:], ocean[end:], north[end:], to_upper[end:], blank]
+    for_west = [m, r[:1], diagonal[:1], to_east[:1], east[:1], ocean[:1], north[:1], to_upper[:1], blank]
+    for_east = jnp.concatenate(for_east, axis=0)
+    for_west = jnp.concatenate(for_west, axis=0)
+    to_first[...] = jnp.where(lon_odd == 0, for_east, for_west)
+    to_second[...] = jnp.where(lon_odd == 0, for_west, for_east)
+
+
+def ghost_kernel(levels, columns, got_second, got_first, field, statics, edge):
+    lat_odd = lax.axis_index("lat") % 2
     group = REACH * levels
 
     def ghost(kind, north):
@@ -158,60 +210,33 @@
         from_first = (lat_odd == 0) if north else (lat_odd == 1)
         planes = jnp.where(from_first, a, b)
         if count == REACH:
-            return planes
+            return planes.T
         blank = jnp.zeros((group - count * levels, columns), jnp.float32)
-        return jnp.concatenate([planes, blank] if north else [blank, planes], axis=0)
-
-    def turned(kind, load):
-        blocks = [ghost(kind, False)]
-        for j in range(0, rows, REACH):
-            blocks.append(jnp.concatenate([load(pl.ds(j + i, levels, stride=rows)) for i in range(REACH)], axis=0))
-        blocks.append(ghost(kind, True))
-        return jnp.concatenate([b.T for b in blocks], axis=1)
-
-    r = turned(0, lambda at: noise[at, :])
+        return jnp.concatenate([planes, blank] if north else [blank, planes], axis=0).T
+
+    r, ocean, north, kappa, east, upper = (
+        jnp.concatenate([ghost(kind, False), ghost(kind, True)], axis=1) for kind in range(6)
+    )
     field[...] = r
-    ocean = turned(1, lambda at: land[at, :].astype(jnp.float32))
-    north = turned(2, lambda at: conduct[1, at, :])
-    kappa = turned(3, lambda at: kappa2[at, :])
-    east = turned(4, lambda at: conduct[0, at, :])
-    upper = turned(5, lambda at: conduct[2, at, :])
-    lane = lax.broadcasted_iota(jnp.int32, (1, lanes), 1)
-    top = (rows + REACH - 1) * levels
-    ends = last_band & (lane >= top) & (lane < top + levels)
-    north = jnp.where(ends, 0.0, north)
-    upper = jnp.where(lane % levels == levels - 1, 0.0, upper)
-    row = lax.broadcasted_iota(jnp.int32, (columns, 1), 0)
-    west = jnp.where(row == 0, 0.0, pltpu.roll(east, 1, 0))
-    ocean_east = jnp.where(row == columns - 1, 1.0, pltpu.roll(ocean, columns - 1, 0))
-    diagonal = ocean * (
-        kappa + east + west + north + pltpu.roll(north, levels, 1) + upper + pltpu.roll(upper, 1, 1)
-    )
-    to_east = east * ocean * ocean_east
-    to_north = north * ocean * pltpu.roll(ocean, lanes - levels, 1)
-    to_upper = upper * ocean * pltpu.roll(ocean, lanes - 1, 1)
-    statics[0] = diagonal
-    statics[1] = to_east
-    statics[2] = to_north
-    statics[3] = to_upper
-    statics[4] = ocean
-    statics[5] = east
-    m = dot(weights[...], r)
-    to_others[...] = m
-    m = m[:4]
-    end = columns - 1
-    blank = jnp.zeros((5, lanes), jnp.float32)
-    for_east = [m, r[end:], diagonal[end:], to_east[end - 1 : end], east[end:], ocean[end:], to_north[end:], to_upper[end:], blank]
-    for_west = [m, r[:1], diagonal[:1], to_east[:1], east[:1], ocean[:1], to_north[:1], to_upper[:1], blank]
-    for_east = jnp.concatenate(for_east, axis=0)
-    for_west = jnp.concatenate(for_west, axis=0)
-    to_first[...] = jnp.where(lon_odd == 0, for_east, for_west)
-    to_second[...] = jnp.where(lon_odd == 0, for_west, for_east)
-
-
-def circle(near, far, own, received):
+    diagonal, to_east, to_upper = coefficients(levels, group, kappa, east, north, upper, ocean)
+    store(statics, edge, diagonal, to_east, north, to_upper, ocean, east)
+
+
+def forward_kernel(group, *refs):
+    lists, (second, first) = refs[:-2], refs[-2:]
+    odd = lax.axis_index("lat") % 2
+    k = 0
+    for x in lists:
+        count, lanes = x.shape
+        low, high = x[:, 0:group], x[:, lanes - group :]
+        first[pl.ds(k, count)] = jnp.where(odd == 0, high, low)
+        second[pl.ds(k, count)] = jnp.where(odd == 0, low, high)
+        k += count
+
+
+def circle(near, far, own, lists):
     lon_odd = lax.axis_index("lon") % 2
-    told = jnp.concatenate([t[0:8] for t in received], axis=0)
+    told = jnp.concatenate([t[0:8] for t in lists], axis=0)
     return dot(near[...], own) + dot(far[lon_odd], told)
 
 
@@ -228,13 +253,14 @@
     )
 
 
-def apply_twice(levels, columns, v, f, diagonal, to_east, north, upper, ocean, rim):
+def apply_twice(levels, columns, v, f, statics, to_east, rim):
+    diagonal, north, upper, ocean = (statics[k] for k in range(4))
     own = pl.ds(EDGE, columns)
     after = pl.ds(EDGE + 1, columns)
     before = pl.ds(EDGE - 1, columns)
     end = EDGE + columns
     e, w = to_east[own], to_east[before]
-    f[own] = stencil(v[own], v[after], v[before], diagonal[...], e, w, north, upper, levels)
+    f[own] = stencil(v[own], v[after], v[before], diagonal, e, w, north, upper, levels)
     pick = lambda a, b: jnp.concatenate([v[a : a + 1], v[b : b + 1], jnp.zeros((6, v.shape[1]), jnp.float32)], axis=0)
     g = stencil(
         pick(EDGE - 1, end), pick(EDGE, end + 1), pick(EDGE - 2, end - 1),
@@ -242,38 +268,71 @@
     )
     f[EDGE - 1 : EDGE] = g[0:1]
     f[end : end + 1] = g[1:2]
-    second = stencil(f[own], f[after], f[before], diagonal[...], e, w, north, upper, levels)
+    second = stencil(f[own], f[after], f[before], diagonal, e, w, north, upper, levels)
     return jnp.where(ocean > 0.5, second, v[own])
 
 
 def first_kernel(
-    levels, columns, others,
-    field, statics, near, far, weights, mine_first, mine_second, *rest,
+    rows, levels, columns, others,
+    own_field, own_statics, own_edge, field, ghost_statics, edge, near, far, weights, side_second, side_first, *rest,
 ):
     received = rest[: 2 + others]
-    precond, image, diagonal, to_east, rim, to_first, to_second, v, f = rest[2 + others :]
-    lon_odd = lax.axis_index("lon") % 2
-    even = lon_odd == 0
-    a, b = received[0][...], received[1][...]
-    east_list = jnp.where(even, a, b)
-    west_list = jnp.where(even, b, a)
-    v[...] = circle(near, far, field[...], received)
-    ocean = statics[4]
+    precond, image, statics, to_east, rim, to_first, to_second, v, f = rest[2 + others :]
+    lat_odd = lax.axis_index("lat") % 2
+    even = lax.axis_index("lon") % 2 == 0
+    group = REACH * levels
+    lanes = rows * levels + 2 * group
+
+    def joined(own, ghost):
+        return jnp.concatenate([ghost[:, :group], own, ghost[:, group:]], axis=1)
+
+    lists, k = [], 0
+    for x in received:
+        count = x.shape[0]
+        a, b = side_first[pl.ds(k, count)], side_second[pl.ds(k, count)]
+        lists.append(jnp.concatenate([jnp.where(lat_odd == 1, a, b), x[...], jnp.where(lat_odd == 1, b, a)], axis=1))
+        k += count
+    v[...] = circle(near, far, joined(own_field[...], field[...]), lists)
+
+    lane = lax.broadcasted_iota(jnp.int32, (1, lanes), 1)
+    first_of_band = ((lane >= group) & (lane < group + levels)) | ((lane >= lanes - group) & (lane < lanes - group + levels))
+
+    def completed(diagonal, north, ocean):
+        diagonal = diagonal + jnp.where(first_of_band, ocean * pltpu.roll(north, levels, 1), 0.0)
+        return diagonal, north * ocean * pltpu.roll(ocean, lanes - levels, 1)
+
+    ocean = joined(own_statics[4], ghost_statics[4])
+    diagonal, north = completed(
+        joined(own_statics[0], ghost_statics[0]), joined(own_statics[2], ghost_statics[2]), ocean
+    )
+    east_list = jnp.where(even, lists[0], lists[1])
+    west_list = jnp.where(even, lists[1], lists[0])
     end = columns - 1
     row = lax.broadcasted_iota(jnp.int32, (columns, 1), 0)
-    full_east = jnp.where(row == end, statics[1] * east_list[8:9], statics[1])
+    full_east = joined(own_statics[1], ghost_statics[1])
+    full_east = jnp.where(row == end, full_east * east_list[8:9], full_east)
     to_east[pl.ds(EDGE, columns)] = full_east
     face_west = west_list[7:8] * west_list[8:9] * ocean[0:1]
     to_east[EDGE - 1 : EDGE] = face_west
-    diagonal[...] = statics[0] + jnp.where(row == 0, ocean * west_list[7:8], 0.0)
-    blank = jnp.zeros((6, ocean.shape[1]), jnp.float32)
+    statics[0] = diagonal + jnp.where(row == 0, ocean * west_list[7:8], 0.0)
+    statics[1] = north
+    statics[2] = joined(own_statics[3], ghost_statics[3])
+    statics[3] = ocean
+    blank = jnp.zeros((6, lanes), jnp.float32)
     stack = lambda p, q: jnp.concatenate([p, q, blank], axis=0)
-    rim[0] = stack(west_list[5:6], east_list[5:6] + east_list[8:9] * statics[5, end:])
+    last_face = joined(own_edge[0:1], edge[0:1])
+    rim_ocean = stack(west_list[8:9], east_list[8:9])
+    rim_diagonal, rim_north = completed(
+        stack(west_list[5:6], east_list[5:6] + east_list[8:9] * last_face),
+        stack(west_list[9:10], east_list[9:10]),
+        rim_ocean,
+    )
+    rim[0] = rim_diagonal
     rim[1] = stack(face_west, east_list[6:7])
     rim[2] = stack(west_list[6:7], full_east[end:])
-    rim[3] = stack(west_list[9:10], east_list[9:10])
+    rim[3] = rim_north
     rim[4] = stack(west_list[10:11], east_list[10:11])
-    w0 = apply_twice(levels, columns, v, f, diagonal, to_east, statics[2], statics[3], ocean, rim)
+    w0 = apply_twice(levels, columns, v, f, statics, to_east, rim)
     precond[...] = v[pl.ds(EDGE, columns)]
     image[...] = w0
     scaled = w0 * SCALE
@@ -287,16 +346,16 @@
 
 def second_kernel(
     levels, columns, rows, others,
-    field, precond, image, statics, near, far, diagonal, to_east, rim, *rest,
+    field, precond, image, statics, near, far, to_east, rim, *rest,
 ):
     received = rest[: 2 + others]
     again, along, sums, v, f = rest[2 + others :]
     v[...] = circle(near, far, image[...] * SCALE, received)
-    out = apply_twice(levels, columns, v, f, diagonal, to_east, statics[2], statics[3], statics[4], rim)
+    out = apply_twice(levels, columns, v, f, statics, to_east, rim)
     own = slice(REACH * levels, (REACH + rows) * levels)
     again[...] = v[pl.ds(EDGE, columns)][:, own]
     along[...] = out[:, own]
-    r, p, w = field[:, own], precond[:, own], image[:, own]
+    r, p, w = field[...], precond[:, own], image[:, own]
     q, z = again[...], along[...]
 
     def part(x):
@@ -365,10 +424,10 @@
     got_second = lax.ppermute(second, "lat", perm_b)
     got_first = lax.ppermute(first, "lat", perm_a)
 
-    field, statics, to_first, to_second, to_others = call(
-        functools.partial(prepare_kernel, rows, levels, columns),
-        [(columns, lanes), (6, columns, lanes), (16, lanes), (16, lanes), (8, lanes)],
-        noise, kappa2, conduct, land, got_second, got_first, weights, near_memory=range(7),
+    own_field, own_statics, own_edge, to_first, to_second, to_others = call(
+        functools.partial(own_kernel, rows, levels, columns),
+        [(columns, flat), (5, columns, flat), (8, flat), (16, flat), (16, flat), (8, flat)],
+        noise, kappa2, conduct, land, weights,
     )
     lon_a, lon_b = pair_perms(count, True)
 
@@ -379,25 +438,34 @@
         return got
 
     told = exchange(to_first, to_second, to_others)
-    precond, image, diagonal, to_east, rim, to_first2, to_second2 = call(
-        functools.partial(first_kernel, levels, columns, others),
-        [(columns, lanes), (columns, lanes), (columns, lanes), (tall, lanes), (5, 8, lanes), (8, lanes), (8, lanes)],
-        field, statics, near, far, weights, to_first, to_second, *told, near_memory=range(9 + others),
+    heights = sum(x.shape[0] for x in told)
+    group = REACH * levels
+    side_second, side_first = call(functools.partial(forward_kernel, group), [(heights, group)] * 2, *told)
+    side_second = lax.ppermute(side_second, "lat", perm_b)
+    side_first = lax.ppermute(side_first, "lat", perm_a)
+    field, ghost_statics, edge = call(
+        functools.partial(ghost_kernel, levels, columns),
+        [(columns, 2 * group), (5, columns, 2 * group), (8, 2 * group)],
+        got_second, got_first,
+    )
+    precond, image, statics, to_east, rim, to_first, to_second = call(
+        functools.partial(first_kernel, rows, levels, columns, others),
+        [(columns, lanes), (columns, lanes), (4, columns, lanes), (tall, lanes), (5, 8, lanes), (8, lanes), (8, lanes)],
+        own_field, own_statics, own_edge, field, ghost_statics, edge, near, far, weights, side_second, side_first, *told,
         scratch=[(tall, lanes), (tall, lanes)],
     )
-    told = exchange(to_first2, to_second2, to_first2)
+    told = exchange(to_first, to_second, to_first)
     again, along, sums = call(
         functools.partial(second_kernel, levels, columns, rows, others),
         [(columns, flat), (columns, flat), (8, 128)],
-        field, precond, image, statics, near, far, diagonal, to_east, rim, *told,
-        near_memory=range(11 + others),
+        own_field, precond, image, statics, near, far, to_east, rim, *told,
         scratch=[(tall, lanes), (tall, lanes)],
     )
     sums = summed(summed(sums, "lon"), "lat")
     answer, left = call(
         functools.partial(combine_kernel, rows, levels),
         [(flat, columns), (flat, columns)],
-        sums, noise, precond, image, again, along, near_memory=range(6), last=True,
+        sums, noise, precond, image, again, along, last=True,
     )
     return answer.reshape(levels, rows, columns), left.reshape(levels, rows, columns)
 

time: 45.8 us -> 42 us (0.917)
  waiting for transfers between devices: 22 us -> 14.7 us
  starting transfers between devices: 14.7 us -> 18.2 us
    ppermute x1, waiting for transfers between devices: 7.78 us -> 0.01 us  [body(): got_first = lax.ppermute(first, 'lat', perm_a)]
    ppermute x0 -> x2, starting transfers between devices: none -> 2.44 us  [the longest x1 1.78 us: body(): side_first = lax.ppermute(side_first, 'lat', perm_a)]
    ppermute x0 -> x2, waiting for transfers between devices: none -> 1.65 us  [the longest x1 1.65 us: body(): side_first = lax.ppermute(side_first, 'lat', perm_a)]
    ppermute x4, waiting for transfers between devices: 8.87 us -> 7.82 us  [summed(): x = x + lax.ppermute(x, axis, [(i, i ^ step) for i in range(count)])]
    ppermute x4, starting transfers between devices: 4.07 us -> 5.12 us  [summed(): x = x + lax.ppermute(x, axis, [(i, i ^ step) for i in range(count)])]
    pallas_call x4 -> x6, Pallas kernels: 6.5 us -> 6.53 us  [call(): pl.pallas_call(kernel, out_shape=[kind(s, jnp.float32) for s in outs], in...]
  transfers between devices with their start and end apart: 12 -> 14, of which waited for: 8 -> 8; matrix products, arithmetic and copies ran while one was open for 0% -> 0% of each run, Pallas kernels for 0% -> 3%
where the time goes in v4:
time: 42 us; the launch traced here: 41.9 us
  starting transfers between devices  18.2 us (43%)
  waiting for transfers between devices  14.7 us (35%)
  Pallas kernels  8.21 us (20%)
  between operations  0.72 us (2%)
    ppermute x4, waiting for transfers between devices, summed(): x = x + lax.ppermute(x, axis, [(i, i ^ step) for i in range(count)])  7.82 us
    pallas_call x6, Pallas kernels, call(): pl.pallas_call(kernel, out_shape=[kind(s, jnp.float32) for s in outs], in...  6.53 us
    ppermute x1, starting transfers between devices, body(): got_first = lax.ppermute(first, 'lat', perm_a)  5.92 us
    ppermute x4, starting transfers between devices, summed(): x = x + lax.ppermute(x, axis, [(i, i ^ step) for i in range(count)])  5.12 us
    ppermute x2, waiting for transfers between devices, exchange(): lax.ppermute(rest, 'lon', [(i, (i + d) % count) for i in range(count)])  3.81 us
    ppermute x4, starting transfers between devices, exchange(): got = [lax.ppermute(one, 'lon', lon_a), lax.ppermute(two, 'lon', lon_b)]  2.95 us
    ppermute x1, starting transfers between devices, body(): side_first = lax.ppermute(side_first, 'lat', perm_a)  1.78 us
    pallas_call x1, Pallas kernels, body(): pl.pallas_call(functools.partial(band_kernel, rows, levels), out_shape=[p...  1.69 us
  transfers between devices with their start and end apart: 14, of which 8 were waited for; matrix products, arithmetic and copies ran while one was open for 0% of the time, Pallas kernels for 3%

profile of v4, /device:TPU:0, one launch (start us, length us, event | category | flops | bytes accessed | tf_op | source)
XLA Modules:
  0.0 41.9 jit_solution(8445537609933445363)
XLA Ops:
  0.6 1.7 %shard_map.86 = (f32[21,32,128]{2,1,0:T(8,128)S(1)}, f32[21,32,128]{2,1,0:T(8,128)S(1)}, f32[512,128]{1,0:T(8,128)S(1)}, f32[512,128]{1,0:T(8,128)S(1)}, f32[3,5...) custom-call(f32[512,128]{1,0:T(8,128)} %bitcast.7, ...), custom_call_target="tpu_custom_call" | custom-call | tf_op jit(solution)/shard_map/pallas_call | solution.py:415
  2.3 0.7 %collective-permute-start = (f32[21,32,128]{2,1,0:T(8,128)S(1)}, f32[21,32,128]{2,1,0:T(8,128)S(1)}, u32[]{:S(2)}, u32[]{:S(2)}) collective-permute-start(f32[21,32,128]{2,1,0:T(8,128)S(1)} %get-tuple-element.42), channel_id=1, source_target_pairs={{1,2},{2,1},{5,6},{6,5},{9,10},{10,9},{13,14},{14,13},{17,18},{18,... | collective-permute-start | bytes 1032200 | tf_op jit(solution)/shard_map/ppermute | solution.py:424
  3.0 5.9 %collective-permute-start.1 = (f32[21,32,128]{2,1,0:T(8,128)S(1)}, f32[21,32,128]{2,1,0:T(8,128)S(1)}, u32[]{:S(2)}, u32[]{:S(2)}) collective-permute-start(f32[21,32,128]{2,1,0:T(8,128)S(1)} %get-tuple-element.43), channel_id=1, source_target_pairs={{0,1},{2,3},{1,0},{3,2},{4,5},{6,7},{5,4},{7,6},{8,9},{10,11},{9,8... | collective-permute-start | bytes 1032200 | tf_op jit(solution)/shard_map/ppermute | solution.py:425
  8.9 0.9 %shard_map.87 = (f32[128,512]{1,0:T(8,128)S(1)}, f32[5,128,512]{2,1,0:T(8,128)S(1)}, f32[8,512]{1,0:T(8,128)S(1)}, f32[16,512]{1,0:T(8,128)S(1)}, f32[16,512]{1,0:T(8,128)S(1)}, /*index=5*/f32[8,512]{1,0:T(8,128)S(1)}) custom-call(f32[512,128]{1,0:T(8,128)S(1)} %get-tuple-element.34.noise, f32[512,128]{1,0:T(8,128)S(1)} %get-tuple-element.35.kappa2, ...), custom_call_target="tpu_custom_call" | custom-call | tf_op jit(solution)/shard_map/pallas_call | solution.py:100
  9.9 0.1 collective-permute-start.2
  10.0 1.6 %collective-permute-start.3 = (f32[16,512]{1,0:T(8,128)S(1)}, f32[16,512]{1,0:T(8,128)S(1)}, u32[]{:S(2)}, u32[]{:S(2)}) collective-permute-start(f32[16,512]{1,0:T(8,128)S(1)} %get-tuple-element.50), channel_id=1, source_target_pairs={{4,8},{12,0},{8,4},{0,12},{5,9},{13,1},{9,5},{1,13},{6,10},{14,2},... | collective-permute-start | bytes 98312 | tf_op jit(solution)/shard_map/ppermute | solution.py:435
  11.5 0.5 %collective-permute-start.4 = (f32[8,512]{1,0:T(8,128)S(1)}, f32[8,512]{1,0:T(8,128)S(1)}, u32[]{:S(2)}, u32[]{:S(2)}) collective-permute-start(f32[8,512]{1,0:T(8,128)S(1)} %get-tuple-element.51), channel_id=1, source_target_pairs={{0,8},{4,12},{8,0},{12,4},{1,9},{5,13},{9,1},{13,5},{2,10},{6,14},... | collective-permute-start | bytes 49160 | tf_op jit(solution)/shard_map/ppermute | solution.py:437
  12.1 3.2 %collective-permute-done.4.refs_2_.rest_2_ = f32[8,512]{1,0:T(8,128)S(1)} collective-permute-done((f32[8,512]{1,0:T(8,128)S(1)}, f32[8,512]{1,0:T(8,128)S(1)}, u32[]{:S(2)}, u32[]{:S(2)}) %collective-permute-start.4) | collective-permute-done | bytes 16416 | tf_op jit(solution)/shard_map/ppermute | solution.py:437
  15.3 0.0 collective-permute-done.2.refs_0_.rest_0_
  15.3 0.0 collective-permute-done.3.refs_1_.rest_1_
  15.3 0.7 %collective-permute-start.5 = (f32[40,128]{1,0:T(8,128)S(1)}, f32[40,128]{1,0:T(8,128)S(1)}, u32[]{:S(2)}, u32[]{:S(2)}) collective-permute-start(f32[40,128]{1,0:T(8,128)S(1)} %get-tuple-element.52), channel_id=1, source_target_pairs={{1,2},{2,1},{5,6},{6,5},{9,10},{10,9},{13,14},{14,13},{17,18},{18,... | collective-permute-start | bytes 61448 | tf_op jit(solution)/shard_map/ppermute | solution.py:444
  16.0 1.8 %collective-permute-start.6 = (f32[40,128]{1,0:T(8,128)S(1)}, f32[40,128]{1,0:T(8,128)S(1)}, u32[]{:S(2)}, u32[]{:S(2)}) collective-permute-start(f32[40,128]{1,0:T(8,128)S(1)} %get-tuple-element.53), channel_id=1, source_target_pairs={{0,1},{2,3},{1,0},{3,2},{4,5},{6,7},{5,4},{7,6},{8,9},{10,11},{9,8... | collective-permute-start | bytes 61448 | tf_op jit(solution)/shard_map/ppermute | solution.py:445
  17.8 0.0 collective-permute-done.got_second
  17.8 0.0 collective-permute-done.1.got_first
  17.8 0.4 shard_map.88
  18.2 0.0 collective-permute-done.5.side_second
  18.2 1.6 %collective-permute-done.6.side_first = f32[40,128]{1,0:T(8,128)S(1)} collective-permute-done((f32[40,128]{1,0:T(8,128)S(1)}, f32[40,128]{1,0:T(8,128)S(1)}, u32[]{:S(2)}, u32[]{:S(2)}) %collective-permute-start.6) | collective-permute-done | bytes 20512 | tf_op jit(solution)/shard_map/ppermute | solution.py:445
  19.8 2.2 %shard_map.90 = (f32[128,768]{1,0:T(8,128)S(1)}, f32[128,768]{1,0:T(8,128)S(1)}, f32[4,128,768]{2,1,0:T(8,128)S(1)}, f32[144,768]{1,0:T(8,128)S(1)}, f32[5,8,768...) custom-call(f32[128,512]{1,0:T(8,128)S(1)} %get-tuple-element.39.own_field.field, ...), custom_call_target="tpu_custom_call" | custom-call | tf_op jit(solution)/shard_map/pallas_call | solution.py:100
  22.0 0.0 collective-permute-start.8
  22.0 0.6 %collective-permute-start.9 = (f32[8,768]{1,0:T(8,128)S(1)}, f32[8,768]{1,0:T(8,128)S(1)}, u32[]{:S(2)}, u32[]{:S(2)}) collective-permute-start(f32[8,768]{1,0:T(8,128)S(1)} %get-tuple-element.59), channel_id=1, source_target_pairs={{0,8},{4,12},{8,0},{12,4},{1,9},{5,13},{9,1},{13,5},{2,10},{6,14},... | collective-permute-start | bytes 73736 | tf_op jit(solution)/shard_map/ppermute | solution.py:437
  22.6 1.3 %collective-permute-start.7 = (f32[8,768]{1,0:T(8,128)S(1)}, f32[8,768]{1,0:T(8,128)S(1)}, u32[]{:S(2)}, u32[]{:S(2)}) collective-permute-start(f32[8,768]{1,0:T(8,128)S(1)} %get-tuple-element.59), channel_id=1, source_target_pairs={{0,4},{8,12},{4,0},{12,8},{1,5},{9,13},{5,1},{13,9},{2,6},{10,14},... | collective-permute-start | bytes 73736 | tf_op jit(solution)/shard_map/ppermute | solution.py:435
  23.9 1.4 %collective-permute-done.8.rest_1_ = f32[8,768]{1,0:T(8,128)S(1)} collective-permute-done((f32[8,768]{1,0:T(8,128)S(1)}, f32[8,768]{1,0:T(8,128)S(1)}, u32[]{:S(2)}, u32[]{:S(2)}) %collective-permute-start.8) | collective-permute-done | bytes 24608 | tf_op jit(solution)/shard_map/ppermute | solution.py:435
  25.3 0.6 %collective-permute-done.9.rest_2_ = f32[8,768]{1,0:T(8,128)S(1)} collective-permute-done((f32[8,768]{1,0:T(8,128)S(1)}, f32[8,768]{1,0:T(8,128)S(1)}, u32[]{:S(2)}, u32[]{:S(2)}) %collective-permute-start.9) | collective-permute-done | bytes 24608 | tf_op jit(solution)/shard_map/ppermute | solution.py:437
  25.9 0.0 collective-permute-done.7.rest_0_
  25.9 1.7 %shard_map.91 = (f32[128,512]{1,0:T(8,128)S(1)}, f32[128,512]{1,0:T(8,128)S(1)}, f32[8,128]{1,0:T(8,128)S(1)}) custom-call(f32[128,512]{1,0:T(8,128)S(1)} %get-tuple-element.39.own_field.field, f32[128,768]{1,0:T(8,128)S(1)} %get-tuple-element.54.precond, f32[128,768]{1,0:T(8,128)S(1)} %get-tuple-element.55.image, ...), custom_call_target="tpu_custom_call" | custom-call | tf_op jit(solution)/shard_map/pallas_call | solution.py:100
  27.6 0.1 collective-permute-start.10
  27.7 1.2 %collective-permute-done.10 = f32[8,128]{1,0:T(8,128)S(1)} collective-permute-done((f32[8,128]{1,0:T(8,128)S(1)}, f32[8,128]{1,0:T(8,128)S(1)}, u32[]{:S(2)}, u32[]{:S(2)}) %collective-permute-start.10) | collective-permute-done | bytes 4128 | tf_op jit(solution)/shard_map/ppermute | solution.py:396
  28.8 0.6 %collective-permute-start.11 = (f32[8,128]{1,0:T(8,128)S(1)}, f32[8,128]{1,0:T(8,128)S(1)}, u32[]{:S(2)}, u32[]{:S(2)}) collective-permute-start(f32[8,128]{1,0:T(8,128)S(1)} %add.12), channel_id=1, source_target_pairs={{0,8},{4,12},{8,0},{12,4},{1,9},{5,13},{9,1},{13,5},{2,10},{6,14},... | collective-permute-start | bytes 12296 | tf_op jit(solution)/shard_map/ppermute | solution.py:396
  29.5 3.0 %collective-permute-done.11 = f32[8,128]{1,0:T(8,128)S(1)} collective-permute-done((f32[8,128]{1,0:T(8,128)S(1)}, f32[8,128]{1,0:T(8,128)S(1)}, u32[]{:S(2)}, u32[]{:S(2)}) %collective-permute-start.11) | collective-permute-done | bytes 4128 | tf_op jit(solution)/shard_map/ppermute | solution.py:396
  32.5 1.7 %collective-permute-start.12 = (f32[8,128]{1,0:T(8,128)S(1)}, f32[8,128]{1,0:T(8,128)S(1)}, u32[]{:S(2)}, u32[]{:S(2)}) collective-permute-start(f32[8,128]{1,0:T(8,128)S(1)} %add.13), channel_id=1, source_target_pairs={{0,1},{1,0},{2,3},{3,2},{4,5},{5,4},{6,7},{7,6},{8,9},{9,8},{10,11... | collective-permute-start | bytes 12296 | tf_op jit(solution)/shard_map/ppermute | solution.py:396
  34.2 1.9 %collective-permute-done.12 = f32[8,128]{1,0:T(8,128)S(1)} collective-permute-done((f32[8,128]{1,0:T(8,128)S(1)}, f32[8,128]{1,0:T(8,128)S(1)}, u32[]{:S(2)}, u32[]{:S(2)}) %collective-permute-start.12) | collective-permute-done | bytes 4128 | tf_op jit(solution)/shard_map/ppermute | solution.py:396
  36.1 2.7 %collective-permute-start.13 = (f32[8,128]{1,0:T(8,128)S(1)}, f32[8,128]{1,0:T(8,128)S(1)}, u32[]{:S(2)}, u32[]{:S(2)}) collective-permute-start(f32[8,128]{1,0:T(8,128)S(1)} %add.14), channel_id=1, source_target_pairs={{0,2},{1,3},{2,0},{3,1},{4,6},{5,7},{6,4},{7,5},{8,10},{9,11},{10,... | collective-permute-start | bytes 12296 | tf_op jit(solution)/shard_map/ppermute | solution.py:396
  38.8 1.8 %collective-permute-done.13 = f32[8,128]{1,0:T(8,128)S(1)} collective-permute-done((f32[8,128]{1,0:T(8,128)S(1)}, f32[8,128]{1,0:T(8,128)S(1)}, u32[]{:S(2)}, u32[]{:S(2)}) %collective-permute-start.13) | collective-permute-done | bytes 4128 | tf_op jit(solution)/shard_map/ppermute | solution.py:396
  40.6 1.3 %shard_map.92 = (f32[512,128]{1,0:T(8,128)}, f32[512,128]{1,0:T(8,128)}) custom-call(f32[8,128]{1,0:T(8,128)S(1)} %add.15.sums, f32[512,128]{1,0:T(8,128)S(1)} %get-tuple-element.34.noise, f32[128,768]{1,0:T(8,128)S(1)} %get-tuple-element.54.precond, f32[128,768]{1,0:T(8,128)S(1)} %get-tuple-element.55.image, f32[128,512]{1,0:T(8,128)S(1)} %get-tuple-element.62.again, ...), custom_call_target="tpu_custom_call" | custom-call | tf_op jit(solution)/shard_map/pallas_call | solution.py:100
  (5 shorter events, 0.0 us)
Async XLA Ops:
  2.3 15.4 %collective-permute-start = (f32[21,32,128]{2,1,0:T(8,128)S(1)}, f32[21,32,128]{2,1,0:T(8,128)S(1)}, u32[]{:S(2)}, u32[]{:S(2)}) collective-permute-start(f32[21,32,128]{2,1,0:T(8,128)S(1)} %get-tuple-element.42), channel_id=1, source_target_pairs={{1,2},{2,1},{5,6},{6,5},{9,10},{10,9},{13,14},{14,13},{17,18},{18,... | collective-permute-start | bytes 1032200 | tf_op jit(solution)/shard_map/ppermute | solution.py:424
  3.0 14.8 %collective-permute-start.1 = (f32[21,32,128]{2,1,0:T(8,128)S(1)}, f32[21,32,128]{2,1,0:T(8,128)S(1)}, u32[]{:S(2)}, u32[]{:S(2)}) collective-permute-start(f32[21,32,128]{2,1,0:T(8,128)S(1)} %get-tuple-element.43), channel_id=1, source_target_pairs={{0,1},{2,3},{1,0},{3,2},{4,5},{6,7},{5,4},{7,6},{8,9},{10,11},{9,8... | collective-permute-start | bytes 1032200 | tf_op jit(solution)/shard_map/ppermute | solution.py:425
  9.9 5.4 %collective-permute-start.2 = (f32[16,512]{1,0:T(8,128)S(1)}, f32[16,512]{1,0:T(8,128)S(1)}, u32[]{:S(2)}, u32[]{:S(2)}) collective-permute-start(f32[16,512]{1,0:T(8,128)S(1)} %get-tuple-element.49), channel_id=1, source_target_pairs={{0,4},{8,12},{4,0},{12,8},{1,5},{9,13},{5,1},{13,9},{2,6},{10,14},... | collective-permute-start | bytes 98312 | tf_op jit(solution)/shard_map/ppermute | solution.py:435
  10.0 5.3 %collective-permute-start.3 = (f32[16,512]{1,0:T(8,128)S(1)}, f32[16,512]{1,0:T(8,128)S(1)}, u32[]{:S(2)}, u32[]{:S(2)}) collective-permute-start(f32[16,512]{1,0:T(8,128)S(1)} %get-tuple-element.50), channel_id=1, source_target_pairs={{4,8},{12,0},{8,4},{0,12},{5,9},{13,1},{9,5},{1,13},{6,10},{14,2},... | collective-permute-start | bytes 98312 | tf_op jit(solution)/shard_map/ppermute | solution.py:435
  11.5 3.7 %collective-permute-start.4 = (f32[8,512]{1,0:T(8,128)S(1)}, f32[8,512]{1,0:T(8,128)S(1)}, u32[]{:S(2)}, u32[]{:S(2)}) collective-permute-start(f32[8,512]{1,0:T(8,128)S(1)} %get-tuple-element.51), channel_id=1, source_target_pairs={{0,8},{4,12},{8,0},{12,4},{1,9},{5,13},{9,1},{13,5},{2,10},{6,14},... | collective-permute-start | bytes 49160 | tf_op jit(solution)/shard_map/ppermute | solution.py:437
  15.3 2.9 %collective-permute-start.5 = (f32[40,128]{1,0:T(8,128)S(1)}, f32[40,128]{1,0:T(8,128)S(1)}, u32[]{:S(2)}, u32[]{:S(2)}) collective-permute-start(f32[40,128]{1,0:T(8,128)S(1)} %get-tuple-element.52), channel_id=1, source_target_pairs={{1,2},{2,1},{5,6},{6,5},{9,10},{10,9},{13,14},{14,13},{17,18},{18,... | collective-permute-start | bytes 61448 | tf_op jit(solution)/shard_map/ppermute | solution.py:444
  16.0 3.8 %collective-permute-start.6 = (f32[40,128]{1,0:T(8,128)S(1)}, f32[40,128]{1,0:T(8,128)S(1)}, u32[]{:S(2)}, u32[]{:S(2)}) collective-permute-start(f32[40,128]{1,0:T(8,128)S(1)} %get-tuple-element.53), channel_id=1, source_target_pairs={{0,1},{2,3},{1,0},{3,2},{4,5},{6,7},{5,4},{7,6},{8,9},{10,11},{9,8... | collective-permute-start | bytes 61448 | tf_op jit(solution)/shard_map/ppermute | solution.py:445
  22.0 3.3 %collective-permute-start.8 = (f32[8,768]{1,0:T(8,128)S(1)}, f32[8,768]{1,0:T(8,128)S(1)}, u32[]{:S(2)}, u32[]{:S(2)}) collective-permute-start(f32[8,768]{1,0:T(8,128)S(1)} %get-tuple-element.60), channel_id=1, source_target_pairs={{4,8},{12,0},{8,4},{0,12},{5,9},{13,1},{9,5},{1,13},{6,10},{14,2},... | collective-permute-start | bytes 73736 | tf_op jit(solution)/shard_map/ppermute | solution.py:435
  22.0 3.9 %collective-permute-start.9 = (f32[8,768]{1,0:T(8,128)S(1)}, f32[8,768]{1,0:T(8,128)S(1)}, u32[]{:S(2)}, u32[]{:S(2)}) collective-permute-start(f32[8,768]{1,0:T(8,128)S(1)} %get-tuple-element.59), channel_id=1, source_target_pairs={{0,8},{4,12},{8,0},{12,4},{1,9},{5,13},{9,1},{13,5},{2,10},{6,14},... | collective-permute-start | bytes 73736 | tf_op jit(solution)/shard_map/ppermute | solution.py:437
  22.6 3.3 %collective-permute-start.7 = (f32[8,768]{1,0:T(8,128)S(1)}, f32[8,768]{1,0:T(8,128)S(1)}, u32[]{:S(2)}, u32[]{:S(2)}) collective-permute-start(f32[8,768]{1,0:T(8,128)S(1)} %get-tuple-element.59), channel_id=1, source_target_pairs={{0,4},{8,12},{4,0},{12,8},{1,5},{9,13},{5,1},{13,9},{2,6},{10,14},... | collective-permute-start | bytes 73736 | tf_op jit(solution)/shard_map/ppermute | solution.py:435
  27.6 1.2 %collective-permute-start.10 = (f32[8,128]{1,0:T(8,128)S(1)}, f32[8,128]{1,0:T(8,128)S(1)}, u32[]{:S(2)}, u32[]{:S(2)}) collective-permute-start(f32[8,128]{1,0:T(8,128)S(1)} %get-tuple-element.61), channel_id=1, source_target_pairs={{0,4},{4,0},{8,12},{12,8},{1,5},{5,1},{9,13},{13,9},{2,6},{6,2},{1... | collective-permute-start | bytes 12296 | tf_op jit(solution)/shard_map/ppermute | solution.py:396
  28.8 3.6 %collective-permute-start.11 = (f32[8,128]{1,0:T(8,128)S(1)}, f32[8,128]{1,0:T(8,128)S(1)}, u32[]{:S(2)}, u32[]{:S(2)}) collective-permute-start(f32[8,128]{1,0:T(8,128)S(1)} %add.12), channel_id=1, source_target_pairs={{0,8},{4,12},{8,0},{12,4},{1,9},{5,13},{9,1},{13,5},{2,10},{6,14},... | collective-permute-start | bytes 12296 | tf_op jit(solution)/shard_map/ppermute | solution.py:396
  32.5 3.6 %collective-permute-start.12 = (f32[8,128]{1,0:T(8,128)S(1)}, f32[8,128]{1,0:T(8,128)S(1)}, u32[]{:S(2)}, u32[]{:S(2)}) collective-permute-start(f32[8,128]{1,0:T(8,128)S(1)} %add.13), channel_id=1, source_target_pairs={{0,1},{1,0},{2,3},{3,2},{4,5},{5,4},{6,7},{7,6},{8,9},{9,8},{10,11... | collective-permute-start | bytes 12296 | tf_op jit(solution)/shard_map/ppermute | solution.py:396
  36.1 4.5 %collective-permute-start.13 = (f32[8,128]{1,0:T(8,128)S(1)}, f32[8,128]{1,0:T(8,128)S(1)}, u32[]{:S(2)}, u32[]{:S(2)}) collective-permute-start(f32[8,128]{1,0:T(8,128)S(1)} %add.14), channel_id=1, source_target_pairs={{0,2},{1,3},{2,0},{3,1},{4,6},{5,7},{6,4},{7,5},{8,10},{9,11},{10,... | collective-permute-start | bytes 12296 | tf_op jit(solution)/shard_map/ppermute | solution.py:396

commit v5 on v4

--- a/solution.py
+++ b/solution.py
@@ -77,8 +77,8 @@
             np.concatenate([block(count - 1), block(1)] + others, axis=1),
         ]
     )
-    as_f32 = lambda m: np.asarray(m, np.float32)
-    return as_f32(near), as_f32(moments), as_f32(far)
+    spread = np.stack([np.concatenate([near, f], axis=1) for f in far])
+    return np.asarray(spread, np.float32), np.asarray(moments, np.float32)
 
 
 def pair_perms(count, wrap):
@@ -104,6 +104,7 @@
         out_specs=whole(len(outs)),
         scratch_shapes=[pltpu.VMEM(s, jnp.float32) for s in scratch],
         compiler_params=pltpu.CompilerParams(vmem_limit_bytes=24 << 20),
+        name=kernel.func.__name__,
     )(*args)
 
 
@@ -112,7 +113,7 @@
 
 
 def band_kernel(rows, levels, *refs):
-    sources, (second, first), copies, sems = refs[:7], refs[7:9], refs[9:16], refs[16]
+    sources, (second, first), copies, sems = refs[:6], refs[6:8], refs[8:14], refs[14]
     moves = [pltpu.make_async_copy(x, y, sems.at[k]) for k, (x, y) in enumerate(zip(sources, copies))]
     for move in moves:
         move.start()
@@ -234,10 +235,10 @@
         k += count
 
 
-def circle(near, far, own, lists):
+def circle(spread, own, lists):
     lon_odd = lax.axis_index("lon") % 2
-    told = jnp.concatenate([t[0:8] for t in lists], axis=0)
-    return dot(near[...], own) + dot(far[lon_odd], told)
+    told = jnp.concatenate([own] + [t[0:8] for t in lists], axis=0)
+    return dot(spread[lon_odd], told)
 
 
 def stencil(v, east_v, west_v, d, e, w, n, u, levels):
@@ -274,7 +275,7 @@
 
 def first_kernel(
     rows, levels, columns, others,
-    own_field, own_statics, own_edge, field, ghost_statics, edge, near, far, weights, side_second, side_first, *rest,
+    own_field, own_statics, own_edge, field, ghost_statics, edge, spread, weights, side_second, side_first, *rest,
 ):
     received = rest[: 2 + others]
     precond, image, statics, to_east, rim, to_first, to_second, v, f = rest[2 + others :]
@@ -292,7 +293,7 @@
         a, b = side_first[pl.ds(k, count)], side_second[pl.ds(k, count)]
         lists.append(jnp.concatenate([jnp.where(lat_odd == 1, a, b), x[...], jnp.where(lat_odd == 1, b, a)], axis=1))
         k += count
-    v[...] = circle(near, far, joined(own_field[...], field[...]), lists)
+    v[...] = circle(spread, joined(own_field[...], field[...]), lists)
 
     lane = lax.broadcasted_iota(jnp.int32, (1, lanes), 1)
     first_of_band = ((lane >= group) & (lane < group + levels)) | ((lane >= lanes - group) & (lane < lanes - group + levels))
@@ -346,11 +347,11 @@
 
 def second_kernel(
     levels, columns, rows, others,
-    field, precond, image, statics, near, far, to_east, rim, *rest,
+    field, precond, image, statics, spread, to_east, rim, *rest,
 ):
     received = rest[: 2 + others]
     again, along, sums, v, f = rest[2 + others :]
-    v[...] = circle(near, far, image[...] * SCALE, received)
+    v[...] = circle(spread, image[...] * SCALE, received)
     out = apply_twice(levels, columns, v, f, statics, to_east, rim)
     own = slice(REACH * levels, (REACH + rows) * levels)
     again[...] = v[pl.ds(EDGE, columns)][:, own]
@@ -366,8 +367,9 @@
     sums[...] = jnp.concatenate(parts, axis=0)
 
 
-def combine_kernel(rows, levels, sums, noise, precond, image, again, along, answer, left):
-    total = jnp.sum(sums[...], axis=1, keepdims=True)
+def combine_kernel(rows, levels, here, beside, noise, precond, image, again, along, answer, left):
+    odd = lax.axis_index("lon") % 2 == 1
+    total = jnp.sum(jnp.where(odd, here[...], beside[...]), axis=1, keepdims=True)
     energy, curve, mixed, last = total[0:1], total[1:2], total[2:3], total[3:4]
     alpha = energy / curve
     beta = alpha / SCALE
@@ -389,16 +391,26 @@
             left[to, :] = noise[to, :] - yt[part]
 
 
-def summed(x, axis):
-    count = lax.axis_size(axis)
-    step = 1
-    while step < count:
-        x = x + lax.ppermute(x, axis, [(i, i ^ step) for i in range(count)])
-        step *= 2
-    return x
-
-
-def body(near, weights, far, noise, kappa2, conduct, land):
+def doubling(count):
+    steps = []
+    while 2 ** len(steps) < count:
+        steps.append(2 ** len(steps))
+    return steps
+
+
+def summed(x):
+    count, bands = lax.axis_size("lon"), lax.axis_size("lat")
+    x = x + lax.ppermute(x, "lon", [(i, i + 1) for i in range(0, count, 2)])
+    odd = range(1, count, 2)
+    for step in doubling(count)[1:]:
+        x = x + lax.ppermute(x, "lon", [(i, i ^ step) for i in odd])
+    for step in doubling(bands):
+        pairs = [(i * bands + j, i * bands + (j ^ step)) for i in odd for j in range(bands)]
+        x = x + lax.ppermute(x, ("lon", "lat"), pairs)
+    return x, lax.ppermute(x, "lon", [(i, i - 1) for i in odd])
+
+
+def body(spread, weights, noise, kappa2, conduct, land):
     levels, rows, columns = noise.shape
     count = lax.axis_size("lon")
     others = count - 3
@@ -410,15 +422,16 @@
     land = land.reshape(flat, columns)
     conduct = conduct.reshape(3, flat, columns)
 
-    sources = (noise, kappa2, conduct, land, near, far, weights)
+    sources = (noise, kappa2, conduct, land, spread, weights)
     planes = (PLANES, levels, columns)
-    second, first, noise, kappa2, conduct, land, near, far, weights = pl.pallas_call(
+    second, first, noise, kappa2, conduct, land, spread, weights = pl.pallas_call(
         functools.partial(band_kernel, rows, levels),
         out_shape=[pltpu.VMEM(planes, jnp.float32)] * 2 + [pltpu.VMEM(x.shape, x.dtype) for x in sources],
         in_specs=[pl.BlockSpec(memory_space=pltpu.HBM)] * len(sources),
         out_specs=whole(2 + len(sources)),
         scratch_shapes=[pltpu.SemaphoreType.DMA((len(sources),))],
         compiler_params=pltpu.CompilerParams(vmem_limit_bytes=8 << 20),
+        name="band_kernel",
     )(*[pltpu.with_memory_space_constraint(x, pltpu.HBM) for x in sources])
     perm_a, perm_b = pair_perms(lax.axis_size("lat"), False)
     got_second = lax.ppermute(second, "lat", perm_b)
@@ -451,21 +464,21 @@
     precond, image, statics, to_east, rim, to_first, to_second = call(
         functools.partial(first_kernel, rows, levels, columns, others),
         [(columns, lanes), (columns, lanes), (4, columns, lanes), (tall, lanes), (5, 8, lanes), (8, lanes), (8, lanes)],
-        own_field, own_statics, own_edge, field, ghost_statics, edge, near, far, weights, side_second, side_first, *told,
+        own_field, own_statics, own_edge, field, ghost_statics, edge, spread, weights, side_second, side_first, *told,
         scratch=[(tall, lanes), (tall, lanes)],
     )
     told = exchange(to_first, to_second, to_first)
     again, along, sums = call(
         functools.partial(second_kernel, levels, columns, rows, others),
         [(columns, flat), (columns, flat), (8, 128)],
-        own_field, precond, image, statics, near, far, to_east, rim, *told,
+        own_field, precond, image, statics, spread, to_east, rim, *told,
         scratch=[(tall, lanes), (tall, lanes)],
     )
-    sums = summed(summed(sums, "lon"), "lat")
+    here, beside = summed(sums)
     answer, left = call(
         functools.partial(combine_kernel, rows, levels),
         [(flat, columns), (flat, columns)],
-        sums, noise, precond, image, again, along, last=True,
+        here, beside, noise, precond, image, again, along, last=True,
     )
     return answer.reshape(levels, rows, columns), left.reshape(levels, rows, columns)
 
@@ -473,9 +486,9 @@
 def solution(mesh):
     def run(noise, kappa2, conduct, land):
         count = mesh.shape["lon"]
-        near, weights, far = circle_matrices(count, noise.shape[2] // count)
+        spread, weights = circle_matrices(count, noise.shape[2] // count)
         return jax.shard_map(
-            functools.partial(body, near, weights, far),
+            functools.partial(body, spread, weights),
             mesh=mesh,
             in_specs=(
                 P("ens", "lat", "lon"),

time: 42 us -> 47.3 us (1.13)
  waiting for transfers between devices: 14.7 us -> 20.6 us
    ppermute x4 -> x5, waiting for transfers between devices: 7.82 us -> 13.7 us  [the longest x1 12.9 us: summed(): return (x, lax.ppermute(x, 'lon', [(i, i - 1) for i in odd]))]
    ppermute x4 -> x5, starting transfers between devices: 5.12 us -> 4.67 us  [the longest x1 1.41 us: summed(): x = x + lax.ppermute(x, 'lon', [(i, i + 1) for i in range(0, count, 2)])]
  transfers between devices with their start and end apart: 14 -> 15, of which waited for: 8 -> 6; matrix products, arithmetic and copies ran while one was open for 0% -> 0% of each run, Pallas kernels for 3% -> 3%
where the time goes in v5:
time: 47.3 us; the launch traced here: 47 us
  waiting for transfers between devices  20.6 us (44%)
  starting transfers between devices  17.8 us (38%)
  Pallas kernels  7.83 us (17%)
  between operations  0.79 us (2%)
    ppermute x1, waiting for transfers between devices, summed(): return (x, lax.ppermute(x, 'lon', [(i, i - 1) for i in odd]))  12.9 us
    pallas_call x6, Pallas kernels, call(): pl.pallas_call(kernel, out_shape=[kind(s, jnp.float32) for s in outs], in...  6.12 us
    ppermute x1, starting transfers between devices, body(): got_first = lax.ppermute(first, 'lat', perm_a)  5.92 us
    ppermute x2, waiting for transfers between devices, exchange(): lax.ppermute(rest, 'lon', [(i, (i + d) % count) for i in range(count)])  3.81 us
    ppermute x4, starting transfers between devices, exchange(): got = [lax.ppermute(one, 'lon', lon_a), lax.ppermute(two, 'lon', lon_b)]  2.96 us
    ppermute x1, starting transfers between devices, body(): side_first = lax.ppermute(side_first, 'lat', perm_a)  1.78 us
    pallas_call x1, Pallas kernels, body(): pl.pallas_call(functools.partial(band_kernel, rows, levels), out_shape=[p...  1.71 us
    ppermute x1, waiting for transfers between devices, body(): side_first = lax.ppermute(side_first, 'lat', perm_a)  1.65 us
  transfers between devices with their start and end apart: 15, of which 6 were waited for; matrix products, arithmetic and copies ran while one was open for 0% of the time, Pallas kernels for 3%

profile of v5, /device:TPU:0, one launch (start us, length us, event | category | flops | bytes accessed | tf_op | source)
XLA Modules:
  0.0 47.0 jit_solution(15168870460142301739)
XLA Ops:
  0.6 1.7 %band_kernel.1 = (f32[21,32,128]{2,1,0:T(8,128)S(1)}, f32[21,32,128]{2,1,0:T(8,128)S(1)}, f32[512,128]{1,0:T(8,128)S(1)}, f32[512,128]{1,0:T(8,128)S(1)}, f32[3,...) custom-call(f32[512,128]{1,0:T(8,128)} %bitcast.7, ...), custom_call_target="tpu_custom_call" | custom-call | tf_op jit(solution)/shard_map/band_kernel/pallas_call | solution.py:427
  2.3 0.7 %collective-permute-start = (f32[21,32,128]{2,1,0:T(8,128)S(1)}, f32[21,32,128]{2,1,0:T(8,128)S(1)}, u32[]{:S(2)}, u32[]{:S(2)}) collective-permute-start(f32[21,32,128]{2,1,0:T(8,128)S(1)} %get-tuple-element.41), channel_id=1, source_target_pairs={{1,2},{2,1},{5,6},{6,5},{9,10},{10,9},{13,14},{14,13},{17,18},{18,... | collective-permute-start | bytes 1032200 | tf_op jit(solution)/shard_map/ppermute | solution.py:437
  3.0 5.9 %collective-permute-start.1 = (f32[21,32,128]{2,1,0:T(8,128)S(1)}, f32[21,32,128]{2,1,0:T(8,128)S(1)}, u32[]{:S(2)}, u32[]{:S(2)}) collective-permute-start(f32[21,32,128]{2,1,0:T(8,128)S(1)} %get-tuple-element.42), channel_id=1, source_target_pairs={{0,1},{2,3},{1,0},{3,2},{4,5},{6,7},{5,4},{7,6},{8,9},{10,11},{9,8... | collective-permute-start | bytes 1032200 | tf_op jit(solution)/shard_map/ppermute | solution.py:438
  9.0 0.9 %own_kernel.1 = (f32[128,512]{1,0:T(8,128)S(1)}, f32[5,128,512]{2,1,0:T(8,128)S(1)}, f32[8,512]{1,0:T(8,128)S(1)}, f32[16,512]{1,0:T(8,128)S(1)}, f32[16,512]{1,0:T(8,128)S(1)}, /*index=5*/f32[8,512]{1,0:T(8,128)S(1)}) custom-call(f32[512,128]{1,0:T(8,128)S(1)} %get-tuple-element.33.noise, f32[512,128]{1,0:T(8,128)S(1)} %get-tuple-element.34.kappa2, ...), custom_call_target="tpu_custom_call" | custom-call | tf_op jit(solution)/shard_map/own_kernel/pallas_call | solution.py:100
  9.9 0.1 collective-permute-start.2
  10.0 1.6 %collective-permute-start.3 = (f32[16,512]{1,0:T(8,128)S(1)}, f32[16,512]{1,0:T(8,128)S(1)}, u32[]{:S(2)}, u32[]{:S(2)}) collective-permute-start(f32[16,512]{1,0:T(8,128)S(1)} %get-tuple-element.48), channel_id=1, source_target_pairs={{4,8},{12,0},{8,4},{0,12},{5,9},{13,1},{9,5},{1,13},{6,10},{14,2},... | collective-permute-start | bytes 98312 | tf_op jit(solution)/shard_map/ppermute | solution.py:448
  11.6 0.5 %collective-permute-start.4 = (f32[8,512]{1,0:T(8,128)S(1)}, f32[8,512]{1,0:T(8,128)S(1)}, u32[]{:S(2)}, u32[]{:S(2)}) collective-permute-start(f32[8,512]{1,0:T(8,128)S(1)} %get-tuple-element.49), channel_id=1, source_target_pairs={{0,8},{4,12},{8,0},{12,4},{1,9},{5,13},{9,1},{13,5},{2,10},{6,14},... | collective-permute-start | bytes 49160 | tf_op jit(solution)/shard_map/ppermute | solution.py:450
  12.1 3.2 %collective-permute-done.4.refs_2_.rest_2_ = f32[8,512]{1,0:T(8,128)S(1)} collective-permute-done((f32[8,512]{1,0:T(8,128)S(1)}, f32[8,512]{1,0:T(8,128)S(1)}, u32[]{:S(2)}, u32[]{:S(2)}) %collective-permute-start.4) | collective-permute-done | bytes 16416 | tf_op jit(solution)/shard_map/ppermute | solution.py:450
  15.3 0.0 collective-permute-done.2.refs_0_.rest_0_
  15.3 0.0 collective-permute-done.3.refs_1_.rest_1_
  15.3 0.7 %collective-permute-start.5 = (f32[40,128]{1,0:T(8,128)S(1)}, f32[40,128]{1,0:T(8,128)S(1)}, u32[]{:S(2)}, u32[]{:S(2)}) collective-permute-start(f32[40,128]{1,0:T(8,128)S(1)} %get-tuple-element.50), channel_id=1, source_target_pairs={{1,2},{2,1},{5,6},{6,5},{9,10},{10,9},{13,14},{14,13},{17,18},{18,... | collective-permute-start | bytes 61448 | tf_op jit(solution)/shard_map/ppermute | solution.py:457
  16.0 1.8 %collective-permute-start.6 = (f32[40,128]{1,0:T(8,128)S(1)}, f32[40,128]{1,0:T(8,128)S(1)}, u32[]{:S(2)}, u32[]{:S(2)}) collective-permute-start(f32[40,128]{1,0:T(8,128)S(1)} %get-tuple-element.51), channel_id=1, source_target_pairs={{0,1},{2,3},{1,0},{3,2},{4,5},{6,7},{5,4},{7,6},{8,9},{10,11},{9,8... | collective-permute-start | bytes 61448 | tf_op jit(solution)/shard_map/ppermute | solution.py:458
  17.8 0.0 collective-permute-done.got_second
  17.8 0.0 collective-permute-done.1.got_first
  17.8 0.4 ghost_kernel.1
  18.2 0.0 collective-permute-done.5.side_second
  18.2 1.6 %collective-permute-done.6.side_first = f32[40,128]{1,0:T(8,128)S(1)} collective-permute-done((f32[40,128]{1,0:T(8,128)S(1)}, f32[40,128]{1,0:T(8,128)S(1)}, u32[]{:S(2)}, u32[]{:S(2)}) %collective-permute-start.6) | collective-permute-done | bytes 20512 | tf_op jit(solution)/shard_map/ppermute | solution.py:458
  19.8 2.0 %first_kernel.1 = (f32[128,768]{1,0:T(8,128)S(1)}, f32[128,768]{1,0:T(8,128)S(1)}, f32[4,128,768]{2,1,0:T(8,128)S(1)}, f32[144,768]{1,0:T(8,128)S(1)}, f32[5,8,7...) custom-call(f32[128,512]{1,0:T(8,128)S(1)} %get-tuple-element.38.own_field.field, ...), custom_call_target="tpu_custom_call" | custom-call | tf_op jit(solution)/shard_map/first_kernel/pallas_call | solution.py:100
  21.9 0.0 collective-permute-start.8
  21.9 0.6 %collective-permute-start.9 = (f32[8,768]{1,0:T(8,128)S(1)}, f32[8,768]{1,0:T(8,128)S(1)}, u32[]{:S(2)}, u32[]{:S(2)}) collective-permute-start(f32[8,768]{1,0:T(8,128)S(1)} %get-tuple-element.57), channel_id=1, source_target_pairs={{0,8},{4,12},{8,0},{12,4},{1,9},{5,13},{9,1},{13,5},{2,10},{6,14},... | collective-permute-start | bytes 73736 | tf_op jit(solution)/shard_map/ppermute | solution.py:450
  22.5 1.3 %collective-permute-start.7 = (f32[8,768]{1,0:T(8,128)S(1)}, f32[8,768]{1,0:T(8,128)S(1)}, u32[]{:S(2)}, u32[]{:S(2)}) collective-permute-start(f32[8,768]{1,0:T(8,128)S(1)} %get-tuple-element.57), channel_id=1, source_target_pairs={{0,4},{8,12},{4,0},{12,8},{1,5},{9,13},{5,1},{13,9},{2,6},{10,14},... | collective-permute-start | bytes 73736 | tf_op jit(solution)/shard_map/ppermute | solution.py:448
  23.8 1.4 %collective-permute-done.8.rest_1_ = f32[8,768]{1,0:T(8,128)S(1)} collective-permute-done((f32[8,768]{1,0:T(8,128)S(1)}, f32[8,768]{1,0:T(8,128)S(1)}, u32[]{:S(2)}, u32[]{:S(2)}) %collective-permute-start.8) | collective-permute-done | bytes 24608 | tf_op jit(solution)/shard_map/ppermute | solution.py:448
  25.1 0.6 %collective-permute-done.9.rest_2_ = f32[8,768]{1,0:T(8,128)S(1)} collective-permute-done((f32[8,768]{1,0:T(8,128)S(1)}, f32[8,768]{1,0:T(8,128)S(1)}, u32[]{:S(2)}, u32[]{:S(2)}) %collective-permute-start.9) | collective-permute-done | bytes 24608 | tf_op jit(solution)/shard_map/ppermute | solution.py:450
  25.8 0.0 collective-permute-done.7.rest_0_
  25.8 1.5 %second_kernel.1 = (f32[128,512]{1,0:T(8,128)S(1)}, f32[128,512]{1,0:T(8,128)S(1)}, f32[8,128]{1,0:T(8,128)S(1)}) custom-call(f32[128,512]{1,0:T(8,128)S(1)} %get-tuple-element.38.own_field.field, f32[128,768]{1,0:T(8,128)S(1)} %get-tuple-element.52.precond, f32[128,768]{1,0:T(8,128)S(1)} %get-tuple-element.53.image, ...), custom_call_target="tpu_custom_call" | custom-call | tf_op jit(solution)/shard_map/second_kernel/pallas_call | solution.py:100
  27.2 1.4 %collective-permute-start.10 = (f32[8,128]{1,0:T(8,128)S(1)}, f32[8,128]{1,0:T(8,128)S(1)}, u32[]{:S(2)}, u32[]{:S(2)}) collective-permute-start(f32[8,128]{1,0:T(8,128)S(1)} %get-tuple-element.59), channel_id=1, source_target_pairs={{0,4},{8,12},{1,5},{9,13},{2,6},{10,14},{3,7},{11,15},{16,20},{24,... | collective-permute-start | bytes 12296 | tf_op jit(solution)/shard_map/ppermute | solution.py:403
  28.6 0.8 %collective-permute-done.10 = f32[8,128]{1,0:T(8,128)S(1)} collective-permute-done((f32[8,128]{1,0:T(8,128)S(1)}, f32[8,128]{1,0:T(8,128)S(1)}, u32[]{:S(2)}, u32[]{:S(2)}) %collective-permute-start.10) | collective-permute-done | bytes 4128 | tf_op jit(solution)/shard_map/ppermute | solution.py:403
  29.4 0.6 %collective-permute-start.11 = (f32[8,128]{1,0:T(8,128)S(1)}, f32[8,128]{1,0:T(8,128)S(1)}, u32[]{:S(2)}, u32[]{:S(2)}) collective-permute-start(f32[8,128]{1,0:T(8,128)S(1)} %add.12), channel_id=1, source_target_pairs={{4,12},{12,4},{5,13},{13,5},{6,14},{14,6},{7,15},{15,7},{20,28},{2... | collective-permute-start | bytes 12296 | tf_op jit(solution)/shard_map/ppermute | solution.py:406
  30.1 0.0 collective-permute-done.11
  30.1 0.7 %collective-permute-start.12 = (f32[8,128]{1,0:T(8,128)S(1)}, f32[8,128]{1,0:T(8,128)S(1)}, u32[]{:S(2)}, u32[]{:S(2)}) collective-permute-start(f32[8,128]{1,0:T(8,128)S(1)} %add.13), channel_id=1, source_target_pairs={{4,5},{5,4},{6,7},{7,6},{12,13},{13,12},{14,15},{15,14},{20,21},{2... | collective-permute-start | bytes 12296 | tf_op jit(solution)/shard_map/ppermute | solution.py:409
  30.8 0.0 collective-permute-done.12
  30.8 0.7 %collective-permute-start.13 = (f32[8,128]{1,0:T(8,128)S(1)}, f32[8,128]{1,0:T(8,128)S(1)}, u32[]{:S(2)}, u32[]{:S(2)}) collective-permute-start(f32[8,128]{1,0:T(8,128)S(1)} %add.14), channel_id=1, source_target_pairs={{4,6},{5,7},{6,4},{7,5},{12,14},{13,15},{14,12},{15,13},{20,22},{2... | collective-permute-start | bytes 12296 | tf_op jit(solution)/shard_map/ppermute | solution.py:409
  31.5 0.0 collective-permute-done.13
  31.5 1.3 %collective-permute-start.14 = (f32[8,128]{1,0:T(8,128)S(1)}, f32[8,128]{1,0:T(8,128)S(1)}, u32[]{:S(2)}, u32[]{:S(2)}) collective-permute-start(f32[8,128]{1,0:T(8,128)S(1)} %add.15.here), channel_id=1, source_target_pairs={{4,0},{12,8},{5,1},{13,9},{6,2},{14,10},{7,3},{15,11},{20,16},{28,... | collective-permute-start | bytes 12296 | tf_op jit(solution)/shard_map/ppermute | solution.py:410
  32.8 12.9 %collective-permute-done.14.beside = f32[8,128]{1,0:T(8,128)S(1)} collective-permute-done((f32[8,128]{1,0:T(8,128)S(1)}, f32[8,128]{1,0:T(8,128)S(1)}, u32[]{:S(2)}, u32[]{:S(2)}) %collective-permute-start.14) | collective-permute-done | bytes 4128 | tf_op jit(solution)/shard_map/ppermute | solution.py:410
  45.7 1.3 %combine_kernel.1 = (f32[512,128]{1,0:T(8,128)}, f32[512,128]{1,0:T(8,128)}) custom-call(f32[8,128]{1,0:T(8,128)S(1)} %add.15.here, f32[8,128]{1,0:T(8,128)S(1)} %collective-permute-done.14.beside, f32[512,128]{1,0:T(8,128)S(1)} %get-tuple-element.33.noise, f32[128,768]{1,0:T(8,128)S(1)} %get-tuple-element.52.precond, ...), custom_call_target="tpu_custom_call" | custom-call | tf_op jit(solution)/shard_map/combine_kernel/pallas_call | solution.py:100
  (5 shorter events, 0.0 us)
Async XLA Ops:
  2.3 15.4 %collective-permute-start = (f32[21,32,128]{2,1,0:T(8,128)S(1)}, f32[21,32,128]{2,1,0:T(8,128)S(1)}, u32[]{:S(2)}, u32[]{:S(2)}) collective-permute-start(f32[21,32,128]{2,1,0:T(8,128)S(1)} %get-tuple-element.41), channel_id=1, source_target_pairs={{1,2},{2,1},{5,6},{6,5},{9,10},{10,9},{13,14},{14,13},{17,18},{18,... | collective-permute-start | bytes 1032200 | tf_op jit(solution)/shard_map/ppermute | solution.py:437
  3.0 14.7 %collective-permute-start.1 = (f32[21,32,128]{2,1,0:T(8,128)S(1)}, f32[21,32,128]{2,1,0:T(8,128)S(1)}, u32[]{:S(2)}, u32[]{:S(2)}) collective-permute-start(f32[21,32,128]{2,1,0:T(8,128)S(1)} %get-tuple-element.42), channel_id=1, source_target_pairs={{0,1},{2,3},{1,0},{3,2},{4,5},{6,7},{5,4},{7,6},{8,9},{10,11},{9,8... | collective-permute-start | bytes 1032200 | tf_op jit(solution)/shard_map/ppermute | solution.py:438
  9.9 5.4 %collective-permute-start.2 = (f32[16,512]{1,0:T(8,128)S(1)}, f32[16,512]{1,0:T(8,128)S(1)}, u32[]{:S(2)}, u32[]{:S(2)}) collective-permute-start(f32[16,512]{1,0:T(8,128)S(1)} %get-tuple-element.47), channel_id=1, source_target_pairs={{0,4},{8,12},{4,0},{12,8},{1,5},{9,13},{5,1},{13,9},{2,6},{10,14},... | collective-permute-start | bytes 98312 | tf_op jit(solution)/shard_map/ppermute | solution.py:448
  10.0 5.3 %collective-permute-start.3 = (f32[16,512]{1,0:T(8,128)S(1)}, f32[16,512]{1,0:T(8,128)S(1)}, u32[]{:S(2)}, u32[]{:S(2)}) collective-permute-start(f32[16,512]{1,0:T(8,128)S(1)} %get-tuple-element.48), channel_id=1, source_target_pairs={{4,8},{12,0},{8,4},{0,12},{5,9},{13,1},{9,5},{1,13},{6,10},{14,2},... | collective-permute-start | bytes 98312 | tf_op jit(solution)/shard_map/ppermute | solution.py:448
  11.6 3.7 %collective-permute-start.4 = (f32[8,512]{1,0:T(8,128)S(1)}, f32[8,512]{1,0:T(8,128)S(1)}, u32[]{:S(2)}, u32[]{:S(2)}) collective-permute-start(f32[8,512]{1,0:T(8,128)S(1)} %get-tuple-element.49), channel_id=1, source_target_pairs={{0,8},{4,12},{8,0},{12,4},{1,9},{5,13},{9,1},{13,5},{2,10},{6,14},... | collective-permute-start | bytes 49160 | tf_op jit(solution)/shard_map/ppermute | solution.py:450
  15.3 2.9 %collective-permute-start.5 = (f32[40,128]{1,0:T(8,128)S(1)}, f32[40,128]{1,0:T(8,128)S(1)}, u32[]{:S(2)}, u32[]{:S(2)}) collective-permute-start(f32[40,128]{1,0:T(8,128)S(1)} %get-tuple-element.50), channel_id=1, source_target_pairs={{1,2},{2,1},{5,6},{6,5},{9,10},{10,9},{13,14},{14,13},{17,18},{18,... | collective-permute-start | bytes 61448 | tf_op jit(solution)/shard_map/ppermute | solution.py:457
  16.0 3.8 %collective-permute-start.6 = (f32[40,128]{1,0:T(8,128)S(1)}, f32[40,128]{1,0:T(8,128)S(1)}, u32[]{:S(2)}, u32[]{:S(2)}) collective-permute-start(f32[40,128]{1,0:T(8,128)S(1)} %get-tuple-element.51), channel_id=1, source_target_pairs={{0,1},{2,3},{1,0},{3,2},{4,5},{6,7},{5,4},{7,6},{8,9},{10,11},{9,8... | collective-permute-start | bytes 61448 | tf_op jit(solution)/shard_map/ppermute | solution.py:458
  21.9 3.3 %collective-permute-start.8 = (f32[8,768]{1,0:T(8,128)S(1)}, f32[8,768]{1,0:T(8,128)S(1)}, u32[]{:S(2)}, u32[]{:S(2)}) collective-permute-start(f32[8,768]{1,0:T(8,128)S(1)} %get-tuple-element.58), channel_id=1, source_target_pairs={{4,8},{12,0},{8,4},{0,12},{5,9},{13,1},{9,5},{1,13},{6,10},{14,2},... | collective-permute-start | bytes 73736 | tf_op jit(solution)/shard_map/ppermute | solution.py:448
  21.9 3.9 %collective-permute-start.9 = (f32[8,768]{1,0:T(8,128)S(1)}, f32[8,768]{1,0:T(8,128)S(1)}, u32[]{:S(2)}, u32[]{:S(2)}) collective-permute-start(f32[8,768]{1,0:T(8,128)S(1)} %get-tuple-element.57), channel_id=1, source_target_pairs={{0,8},{4,12},{8,0},{12,4},{1,9},{5,13},{9,1},{13,5},{2,10},{6,14},... | collective-permute-start | bytes 73736 | tf_op jit(solution)/shard_map/ppermute | solution.py:450
  22.5 3.3 %collective-permute-start.7 = (f32[8,768]{1,0:T(8,128)S(1)}, f32[8,768]{1,0:T(8,128)S(1)}, u32[]{:S(2)}, u32[]{:S(2)}) collective-permute-start(f32[8,768]{1,0:T(8,128)S(1)} %get-tuple-element.57), channel_id=1, source_target_pairs={{0,4},{8,12},{4,0},{12,8},{1,5},{9,13},{5,1},{13,9},{2,6},{10,14},... | collective-permute-start | bytes 73736 | tf_op jit(solution)/shard_map/ppermute | solution.py:448
  27.2 2.2 %collective-permute-start.10 = (f32[8,128]{1,0:T(8,128)S(1)}, f32[8,128]{1,0:T(8,128)S(1)}, u32[]{:S(2)}, u32[]{:S(2)}) collective-permute-start(f32[8,128]{1,0:T(8,128)S(1)} %get-tuple-element.59), channel_id=1, source_target_pairs={{0,4},{8,12},{1,5},{9,13},{2,6},{10,14},{3,7},{11,15},{16,20},{24,... | collective-permute-start | bytes 12296 | tf_op jit(solution)/shard_map/ppermute | solution.py:403
  29.4 0.7 %collective-permute-start.11 = (f32[8,128]{1,0:T(8,128)S(1)}, f32[8,128]{1,0:T(8,128)S(1)}, u32[]{:S(2)}, u32[]{:S(2)}) collective-permute-start(f32[8,128]{1,0:T(8,128)S(1)} %add.12), channel_id=1, source_target_pairs={{4,12},{12,4},{5,13},{13,5},{6,14},{14,6},{7,15},{15,7},{20,28},{2... | collective-permute-start | bytes 12296 | tf_op jit(solution)/shard_map/ppermute | solution.py:406
  30.1 0.7 %collective-permute-start.12 = (f32[8,128]{1,0:T(8,128)S(1)}, f32[8,128]{1,0:T(8,128)S(1)}, u32[]{:S(2)}, u32[]{:S(2)}) collective-permute-start(f32[8,128]{1,0:T(8,128)S(1)} %add.13), channel_id=1, source_target_pairs={{4,5},{5,4},{6,7},{7,6},{12,13},{13,12},{14,15},{15,14},{20,21},{2... | collective-permute-start | bytes 12296 | tf_op jit(solution)/shard_map/ppermute | solution.py:409
  30.8 0.7 %collective-permute-start.13 = (f32[8,128]{1,0:T(8,128)S(1)}, f32[8,128]{1,0:T(8,128)S(1)}, u32[]{:S(2)}, u32[]{:S(2)}) collective-permute-start(f32[8,128]{1,0:T(8,128)S(1)} %add.14), channel_id=1, source_target_pairs={{4,6},{5,7},{6,4},{7,5},{12,14},{13,15},{14,12},{15,13},{20,22},{2... | collective-permute-start | bytes 12296 | tf_op jit(solution)/shard_map/ppermute | solution.py:409
  31.5 14.2 %collective-permute-start.14 = (f32[8,128]{1,0:T(8,128)S(1)}, f32[8,128]{1,0:T(8,128)S(1)}, u32[]{:S(2)}, u32[]{:S(2)}) collective-permute-start(f32[8,128]{1,0:T(8,128)S(1)} %add.15.here), channel_id=1, source_target_pairs={{4,0},{12,8},{5,1},{13,9},{6,2},{14,10},{7,3},{15,11},{20,16},{28,... | collective-permute-start | bytes 12296 | tf_op jit(solution)/shard_map/ppermute | solution.py:410

commit v6 on v5

--- a/solution.py
+++ b/solution.py
@@ -70,24 +70,31 @@
             out[EDGE - 2, 4] += amend
         return out * used[:, None]
 
-    others = [block(count - d) for d in range(2, count - 1)]
-    far = np.stack(
-        [
-            np.concatenate([block(1), block(count - 1)] + others, axis=1),
-            np.concatenate([block(count - 1), block(1)] + others, axis=1),
-        ]
-    )
-    spread = np.stack([np.concatenate([near, f], axis=1) for f in far])
+    def blocks(sign):
+        offsets = [(e, 0) for e in (1, -1, -2)] + [(e, k) for k in range(4, count, 4) for e in (0, 1, -1, -2)]
+        return np.concatenate([block((sign * e - k) % count) for e, k in offsets], axis=1)
+
+    spread = np.stack([np.concatenate([near, blocks(sign)], axis=1) for sign in (1, -1)])
     return np.asarray(spread, np.float32), np.asarray(moments, np.float32)
 
 
-def pair_perms(count, wrap):
-    first = [(i, i + 1) for i in range(0, count - 1, 2)]
-    second = [(i, i + 1) for i in range(1, count - 1, 2)]
-    if wrap:
-        second.append((count - 1, 0))
-    both = lambda pairs: pairs + [(j, i) for i, j in pairs]
-    return both(first), both(second)
+def lon_perms(count):
+    first = [(i, i ^ 1) for i in range(count)]
+    return first, [(i, (i - 1 + 2 * (i % 2)) % count) for i in range(count)]
+
+
+def lat_perms(count, bands):
+    first, second = [], []
+    for i in range(count):
+        for j in range(bands):
+            k = j - 1 + 2 * (j % 2)
+            first.append((i * bands + j, i * bands + (j ^ 1)))
+            second.append((i * bands + j, i * bands + k if 0 <= k < bands else (i ^ 1) * bands + j))
+    return first, second
+
+
+def inner_band():
+    return (lax.axis_index("lat") > 0) & (lax.axis_index("lat") < lax.axis_size("lat") - 1)
 
 
 def whole(n):
@@ -104,7 +111,7 @@
         out_specs=whole(len(outs)),
         scratch_shapes=[pltpu.VMEM(s, jnp.float32) for s in scratch],
         compiler_params=pltpu.CompilerParams(vmem_limit_bytes=24 << 20),
-        name=kernel.func.__name__,
+        name=getattr(kernel, "func", kernel).__name__,
     )(*args)
 
 
@@ -166,7 +173,7 @@
 def own_kernel(
     rows, levels, columns,
     noise, kappa2, conduct, land, weights,
-    field, statics, edge, to_first, to_second, to_others,
+    field, statics, edge, to_first, to_second,
 ):
     last_band = lax.axis_index("lat") == lax.axis_size("lat") - 1
     lon_odd = lax.axis_index("lon") % 2
@@ -186,9 +193,7 @@
     north = jnp.where(last_band & (lane >= lanes - levels), 0.0, north)
     diagonal, to_east, to_upper = coefficients(levels, lanes, kappa, east, north, upper, ocean)
     store(statics, edge, diagonal, to_east, north, to_upper, ocean, east)
-    m = dot(weights[...], r)
-    to_others[...] = m
-    m = m[:4]
+    m = dot(weights[...], r)[:4]
     end = columns - 1
     blank = jnp.zeros((5, lanes), jnp.float32)
     for_east = [m, r[end:], diagonal[end:], to_east[end - 1 : end], east[end:], ocean[end:], north[end:], to_upper[end:], blank]
@@ -207,7 +212,7 @@
         count = FULL if kind < 3 else PART
         k = kind * FULL if kind < 3 else 3 * FULL + (kind - 3) * PART
         a = got_first[pl.ds(k, count)].reshape(count * levels, columns)
-        b = got_second[pl.ds(k, count)].reshape(count * levels, columns)
+        b = jnp.where(inner_band(), got_second[pl.ds(k, count)], 0.0).reshape(count * levels, columns)
         from_first = (lat_odd == 0) if north else (lat_odd == 1)
         planes = jnp.where(from_first, a, b)
         if count == REACH:
@@ -237,8 +242,21 @@
 
 def circle(spread, own, lists):
     lon_odd = lax.axis_index("lon") % 2
-    told = jnp.concatenate([own] + [t[0:8] for t in lists], axis=0)
-    return dot(spread[lon_odd], told)
+    first, second = lists[0], lists[1]
+    told = [first[0:8], second[0:8], second[second.shape[0] - 8 :]] + [t[...] for t in lists[2:]]
+    return dot(spread[lon_odd], jnp.concatenate([own] + told, axis=0))
+
+
+def stack_kernel(own, got, out):
+    out[0 : own.shape[0]] = own[...]
+    out[own.shape[0] :] = got[0:8]
+
+
+def quad_kernel(own, first, second, out):
+    out[0:8] = own[0:8]
+    out[8:16] = first[0:8]
+    out[16:24] = second[0:8]
+    out[24:32] = second[second.shape[0] - 8 :]
 
 
 def stencil(v, east_v, west_v, d, e, w, n, u, levels):
@@ -277,8 +295,8 @@
     rows, levels, columns, others,
     own_field, own_statics, own_edge, field, ghost_statics, edge, spread, weights, side_second, side_first, *rest,
 ):
-    received = rest[: 2 + others]
-    precond, image, statics, to_east, rim, to_first, to_second, v, f = rest[2 + others :]
+    received = rest[: 1 + others]
+    precond, image, statics, to_east, rim, to_first, to_second, v, f = rest[1 + others :]
     lat_odd = lax.axis_index("lat") % 2
     even = lax.axis_index("lon") % 2 == 0
     group = REACH * levels
@@ -290,7 +308,8 @@
     lists, k = [], 0
     for x in received:
         count = x.shape[0]
-        a, b = side_first[pl.ds(k, count)], side_second[pl.ds(k, count)]
+        a = side_first[pl.ds(k, count)]
+        b = jnp.where(inner_band(), side_second[pl.ds(k, count)], 0.0)
         lists.append(jnp.concatenate([jnp.where(lat_odd == 1, a, b), x[...], jnp.where(lat_odd == 1, b, a)], axis=1))
         k += count
     v[...] = circle(spread, joined(own_field[...], field[...]), lists)
@@ -306,8 +325,8 @@
     diagonal, north = completed(
         joined(own_statics[0], ghost_statics[0]), joined(own_statics[2], ghost_statics[2]), ocean
     )
-    east_list = jnp.where(even, lists[0], lists[1])
-    west_list = jnp.where(even, lists[1], lists[0])
+    one, two = lists[0][0:16], lists[1][0:16]
+    east_list, west_list = jnp.where(even, one, two), jnp.where(even, two, one)
     end = columns - 1
     row = lax.broadcasted_iota(jnp.int32, (columns, 1), 0)
     full_east = joined(own_statics[1], ghost_statics[1])
@@ -349,8 +368,8 @@
     levels, columns, rows, others,
     field, precond, image, statics, spread, to_east, rim, *rest,
 ):
-    received = rest[: 2 + others]
-    again, along, sums, v, f = rest[2 + others :]
+    received = rest[: 1 + others]
+    again, along, sums, v, f = rest[1 + others :]
     v[...] = circle(spread, image[...] * SCALE, received)
     out = apply_twice(levels, columns, v, f, statics, to_east, rim)
     own = slice(REACH * levels, (REACH + rows) * levels)
@@ -367,9 +386,8 @@
     sums[...] = jnp.concatenate(parts, axis=0)
 
 
-def combine_kernel(rows, levels, here, beside, noise, precond, image, again, along, answer, left):
-    odd = lax.axis_index("lon") % 2 == 1
-    total = jnp.sum(jnp.where(odd, here[...], beside[...]), axis=1, keepdims=True)
+def combine_kernel(rows, levels, sums, noise, precond, image, again, along, answer, left):
+    total = jnp.sum(sums[...], axis=1, keepdims=True)
     energy, curve, mixed, last = total[0:1], total[1:2], total[2:3], total[3:4]
     alpha = energy / curve
     beta = alpha / SCALE
@@ -400,20 +418,19 @@
 
 def summed(x):
     count, bands = lax.axis_size("lon"), lax.axis_size("lat")
-    x = x + lax.ppermute(x, "lon", [(i, i + 1) for i in range(0, count, 2)])
-    odd = range(1, count, 2)
+    x = x + lax.ppermute(x, "lon", [(i, i ^ 1) for i in range(count)])
     for step in doubling(count)[1:]:
-        x = x + lax.ppermute(x, "lon", [(i, i ^ step) for i in odd])
+        x = x + lax.ppermute(x, "lon", [(i, i ^ step ^ 1) for i in range(count)])
     for step in doubling(bands):
-        pairs = [(i * bands + j, i * bands + (j ^ step)) for i in odd for j in range(bands)]
+        pairs = [(i * bands + j, (i ^ 1) * bands + (j ^ step)) for i in range(count) for j in range(bands)]
         x = x + lax.ppermute(x, ("lon", "lat"), pairs)
-    return x, lax.ppermute(x, "lon", [(i, i - 1) for i in odd])
+    return x
 
 
 def body(spread, weights, noise, kappa2, conduct, land):
     levels, rows, columns = noise.shape
     count = lax.axis_size("lon")
-    others = count - 3
+    others = count // 4
     flat = levels * rows
     lanes = (rows + 2 * REACH) * levels
     tall = columns + 2 * EDGE
@@ -433,29 +450,35 @@
         compiler_params=pltpu.CompilerParams(vmem_limit_bytes=8 << 20),
         name="band_kernel",
     )(*[pltpu.with_memory_space_constraint(x, pltpu.HBM) for x in sources])
-    perm_a, perm_b = pair_perms(lax.axis_size("lat"), False)
-    got_second = lax.ppermute(second, "lat", perm_b)
-    got_first = lax.ppermute(first, "lat", perm_a)
-
-    own_field, own_statics, own_edge, to_first, to_second, to_others = call(
+    perm_a, perm_b = lat_perms(count, lax.axis_size("lat"))
+    got_second = lax.ppermute(second, ("lon", "lat"), perm_b)
+    got_first = lax.ppermute(first, ("lon", "lat"), perm_a)
+
+    own_field, own_statics, own_edge, to_first, to_second = call(
         functools.partial(own_kernel, rows, levels, columns),
-        [(columns, flat), (5, columns, flat), (8, flat), (16, flat), (16, flat), (8, flat)],
+        [(columns, flat), (5, columns, flat), (8, flat), (16, flat), (16, flat)],
         noise, kappa2, conduct, land, weights,
     )
-    lon_a, lon_b = pair_perms(count, True)
-
-    def exchange(one, two, rest):
-        got = [lax.ppermute(one, "lon", lon_a), lax.ppermute(two, "lon", lon_b)]
-        for d in range(2, count - 1):
-            got.append(lax.ppermute(rest, "lon", [(i, (i + d) % count) for i in range(count)]))
-        return got
-
-    told = exchange(to_first, to_second, to_others)
+    lon_a, lon_b = lon_perms(count)
+
+    def exchange(one, two):
+        height, wide = two.shape
+        got_one = lax.ppermute(one, "lon", lon_a)
+        (two,) = call(stack_kernel, [(height + 8, wide)], two, got_one)
+        got_two = lax.ppermute(two, "lon", lon_b)
+        if count == 4:
+            return [got_one, got_two]
+        (four,) = call(quad_kernel, [(32, wide)], two, got_one, got_two)
+        return [got_one, got_two] + [
+            lax.ppermute(four, "lon", [(i, (i + d) % count) for i in range(count)]) for d in range(4, count, 4)
+        ]
+
+    told = exchange(to_first, to_second)
     heights = sum(x.shape[0] for x in told)
     group = REACH * levels
     side_second, side_first = call(functools.partial(forward_kernel, group), [(heights, group)] * 2, *told)
-    side_second = lax.ppermute(side_second, "lat", perm_b)
-    side_first = lax.ppermute(side_first, "lat", perm_a)
+    side_second = lax.ppermute(side_second, ("lon", "lat"), perm_b)
+    side_first = lax.ppermute(side_first, ("lon", "lat"), perm_a)
     field, ghost_statics, edge = call(
         functools.partial(ghost_kernel, levels, columns),
         [(columns, 2 * group), (5, columns, 2 * group), (8, 2 * group)],
@@ -467,18 +490,18 @@
         own_field, own_statics, own_edge, field, ghost_statics, edge, spread, weights, side_second, side_first, *told,
         scratch=[(tall, lanes), (tall, lanes)],
     )
-    told = exchange(to_first, to_second, to_first)
+    told = exchange(to_first, to_second)
     again, along, sums = call(
         functools.partial(second_kernel, levels, columns, rows, others),
         [(columns, flat), (columns, flat), (8, 128)],
         own_field, precond, image, statics, spread, to_east, rim, *told,
         scratch=[(tall, lanes), (tall, lanes)],
     )
-    here, beside = summed(sums)
+    sums = summed(sums)
     answer, left = call(
         functools.partial(combine_kernel, rows, levels),
         [(flat, columns), (flat, columns)],
-        here, beside, noise, precond, image, again, along, last=True,
+        sums, noise, precond, image, again, along, last=True,
     )
     return answer.reshape(levels, rows, columns), left.reshape(levels, rows, columns)
 

time: 47.3 us -> 38.4 us (0.81)
  starting transfers between devices: 17.8 us -> 12.2 us
  waiting for transfers between devices: 20.6 us -> 17.4 us
    ppermute x13 -> x10, waiting for transfers between devices: 20.6 us -> 12.2 us  [the longest x2 4.87 us: exchange(): got_two = lax.ppermute(two, 'lon', lon_b)]
    ppermute x13 -> x10, starting transfers between devices: 16.5 us -> 10.5 us  [the longest x1 4.14 us: body(): got_first = lax.ppermute(first, ('lon', 'lat'), perm_a)]
    ppermute x2, waiting for transfers between devices: 0.01 us -> 5.22 us  [summed(): x = x + lax.ppermute(x, ('lon', 'lat'), pairs)]
    pallas_call x6 -> x8, Pallas kernels: 6.12 us -> 6.11 us  [call(): pl.pallas_call(kernel, out_shape=[kind(s, jnp.float32) for s in outs], in...]
  transfers between devices with their start and end apart: 15 -> 12, of which waited for: 6 -> 10; matrix products, arithmetic and copies ran while one was open for 0% -> 0% of each run, Pallas kernels for 3% -> 3%
where the time goes in v6:
time: 38.4 us; the launch traced here: 38.2 us
  waiting for transfers between devices  17.4 us (45%)
  starting transfers between devices  12.2 us (32%)
  Pallas kernels  7.82 us (20%)
  between operations  0.69 us (2%)
    pallas_call x8, Pallas kernels, call(): pl.pallas_call(kernel, out_shape=[kind(s, jnp.float32) for s in outs], in...  6.11 us
    ppermute x2, waiting for transfers between devices, summed(): x = x + lax.ppermute(x, ('lon', 'lat'), pairs)  5.22 us
    ppermute x2, waiting for transfers between devices, exchange(): got_two = lax.ppermute(two, 'lon', lon_b)  4.87 us
    ppermute x1, starting transfers between devices, body(): got_first = lax.ppermute(first, ('lon', 'lat'), perm_a)  4.14 us
    ppermute x2, starting transfers between devices, exchange(): got_two = lax.ppermute(two, 'lon', lon_b)  2.52 us
    ppermute x2, waiting for transfers between devices, exchange(): got_one = lax.ppermute(one, 'lon', lon_a)  2.4 us
    ppermute x1, waiting for transfers between devices, body(): side_first = lax.ppermute(side_first, ('lon', 'lat'), perm_a)  2.04 us
    ppermute x1, waiting for transfers between devices, summed(): x = x + lax.ppermute(x, 'lon', [(i, i ^ step ^ 1) for i in range(count)])  1.77 us
  transfers between devices with their start and end apart: 12, of which 10 were waited for; matrix products, arithmetic and copies ran while one was open for 0% of the time, Pallas kernels for 3%

profile of v6, /device:TPU:0, one launch (start us, length us, event | category | flops | bytes accessed | tf_op | source)
XLA Modules:
  0.0 38.2 jit_solution(8031493893038267700)
XLA Ops:
  0.6 1.7 %band_kernel.1 = (f32[21,32,128]{2,1,0:T(8,128)S(1)}, f32[21,32,128]{2,1,0:T(8,128)S(1)}, f32[512,128]{1,0:T(8,128)S(1)}, f32[512,128]{1,0:T(8,128)S(1)}, f32[3,...) custom-call(f32[512,128]{1,0:T(8,128)} %bitcast.7, ...), custom_call_target="tpu_custom_call" | custom-call | tf_op jit(solution)/shard_map/band_kernel/pallas_call | solution.py:444
  2.3 0.6 %collective-permute-start = (f32[21,32,128]{2,1,0:T(8,128)S(1)}, f32[21,32,128]{2,1,0:T(8,128)S(1)}, u32[]{:S(2)}, u32[]{:S(2)}) collective-permute-start(f32[21,32,128]{2,1,0:T(8,128)S(1)} %get-tuple-element.40), channel_id=1, source_target_pairs={{0,4},{1,2},{2,1},{3,7},{4,0},{5,6},{6,5},{7,3},{8,12},{9,10},{10,... | collective-permute-start | bytes 1032200 | tf_op jit(solution)/shard_map/ppermute | solution.py:454
  2.9 4.1 %collective-permute-start.1 = (f32[21,32,128]{2,1,0:T(8,128)S(1)}, f32[21,32,128]{2,1,0:T(8,128)S(1)}, u32[]{:S(2)}, u32[]{:S(2)}) collective-permute-start(f32[21,32,128]{2,1,0:T(8,128)S(1)} %get-tuple-element.41), channel_id=1, source_target_pairs={{0,1},{1,0},{2,3},{3,2},{4,5},{5,4},{6,7},{7,6},{8,9},{9,8},{10,11... | collective-permute-start | bytes 1032200 | tf_op jit(solution)/shard_map/ppermute | solution.py:455
  7.0 0.9 %own_kernel.1 = (f32[128,512]{1,0:T(8,128)S(1)}, f32[5,128,512]{2,1,0:T(8,128)S(1)}, f32[8,512]{1,0:T(8,128)S(1)}, f32[16,512]{1,0:T(8,128)S(1)}, f32[16,512]{1,0:T(8,128)S(1)}) custom-call(f32[512,128]{1,0:T(8,128)S(1)} %get-tuple-element.32.noise, f32[512,128]{1,0:T(8,128)S(1)} %get-tuple-element.33.kappa2, f32[3,512,128]{2,1,0:T(8,128)S(1)} %get-tuple-element.34.conduct, ...), custom_call_target="tpu_custom_call" | custom-call | tf_op jit(solution)/shard_map/own_kernel/pallas_call | solution.py:107
  8.0 0.1 collective-permute-start.2
  8.1 1.2 %collective-permute-done.2.got.refs_0_.rest_0_ = f32[16,512]{1,0:T(8,128)S(1)} collective-permute-done((f32[16,512]{1,0:T(8,128)S(1)}, f32[16,512]{1,0:T(8,128)S(1)}, u32[]{:S(2)}, u32[]{:S(2)}) %collective-permute-start.2) | collective-permute-done | bytes 32800 | tf_op jit(solution)/shard_map/ppermute | solution.py:466
  9.3 1.3 %collective-permute-start.3 = (f32[24,512]{1,0:T(8,128)S(1)}, f32[24,512]{1,0:T(8,128)S(1)}, u32[]{:S(2)}, u32[]{:S(2)}) collective-permute-start(f32[24,512]{1,0:T(8,128)S(1)} %stack_kernel.2), channel_id=1, source_target_pairs={{0,12},{4,8},{8,4},{12,0},{1,13},{5,9},{9,5},{13,1},{2,14},{6,10},... | collective-permute-start | bytes 147464 | tf_op jit(solution)/shard_map/ppermute | solution.py:468
  10.5 2.4 %collective-permute-done.3.refs_1_.rest_1_ = f32[24,512]{1,0:T(8,128)S(1)} collective-permute-done((f32[24,512]{1,0:T(8,128)S(1)}, f32[24,512]{1,0:T(8,128)S(1)}, u32[]{:S(2)}, u32[]{:S(2)}) %collective-permute-start.3) | collective-permute-done | bytes 49184 | tf_op jit(solution)/shard_map/ppermute | solution.py:468
  13.0 0.5 %collective-permute-start.4 = (f32[40,128]{1,0:T(8,128)S(1)}, f32[40,128]{1,0:T(8,128)S(1)}, u32[]{:S(2)}, u32[]{:S(2)}) collective-permute-start(f32[40,128]{1,0:T(8,128)S(1)} %get-tuple-element.48), channel_id=1, source_target_pairs={{0,4},{1,2},{2,1},{3,7},{4,0},{5,6},{6,5},{7,3},{8,12},{9,10},{10,... | collective-permute-start | bytes 61448 | tf_op jit(solution)/shard_map/ppermute | solution.py:480
  13.5 1.2 %collective-permute-start.5 = (f32[40,128]{1,0:T(8,128)S(1)}, f32[40,128]{1,0:T(8,128)S(1)}, u32[]{:S(2)}, u32[]{:S(2)}) collective-permute-start(f32[40,128]{1,0:T(8,128)S(1)} %get-tuple-element.49), channel_id=1, source_target_pairs={{0,1},{1,0},{2,3},{3,2},{4,5},{5,4},{6,7},{7,6},{8,9},{9,8},{10,11... | collective-permute-start | bytes 61448 | tf_op jit(solution)/shard_map/ppermute | solution.py:481
  14.7 0.0 collective-permute-done.got_second
  14.7 0.1 collective-permute-done.1.got_first
  14.8 0.4 %ghost_kernel.1 = (f32[128,256]{1,0:T(8,128)S(1)}, f32[5,128,256]{2,1,0:T(8,128)S(1)}, f32[8,256]{1,0:T(8,128)S(1)}) custom-call(f32[21,32,128]{2,1,0:T(8,128)S(1)} %collective-permute-done.got_second, f32[21,32,128]{2,1,0:T(8,128)S(1)} %collective-permute-done.1.got_first), custom_call_target="tpu_custom_call" | custom-call | tf_op jit(solution)/shard_map/ghost_kernel/pallas_call | solution.py:107
  15.2 0.0 collective-permute-done.4.side_second
  15.2 2.0 %collective-permute-done.5.side_first = f32[40,128]{1,0:T(8,128)S(1)} collective-permute-done((f32[40,128]{1,0:T(8,128)S(1)}, f32[40,128]{1,0:T(8,128)S(1)}, u32[]{:S(2)}, u32[]{:S(2)}) %collective-permute-start.5) | collective-permute-done | bytes 20512 | tf_op jit(solution)/shard_map/ppermute | solution.py:481
  17.3 2.0 %first_kernel.1 = (f32[128,768]{1,0:T(8,128)S(1)}, f32[128,768]{1,0:T(8,128)S(1)}, f32[4,128,768]{2,1,0:T(8,128)S(1)}, f32[144,768]{1,0:T(8,128)S(1)}, f32[5,8,7...) custom-call(f32[128,512]{1,0:T(8,128)S(1)} %get-tuple-element.37.own_field.field, ...), custom_call_target="tpu_custom_call" | custom-call | tf_op jit(solution)/shard_map/first_kernel/pallas_call | solution.py:107
  19.3 0.0 collective-permute-start.6
  19.3 1.2 %collective-permute-done.6.got.rest_0_ = f32[8,768]{1,0:T(8,128)S(1)} collective-permute-done((f32[8,768]{1,0:T(8,128)S(1)}, f32[8,768]{1,0:T(8,128)S(1)}, u32[]{:S(2)}, u32[]{:S(2)}) %collective-permute-start.6) | collective-permute-done | bytes 24608 | tf_op jit(solution)/shard_map/ppermute | solution.py:466
  20.5 1.3 %collective-permute-start.7 = (f32[16,768]{1,0:T(8,128)S(1)}, f32[16,768]{1,0:T(8,128)S(1)}, u32[]{:S(2)}, u32[]{:S(2)}) collective-permute-start(f32[16,768]{1,0:T(8,128)S(1)} %stack_kernel.3), channel_id=1, source_target_pairs={{0,12},{4,8},{8,4},{12,0},{1,13},{5,9},{9,5},{13,1},{2,14},{6,10},... | collective-permute-start | bytes 147464 | tf_op jit(solution)/shard_map/ppermute | solution.py:468
  21.8 2.4 %collective-permute-done.7.rest_1_ = f32[16,768]{1,0:T(8,128)S(1)} collective-permute-done((f32[16,768]{1,0:T(8,128)S(1)}, f32[16,768]{1,0:T(8,128)S(1)}, u32[]{:S(2)}, u32[]{:S(2)}) %collective-permute-start.7) | collective-permute-done | bytes 49184 | tf_op jit(solution)/shard_map/ppermute | solution.py:468
  24.2 1.5 %second_kernel.1 = (f32[128,512]{1,0:T(8,128)S(1)}, f32[128,512]{1,0:T(8,128)S(1)}, f32[8,128]{1,0:T(8,128)S(1)}) custom-call(f32[128,512]{1,0:T(8,128)S(1)} %get-tuple-element.37.own_field.field, f32[128,768]{1,0:T(8,128)S(1)} %get-tuple-element.50.precond, f32[128,768]{1,0:T(8,128)S(1)} %get-tuple-element.51.image, ...), custom_call_target="tpu_custom_call" | custom-call | tf_op jit(solution)/shard_map/second_kernel/pallas_call | solution.py:107
  25.7 0.2 collective-permute-start.8
  25.9 1.0 %collective-permute-done.8 = f32[8,128]{1,0:T(8,128)S(1)} collective-permute-done((f32[8,128]{1,0:T(8,128)S(1)}, f32[8,128]{1,0:T(8,128)S(1)}, u32[]{:S(2)}, u32[]{:S(2)}) %collective-permute-start.8) | collective-permute-done | bytes 4128 | tf_op jit(solution)/shard_map/ppermute | solution.py:421
  26.9 1.3 %collective-permute-start.9 = (f32[8,128]{1,0:T(8,128)S(1)}, f32[8,128]{1,0:T(8,128)S(1)}, u32[]{:S(2)}, u32[]{:S(2)}) collective-permute-start(f32[8,128]{1,0:T(8,128)S(1)} %add.12), channel_id=1, source_target_pairs={{0,12},{4,8},{8,4},{12,0},{1,13},{5,9},{9,5},{13,1},{2,14},{6,10},... | collective-permute-start | bytes 12296 | tf_op jit(solution)/shard_map/ppermute | solution.py:423
  28.2 1.8 %collective-permute-done.9 = f32[8,128]{1,0:T(8,128)S(1)} collective-permute-done((f32[8,128]{1,0:T(8,128)S(1)}, f32[8,128]{1,0:T(8,128)S(1)}, u32[]{:S(2)}, u32[]{:S(2)}) %collective-permute-start.9) | collective-permute-done | bytes 4128 | tf_op jit(solution)/shard_map/ppermute | solution.py:423
  29.9 1.0 %collective-permute-start.10 = (f32[8,128]{1,0:T(8,128)S(1)}, f32[8,128]{1,0:T(8,128)S(1)}, u32[]{:S(2)}, u32[]{:S(2)}) collective-permute-start(f32[8,128]{1,0:T(8,128)S(1)} %add.13), channel_id=1, source_target_pairs={{0,5},{1,4},{2,7},{3,6},{4,1},{5,0},{6,3},{7,2},{8,13},{9,12},{10,... | collective-permute-start | bytes 12296 | tf_op jit(solution)/shard_map/ppermute | solution.py:426
  30.9 2.1 %collective-permute-done.10 = f32[8,128]{1,0:T(8,128)S(1)} collective-permute-done((f32[8,128]{1,0:T(8,128)S(1)}, f32[8,128]{1,0:T(8,128)S(1)}, u32[]{:S(2)}, u32[]{:S(2)}) %collective-permute-start.10) | collective-permute-done | bytes 4128 | tf_op jit(solution)/shard_map/ppermute | solution.py:426
  33.0 0.8 %collective-permute-start.11 = (f32[8,128]{1,0:T(8,128)S(1)}, f32[8,128]{1,0:T(8,128)S(1)}, u32[]{:S(2)}, u32[]{:S(2)}) collective-permute-start(f32[8,128]{1,0:T(8,128)S(1)} %add.14), channel_id=1, source_target_pairs={{0,6},{1,7},{2,4},{3,5},{4,2},{5,3},{6,0},{7,1},{8,14},{9,15},{10,... | collective-permute-start | bytes 12296 | tf_op jit(solution)/shard_map/ppermute | solution.py:426
  33.8 3.2 %collective-permute-done.11 = f32[8,128]{1,0:T(8,128)S(1)} collective-permute-done((f32[8,128]{1,0:T(8,128)S(1)}, f32[8,128]{1,0:T(8,128)S(1)}, u32[]{:S(2)}, u32[]{:S(2)}) %collective-permute-start.11) | collective-permute-done | bytes 4128 | tf_op jit(solution)/shard_map/ppermute | solution.py:426
  36.9 1.3 %combine_kernel.1 = (f32[512,128]{1,0:T(8,128)}, f32[512,128]{1,0:T(8,128)}) custom-call(f32[8,128]{1,0:T(8,128)S(1)} %add.15.sums, f32[512,128]{1,0:T(8,128)S(1)} %get-tuple-element.32.noise, f32[128,768]{1,0:T(8,128)S(1)} %get-tuple-element.50.precond, f32[128,768]{1,0:T(8,128)S(1)} %get-tuple-element.51.image, f32[128,512]{1,0:T(8,128)S(1)} %get-tuple-element.58.again, ...), custom_call_target="tpu_custom_call" | custom-call | tf_op jit(solution)/shard_map/combine_kernel/pallas_call | solution.py:107
  (7 shorter events, 0.0 us)
Async XLA Ops:
  2.3 12.3 %collective-permute-start = (f32[21,32,128]{2,1,0:T(8,128)S(1)}, f32[21,32,128]{2,1,0:T(8,128)S(1)}, u32[]{:S(2)}, u32[]{:S(2)}) collective-permute-start(f32[21,32,128]{2,1,0:T(8,128)S(1)} %get-tuple-element.40), channel_id=1, source_target_pairs={{0,4},{1,2},{2,1},{3,7},{4,0},{5,6},{6,5},{7,3},{8,12},{9,10},{10,... | collective-permute-start | bytes 1032200 | tf_op jit(solution)/shard_map/ppermute | solution.py:454
  2.9 11.9 %collective-permute-start.1 = (f32[21,32,128]{2,1,0:T(8,128)S(1)}, f32[21,32,128]{2,1,0:T(8,128)S(1)}, u32[]{:S(2)}, u32[]{:S(2)}) collective-permute-start(f32[21,32,128]{2,1,0:T(8,128)S(1)} %get-tuple-element.41), channel_id=1, source_target_pairs={{0,1},{1,0},{2,3},{3,2},{4,5},{5,4},{6,7},{7,6},{8,9},{9,8},{10,11... | collective-permute-start | bytes 1032200 | tf_op jit(solution)/shard_map/ppermute | solution.py:455
  8.0 1.3 %collective-permute-start.2 = (f32[16,512]{1,0:T(8,128)S(1)}, f32[16,512]{1,0:T(8,128)S(1)}, u32[]{:S(2)}, u32[]{:S(2)}) collective-permute-start(f32[16,512]{1,0:T(8,128)S(1)} %get-tuple-element.46), channel_id=1, source_target_pairs={{0,4},{4,0},{8,12},{12,8},{1,5},{5,1},{9,13},{13,9},{2,6},{6,2},{1... | collective-permute-start | bytes 98312 | tf_op jit(solution)/shard_map/ppermute | solution.py:466
  9.3 3.7 %collective-permute-start.3 = (f32[24,512]{1,0:T(8,128)S(1)}, f32[24,512]{1,0:T(8,128)S(1)}, u32[]{:S(2)}, u32[]{:S(2)}) collective-permute-start(f32[24,512]{1,0:T(8,128)S(1)} %stack_kernel.2), channel_id=1, source_target_pairs={{0,12},{4,8},{8,4},{12,0},{1,13},{5,9},{9,5},{13,1},{2,14},{6,10},... | collective-permute-start | bytes 147464 | tf_op jit(solution)/shard_map/ppermute | solution.py:468
  13.0 2.3 %collective-permute-start.4 = (f32[40,128]{1,0:T(8,128)S(1)}, f32[40,128]{1,0:T(8,128)S(1)}, u32[]{:S(2)}, u32[]{:S(2)}) collective-permute-start(f32[40,128]{1,0:T(8,128)S(1)} %get-tuple-element.48), channel_id=1, source_target_pairs={{0,4},{1,2},{2,1},{3,7},{4,0},{5,6},{6,5},{7,3},{8,12},{9,10},{10,... | collective-permute-start | bytes 61448 | tf_op jit(solution)/shard_map/ppermute | solution.py:480
  13.5 3.8 %collective-permute-start.5 = (f32[40,128]{1,0:T(8,128)S(1)}, f32[40,128]{1,0:T(8,128)S(1)}, u32[]{:S(2)}, u32[]{:S(2)}) collective-permute-start(f32[40,128]{1,0:T(8,128)S(1)} %get-tuple-element.49), channel_id=1, source_target_pairs={{0,1},{1,0},{2,3},{3,2},{4,5},{5,4},{6,7},{7,6},{8,9},{9,8},{10,11... | collective-permute-start | bytes 61448 | tf_op jit(solution)/shard_map/ppermute | solution.py:481
  19.3 1.2 %collective-permute-start.6 = (f32[8,768]{1,0:T(8,128)S(1)}, f32[8,768]{1,0:T(8,128)S(1)}, u32[]{:S(2)}, u32[]{:S(2)}) collective-permute-start(f32[8,768]{1,0:T(8,128)S(1)} %get-tuple-element.55), channel_id=1, source_target_pairs={{0,4},{4,0},{8,12},{12,8},{1,5},{5,1},{9,13},{13,9},{2,6},{6,2},{1... | collective-permute-start | bytes 73736 | tf_op jit(solution)/shard_map/ppermute | solution.py:466
  20.5 3.7 %collective-permute-start.7 = (f32[16,768]{1,0:T(8,128)S(1)}, f32[16,768]{1,0:T(8,128)S(1)}, u32[]{:S(2)}, u32[]{:S(2)}) collective-permute-start(f32[16,768]{1,0:T(8,128)S(1)} %stack_kernel.3), channel_id=1, source_target_pairs={{0,12},{4,8},{8,4},{12,0},{1,13},{5,9},{9,5},{13,1},{2,14},{6,10},... | collective-permute-start | bytes 147464 | tf_op jit(solution)/shard_map/ppermute | solution.py:468
  25.7 1.2 %collective-permute-start.8 = (f32[8,128]{1,0:T(8,128)S(1)}, f32[8,128]{1,0:T(8,128)S(1)}, u32[]{:S(2)}, u32[]{:S(2)}) collective-permute-start(f32[8,128]{1,0:T(8,128)S(1)} %get-tuple-element.57), channel_id=1, source_target_pairs={{0,4},{4,0},{8,12},{12,8},{1,5},{5,1},{9,13},{13,9},{2,6},{6,2},{1... | collective-permute-start | bytes 12296 | tf_op jit(solution)/shard_map/ppermute | solution.py:421
  26.9 3.0 %collective-permute-start.9 = (f32[8,128]{1,0:T(8,128)S(1)}, f32[8,128]{1,0:T(8,128)S(1)}, u32[]{:S(2)}, u32[]{:S(2)}) collective-permute-start(f32[8,128]{1,0:T(8,128)S(1)} %add.12), channel_id=1, source_target_pairs={{0,12},{4,8},{8,4},{12,0},{1,13},{5,9},{9,5},{13,1},{2,14},{6,10},... | collective-permute-start | bytes 12296 | tf_op jit(solution)/shard_map/ppermute | solution.py:423
  29.9 3.0 %collective-permute-start.10 = (f32[8,128]{1,0:T(8,128)S(1)}, f32[8,128]{1,0:T(8,128)S(1)}, u32[]{:S(2)}, u32[]{:S(2)}) collective-permute-start(f32[8,128]{1,0:T(8,128)S(1)} %add.13), channel_id=1, source_target_pairs={{0,5},{1,4},{2,7},{3,6},{4,1},{5,0},{6,3},{7,2},{8,13},{9,12},{10,... | collective-permute-start | bytes 12296 | tf_op jit(solution)/shard_map/ppermute | solution.py:426
  33.0 3.9 %collective-permute-start.11 = (f32[8,128]{1,0:T(8,128)S(1)}, f32[8,128]{1,0:T(8,128)S(1)}, u32[]{:S(2)}, u32[]{:S(2)}) collective-permute-start(f32[8,128]{1,0:T(8,128)S(1)} %add.14), channel_id=1, source_target_pairs={{0,6},{1,7},{2,4},{3,5},{4,2},{5,3},{6,0},{7,1},{8,14},{9,15},{10,... | collective-permute-start | bytes 12296 | tf_op jit(solution)/shard_map/ppermute | solution.py:426

commit v7 on v6

v7 whole, which is shorter than its diff:
```python
import functools
import math

import jax
import jax.numpy as jnp
import numpy as np
from jax import lax
from jax.experimental import pallas as pl
from jax.experimental.pallas import tpu as pltpu
from jax.sharding import PartitionSpec as P

base_kappa = 0.001
base_conduct = 1.0

SCALE = 2.0**-31
REACH = 4
EDGE = 8

HIGHEST = lax.Precision.HIGHEST


def dot(a, b):
    return jnp.dot(a, b, precision=HIGHEST, preferred_element_type=jnp.float32)


def circle_kernel(total):
    middle = 2.0 + base_kappa / base_conduct
    rho = (middle - math.sqrt(middle * middle - 4.0)) / 2.0
    height = 1.0 / (1.0 / rho - rho) / base_conduct
    wrap = rho**total
    shift = (1.0 + rho * rho) / (1.0 - rho * rho) + total * wrap / (1.0 - wrap)
    front = height * height / (1.0 - wrap)
    return rho, front, shift


def circle_matrices(count, columns):
    total = count * columns
    rho, front, shift = circle_kernel(total)

    def one_side(n):
        return front * rho**n * (n + shift)

    def both_sides(n):
        return one_side(n) + one_side(total - n)

    place = np.arange(columns)
    rows = columns + 2 * EDGE
    x = np.arange(rows) - EDGE
    used = (x >= -2) & (x < columns + 2)
    near = both_sides(np.abs(x[:, None] - place[None, :])) * used[:, None]
    back = columns - 1 - place
    moments = np.zeros((8, columns))
    moments[0] = rho**place
    moments[1] = place * rho**place
    moments[2] = rho**back
    moments[3] = back * rho**back

    def block(start, size, neighbour):
        start = start % count * columns
        a = start - x
        b = total - start + x - (size * columns - 1)
        out = np.zeros((rows, 8))
        out[:, 0] = front * rho**a * (a + shift)
        out[:, 1] = front * rho**a
        out[:, 2] = front * rho**b * (b + shift)
        out[:, 3] = front * rho**b
        amend = both_sides(1) - both_sides(-1)
        if neighbour == "east":
            out[EDGE + columns + 1, 4] = amend
        if neighbour == "west":
            out[EDGE - 2, 4] = amend
        return out * used[:, None]

    fours = range(4, count, 4)
    even = [block(1, 1, "east"), block(-2, 2, "west")] + [block(-2 - d, 4, "") for d in fours]
    odd = [block(-1, 1, "west"), block(1, 2, "east")] + [block(-1 - d, 4, "") for d in fours]
    far = np.stack([np.concatenate(even, axis=1), np.concatenate(odd, axis=1)])
    as_f32 = lambda m: np.asarray(m, np.float32)
    return as_f32(near), as_f32(far), as_f32(moments)


def lon_perms(count):
    first = [(i, i ^ 1) for i in range(count)]
    return first, [(i, (i - 1 + 2 * (i % 2)) % count) for i in range(count)]


def lat_perms(count, bands):
    first, second = [], []
    for i in range(count):
        for j in range(bands):
            k = j - 1 + 2 * (j % 2)
            first.append((i * bands + j, i * bands + (j ^ 1)))
            second.append((i * bands + j, i * bands + k if 0 <= k < bands else (i ^ 1) * bands + j))
    return first, second


def inner_band():
    return (lax.axis_index("lat") > 0) & (lax.axis_index("lat") < lax.axis_size("lat") - 1)


def whole(n):
    return [pl.BlockSpec(memory_space=pltpu.VMEM)] * n


def call(kernel, outs, *args, scratch=()):
    args = [pltpu.with_memory_space_constraint(a, pltpu.VMEM) for a in args]
    return pl.pallas_call(
        kernel,
        out_shape=[pltpu.VMEM(s, jnp.float32) for s in outs],
        in_specs=whole(len(args)),
        out_specs=whole(len(outs)),
        scratch_shapes=[pltpu.VMEM(s, jnp.float32) for s in scratch],
        compiler_params=pltpu.CompilerParams(vmem_limit_bytes=24 << 20),
        name=getattr(kernel, "func", kernel).__name__,
    )(*args)


FULL, PART = REACH, REACH - 1
PLANES = 3 * FULL + 3 * PART


def band_kernel(rows, levels, *refs):
    sources, (second, first), copies, sems = refs[:7], refs[7:9], refs[9:16], refs[16]
    moves = [pltpu.make_async_copy(x, y, sems.at[k]) for k, (x, y) in enumerate(zip(sources, copies))]
    for move in moves:
        move.start()
    for move in moves:
        move.wait()
    noise, kappa2, conduct, land = copies[:4]
    odd = lax.axis_index("lat") % 2
    top = rows - REACH
    loads = (
        lambda at: noise[at, :],
        lambda at: land[at, :].astype(jnp.float32),
        lambda at: conduct[1, at, :],
        lambda at: kappa2[at, :],
        lambda at: conduct[0, at, :],
        lambda at: conduct[2, at, :],
    )
    for out, side in ((first, odd), (second, 1 - odd)):
        k = 0
        for kind, load in enumerate(loads):
            count = FULL if kind < 3 else PART
            start = (1 - side) * (rows - count)
            for j in range(count):
                out[k] = load(pl.ds(start + j, levels, stride=rows))
                k += 1


def turned(planes, rows_of_planes):
    blocks = [jnp.concatenate(planes[j : j + REACH], axis=0) for j in range(0, rows_of_planes, REACH)]
    return jnp.concatenate([b.T for b in blocks], axis=1)


def coefficients(levels, band, kappa, east, north, upper, ocean):
    columns, lanes = kappa.shape
    lane = lax.broadcasted_iota(jnp.int32, (1, lanes), 1)
    row = lax.broadcasted_iota(jnp.int32, (columns, 1), 0)
    upper = jnp.where(lane % levels == levels - 1, 0.0, upper)
    south = jnp.where(lane % band < levels, 0.0, pltpu.roll(north, levels, 1))
    west = jnp.where(row == 0, 0.0, pltpu.roll(east, 1, 0))
    ocean_east = jnp.where(row == columns - 1, 1.0, pltpu.roll(ocean, columns - 1, 0))
    diagonal = ocean * (kappa + east + west + north + south + upper + pltpu.roll(upper, 1, 1))
    return diagonal, east * ocean * ocean_east, upper * ocean * pltpu.roll(ocean, lanes - 1, 1)


def store(statics, edge, diagonal, to_east, north, to_upper, ocean, east):
    for k, x in enumerate((diagonal, to_east, north, to_upper, ocean)):
        statics[k] = x
    edge[0:1] = east[east.shape[0] - 1 :]


def own_kernel(
    rows, levels, columns,
    noise, kappa2, conduct, land, weights,
    field, statics, edge, to_first, to_second,
):
    last_band = lax.axis_index("lat") == lax.axis_size("lat") - 1
    lon_odd = lax.axis_index("lon") % 2
    lanes = rows * levels

    def own(load):
        return turned([load(pl.ds(j, levels, stride=rows)) for j in range(rows)], rows)

    r = own(lambda at: noise[at, :])
    field[...] = r
    ocean = own(lambda at: land[at, :].astype(jnp.float32))
    north = own(lambda at: conduct[1, at, :])
    kappa = own(lambda at: kappa2[at, :])
    east = own(lambda at: conduct[0, at, :])
    upper = own(lambda at: conduct[2, at, :])
    lane = lax.broadcasted_iota(jnp.int32, (1, lanes), 1)
    north = jnp.where(last_band & (lane >= lanes - levels), 0.0, north)
    diagonal, to_east, to_upper = coefficients(levels, lanes, kappa, east, north, upper, ocean)
    store(statics, edge, diagonal, to_east, north, to_upper, ocean, east)
    m = dot(weights[...], r)[:4]
    end = columns - 1
    blank = jnp.zeros((5, lanes), jnp.float32)
    for_east = [m, r[end:], diagonal[end:], to_east[end - 1 : end], east[end:], ocean[end:], north[end:], to_upper[end:], blank]
    for_west = [m, r[:1], diagonal[:1], to_east[:1], east[:1], ocean[:1], north[:1], to_upper[:1], blank]
    for_east = jnp.concatenate(for_east, axis=0)
    for_west = jnp.concatenate(for_west, axis=0)
    to_first[...] = jnp.where(lon_odd == 0, for_east, for_west)
    to_second[...] = jnp.where(lon_odd == 0, for_west, for_east)


def ghost_kernel(levels, columns, got_second, got_first, near, spread, statics, edge):
    lat_odd = lax.axis_index("lat") % 2
    group = REACH * levels

    def ghost(kind, north):
        count = FULL if kind < 3 else PART
        k = kind * FULL if kind < 3 else 3 * FULL + (kind - 3) * PART
        a = got_first[pl.ds(k, count)].reshape(count * levels, columns)
        b = jnp.where(inner_band(), got_second[pl.ds(k, count)], 0.0).reshape(count * levels, columns)
        from_first = (lat_odd == 0) if north else (lat_odd == 1)
        planes = jnp.where(from_first, a, b)
        if count == REACH:
            return planes.T
        blank = jnp.zeros((group - count * levels, columns), jnp.float32)
        return jnp.concatenate([planes, blank] if north else [blank, planes], axis=0).T

    r, ocean, north, kappa, east, upper = (
        jnp.concatenate([ghost(kind, False), ghost(kind, True)], axis=1) for kind in range(6)
    )
    spread[...] = dot(near[...], r)
    diagonal, to_east, to_upper = coefficients(levels, group, kappa, east, north, upper, ocean)
    store(statics, edge, diagonal, to_east, north, to_upper, ocean, east)


def forward_kernel(group, *refs):
    lists, (second, first) = refs[:-2], refs[-2:]
    odd = lax.axis_index("lat") % 2
    k = 0
    for x in lists:
        count, lanes = x.shape
        low, high = x[:, 0:group], x[:, lanes - group :]
        first[pl.ds(k, count)] = jnp.where(odd == 0, high, low)
        second[pl.ds(k, count)] = jnp.where(odd == 0, low, high)
        k += count


def joint_moments(left, right, rho, width):
    c = rho**width
    return jnp.concatenate(
        [
            left[0:1] + c * right[0:1],
            left[1:2] + c * (right[1:2] + width * right[0:1]),
            right[2:3] + c * left[2:3],
            right[3:4] + c * (left[3:4] + width * left[2:3]),
        ],
        axis=0,
    )


def chip_kernel(rho, columns, own, got, out):
    even = lax.axis_index("lon") % 2 == 0
    mine, its = own[0:4], got[0:4]
    out[...] = own[...]
    out[0:4] = joint_moments(jnp.where(even, mine, its), jnp.where(even, its, mine), rho, columns)


def quad_kernel(rho, columns, mine, got, out):
    even = lax.axis_index("lon") % 2 == 0
    a, b = mine[0:4], got[0:4]
    m = joint_moments(jnp.where(even, b, a), jnp.where(even, a, b), rho, 2 * columns)
    out[...] = jnp.concatenate([m, jnp.zeros_like(m)], axis=0)


def near_kernel(near, field, spread):
    spread[...] = dot(near[...], field[...])


def told(far, lists):
    return dot(far[lax.axis_index("lon") % 2], jnp.concatenate([t[0:8] for t in lists], axis=0))


TILE = 8


def faces(v, n, s, u, low, levels):
    lanes = v.shape[1]
    return (
        n * pltpu.roll(v, lanes - levels, 1)
        + s * pltpu.roll(v, levels, 1)
        + u * pltpu.roll(v, lanes - 1, 1)
        + low * pltpu.roll(v, 1, 1)
    )


def apply_tile(levels, v, statics, at):
    d, e, w, n, s, u, low = (statics[k, pl.ds(at, TILE)] for k in range(7))
    i = at + EDGE
    here = v[pl.ds(i, TILE)]
    out = d * here - e * v[pl.ds(i + 1, TILE)] - w * v[pl.ds(i - 1, TILE)]
    return here, out - faces(here, n, s, u, low, levels)


def apply_rim(levels, columns, v, f, rim):
    end = EDGE + columns
    pick = lambda a, b: jnp.concatenate([v[a : a + 1], v[b : b + 1], jnp.zeros((6, v.shape[1]), jnp.float32)], axis=0)
    here = pick(EDGE - 1, end)
    g = rim[0] * here - rim[1] * pick(EDGE, end + 1) - rim[2] * pick(EDGE - 2, end - 1)
    g = g - faces(here, rim[3], rim[4], rim[5], rim[6], levels)
    f[EDGE - 1 : EDGE] = g[0:1]
    f[end : end + 1] = g[1:2]


def first_kernel(
    rows, levels, columns, others,
    own_spread, own_statics, own_edge, ghost_spread, ghost_statics, edge, far, weights, side_second, side_first, *rest,
):
    received = rest[: 1 + others]
    v, image, statics, rim, to_first, to_second, f, scaled = rest[1 + others :]
    lat_odd = lax.axis_index("lat") % 2
    even = lax.axis_index("lon") % 2 == 0
    group = REACH * levels
    lanes = rows * levels + 2 * group

    def joined(own, ghost):
        return jnp.concatenate([ghost[:, :group], own, ghost[:, group:]], axis=1)

    lists, k = [], 0
    for x in received:
        count = x.shape[0]
        a = side_first[pl.ds(k, count)]
        b = jnp.where(inner_band(), side_second[pl.ds(k, count)], 0.0)
        lists.append(jnp.concatenate([jnp.where(lat_odd == 1, a, b), x[...], jnp.where(lat_odd == 1, b, a)], axis=1))
        k += count
    v[...] = joined(own_spread[...], ghost_spread[...]) + told(far, lists)

    lane = lax.broadcasted_iota(jnp.int32, (1, lanes), 1)
    first_of_band = ((lane >= group) & (lane < group + levels)) | ((lane >= lanes - group) & (lane < lanes - group + levels))

    def completed(diagonal, north, ocean):
        diagonal = diagonal + jnp.where(first_of_band, ocean * pltpu.roll(north, levels, 1), 0.0)
        return diagonal, north * ocean * pltpu.roll(ocean, lanes - levels, 1)

    one, two = lists[0][0:16], lists[1][0:16]
    east_list, west_list = jnp.where(even, one, two), jnp.where(even, two, one)
    end = columns - 1
    for at in range(0, columns, TILE):
        tile = pl.ds(at, TILE)
        d, e, n, u, ocean = (joined(own_statics[k, tile], ghost_statics[k, tile]) for k in range(5))
        row = at + lax.broadcasted_iota(jnp.int32, (TILE, 1), 0)
        d, n = completed(d, n, ocean)
        if at == 0:
            face_west = west_list[7:8] * west_list[8:9] * ocean[0:1]
            d = d + jnp.where(row == 0, ocean * west_list[7:8], 0.0)
            carried = face_west
        if at + TILE == columns:
            e = jnp.where(row == end, e * east_list[8:9], e)
            last_east = e[TILE - 1 :]
        statics[0, tile] = d
        statics[1, tile] = e
        statics[2, tile] = jnp.where(row == at, carried, pltpu.roll(e, 1, 0))
        statics[3, tile] = n
        statics[4, tile] = pltpu.roll(n, levels, 1)
        statics[5, tile] = u
        statics[6, tile] = pltpu.roll(u, 1, 1)
        statics[7, tile] = ocean
        carried = e[TILE - 1 :]
    blank = jnp.zeros((6, lanes), jnp.float32)
    stack = lambda p, q: jnp.concatenate([p, q, blank], axis=0)
    last_face = joined(own_edge[0:1], edge[0:1])
    rim_diagonal, rim_north = completed(
        stack(west_list[5:6], east_list[5:6] + east_list[8:9] * last_face),
        stack(west_list[9:10], east_list[9:10]),
        stack(west_list[8:9], east_list[8:9]),
    )
    rim_upper = stack(west_list[10:11], east_list[10:11])
    rim[0] = rim_diagonal
    rim[1] = stack(face_west, east_list[6:7])
    rim[2] = stack(west_list[6:7], last_east)
    rim[3] = rim_north
    rim[4] = pltpu.roll(rim_north, levels, 1)
    rim[5] = rim_upper
    rim[6] = pltpu.roll(rim_upper, 1, 1)

    for at in range(0, columns, TILE):
        f[pl.ds(EDGE + at, TILE)] = apply_tile(levels, v, statics, at)[1]
    apply_rim(levels, columns, v, f, rim)
    for at in range(0, columns, TILE):
        second = apply_tile(levels, f, statics, at)[1]
        w = jnp.where(statics[7, pl.ds(at, TILE)] > 0.5, second, v[pl.ds(EDGE + at, TILE)])
        image[pl.ds(at, TILE)] = w
        scaled[pl.ds(at, TILE)] = w * SCALE
    m = dot(weights[...], scaled[...])[:4]
    pad = jnp.zeros((3, lanes), jnp.float32)
    for_east = jnp.concatenate([m, scaled[end:], pad], axis=0)
    for_west = jnp.concatenate([m, scaled[:1], pad], axis=0)
    to_first[...] = jnp.where(even, for_east, for_west)
    to_second[...] = jnp.where(even, for_west, for_east)


def lane_sums(tiles):
    total = functools.reduce(lambda a, b: a + b, tiles)
    s = jnp.sum(total, axis=0, keepdims=True)
    return functools.reduce(lambda a, b: a + b, [s[:, k : k + 128] for k in range(0, s.shape[1], 128)])


def own_lanes(rows, levels):
    return slice(REACH * levels, (REACH + rows) * levels)


def between_kernel(rows, levels, columns, near, field, precond, image, spread, sums):
    own = own_lanes(rows, levels)
    spread[...] = dot(near[...], image[...] * SCALE)
    energy, curve = [], []
    for at in range(0, columns, TILE):
        tile = pl.ds(at, TILE)
        p = precond[pl.ds(EDGE + at, TILE), own]
        energy.append(field[tile] * p)
        curve.append(p * image[tile, own])
    sums[...] = jnp.concatenate([lane_sums(energy), lane_sums(curve), jnp.zeros((6, 128), jnp.float32)], axis=0)


def second_kernel(levels, columns, rows, others, spread, early, image, statics, far, rim, *rest):
    received = rest[: 1 + others]
    v, f, sums = rest[1 + others :]
    v[...] = spread[...] + told(far, received)
    own = own_lanes(rows, levels)
    mixed, last = [], []
    for at in range(0, columns, TILE):
        tile = pl.ds(at, TILE)
        q, b = apply_tile(levels, v, statics, at)
        f[pl.ds(EDGE + at, TILE)] = b
        q, b, ocean = q[:, own], b[:, own], statics[7, tile, own]
        mixed.append(image[tile, own] * q)
        still = jnp.where(ocean > 0.5, b, q)
        last.append(still * still)
    apply_rim(levels, columns, v, f, rim)
    sums[...] = jnp.concatenate([early[0:2], lane_sums(mixed), lane_sums(last), early[4:8]], axis=0)


def turn_kernel(rows, levels, columns, precond, image, again, f, statics, *outs):
    z = outs[4]
    own = own_lanes(rows, levels)
    for at in range(0, columns, TILE):
        second = apply_tile(levels, f, statics, at)[1]
        tile = pl.ds(at, TILE)
        z[tile] = jnp.where(statics[7, tile] > 0.5, second, again[pl.ds(EDGE + at, TILE)])
    group = REACH * levels
    slab = pl.ds(EDGE, columns)
    for j in range(0, rows, REACH):
        at = slice(own.start + j * levels, own.start + j * levels + group)
        for out, x in zip(outs, (precond[slab, at], image[:, at], again[slab, at], z[:, at])):
            t = x.T
            for i in range(REACH):
                out[pl.ds(j + i, levels, stride=rows), :] = t[i * levels : (i + 1) * levels]


PIECES = 4


def combine_kernel(sums, noise, precond, image, again, along, answer, left, x, y, sems):
    total = jnp.sum(sums[...], axis=1, keepdims=True)
    energy, curve, mixed, last = total[0:1], total[1:2], total[2:3], total[3:4]
    alpha = energy / curve
    beta = alpha / SCALE
    growth = alpha * beta * mixed / energy
    step = energy * (growth - 1.0) / (beta * beta * last - growth * growth * curve)
    keep = alpha + step * growth
    back = step * beta
    size = noise.shape[0] // PIECES
    moves = []
    for k in range(PIECES):
        part = pl.ds(k * size, size)
        x[part] = keep * precond[part] - back * again[part]
        moves.append(pltpu.make_async_copy(x.at[part], answer.at[part], sems.at[0, k]))
        moves[-1].start()
        y[part] = noise[part] - (keep * image[part] - back * along[part])
        moves.append(pltpu.make_async_copy(y.at[part], left.at[part], sems.at[1, k]))
        moves[-1].start()
    for move in moves:
        move.wait()


def doubling(count):
    steps = []
    while 2 ** len(steps) < count:
        steps.append(2 ** len(steps))
    return steps


def summed(x):
    count, bands = lax.axis_size("lon"), lax.axis_size("lat")
    x = x + lax.ppermute(x, "lon", [(i, i ^ 1) for i in range(count)])
    for step in doubling(count)[1:]:
        x = x + lax.ppermute(x, "lon", [(i, i ^ step ^ 1) for i in range(count)])
    for step in doubling(bands):
        pairs = [(i * bands + j, (i ^ 1) * bands + (j ^ step)) for i in range(count) for j in range(bands)]
        x = x + lax.ppermute(x, ("lon", "lat"), pairs)
    return x


def body(near, far, weights, noise, kappa2, conduct, land):
    levels, rows, columns = noise.shape
    count = lax.axis_size("lon")
    others = count // 4
    flat = levels * rows
    group = REACH * levels
    lanes = flat + 2 * group
    tall = columns + 2 * EDGE
    rho = circle_kernel(count * columns)[0]
    noise = noise.reshape(flat, columns)
    kappa2 = kappa2.reshape(flat, columns)
    land = land.reshape(flat, columns)
    conduct = conduct.reshape(3, flat, columns)

    sources = (noise, kappa2, conduct, land, near, far, weights)
    planes = (PLANES, levels, columns)
    second, first, noise, kappa2, conduct, land, near, far, weights = pl.pallas_call(
        functools.partial(band_kernel, rows, levels),
        out_shape=[pltpu.VMEM(planes, jnp.float32)] * 2 + [pltpu.VMEM(x.shape, x.dtype) for x in sources],
        in_specs=[pl.BlockSpec(memory_space=pltpu.HBM)] * len(sources),
        out_specs=whole(2 + len(sources)),
        scratch_shapes=[pltpu.SemaphoreType.DMA((len(sources),))],
        compiler_params=pltpu.CompilerParams(vmem_limit_bytes=8 << 20),
        name="band_kernel",
    )(*[pltpu.with_memory_space_constraint(x, pltpu.HBM) for x in sources])
    lat_a, lat_b = lat_perms(count, lax.axis_size("lat"))
    to_band = lambda x, pairs: lax.ppermute(x, ("lon", "lat"), pairs)
    got_second, got_first = to_band(second, lat_b), to_band(first, lat_a)

    own_field, own_statics, own_edge, to_first, to_second = call(
        functools.partial(own_kernel, rows, levels, columns),
        [(columns, flat), (5, columns, flat), (8, flat), (16, flat), (16, flat)],
        noise, kappa2, conduct, land, weights,
    )
    lon_a, lon_b = lon_perms(count)

    def exchange(one, two):
        wide = two.shape[1]
        got_one = lax.ppermute(one, "lon", lon_a)
        (two,) = call(functools.partial(chip_kernel, rho, columns), [two.shape], two, got_one)
        got_two = lax.ppermute(two, "lon", lon_b)
        if count == 4:
            return [got_one, got_two]
        (four,) = call(functools.partial(quad_kernel, rho, columns), [(8, wide)], two, got_two)
        return [got_one, got_two] + [
            lax.ppermute(four, "lon", [(i, (i + d) % count) for i in range(count)]) for d in range(4, count, 4)
        ]

    lists = exchange(to_first, to_second)
    (own_spread,) = call(near_kernel, [(tall, flat)], near, own_field)
    heights = sum(x.shape[0] for x in lists)
    side_second, side_first = call(functools.partial(forward_kernel, group), [(heights, group)] * 2, *lists)
    side_second, side_first = to_band(side_second, lat_b), to_band(side_first, lat_a)
    ghost_spread, ghost_statics, edge = call(
        functools.partial(ghost_kernel, levels, columns),
        [(tall, 2 * group), (5, columns, 2 * group), (8, 2 * group)],
        got_second, got_first, near,
    )
    precond, image, statics, rim, to_first, to_second = call(
        functools.partial(first_kernel, rows, levels, columns, others),
        [(tall, lanes), (columns, lanes), (8, columns, lanes), (7, 8, lanes), (8, lanes), (8, lanes)],
        own_spread, own_statics, own_edge, ghost_spread, ghost_statics, edge, far, weights, side_second, side_first, *lists,
        scratch=[(tall, lanes), (columns, lanes)],
    )
    lists = exchange(to_first, to_second)
    spread, sums = call(
        functools.partial(between_kernel, rows, levels, columns),
        [(tall, lanes), (8, 128)],
        near, own_field, precond, image,
    )
    again, half, sums = call(
        functools.partial(second_kernel, levels, columns, rows, others),
        [(tall, lanes), (tall, lanes), (8, 128)],
        spread, sums, image, statics, far, rim, *lists,
    )
    sums = summed(sums)
    turned_back = call(
        functools.partial(turn_kernel, rows, levels, columns),
        [(flat, columns)] * 4 + [(columns, lanes)],
        precond, image, again, half, statics,
    )[:4]
    operands = [pltpu.with_memory_space_constraint(x, pltpu.VMEM) for x in (sums, noise, *turned_back)]
    answer, left = pl.pallas_call(
        combine_kernel,
        out_shape=[jax.ShapeDtypeStruct((flat, columns), jnp.float32)] * 2,
        in_specs=whole(len(operands)),
        out_specs=[pl.BlockSpec(memory_space=pltpu.HBM)] * 2,
        scratch_shapes=[pltpu.VMEM((flat, columns), jnp.float32)] * 2 + [pltpu.SemaphoreType.DMA((2, PIECES))],
        compiler_params=pltpu.CompilerParams(vmem_limit_bytes=8 << 20),
        name="combine_kernel",
    )(*operands)
    return answer.reshape(levels, rows, columns), left.reshape(levels, rows, columns)


def solution(mesh):
    def run(noise, kappa2, conduct, land):
        count = mesh.shape["lon"]
        matrices = circle_matrices(count, noise.shape[2] // count)
        return jax.shard_map(
            functools.partial(body, *matrices),
            mesh=mesh,
            in_specs=(
                P("ens", "lat", "lon"),
                P(None, "lat", "lon"),
                P(None, None, "lat", "lon"),
                P(None, "lat", "lon"),
            ),
            out_specs=(P("ens", "lat", "lon"), P("ens", "lat", "lon")),
            check_vma=False,
        )(noise, kappa2, conduct, land)

    return run
```

time: 38.4 us -> 37.6 us (0.979)
  waiting for transfers between devices: 17.4 us -> 14 us
  Pallas kernels: 7.82 us -> 10.3 us
    pallas_call x8 -> x11, Pallas kernels: 6.11 us -> 8.66 us  [the longest x10 7.66 us: call(): pl.pallas_call(kernel, out_shape=[pltpu.VMEM(s, jnp.float32) for s in out...]
    ppermute x2, waiting for transfers between devices: 5.22 us -> 3.59 us  [summed(): x = x + lax.ppermute(x, ('lon', 'lat'), pairs)]
    ppermute x2, waiting for transfers between devices: 4.87 us -> 3.57 us  [exchange(): got_two = lax.ppermute(two, 'lon', lon_b)]
    ppermute x4, waiting for transfers between devices: 2.18 us -> 1.69 us  [body(): to_band = lambda x, pairs: lax.ppermute(x, ('lon', 'lat'), pairs)]
  transfers between devices with their start and end apart: 12 -> 12, of which waited for: 10 -> 10; matrix products, arithmetic and copies ran while one was open for 0% -> 0% of each run, Pallas kernels for 3% -> 10%
where the time goes in v7:
time: 37.6 us; the launch traced here: 37.4 us
  waiting for transfers between devices  14 us (37%)
  starting transfers between devices  12.3 us (33%)
  Pallas kernels  10.3 us (27%)
  between operations  0.72 us (2%)
    pallas_call x10, Pallas kernels, call(): pl.pallas_call(kernel, out_shape=[pltpu.VMEM(s, jnp.float32) for s in out...  7.66 us
    ppermute x4, starting transfers between devices, body(): to_band = lambda x, pairs: lax.ppermute(x, ('lon', 'lat'), pairs)  6.35 us
    ppermute x2, waiting for transfers between devices, summed(): x = x + lax.ppermute(x, ('lon', 'lat'), pairs)  3.59 us
    ppermute x2, waiting for transfers between devices, exchange(): got_two = lax.ppermute(two, 'lon', lon_b)  3.57 us
    ppermute x2, starting transfers between devices, exchange(): got_two = lax.ppermute(two, 'lon', lon_b)  2.65 us
    ppermute x2, waiting for transfers between devices, exchange(): got_one = lax.ppermute(one, 'lon', lon_a)  2.4 us
    ppermute x1, waiting for transfers between devices, summed(): x = x + lax.ppermute(x, 'lon', [(i, i ^ step ^ 1) for i in range(count)])  1.77 us
    ppermute x2, starting transfers between devices, summed(): x = x + lax.ppermute(x, ('lon', 'lat'), pairs)  1.74 us
  transfers between devices with their start and end apart: 12, of which 10 were waited for; matrix products, arithmetic and copies ran while one was open for 0% of the time, Pallas kernels for 10%

profile of v7, /device:TPU:0, one launch (start us, length us, event | category | flops | bytes accessed | tf_op | source)
XLA Modules:
  0.0 37.4 jit_solution(7562999080125203995)
XLA Ops:
  0.6 1.7 %band_kernel.1 = (f32[21,32,128]{2,1,0:T(8,128)S(1)}, f32[21,32,128]{2,1,0:T(8,128)S(1)}, f32[512,128]{1,0:T(8,128)S(1)}, f32[512,128]{1,0:T(8,128)S(1)}, f32[3,...) custom-call(f32[512,128]{1,0:T(8,128)} %bitcast.7, ...), custom_call_target="tpu_custom_call" | custom-call | tf_op jit(solution)/shard_map/band_kernel/pallas_call | solution.py:513
  2.3 0.6 %collective-permute-start = (f32[21,32,128]{2,1,0:T(8,128)S(1)}, f32[21,32,128]{2,1,0:T(8,128)S(1)}, u32[]{:S(2)}, u32[]{:S(2)}) collective-permute-start(f32[21,32,128]{2,1,0:T(8,128)S(1)} %get-tuple-element.47), channel_id=1, source_target_pairs={{0,4},{1,2},{2,1},{3,7},{4,0},{5,6},{6,5},{7,3},{8,12},{9,10},{10,... | collective-permute-start | bytes 1032200 | tf_op jit(solution)/shard_map/ppermute | solution.py:523
  2.9 4.1 %collective-permute-start.1 = (f32[21,32,128]{2,1,0:T(8,128)S(1)}, f32[21,32,128]{2,1,0:T(8,128)S(1)}, u32[]{:S(2)}, u32[]{:S(2)}) collective-permute-start(f32[21,32,128]{2,1,0:T(8,128)S(1)} %get-tuple-element.48), channel_id=1, source_target_pairs={{0,1},{1,0},{2,3},{3,2},{4,5},{5,4},{6,7},{7,6},{8,9},{9,8},{10,11... | collective-permute-start | bytes 1032200 | tf_op jit(solution)/shard_map/ppermute | solution.py:523
  7.0 0.9 %own_kernel.1 = (f32[128,512]{1,0:T(8,128)S(1)}, f32[5,128,512]{2,1,0:T(8,128)S(1)}, f32[8,512]{1,0:T(8,128)S(1)}, f32[16,512]{1,0:T(8,128)S(1)}, f32[16,512]{1,0:T(8,128)S(1)}) custom-call(f32[512,128]{1,0:T(8,128)S(1)} %get-tuple-element.39.noise, f32[512,128]{1,0:T(8,128)S(1)} %get-tuple-element.40.kappa2, f32[3,512,128]{2,1,0:T(8,128)S(1)} %get-tuple-element.41.conduct, ...), custom_call_target="tpu_custom_call" | custom-call | tf_op jit(solution)/shard_map/own_kernel/pallas_call | solution.py:107
  7.9 0.1 collective-permute-start.2
  8.0 1.2 %collective-permute-done.2.got.refs_0_.rest_0_ = f32[16,512]{1,0:T(8,128)S(1)} collective-permute-done((f32[16,512]{1,0:T(8,128)S(1)}, f32[16,512]{1,0:T(8,128)S(1)}, u32[]{:S(2)}, u32[]{:S(2)}) %collective-permute-start.2) | collective-permute-done | bytes 32800 | tf_op jit(solution)/shard_map/ppermute | solution.py:535
  9.2 1.3 %collective-permute-start.3 = (f32[16,512]{1,0:T(8,128)S(1)}, f32[16,512]{1,0:T(8,128)S(1)}, u32[]{:S(2)}, u32[]{:S(2)}) collective-permute-start(f32[16,512]{1,0:T(8,128)S(1)} %chip_kernel.2), channel_id=1, source_target_pairs={{0,12},{4,8},{8,4},{12,0},{1,13},{5,9},{9,5},{13,1},{2,14},{6,10},... | collective-permute-start | bytes 98312 | tf_op jit(solution)/shard_map/ppermute | solution.py:537
  10.6 2.1 %collective-permute-done.3.refs_1_.rest_1_ = f32[16,512]{1,0:T(8,128)S(1)} collective-permute-done((f32[16,512]{1,0:T(8,128)S(1)}, f32[16,512]{1,0:T(8,128)S(1)}, u32[]{:S(2)}, u32[]{:S(2)}) %collective-permute-start.3) | collective-permute-done | bytes 32800 | tf_op jit(solution)/shard_map/ppermute | solution.py:537
  12.7 0.5 %collective-permute-start.4 = (f32[32,128]{1,0:T(8,128)S(1)}, f32[32,128]{1,0:T(8,128)S(1)}, u32[]{:S(2)}, u32[]{:S(2)}) collective-permute-start(f32[32,128]{1,0:T(8,128)S(1)} %get-tuple-element.55), channel_id=1, source_target_pairs={{0,4},{1,2},{2,1},{3,7},{4,0},{5,6},{6,5},{7,3},{8,12},{9,10},{10,... | collective-permute-start | bytes 49160 | tf_op jit(solution)/shard_map/ppermute | solution.py:523
  13.1 1.2 %collective-permute-start.5 = (f32[32,128]{1,0:T(8,128)S(1)}, f32[32,128]{1,0:T(8,128)S(1)}, u32[]{:S(2)}, u32[]{:S(2)}) collective-permute-start(f32[32,128]{1,0:T(8,128)S(1)} %get-tuple-element.56), channel_id=1, source_target_pairs={{0,1},{1,0},{2,3},{3,2},{4,5},{5,4},{6,7},{7,6},{8,9},{9,8},{10,11... | collective-permute-start | bytes 49160 | tf_op jit(solution)/shard_map/ppermute | solution.py:523
  14.3 0.4 %near_kernel.1.own_spread = f32[144,512]{1,0:T(8,128)S(1)} custom-call(f32[144,128]{1,0:T(8,128)S(1)} %get-tuple-element.38.near, f32[128,512]{1,0:T(8,128)S(1)} %get-tuple-element.44.field), custom_call_target="tpu_custom_call" | custom-call | tf_op jit(solution)/shard_map/near_kernel/pallas_call | solution.py:107
  14.7 0.0 collective-permute-done.got_second
  14.7 0.1 collective-permute-done.1.got_first
  14.8 0.4 %ghost_kernel.1 = (f32[144,256]{1,0:T(8,128)S(1)}, f32[5,128,256]{2,1,0:T(8,128)S(1)}, f32[8,256]{1,0:T(8,128)S(1)}) custom-call(f32[21,32,128]{2,1,0:T(8,128)S(1)} %collective-permute-done.got_second, f32[21,32,128]{2,1,0:T(8,128)S(1)} %collective-permute-done.1.got_first, f32[144,128]{1,0:T(8,128)S(1)} %get-tuple-element.38.near), custom_call_target="tpu_custom_call" | custom-call | tf_op jit(solution)/shard_map/ghost_kernel/pallas_call | solution.py:107
  15.2 0.0 collective-permute-done.4.side_second
  15.2 1.6 %collective-permute-done.5.side_first = f32[32,128]{1,0:T(8,128)S(1)} collective-permute-done((f32[32,128]{1,0:T(8,128)S(1)}, f32[32,128]{1,0:T(8,128)S(1)}, u32[]{:S(2)}, u32[]{:S(2)}) %collective-permute-start.5) | collective-permute-done | bytes 16416 | tf_op jit(solution)/shard_map/ppermute | solution.py:523
  16.9 2.7 %first_kernel.1 = (f32[144,768]{1,0:T(8,128)S(1)}, f32[128,768]{1,0:T(8,128)S(1)}, f32[8,128,768]{2,1,0:T(8,128)S(1)}, f32[7,8,768]{2,1,0:T(8,128)S(1)}, f32[8,768]{1,0:T(8,128)S(1)}, /*index=5*/f32[8,768]{1,0:T(8,128)S(1)}) custom-call(f32[144,512]{1,0:T(8,128)S(1)} %near_kernel.1.own_spread, f32[5,128,512]{2,1,0:T(8,128)S(1)} %get-tuple-element.45.own_statics, ...), custom_call_target="tpu_custom_call" | custom-call | tf_op jit(solution)/shard_map/first_kernel/pallas_call | solution.py:107
  19.6 0.0 collective-permute-start.6
  19.6 1.2 %collective-permute-done.6.got.rest_0_ = f32[8,768]{1,0:T(8,128)S(1)} collective-permute-done((f32[8,768]{1,0:T(8,128)S(1)}, f32[8,768]{1,0:T(8,128)S(1)}, u32[]{:S(2)}, u32[]{:S(2)}) %collective-permute-start.6) | collective-permute-done | bytes 24608 | tf_op jit(solution)/shard_map/ppermute | solution.py:535
  20.8 1.3 %collective-permute-start.7 = (f32[8,768]{1,0:T(8,128)S(1)}, f32[8,768]{1,0:T(8,128)S(1)}, u32[]{:S(2)}, u32[]{:S(2)}) collective-permute-start(f32[8,768]{1,0:T(8,128)S(1)} %chip_kernel.3), channel_id=1, source_target_pairs={{0,12},{4,8},{8,4},{12,0},{1,13},{5,9},{9,5},{13,1},{2,14},{6,10},... | collective-permute-start | bytes 73736 | tf_op jit(solution)/shard_map/ppermute | solution.py:537
  22.2 0.5 %between_kernel.1 = (f32[144,768]{1,0:T(8,128)S(1)}, f32[8,128]{1,0:T(8,128)S(1)}) custom-call(f32[144,128]{1,0:T(8,128)S(1)} %get-tuple-element.38.near, f32[128,512]{1,0:T(8,128)S(1)} %get-tuple-element.44.field, f32[144,768]{1,0:T(8,128)S(1)} %get-tuple-element.57.precond, f32[128,768]{1,0:T(8,128)S(1)} %get-tuple-element.58.image), custom_call_target="tpu_custom_call" | custom-call | tf_op jit(solution)/shard_map/between_kernel/pallas_call | solution.py:107
  22.7 1.5 %collective-permute-done.7.rest_1_ = f32[8,768]{1,0:T(8,128)S(1)} collective-permute-done((f32[8,768]{1,0:T(8,128)S(1)}, f32[8,768]{1,0:T(8,128)S(1)}, u32[]{:S(2)}, u32[]{:S(2)}) %collective-permute-start.7) | collective-permute-done | bytes 24608 | tf_op jit(solution)/shard_map/ppermute | solution.py:537
  24.2 1.0 %second_kernel.1 = (f32[144,768]{1,0:T(8,128)S(1)}, f32[144,768]{1,0:T(8,128)S(1)}, f32[8,128]{1,0:T(8,128)S(1)}) custom-call(f32[144,768]{1,0:T(8,128)S(1)} %get-tuple-element.59.spread, f32[8,128]{1,0:T(8,128)S(1)} %get-tuple-element.60.early, f32[128,768]{1,0:T(8,128)S(1)} %get-tuple-element.58.image, f32[8,128,768]{2,1,0:T(8,128)S(1)} %get-tuple-element.61.statics, ...), custom_call_target="tpu_custom_call" | custom-call | tf_op jit(solution)/shard_map/second_kernel/pallas_call | solution.py:107
  25.2 0.2 collective-permute-start.8
  25.4 1.0 %collective-permute-done.8 = f32[8,128]{1,0:T(8,128)S(1)} collective-permute-done((f32[8,128]{1,0:T(8,128)S(1)}, f32[8,128]{1,0:T(8,128)S(1)}, u32[]{:S(2)}, u32[]{:S(2)}) %collective-permute-start.8) | collective-permute-done | bytes 4128 | tf_op jit(solution)/shard_map/ppermute | solution.py:488
  26.4 1.3 %collective-permute-start.9 = (f32[8,128]{1,0:T(8,128)S(1)}, f32[8,128]{1,0:T(8,128)S(1)}, u32[]{:S(2)}, u32[]{:S(2)}) collective-permute-start(f32[8,128]{1,0:T(8,128)S(1)} %add.12), channel_id=1, source_target_pairs={{0,12},{4,8},{8,4},{12,0},{1,13},{5,9},{9,5},{13,1},{2,14},{6,10},... | collective-permute-start | bytes 12296 | tf_op jit(solution)/shard_map/ppermute | solution.py:490
  27.7 1.8 %collective-permute-done.9 = f32[8,128]{1,0:T(8,128)S(1)} collective-permute-done((f32[8,128]{1,0:T(8,128)S(1)}, f32[8,128]{1,0:T(8,128)S(1)}, u32[]{:S(2)}, u32[]{:S(2)}) %collective-permute-start.9) | collective-permute-done | bytes 4128 | tf_op jit(solution)/shard_map/ppermute | solution.py:490
  29.4 1.0 %collective-permute-start.10 = (f32[8,128]{1,0:T(8,128)S(1)}, f32[8,128]{1,0:T(8,128)S(1)}, u32[]{:S(2)}, u32[]{:S(2)}) collective-permute-start(f32[8,128]{1,0:T(8,128)S(1)} %add.13), channel_id=1, source_target_pairs={{0,5},{1,4},{2,7},{3,6},{4,1},{5,0},{6,3},{7,2},{8,13},{9,12},{10,... | collective-permute-start | bytes 12296 | tf_op jit(solution)/shard_map/ppermute | solution.py:493
  30.4 2.1 %collective-permute-done.10 = f32[8,128]{1,0:T(8,128)S(1)} collective-permute-done((f32[8,128]{1,0:T(8,128)S(1)}, f32[8,128]{1,0:T(8,128)S(1)}, u32[]{:S(2)}, u32[]{:S(2)}) %collective-permute-start.10) | collective-permute-done | bytes 4128 | tf_op jit(solution)/shard_map/ppermute | solution.py:493
  32.5 0.8 %collective-permute-start.11 = (f32[8,128]{1,0:T(8,128)S(1)}, f32[8,128]{1,0:T(8,128)S(1)}, u32[]{:S(2)}, u32[]{:S(2)}) collective-permute-start(f32[8,128]{1,0:T(8,128)S(1)} %add.14), channel_id=1, source_target_pairs={{0,6},{1,7},{2,4},{3,5},{4,2},{5,3},{6,0},{7,1},{8,14},{9,15},{10,... | collective-permute-start | bytes 12296 | tf_op jit(solution)/shard_map/ppermute | solution.py:493
  33.3 1.6 %turn_kernel.1 = (f32[512,128]{1,0:T(8,128)S(1)}, f32[512,128]{1,0:T(8,128)S(1)}, f32[512,128]{1,0:T(8,128)S(1)}, f32[512,128]{1,0:T(8,128)S(1)}, f32[128,768]{1,0:T(8,128)}) custom-call(f32[144,768]{1,0:T(8,128)S(1)} %get-tuple-element.57.precond, f32[128,768]{1,0:T(8,128)S(1)} %get-tuple-element.58.image, f32[144,768]{1,0:T(8,128)S(1)} %get-tuple-element.66.again, ...), custom_call_target="tpu_custom_call" | custom-call | tf_op jit(solution)/shard_map/turn_kernel/pallas_call | solution.py:107
  34.9 1.5 %collective-permute-done.11 = f32[8,128]{1,0:T(8,128)S(1)} collective-permute-done((f32[8,128]{1,0:T(8,128)S(1)}, f32[8,128]{1,0:T(8,128)S(1)}, u32[]{:S(2)}, u32[]{:S(2)}) %collective-permute-start.11) | collective-permute-done | bytes 4128 | tf_op jit(solution)/shard_map/ppermute | solution.py:493
  36.4 1.0 %combine_kernel.1 = (f32[512,128]{1,0:T(8,128)}, f32[512,128]{1,0:T(8,128)}) custom-call(f32[8,128]{1,0:T(8,128)S(1)} %add.15.sums, f32[512,128]{1,0:T(8,128)S(1)} %get-tuple-element.39.noise, f32[512,128]{1,0:T(8,128)S(1)} %get-tuple-element.68.precond, f32[512,128]{1,0:T(8,128)S(1)} %get-tuple-element.69.image, f32[512,128]{1,0:T(8,128)S(1)} %get-tuple-element.70.again, ...), custom_call_target="tpu_custom_call" | custom-call | tf_op jit(solution)/shard_map/combine_kernel/pallas_call | solution.py:579
  (7 shorter events, 0.1 us)
Async XLA Ops:
  2.3 12.4 %collective-permute-start = (f32[21,32,128]{2,1,0:T(8,128)S(1)}, f32[21,32,128]{2,1,0:T(8,128)S(1)}, u32[]{:S(2)}, u32[]{:S(2)}) collective-permute-start(f32[21,32,128]{2,1,0:T(8,128)S(1)} %get-tuple-element.47), channel_id=1, source_target_pairs={{0,4},{1,2},{2,1},{3,7},{4,0},{5,6},{6,5},{7,3},{8,12},{9,10},{10,... | collective-permute-start | bytes 1032200 | tf_op jit(solution)/shard_map/ppermute | solution.py:523
  2.9 11.9 %collective-permute-start.1 = (f32[21,32,128]{2,1,0:T(8,128)S(1)}, f32[21,32,128]{2,1,0:T(8,128)S(1)}, u32[]{:S(2)}, u32[]{:S(2)}) collective-permute-start(f32[21,32,128]{2,1,0:T(8,128)S(1)} %get-tuple-element.48), channel_id=1, source_target_pairs={{0,1},{1,0},{2,3},{3,2},{4,5},{5,4},{6,7},{7,6},{8,9},{9,8},{10,11... | collective-permute-start | bytes 1032200 | tf_op jit(solution)/shard_map/ppermute | solution.py:523
  7.9 1.3 %collective-permute-start.2 = (f32[16,512]{1,0:T(8,128)S(1)}, f32[16,512]{1,0:T(8,128)S(1)}, u32[]{:S(2)}, u32[]{:S(2)}) collective-permute-start(f32[16,512]{1,0:T(8,128)S(1)} %get-tuple-element.53), channel_id=1, source_target_pairs={{0,4},{4,0},{8,12},{12,8},{1,5},{5,1},{9,13},{13,9},{2,6},{6,2},{1... | collective-permute-start | bytes 98312 | tf_op jit(solution)/shard_map/ppermute | solution.py:535
  9.2 3.4 %collective-permute-start.3 = (f32[16,512]{1,0:T(8,128)S(1)}, f32[16,512]{1,0:T(8,128)S(1)}, u32[]{:S(2)}, u32[]{:S(2)}) collective-permute-start(f32[16,512]{1,0:T(8,128)S(1)} %chip_kernel.2), channel_id=1, source_target_pairs={{0,12},{4,8},{8,4},{12,0},{1,13},{5,9},{9,5},{13,1},{2,14},{6,10},... | collective-permute-start | bytes 98312 | tf_op jit(solution)/shard_map/ppermute | solution.py:537
  12.7 2.6 %collective-permute-start.4 = (f32[32,128]{1,0:T(8,128)S(1)}, f32[32,128]{1,0:T(8,128)S(1)}, u32[]{:S(2)}, u32[]{:S(2)}) collective-permute-start(f32[32,128]{1,0:T(8,128)S(1)} %get-tuple-element.55), channel_id=1, source_target_pairs={{0,4},{1,2},{2,1},{3,7},{4,0},{5,6},{6,5},{7,3},{8,12},{9,10},{10,... | collective-permute-start | bytes 49160 | tf_op jit(solution)/shard_map/ppermute | solution.py:523
  13.1 3.7 %collective-permute-start.5 = (f32[32,128]{1,0:T(8,128)S(1)}, f32[32,128]{1,0:T(8,128)S(1)}, u32[]{:S(2)}, u32[]{:S(2)}) collective-permute-start(f32[32,128]{1,0:T(8,128)S(1)} %get-tuple-element.56), channel_id=1, source_target_pairs={{0,1},{1,0},{2,3},{3,2},{4,5},{5,4},{6,7},{7,6},{8,9},{9,8},{10,11... | collective-permute-start | bytes 49160 | tf_op jit(solution)/shard_map/ppermute | solution.py:523
  19.6 1.2 %collective-permute-start.6 = (f32[8,768]{1,0:T(8,128)S(1)}, f32[8,768]{1,0:T(8,128)S(1)}, u32[]{:S(2)}, u32[]{:S(2)}) collective-permute-start(f32[8,768]{1,0:T(8,128)S(1)} %get-tuple-element.63), channel_id=1, source_target_pairs={{0,4},{4,0},{8,12},{12,8},{1,5},{5,1},{9,13},{13,9},{2,6},{6,2},{1... | collective-permute-start | bytes 73736 | tf_op jit(solution)/shard_map/ppermute | solution.py:535
  20.8 3.3 %collective-permute-start.7 = (f32[8,768]{1,0:T(8,128)S(1)}, f32[8,768]{1,0:T(8,128)S(1)}, u32[]{:S(2)}, u32[]{:S(2)}) collective-permute-start(f32[8,768]{1,0:T(8,128)S(1)} %chip_kernel.3), channel_id=1, source_target_pairs={{0,12},{4,8},{8,4},{12,0},{1,13},{5,9},{9,5},{13,1},{2,14},{6,10},... | collective-permute-start | bytes 73736 | tf_op jit(solution)/shard_map/ppermute | solution.py:537
  25.2 1.2 %collective-permute-start.8 = (f32[8,128]{1,0:T(8,128)S(1)}, f32[8,128]{1,0:T(8,128)S(1)}, u32[]{:S(2)}, u32[]{:S(2)}) collective-permute-start(f32[8,128]{1,0:T(8,128)S(1)} %get-tuple-element.65), channel_id=1, source_target_pairs={{0,4},{4,0},{8,12},{12,8},{1,5},{5,1},{9,13},{13,9},{2,6},{6,2},{1... | collective-permute-start | bytes 12296 | tf_op jit(solution)/shard_map/ppermute | solution.py:488
  26.4 3.0 %collective-permute-start.9 = (f32[8,128]{1,0:T(8,128)S(1)}, f32[8,128]{1,0:T(8,128)S(1)}, u32[]{:S(2)}, u32[]{:S(2)}) collective-permute-start(f32[8,128]{1,0:T(8,128)S(1)} %add.12), channel_id=1, source_target_pairs={{0,12},{4,8},{8,4},{12,0},{1,13},{5,9},{9,5},{13,1},{2,14},{6,10},... | collective-permute-start | bytes 12296 | tf_op jit(solution)/shard_map/ppermute | solution.py:490
  29.4 3.0 %collective-permute-start.10 = (f32[8,128]{1,0:T(8,128)S(1)}, f32[8,128]{1,0:T(8,128)S(1)}, u32[]{:S(2)}, u32[]{:S(2)}) collective-permute-start(f32[8,128]{1,0:T(8,128)S(1)} %add.13), channel_id=1, source_target_pairs={{0,5},{1,4},{2,7},{3,6},{4,1},{5,0},{6,3},{7,2},{8,13},{9,12},{10,... | collective-permute-start | bytes 12296 | tf_op jit(solution)/shard_map/ppermute | solution.py:493
  32.5 3.9 %collective-permute-start.11 = (f32[8,128]{1,0:T(8,128)S(1)}, f32[8,128]{1,0:T(8,128)S(1)}, u32[]{:S(2)}, u32[]{:S(2)}) collective-permute-start(f32[8,128]{1,0:T(8,128)S(1)} %add.14), channel_id=1, source_target_pairs={{0,6},{1,7},{2,4},{3,5},{4,2},{5,3},{6,0},{7,1},{8,14},{9,15},{10,... | collective-permute-start | bytes 12296 | tf_op jit(solution)/shard_map/ppermute | solution.py:493

commit v8 on v7

--- a/solution.py
+++ b/solution.py
@@ -14,6 +14,7 @@
 
 SCALE = 2.0**-31
 REACH = 4
+TILE = 8
 EDGE = 8
 
 HIGHEST = lax.Precision.HIGHEST
@@ -75,8 +76,12 @@
     even = [block(1, 1, "east"), block(-2, 2, "west")] + [block(-2 - d, 4, "") for d in fours]
     odd = [block(-1, 1, "west"), block(1, 2, "east")] + [block(-1 - d, 4, "") for d in fours]
     far = np.stack([np.concatenate(even, axis=1), np.concatenate(odd, axis=1)])
+    far = np.pad(far, ((0, 0), (0, 0), (0, -far.shape[2] % 16))).astype(np.float32)
+    high, middle, low = thirds(far, lambda x: x.astype(np.float32))
+    far = np.concatenate([high, high, middle, high, middle, low], axis=2)
+    columns_of = np.broadcast_to(moments[:4, :, None], (4, columns, 128))
     as_f32 = lambda m: np.asarray(m, np.float32)
-    return as_f32(near), as_f32(far), as_f32(moments)
+    return as_f32(near), far, as_f32(moments), as_f32(columns_of)
 
 
 def lon_perms(count):
@@ -96,6 +101,24 @@
 
 def inner_band():
     return (lax.axis_index("lat") > 0) & (lax.axis_index("lat") < lax.axis_size("lat") - 1)
+
+
+def lane_roll(x, by):
+    count = x.shape[1] // 128
+    skip, by = divmod(by % x.shape[1], 128)
+    parts = [x[:, k * 128 : (k + 1) * 128] for k in range(count)]
+    if by:
+        turned = [pltpu.roll(p, by, 1) for p in parts]
+        lane = lax.broadcasted_iota(jnp.int32, (1, 128), 1)
+        parts = [jnp.where(lane < by, turned[k - 1], turned[k]) for k in range(count)]
+    return jnp.concatenate([parts[(k - skip) % count] for k in range(count)], axis=1)
+
+
+def thirds(x, cast):
+    high = x.astype(jnp.bfloat16)
+    rest = x - cast(high)
+    middle = rest.astype(jnp.bfloat16)
+    return high, middle, (rest - cast(middle)).astype(jnp.bfloat16)
 
 
 def whole(n):
@@ -120,7 +143,7 @@
 
 
 def band_kernel(rows, levels, *refs):
-    sources, (second, first), copies, sems = refs[:7], refs[7:9], refs[9:16], refs[16]
+    sources, (second, first), copies, sems = refs[:8], refs[8:10], refs[10:18], refs[18]
     moves = [pltpu.make_async_copy(x, y, sems.at[k]) for k, (x, y) in enumerate(zip(sources, copies))]
     for move in moves:
         move.start()
@@ -157,17 +180,11 @@
     lane = lax.broadcasted_iota(jnp.int32, (1, lanes), 1)
     row = lax.broadcasted_iota(jnp.int32, (columns, 1), 0)
     upper = jnp.where(lane % levels == levels - 1, 0.0, upper)
-    south = jnp.where(lane % band < levels, 0.0, pltpu.roll(north, levels, 1))
+    south = jnp.where(lane % band < levels, 0.0, lane_roll(north, levels))
     west = jnp.where(row == 0, 0.0, pltpu.roll(east, 1, 0))
     ocean_east = jnp.where(row == columns - 1, 1.0, pltpu.roll(ocean, columns - 1, 0))
-    diagonal = ocean * (kappa + east + west + north + south + upper + pltpu.roll(upper, 1, 1))
-    return diagonal, east * ocean * ocean_east, upper * ocean * pltpu.roll(ocean, lanes - 1, 1)
-
-
-def store(statics, edge, diagonal, to_east, north, to_upper, ocean, east):
-    for k, x in enumerate((diagonal, to_east, north, to_upper, ocean)):
-        statics[k] = x
-    edge[0:1] = east[east.shape[0] - 1 :]
+    diagonal = ocean * (kappa + east + west + north + south + upper + lane_roll(upper, 1))
+    return diagonal, east * ocean * ocean_east, upper * ocean * lane_roll(ocean, -1)
 
 
 def own_kernel(
@@ -192,7 +209,9 @@
     lane = lax.broadcasted_iota(jnp.int32, (1, lanes), 1)
     north = jnp.where(last_band & (lane >= lanes - levels), 0.0, north)
     diagonal, to_east, to_upper = coefficients(levels, lanes, kappa, east, north, upper, ocean)
-    store(statics, edge, diagonal, to_east, north, to_upper, ocean, east)
+    for k, x in enumerate((diagonal, to_east, north, to_upper, ocean)):
+        statics[k] = x
+    edge[0:1] = east[columns - 1 :]
     m = dot(weights[...], r)[:4]
     end = columns - 1
     blank = jnp.zeros((5, lanes), jnp.float32)
@@ -204,7 +223,7 @@
     to_second[...] = jnp.where(lon_odd == 0, for_west, for_east)
 
 
-def ghost_kernel(levels, columns, got_second, got_first, near, spread, statics, edge):
+def ghost_kernel(levels, columns, got_second, got_first, near, own, spread, statics, edge):
     lat_odd = lax.axis_index("lat") % 2
     group = REACH * levels
 
@@ -225,7 +244,19 @@
     )
     spread[...] = dot(near[...], r)
     diagonal, to_east, to_upper = coefficients(levels, group, kappa, east, north, upper, ocean)
-    store(statics, edge, diagonal, to_east, north, to_upper, ocean, east)
+    edge[0:1] = east[columns - 1 :]
+    for at in range(0, columns, TILE):
+        tile = slice(at, at + TILE)
+        d, e, n, u, o = (
+            joined(own[k, pl.ds(at, TILE)], x[tile]) for k, x in enumerate((diagonal, to_east, north, to_upper, ocean))
+        )
+        d, n = completed(levels, group, d, n, o)
+        row = lax.broadcasted_iota(jnp.int32, (TILE, 1), 0)
+        w = pltpu.roll(e, 1, 0)
+        w = jnp.where(row == 0, carried, w) if at else w
+        carried = e[TILE - 1 :]
+        for k, x in enumerate((d, e, w, n, lane_roll(n, levels), u, lane_roll(u, 1), o)):
+            statics[k, pl.ds(at, TILE)] = x
 
 
 def forward_kernel(group, *refs):
@@ -272,24 +303,25 @@
 
 
 def told(far, lists):
-    return dot(far[lax.axis_index("lon") % 2], jnp.concatenate([t[0:8] for t in lists], axis=0))
-
-
-TILE = 8
+    x = jnp.concatenate([t[0:8] for t in lists], axis=0)
+    if x.shape[0] % 16:
+        x = jnp.concatenate([x, jnp.zeros((8, x.shape[1]), jnp.float32)], axis=0)
+    high, middle, low = thirds(x, lambda p: p.astype(jnp.float32))
+    stacked = jnp.concatenate([high, middle, high, low, middle, high], axis=0)
+    return jnp.dot(far[lax.axis_index("lon") % 2], stacked, preferred_element_type=jnp.float32)
 
 
 def faces(v, n, s, u, low, levels):
-    lanes = v.shape[1]
-    return (
-        n * pltpu.roll(v, lanes - levels, 1)
-        + s * pltpu.roll(v, levels, 1)
-        + u * pltpu.roll(v, lanes - 1, 1)
-        + low * pltpu.roll(v, 1, 1)
-    )
-
-
-def apply_tile(levels, v, statics, at):
-    d, e, w, n, s, u, low = (statics[k, pl.ds(at, TILE)] for k in range(7))
+    return n * lane_roll(v, -levels) + s * lane_roll(v, levels) + u * lane_roll(v, -1) + low * lane_roll(v, 1)
+
+
+def apply_tile(levels, v, statics, ends, at):
+    source, k = statics, at
+    if at == 0:
+        source, k = ends, 0
+    if at + TILE == statics.shape[1]:
+        source, k = ends, TILE
+    d, e, w, n, s, u, low = (source[i, pl.ds(k, TILE)] for i in range(7))
     i = at + EDGE
     here = v[pl.ds(i, TILE)]
     out = d * here - e * v[pl.ds(i + 1, TILE)] - w * v[pl.ds(i - 1, TILE)]
@@ -306,20 +338,29 @@
     f[end : end + 1] = g[1:2]
 
 
+def joined(own, ghost):
+    group = ghost.shape[1] // 2
+    return jnp.concatenate([ghost[:, :group], own, ghost[:, group:]], axis=1)
+
+
+def completed(levels, group, diagonal, north, ocean):
+    lanes = ocean.shape[1]
+    lane = lax.broadcasted_iota(jnp.int32, (1, lanes), 1)
+    first_of_band = ((lane >= group) & (lane < group + levels)) | ((lane >= lanes - group) & (lane < lanes - group + levels))
+    diagonal = diagonal + jnp.where(first_of_band, ocean * lane_roll(north, levels), 0.0)
+    return diagonal, north * ocean * lane_roll(ocean, -levels)
+
+
 def first_kernel(
     rows, levels, columns, others,
-    own_spread, own_statics, own_edge, ghost_spread, ghost_statics, edge, far, weights, side_second, side_first, *rest,
+    own_spread, own_edge, ghost_spread, statics, edge, far, weights, side_second, side_first, *rest,
 ):
     received = rest[: 1 + others]
-    v, image, statics, rim, to_first, to_second, f, scaled = rest[1 + others :]
+    v, image, ends, rim, to_first, to_second, f = rest[1 + others :]
     lat_odd = lax.axis_index("lat") % 2
     even = lax.axis_index("lon") % 2 == 0
     group = REACH * levels
     lanes = rows * levels + 2 * group
-
-    def joined(own, ghost):
-        return jnp.concatenate([ghost[:, :group], own, ghost[:, group:]], axis=1)
-
     lists, k = [], 0
     for x in received:
         count = x.shape[0]
@@ -329,41 +370,24 @@
         k += count
     v[...] = joined(own_spread[...], ghost_spread[...]) + told(far, lists)
 
-    lane = lax.broadcasted_iota(jnp.int32, (1, lanes), 1)
-    first_of_band = ((lane >= group) & (lane < group + levels)) | ((lane >= lanes - group) & (lane < lanes - group + levels))
-
-    def completed(diagonal, north, ocean):
-        diagonal = diagonal + jnp.where(first_of_band, ocean * pltpu.roll(north, levels, 1), 0.0)
-        return diagonal, north * ocean * pltpu.roll(ocean, lanes - levels, 1)
-
-    one, two = lists[0][0:16], lists[1][0:16]
+    one, two = lists[0], lists[1]
     east_list, west_list = jnp.where(even, one, two), jnp.where(even, two, one)
     end = columns - 1
-    for at in range(0, columns, TILE):
-        tile = pl.ds(at, TILE)
-        d, e, n, u, ocean = (joined(own_statics[k, tile], ghost_statics[k, tile]) for k in range(5))
-        row = at + lax.broadcasted_iota(jnp.int32, (TILE, 1), 0)
-        d, n = completed(d, n, ocean)
-        if at == 0:
-            face_west = west_list[7:8] * west_list[8:9] * ocean[0:1]
-            d = d + jnp.where(row == 0, ocean * west_list[7:8], 0.0)
-            carried = face_west
-        if at + TILE == columns:
-            e = jnp.where(row == end, e * east_list[8:9], e)
-            last_east = e[TILE - 1 :]
-        statics[0, tile] = d
-        statics[1, tile] = e
-        statics[2, tile] = jnp.where(row == at, carried, pltpu.roll(e, 1, 0))
-        statics[3, tile] = n
-        statics[4, tile] = pltpu.roll(n, levels, 1)
-        statics[5, tile] = u
-        statics[6, tile] = pltpu.roll(u, 1, 1)
-        statics[7, tile] = ocean
-        carried = e[TILE - 1 :]
+    low_tile, high_tile = pl.ds(0, TILE), pl.ds(columns - TILE, TILE)
+    for k in range(7):
+        ends[k, 0:TILE] = statics[k, low_tile]
+        ends[k, TILE : 2 * TILE] = statics[k, high_tile]
+    ocean = statics[7, 0:1]
+    face_west = west_list[7:8] * west_list[8:9] * ocean
+    last_east = statics[1, end:] * east_list[8:9]
+    ends[0, 0:1] = statics[0, 0:1] + ocean * west_list[7:8]
+    ends[2, 0:1] = face_west
+    ends[1, 2 * TILE - 1 : 2 * TILE] = last_east
     blank = jnp.zeros((6, lanes), jnp.float32)
     stack = lambda p, q: jnp.concatenate([p, q, blank], axis=0)
     last_face = joined(own_edge[0:1], edge[0:1])
     rim_diagonal, rim_north = completed(
+        levels, group,
         stack(west_list[5:6], east_list[5:6] + east_list[8:9] * last_face),
         stack(west_list[9:10], east_list[9:10]),
         stack(west_list[8:9], east_list[8:9]),
@@ -373,22 +397,26 @@
     rim[1] = stack(face_west, east_list[6:7])
     rim[2] = stack(west_list[6:7], last_east)
     rim[3] = rim_north
-    rim[4] = pltpu.roll(rim_north, levels, 1)
+    rim[4] = lane_roll(rim_north, levels)
     rim[5] = rim_upper
-    rim[6] = pltpu.roll(rim_upper, 1, 1)
+    rim[6] = lane_roll(rim_upper, 1)
 
     for at in range(0, columns, TILE):
-        f[pl.ds(EDGE + at, TILE)] = apply_tile(levels, v, statics, at)[1]
+        f[pl.ds(EDGE + at, TILE)] = apply_tile(levels, v, statics, ends, at)[1]
     apply_rim(levels, columns, v, f, rim)
+    m = [0.0] * 4
     for at in range(0, columns, TILE):
-        second = apply_tile(levels, f, statics, at)[1]
-        w = jnp.where(statics[7, pl.ds(at, TILE)] > 0.5, second, v[pl.ds(EDGE + at, TILE)])
-        image[pl.ds(at, TILE)] = w
-        scaled[pl.ds(at, TILE)] = w * SCALE
-    m = dot(weights[...], scaled[...])[:4]
+        tile = pl.ds(at, TILE)
+        second = apply_tile(levels, f, statics, ends, at)[1]
+        w = jnp.where(statics[7, tile] > 0.5, second, v[pl.ds(EDGE + at, TILE)])
+        image[tile] = w
+        for k in range(4):
+            spread = weights[k, tile]
+            m[k] = m[k] + w * jnp.concatenate([spread] * (lanes // 128), axis=1)
+    m = [jnp.sum(x, axis=0, keepdims=True) * SCALE for x in m]
     pad = jnp.zeros((3, lanes), jnp.float32)
-    for_east = jnp.concatenate([m, scaled[end:], pad], axis=0)
-    for_west = jnp.concatenate([m, scaled[:1], pad], axis=0)
+    for_east = jnp.concatenate(m + [image[end:] * SCALE, pad], axis=0)
+    for_west = jnp.concatenate(m + [image[:1] * SCALE, pad], axis=0)
     to_first[...] = jnp.where(even, for_east, for_west)
     to_second[...] = jnp.where(even, for_west, for_east)
 
@@ -415,7 +443,7 @@
     sums[...] = jnp.concatenate([lane_sums(energy), lane_sums(curve), jnp.zeros((6, 128), jnp.float32)], axis=0)
 
 
-def second_kernel(levels, columns, rows, others, spread, early, image, statics, far, rim, *rest):
+def second_kernel(levels, columns, rows, others, spread, early, image, statics, ends, far, rim, *rest):
     received = rest[: 1 + others]
     v, f, sums = rest[1 + others :]
     v[...] = spread[...] + told(far, received)
@@ -423,7 +451,7 @@
     mixed, last = [], []
     for at in range(0, columns, TILE):
         tile = pl.ds(at, TILE)
-        q, b = apply_tile(levels, v, statics, at)
+        q, b = apply_tile(levels, v, statics, ends, at)
         f[pl.ds(EDGE + at, TILE)] = b
         q, b, ocean = q[:, own], b[:, own], statics[7, tile, own]
         mixed.append(image[tile, own] * q)
@@ -433,11 +461,11 @@
     sums[...] = jnp.concatenate([early[0:2], lane_sums(mixed), lane_sums(last), early[4:8]], axis=0)
 
 
-def turn_kernel(rows, levels, columns, precond, image, again, f, statics, *outs):
+def turn_kernel(rows, levels, columns, precond, image, again, f, statics, ends, *outs):
     z = outs[4]
     own = own_lanes(rows, levels)
     for at in range(0, columns, TILE):
-        second = apply_tile(levels, f, statics, at)[1]
+        second = apply_tile(levels, f, statics, ends, at)[1]
         tile = pl.ds(at, TILE)
         z[tile] = jnp.where(statics[7, tile] > 0.5, second, again[pl.ds(EDGE + at, TILE)])
     group = REACH * levels
@@ -494,7 +522,7 @@
     return x
 
 
-def body(near, far, weights, noise, kappa2, conduct, land):
+def body(near, far, weights, columns_of, noise, kappa2, conduct, land):
     levels, rows, columns = noise.shape
     count = lax.axis_size("lon")
     others = count // 4
@@ -508,9 +536,9 @@
     land = land.reshape(flat, columns)
     conduct = conduct.reshape(3, flat, columns)
 
-    sources = (noise, kappa2, conduct, land, near, far, weights)
+    sources = (noise, kappa2, conduct, land, near, far, weights, columns_of)
     planes = (PLANES, levels, columns)
-    second, first, noise, kappa2, conduct, land, near, far, weights = pl.pallas_call(
+    second, first, noise, kappa2, conduct, land, near, far, weights, columns_of = pl.pallas_call(
         functools.partial(band_kernel, rows, levels),
         out_shape=[pltpu.VMEM(planes, jnp.float32)] * 2 + [pltpu.VMEM(x.shape, x.dtype) for x in sources],
         in_specs=[pl.BlockSpec(memory_space=pltpu.HBM)] * len(sources),
@@ -547,16 +575,16 @@
     heights = sum(x.shape[0] for x in lists)
     side_second, side_first = call(functools.partial(forward_kernel, group), [(heights, group)] * 2, *lists)
     side_second, side_first = to_band(side_second, lat_b), to_band(side_first, lat_a)
-    ghost_spread, ghost_statics, edge = call(
+    ghost_spread, statics, edge = call(
         functools.partial(ghost_kernel, levels, columns),
-        [(tall, 2 * group), (5, columns, 2 * group), (8, 2 * group)],
-        got_second, got_first, near,
-    )
-    precond, image, statics, rim, to_first, to_second = call(
+        [(tall, 2 * group), (8, columns, lanes), (8, 2 * group)],
+        got_second, got_first, near, own_statics,
+    )
+    precond, image, ends, rim, to_first, to_second = call(
         functools.partial(first_kernel, rows, levels, columns, others),
-        [(tall, lanes), (columns, lanes), (8, columns, lanes), (7, 8, lanes), (8, lanes), (8, lanes)],
-        own_spread, own_statics, own_edge, ghost_spread, ghost_statics, edge, far, weights, side_second, side_first, *lists,
-        scratch=[(tall, lanes), (columns, lanes)],
+        [(tall, lanes), (columns, lanes), (7, 2 * TILE, lanes), (7, 8, lanes), (8, lanes), (8, lanes)],
+        own_spread, own_edge, ghost_spread, statics, edge, far, columns_of, side_second, side_first, *lists,
+        scratch=[(tall, lanes)],
     )
     lists = exchange(to_first, to_second)
     spread, sums = call(
@@ -567,13 +595,13 @@
     again, half, sums = call(
         functools.partial(second_kernel, levels, columns, rows, others),
         [(tall, lanes), (tall, lanes), (8, 128)],
-        spread, sums, image, statics, far, rim, *lists,
+        spread, sums, image, statics, ends, far, rim, *lists,
     )
     sums = summed(sums)
     turned_back = call(
         functools.partial(turn_kernel, rows, levels, columns),
         [(flat, columns)] * 4 + [(columns, lanes)],
-        precond, image, again, half, statics,
+        precond, image, again, half, statics, ends,
     )[:4]
     operands = [pltpu.with_memory_space_constraint(x, pltpu.VMEM) for x in (sums, noise, *turned_back)]
     answer, left = pl.pallas_call(

time: 37.6 us -> 35.9 us (0.955)
  waiting for transfers between devices: 14 us -> 12 us
  starting transfers between devices: 12.3 us -> 13.2 us
  Pallas kernels: 10.3 us -> 9.9 us
    ppermute x4, waiting for transfers between devices: 1.69 us -> 0.49 us  [body(): to_band = lambda x, pairs: lax.ppermute(x, ('lon', 'lat'), pairs)]
    ppermute x2, waiting for transfers between devices: 3.59 us -> 2.74 us  [summed(): x = x + lax.ppermute(x, ('lon', 'lat'), pairs)]
    ppermute x2, starting transfers between devices: 1.74 us -> 2.56 us  [summed(): x = x + lax.ppermute(x, ('lon', 'lat'), pairs)]
    pallas_call x10, Pallas kernels: 7.66 us -> 7.13 us  [call(): pl.pallas_call(kernel, out_shape=[pltpu.VMEM(s, jnp.float32) for s in out...]
  transfers between devices with their start and end apart: 12 -> 12, of which waited for: 10 -> 10; matrix products, arithmetic and copies ran while one was open for 0% -> 0% of each run, Pallas kernels for 10% -> 14%
where the time goes in v8:
time: 35.9 us; the launch traced here: 35.8 us
  starting transfers between devices  13.2 us (37%)
  waiting for transfers between devices  12 us (33%)
  Pallas kernels  9.9 us (28%)
  between operations  0.73 us (2%)
    pallas_call x10, Pallas kernels, call(): pl.pallas_call(kernel, out_shape=[pltpu.VMEM(s, jnp.float32) for s in out...  7.13 us
    ppermute x4, starting transfers between devices, body(): to_band = lambda x, pairs: lax.ppermute(x, ('lon', 'lat'), pairs)  6.35 us
    ppermute x2, waiting for transfers between devices, exchange(): got_two = lax.ppermute(two, 'lon', lon_b)  3.58 us
    ppermute x2, waiting for transfers between devices, summed(): x = x + lax.ppermute(x, ('lon', 'lat'), pairs)  2.74 us
    ppermute x2, starting transfers between devices, exchange(): got_two = lax.ppermute(two, 'lon', lon_b)  2.64 us
    ppermute x2, starting transfers between devices, summed(): x = x + lax.ppermute(x, ('lon', 'lat'), pairs)  2.56 us
    ppermute x2, waiting for transfers between devices, exchange(): got_one = lax.ppermute(one, 'lon', lon_a)  2.38 us
    pallas_call x1, Pallas kernels, body(): pl.pallas_call(functools.partial(band_kernel, rows, levels), out_shape=[p...  1.78 us
  transfers between devices with their start and end apart: 12, of which 10 were waited for; matrix products, arithmetic and copies ran while one was open for 0% of the time, Pallas kernels for 14%

profile of v8, /device:TPU:0, one launch (start us, length us, event | category | flops | bytes accessed | tf_op | source)
XLA Modules:
  0.0 35.8 jit_solution(7260765688859142923)
XLA Ops:
  0.6 1.8 %band_kernel.1 = (f32[21,32,128]{2,1,0:T(8,128)S(1)}, f32[21,32,128]{2,1,0:T(8,128)S(1)}, f32[512,128]{1,0:T(8,128)S(1)}, f32[512,128]{1,0:T(8,128)S(1)}, f32[3,...) custom-call(f32[512,128]{1,0:T(8,128)} %bitcast.7, ...), custom_call_target="tpu_custom_call" | custom-call | tf_op jit(solution)/shard_map/band_kernel/pallas_call | solution.py:541
  2.4 0.6 %collective-permute-start = (f32[21,32,128]{2,1,0:T(8,128)S(1)}, f32[21,32,128]{2,1,0:T(8,128)S(1)}, u32[]{:S(2)}, u32[]{:S(2)}) collective-permute-start(f32[21,32,128]{2,1,0:T(8,128)S(1)} %get-tuple-element.47), channel_id=1, source_target_pairs={{0,4},{1,2},{2,1},{3,7},{4,0},{5,6},{6,5},{7,3},{8,12},{9,10},{10,... | collective-permute-start | bytes 1032200 | tf_op jit(solution)/shard_map/ppermute | solution.py:551
  3.0 4.1 %collective-permute-start.1 = (f32[21,32,128]{2,1,0:T(8,128)S(1)}, f32[21,32,128]{2,1,0:T(8,128)S(1)}, u32[]{:S(2)}, u32[]{:S(2)}) collective-permute-start(f32[21,32,128]{2,1,0:T(8,128)S(1)} %get-tuple-element.48), channel_id=1, source_target_pairs={{0,1},{1,0},{2,3},{3,2},{4,5},{5,4},{6,7},{7,6},{8,9},{9,8},{10,11... | collective-permute-start | bytes 1032200 | tf_op jit(solution)/shard_map/ppermute | solution.py:551
  7.1 0.9 %own_kernel.1 = (f32[128,512]{1,0:T(8,128)S(1)}, f32[5,128,512]{2,1,0:T(8,128)S(1)}, f32[8,512]{1,0:T(8,128)S(1)}, f32[16,512]{1,0:T(8,128)S(1)}, f32[16,512]{1,0:T(8,128)S(1)}) custom-call(f32[512,128]{1,0:T(8,128)S(1)} %get-tuple-element.40.noise, f32[512,128]{1,0:T(8,128)S(1)} %get-tuple-element.41.kappa2, f32[3,512,128]{2,1,0:T(8,128)S(1)} %get-tuple-element.42.conduct, ...), custom_call_target="tpu_custom_call" | custom-call | tf_op jit(solution)/shard_map/own_kernel/pallas_call | solution.py:130
  8.0 0.1 collective-permute-start.2
  8.1 1.2 %collective-permute-done.2.got.refs_0_.rest_0_ = f32[16,512]{1,0:T(8,128)S(1)} collective-permute-done((f32[16,512]{1,0:T(8,128)S(1)}, f32[16,512]{1,0:T(8,128)S(1)}, u32[]{:S(2)}, u32[]{:S(2)}) %collective-permute-start.2) | collective-permute-done | bytes 32800 | tf_op jit(solution)/shard_map/ppermute | solution.py:563
  9.3 1.3 %collective-permute-start.3 = (f32[16,512]{1,0:T(8,128)S(1)}, f32[16,512]{1,0:T(8,128)S(1)}, u32[]{:S(2)}, u32[]{:S(2)}) collective-permute-start(f32[16,512]{1,0:T(8,128)S(1)} %chip_kernel.2), channel_id=1, source_target_pairs={{0,12},{4,8},{8,4},{12,0},{1,13},{5,9},{9,5},{13,1},{2,14},{6,10},... | collective-permute-start | bytes 98312 | tf_op jit(solution)/shard_map/ppermute | solution.py:565
  10.7 2.1 %collective-permute-done.3.refs_1_.rest_1_ = f32[16,512]{1,0:T(8,128)S(1)} collective-permute-done((f32[16,512]{1,0:T(8,128)S(1)}, f32[16,512]{1,0:T(8,128)S(1)}, u32[]{:S(2)}, u32[]{:S(2)}) %collective-permute-start.3) | collective-permute-done | bytes 32800 | tf_op jit(solution)/shard_map/ppermute | solution.py:565
  12.8 0.5 %collective-permute-start.4 = (f32[32,128]{1,0:T(8,128)S(1)}, f32[32,128]{1,0:T(8,128)S(1)}, u32[]{:S(2)}, u32[]{:S(2)}) collective-permute-start(f32[32,128]{1,0:T(8,128)S(1)} %get-tuple-element.57), channel_id=1, source_target_pairs={{0,4},{1,2},{2,1},{3,7},{4,0},{5,6},{6,5},{7,3},{8,12},{9,10},{10,... | collective-permute-start | bytes 49160 | tf_op jit(solution)/shard_map/ppermute | solution.py:551
  13.2 1.2 %collective-permute-start.5 = (f32[32,128]{1,0:T(8,128)S(1)}, f32[32,128]{1,0:T(8,128)S(1)}, u32[]{:S(2)}, u32[]{:S(2)}) collective-permute-start(f32[32,128]{1,0:T(8,128)S(1)} %get-tuple-element.58), channel_id=1, source_target_pairs={{0,1},{1,0},{2,3},{3,2},{4,5},{5,4},{6,7},{7,6},{8,9},{9,8},{10,11... | collective-permute-start | bytes 49160 | tf_op jit(solution)/shard_map/ppermute | solution.py:551
  14.4 0.4 %near_kernel.1.own_spread = f32[144,512]{1,0:T(8,128)S(1)} custom-call(f32[144,128]{1,0:T(8,128)S(1)} %get-tuple-element.39.near, f32[128,512]{1,0:T(8,128)S(1)} %get-tuple-element.45.field), custom_call_target="tpu_custom_call" | custom-call | tf_op jit(solution)/shard_map/near_kernel/pallas_call | solution.py:130
  14.8 0.0 collective-permute-done.got_second
  14.8 0.1 collective-permute-done.1.got_first
  14.9 1.6 %ghost_kernel.1 = (f32[144,256]{1,0:T(8,128)S(1)}, f32[8,128,768]{2,1,0:T(8,128)S(1)}, f32[8,256]{1,0:T(8,128)S(1)}) custom-call(f32[21,32,128]{2,1,0:T(8,128)S(1)} %collective-permute-done.got_second, f32[21,32,128]{2,1,0:T(8,128)S(1)} %collective-permute-done.1.got_first, f32[144,128]{1,0:T(8,128)S(1)} %get-tuple-element.39.near, ...), custom_call_target="tpu_custom_call" | custom-call | tf_op jit(solution)/shard_map/ghost_kernel/pallas_call | solution.py:130
  16.5 0.0 collective-permute-done.4.side_second
  16.5 0.4 %collective-permute-done.5.side_first = f32[32,128]{1,0:T(8,128)S(1)} collective-permute-done((f32[32,128]{1,0:T(8,128)S(1)}, f32[32,128]{1,0:T(8,128)S(1)}, u32[]{:S(2)}, u32[]{:S(2)}) %collective-permute-start.5) | collective-permute-done | bytes 16416 | tf_op jit(solution)/shard_map/ppermute | solution.py:551
  17.0 1.2 %first_kernel.1 = (f32[144,768]{1,0:T(8,128)S(1)}, f32[128,768]{1,0:T(8,128)S(1)}, f32[7,16,768]{2,1,0:T(8,128)S(1)}, f32[7,8,768]{2,1,0:T(8,128)S(1)}, f32[8,768]{1,0:T(8,128)S(1)}, /*index=5*/f32[8,768]{1,0:T(8,128)S(1)}) custom-call(f32[144,512]{1,0:T(8,128)S(1)} %near_kernel.1.own_spread, f32[8,512]{1,0:T(8,128)S(1)} %get-tuple-element.46.own_edge, ...), custom_call_target="tpu_custom_call" | custom-call | tf_op jit(solution)/shard_map/first_kernel/pallas_call | solution.py:130
  18.2 0.1 collective-permute-start.6
  18.3 1.2 %collective-permute-done.6.got.rest_0_ = f32[8,768]{1,0:T(8,128)S(1)} collective-permute-done((f32[8,768]{1,0:T(8,128)S(1)}, f32[8,768]{1,0:T(8,128)S(1)}, u32[]{:S(2)}, u32[]{:S(2)}) %collective-permute-start.6) | collective-permute-done | bytes 24608 | tf_op jit(solution)/shard_map/ppermute | solution.py:563
  19.5 1.3 %collective-permute-start.7 = (f32[8,768]{1,0:T(8,128)S(1)}, f32[8,768]{1,0:T(8,128)S(1)}, u32[]{:S(2)}, u32[]{:S(2)}) collective-permute-start(f32[8,768]{1,0:T(8,128)S(1)} %chip_kernel.3), channel_id=1, source_target_pairs={{0,12},{4,8},{8,4},{12,0},{1,13},{5,9},{9,5},{13,1},{2,14},{6,10},... | collective-permute-start | bytes 73736 | tf_op jit(solution)/shard_map/ppermute | solution.py:565
  20.8 0.5 %between_kernel.1 = (f32[144,768]{1,0:T(8,128)S(1)}, f32[8,128]{1,0:T(8,128)S(1)}) custom-call(f32[144,128]{1,0:T(8,128)S(1)} %get-tuple-element.39.near, f32[128,512]{1,0:T(8,128)S(1)} %get-tuple-element.45.field, f32[144,768]{1,0:T(8,128)S(1)} %get-tuple-element.59.precond, f32[128,768]{1,0:T(8,128)S(1)} %get-tuple-element.60.image), custom_call_target="tpu_custom_call" | custom-call | tf_op jit(solution)/shard_map/between_kernel/pallas_call | solution.py:130
  21.3 1.5 %collective-permute-done.7.rest_1_ = f32[8,768]{1,0:T(8,128)S(1)} collective-permute-done((f32[8,768]{1,0:T(8,128)S(1)}, f32[8,768]{1,0:T(8,128)S(1)}, u32[]{:S(2)}, u32[]{:S(2)}) %collective-permute-start.7) | collective-permute-done | bytes 24608 | tf_op jit(solution)/shard_map/ppermute | solution.py:565
  22.8 0.7 %second_kernel.1 = (f32[144,768]{1,0:T(8,128)S(1)}, f32[144,768]{1,0:T(8,128)S(1)}, f32[8,128]{1,0:T(8,128)S(1)}) custom-call(f32[144,768]{1,0:T(8,128)S(1)} %get-tuple-element.61.spread, f32[8,128]{1,0:T(8,128)S(1)} %get-tuple-element.62.early, f32[128,768]{1,0:T(8,128)S(1)} %get-tuple-element.60.image, f32[8,128,768]{2,1,0:T(8,128)S(1)} %get-tuple-element.51.statics, ...), custom_call_target="tpu_custom_call" | custom-call | tf_op jit(solution)/shard_map/second_kernel/pallas_call | solution.py:130
  23.6 0.2 collective-permute-start.8
  23.8 1.0 %collective-permute-done.8 = f32[8,128]{1,0:T(8,128)S(1)} collective-permute-done((f32[8,128]{1,0:T(8,128)S(1)}, f32[8,128]{1,0:T(8,128)S(1)}, u32[]{:S(2)}, u32[]{:S(2)}) %collective-permute-start.8) | collective-permute-done | bytes 4128 | tf_op jit(solution)/shard_map/ppermute | solution.py:516
  24.8 1.3 %collective-permute-start.9 = (f32[8,128]{1,0:T(8,128)S(1)}, f32[8,128]{1,0:T(8,128)S(1)}, u32[]{:S(2)}, u32[]{:S(2)}) collective-permute-start(f32[8,128]{1,0:T(8,128)S(1)} %add.12), channel_id=1, source_target_pairs={{0,12},{4,8},{8,4},{12,0},{1,13},{5,9},{9,5},{13,1},{2,14},{6,10},... | collective-permute-start | bytes 12296 | tf_op jit(solution)/shard_map/ppermute | solution.py:518
  26.1 1.8 %collective-permute-done.9 = f32[8,128]{1,0:T(8,128)S(1)} collective-permute-done((f32[8,128]{1,0:T(8,128)S(1)}, f32[8,128]{1,0:T(8,128)S(1)}, u32[]{:S(2)}, u32[]{:S(2)}) %collective-permute-start.9) | collective-permute-done | bytes 4128 | tf_op jit(solution)/shard_map/ppermute | solution.py:518
  27.8 1.1 %collective-permute-start.10 = (f32[8,128]{1,0:T(8,128)S(1)}, f32[8,128]{1,0:T(8,128)S(1)}, u32[]{:S(2)}, u32[]{:S(2)}) collective-permute-start(f32[8,128]{1,0:T(8,128)S(1)} %add.13), channel_id=1, source_target_pairs={{0,5},{1,4},{2,7},{3,6},{4,1},{5,0},{6,3},{7,2},{8,13},{9,12},{10,... | collective-permute-start | bytes 12296 | tf_op jit(solution)/shard_map/ppermute | solution.py:521
  28.9 1.9 %collective-permute-done.10 = f32[8,128]{1,0:T(8,128)S(1)} collective-permute-done((f32[8,128]{1,0:T(8,128)S(1)}, f32[8,128]{1,0:T(8,128)S(1)}, u32[]{:S(2)}, u32[]{:S(2)}) %collective-permute-start.10) | collective-permute-done | bytes 4128 | tf_op jit(solution)/shard_map/ppermute | solution.py:521
  30.9 1.5 %collective-permute-start.11 = (f32[8,128]{1,0:T(8,128)S(1)}, f32[8,128]{1,0:T(8,128)S(1)}, u32[]{:S(2)}, u32[]{:S(2)}) collective-permute-start(f32[8,128]{1,0:T(8,128)S(1)} %add.14), channel_id=1, source_target_pairs={{0,6},{1,7},{2,4},{3,5},{4,2},{5,3},{6,0},{7,1},{8,14},{9,15},{10,... | collective-permute-start | bytes 12296 | tf_op jit(solution)/shard_map/ppermute | solution.py:521
  32.3 1.7 %turn_kernel.1 = (f32[512,128]{1,0:T(8,128)S(1)}, f32[512,128]{1,0:T(8,128)S(1)}, f32[512,128]{1,0:T(8,128)S(1)}, f32[512,128]{1,0:T(8,128)S(1)}, f32[128,768]{1,0:T(8,128)}) custom-call(f32[144,768]{1,0:T(8,128)S(1)} %get-tuple-element.59.precond, f32[128,768]{1,0:T(8,128)S(1)} %get-tuple-element.60.image, f32[144,768]{1,0:T(8,128)S(1)} %get-tuple-element.68.again, ...), custom_call_target="tpu_custom_call" | custom-call | tf_op jit(solution)/shard_map/turn_kernel/pallas_call | solution.py:130
  34.0 0.8 %collective-permute-done.11 = f32[8,128]{1,0:T(8,128)S(1)} collective-permute-done((f32[8,128]{1,0:T(8,128)S(1)}, f32[8,128]{1,0:T(8,128)S(1)}, u32[]{:S(2)}, u32[]{:S(2)}) %collective-permute-start.11) | collective-permute-done | bytes 4128 | tf_op jit(solution)/shard_map/ppermute | solution.py:521
  34.8 1.0 %combine_kernel.1 = (f32[512,128]{1,0:T(8,128)}, f32[512,128]{1,0:T(8,128)}) custom-call(f32[8,128]{1,0:T(8,128)S(1)} %add.15.sums, f32[512,128]{1,0:T(8,128)S(1)} %get-tuple-element.40.noise, f32[512,128]{1,0:T(8,128)S(1)} %get-tuple-element.70.precond, f32[512,128]{1,0:T(8,128)S(1)} %get-tuple-element.71.image, f32[512,128]{1,0:T(8,128)S(1)} %get-tuple-element.72.again, ...), custom_call_target="tpu_custom_call" | custom-call | tf_op jit(solution)/shard_map/combine_kernel/pallas_call | solution.py:607
  (7 shorter events, 0.1 us)
Async XLA Ops:
  2.4 12.4 %collective-permute-start = (f32[21,32,128]{2,1,0:T(8,128)S(1)}, f32[21,32,128]{2,1,0:T(8,128)S(1)}, u32[]{:S(2)}, u32[]{:S(2)}) collective-permute-start(f32[21,32,128]{2,1,0:T(8,128)S(1)} %get-tuple-element.47), channel_id=1, source_target_pairs={{0,4},{1,2},{2,1},{3,7},{4,0},{5,6},{6,5},{7,3},{8,12},{9,10},{10,... | collective-permute-start | bytes 1032200 | tf_op jit(solution)/shard_map/ppermute | solution.py:551
  3.0 11.9 %collective-permute-start.1 = (f32[21,32,128]{2,1,0:T(8,128)S(1)}, f32[21,32,128]{2,1,0:T(8,128)S(1)}, u32[]{:S(2)}, u32[]{:S(2)}) collective-permute-start(f32[21,32,128]{2,1,0:T(8,128)S(1)} %get-tuple-element.48), channel_id=1, source_target_pairs={{0,1},{1,0},{2,3},{3,2},{4,5},{5,4},{6,7},{7,6},{8,9},{9,8},{10,11... | collective-permute-start | bytes 1032200 | tf_op jit(solution)/shard_map/ppermute | solution.py:551
  8.0 1.3 %collective-permute-start.2 = (f32[16,512]{1,0:T(8,128)S(1)}, f32[16,512]{1,0:T(8,128)S(1)}, u32[]{:S(2)}, u32[]{:S(2)}) collective-permute-start(f32[16,512]{1,0:T(8,128)S(1)} %get-tuple-element.55), channel_id=1, source_target_pairs={{0,4},{4,0},{8,12},{12,8},{1,5},{5,1},{9,13},{13,9},{2,6},{6,2},{1... | collective-permute-start | bytes 98312 | tf_op jit(solution)/shard_map/ppermute | solution.py:563
  9.3 3.4 %collective-permute-start.3 = (f32[16,512]{1,0:T(8,128)S(1)}, f32[16,512]{1,0:T(8,128)S(1)}, u32[]{:S(2)}, u32[]{:S(2)}) collective-permute-start(f32[16,512]{1,0:T(8,128)S(1)} %chip_kernel.2), channel_id=1, source_target_pairs={{0,12},{4,8},{8,4},{12,0},{1,13},{5,9},{9,5},{13,1},{2,14},{6,10},... | collective-permute-start | bytes 98312 | tf_op jit(solution)/shard_map/ppermute | solution.py:565
  12.8 3.8 %collective-permute-start.4 = (f32[32,128]{1,0:T(8,128)S(1)}, f32[32,128]{1,0:T(8,128)S(1)}, u32[]{:S(2)}, u32[]{:S(2)}) collective-permute-start(f32[32,128]{1,0:T(8,128)S(1)} %get-tuple-element.57), channel_id=1, source_target_pairs={{0,4},{1,2},{2,1},{3,7},{4,0},{5,6},{6,5},{7,3},{8,12},{9,10},{10,... | collective-permute-start | bytes 49160 | tf_op jit(solution)/shard_map/ppermute | solution.py:551
  13.2 3.7 %collective-permute-start.5 = (f32[32,128]{1,0:T(8,128)S(1)}, f32[32,128]{1,0:T(8,128)S(1)}, u32[]{:S(2)}, u32[]{:S(2)}) collective-permute-start(f32[32,128]{1,0:T(8,128)S(1)} %get-tuple-element.58), channel_id=1, source_target_pairs={{0,1},{1,0},{2,3},{3,2},{4,5},{5,4},{6,7},{7,6},{8,9},{9,8},{10,11... | collective-permute-start | bytes 49160 | tf_op jit(solution)/shard_map/ppermute | solution.py:551
  18.2 1.3 %collective-permute-start.6 = (f32[8,768]{1,0:T(8,128)S(1)}, f32[8,768]{1,0:T(8,128)S(1)}, u32[]{:S(2)}, u32[]{:S(2)}) collective-permute-start(f32[8,768]{1,0:T(8,128)S(1)} %get-tuple-element.65), channel_id=1, source_target_pairs={{0,4},{4,0},{8,12},{12,8},{1,5},{5,1},{9,13},{13,9},{2,6},{6,2},{1... | collective-permute-start | bytes 73736 | tf_op jit(solution)/shard_map/ppermute | solution.py:563
  19.5 3.3 %collective-permute-start.7 = (f32[8,768]{1,0:T(8,128)S(1)}, f32[8,768]{1,0:T(8,128)S(1)}, u32[]{:S(2)}, u32[]{:S(2)}) collective-permute-start(f32[8,768]{1,0:T(8,128)S(1)} %chip_kernel.3), channel_id=1, source_target_pairs={{0,12},{4,8},{8,4},{12,0},{1,13},{5,9},{9,5},{13,1},{2,14},{6,10},... | collective-permute-start | bytes 73736 | tf_op jit(solution)/shard_map/ppermute | solution.py:565
  23.6 1.2 %collective-permute-start.8 = (f32[8,128]{1,0:T(8,128)S(1)}, f32[8,128]{1,0:T(8,128)S(1)}, u32[]{:S(2)}, u32[]{:S(2)}) collective-permute-start(f32[8,128]{1,0:T(8,128)S(1)} %get-tuple-element.67), channel_id=1, source_target_pairs={{0,4},{4,0},{8,12},{12,8},{1,5},{5,1},{9,13},{13,9},{2,6},{6,2},{1... | collective-permute-start | bytes 12296 | tf_op jit(solution)/shard_map/ppermute | solution.py:516
  24.8 3.0 %collective-permute-start.9 = (f32[8,128]{1,0:T(8,128)S(1)}, f32[8,128]{1,0:T(8,128)S(1)}, u32[]{:S(2)}, u32[]{:S(2)}) collective-permute-start(f32[8,128]{1,0:T(8,128)S(1)} %add.12), channel_id=1, source_target_pairs={{0,12},{4,8},{8,4},{12,0},{1,13},{5,9},{9,5},{13,1},{2,14},{6,10},... | collective-permute-start | bytes 12296 | tf_op jit(solution)/shard_map/ppermute | solution.py:518
  27.8 3.0 %collective-permute-start.10 = (f32[8,128]{1,0:T(8,128)S(1)}, f32[8,128]{1,0:T(8,128)S(1)}, u32[]{:S(2)}, u32[]{:S(2)}) collective-permute-start(f32[8,128]{1,0:T(8,128)S(1)} %add.13), channel_id=1, source_target_pairs={{0,5},{1,4},{2,7},{3,6},{4,1},{5,0},{6,3},{7,2},{8,13},{9,12},{10,... | collective-permute-start | bytes 12296 | tf_op jit(solution)/shard_map/ppermute | solution.py:521
  30.9 3.9 %collective-permute-start.11 = (f32[8,128]{1,0:T(8,128)S(1)}, f32[8,128]{1,0:T(8,128)S(1)}, u32[]{:S(2)}, u32[]{:S(2)}) collective-permute-start(f32[8,128]{1,0:T(8,128)S(1)} %add.14), channel_id=1, source_target_pairs={{0,6},{1,7},{2,4},{3,5},{4,2},{5,3},{6,0},{7,1},{8,14},{9,15},{10,... | collective-permute-start | bytes 12296 | tf_op jit(solution)/shard_map/ppermute | solution.py:521

commit v9 on v8

--- a/solution.py
+++ b/solution.py
@@ -223,7 +223,7 @@
     to_second[...] = jnp.where(lon_odd == 0, for_west, for_east)
 
 
-def ghost_kernel(levels, columns, got_second, got_first, near, own, spread, statics, edge):
+def ghost_kernel(levels, columns, got_second, got_first, near, made, own, spread, ghosts, patches, edge):
     lat_odd = lax.axis_index("lat") % 2
     group = REACH * levels
 
@@ -245,18 +245,44 @@
     spread[...] = dot(near[...], r)
     diagonal, to_east, to_upper = coefficients(levels, group, kappa, east, north, upper, ocean)
     edge[0:1] = east[columns - 1 :]
-    for at in range(0, columns, TILE):
-        tile = slice(at, at + TILE)
-        d, e, n, u, o = (
-            joined(own[k, pl.ds(at, TILE)], x[tile]) for k, x in enumerate((diagonal, to_east, north, to_upper, ocean))
-        )
-        d, n = completed(levels, group, d, n, o)
-        row = lax.broadcasted_iota(jnp.int32, (TILE, 1), 0)
-        w = pltpu.roll(e, 1, 0)
-        w = jnp.where(row == 0, carried, w) if at else w
-        carried = e[TILE - 1 :]
-        for k, x in enumerate((d, e, w, n, lane_roll(n, levels), u, lane_roll(u, 1), o)):
-            statics[k, pl.ds(at, TILE)] = x
+    last = made.shape[2] - group
+    low, high = slice(0, group), slice(group, 2 * group)
+    lane = lax.broadcasted_iota(jnp.int32, (1, group), 1)
+    first_one, last_one = lane < levels, lane >= group - levels
+    up = lambda x: pltpu.roll(x, levels, 1)
+    down = lambda x: pltpu.roll(x, group - levels, 1)
+    own_low, own_high = pl.ds(0, group), pl.ds(last, group)
+    ocean_low, ocean_high = made[4, :, own_low], made[4, :, own_high]
+    north_high = own[3, :, own_high]
+    north_high = jnp.where(last_one, north_high * down(ocean[:, high]), north_high)
+    north_of = lambda x, o, above: x * o * jnp.where(last_one, down(above), down(o))
+    ghost_low = north_of(north[:, low], ocean[:, low], ocean_low)
+    ghost_high = north_of(north[:, high], ocean[:, high], ocean[:, high])
+    patches[0] = own[0, :, own_low] + jnp.where(first_one, ocean_low * up(north[:, low]), 0.0)
+    patches[1] = jnp.where(first_one, up(ghost_low), own[4, :, own_low])
+    patches[2] = north_high
+    row = lax.broadcasted_iota(jnp.int32, (columns, 1), 0)
+    for part, n, below in ((low, ghost_low, ghost_low), (high, ghost_high, north_high)):
+        d, e, u, o = (x[:, part] for x in (diagonal, to_east, to_upper, ocean))
+        if part is high:
+            d = d + jnp.where(first_one, o * up(made[2, :, own_high]), 0.0)
+        w = jnp.where(row == 0, 0.0, pltpu.roll(e, 1, 0))
+        for k, x in enumerate((d, e, w, n, jnp.where(first_one, up(below), up(n)), u, pltpu.roll(u, 1, 1), o)):
+            ghosts[k, :, part] = x
+
+
+def coefficient(statics, k, at):
+    own, ghosts, patches = statics
+    group = ghosts.shape[2] // 2
+    tile = pl.ds(at, TILE)
+    x = own[k, tile]
+    parts = [x[:, j : j + group] for j in range(0, x.shape[1], group)]
+    if k in (0, 4):
+        parts[0] = patches[0 if k == 0 else 1, tile]
+    if k == 3:
+        parts[-1] = patches[2, tile]
+    g = ghosts[k, tile]
+    return jnp.concatenate([g[:, :group]] + parts + [g[:, group:]], axis=1)
 
 
 def forward_kernel(group, *refs):
@@ -298,8 +324,21 @@
     out[...] = jnp.concatenate([m, jnp.zeros_like(m)], axis=0)
 
 
-def near_kernel(near, field, spread):
+def near_kernel(levels, near, field, made, spread, statics):
     spread[...] = dot(near[...], field[...])
+    columns = field.shape[0]
+    lanes = field.shape[1]
+    lane = lax.broadcasted_iota(jnp.int32, (1, lanes), 1)
+    row = lax.broadcasted_iota(jnp.int32, (TILE, 1), 0)
+    for at in range(0, columns, TILE):
+        tile = pl.ds(at, TILE)
+        d, e, n, u, o = (made[k, tile] for k in range(5))
+        w = pltpu.roll(e, 1, 0)
+        w = jnp.where(row == 0, carried, w) if at else w
+        carried = e[TILE - 1 :]
+        n = n * o * jnp.where(lane >= lanes - levels, 1.0, lane_roll(o, -levels))
+        for k, x in enumerate((d, e, w, n, lane_roll(n, levels), u, lane_roll(u, 1), o)):
+            statics[k, tile] = x
 
 
 def told(far, lists):
@@ -316,12 +355,14 @@
 
 
 def apply_tile(levels, v, statics, ends, at):
-    source, k = statics, at
+    own = statics[0]
     if at == 0:
-        source, k = ends, 0
-    if at + TILE == statics.shape[1]:
-        source, k = ends, TILE
-    d, e, w, n, s, u, low = (source[i, pl.ds(k, TILE)] for i in range(7))
+        faces_of = lambda k: ends[k, 0:TILE]
+    elif at + TILE == own.shape[1]:
+        faces_of = lambda k: ends[k, TILE : 2 * TILE]
+    else:
+        faces_of = lambda k: coefficient(statics, k, at)
+    d, e, w, n, s, u, low = (faces_of(k) for k in range(7))
     i = at + EDGE
     here = v[pl.ds(i, TILE)]
     out = d * here - e * v[pl.ds(i + 1, TILE)] - w * v[pl.ds(i - 1, TILE)]
@@ -353,8 +394,9 @@
 
 def first_kernel(
     rows, levels, columns, others,
-    own_spread, own_edge, ghost_spread, statics, edge, far, weights, side_second, side_first, *rest,
+    own_spread, own_edge, ghost_spread, own_part, ghost_part, patches, edge, far, weights, side_second, side_first, *rest,
 ):
+    statics = own_part, ghost_part, patches
     received = rest[: 1 + others]
     v, image, ends, rim, to_first, to_second, f = rest[1 + others :]
     lat_odd = lax.axis_index("lat") % 2
@@ -373,14 +415,13 @@
     one, two = lists[0], lists[1]
     east_list, west_list = jnp.where(even, one, two), jnp.where(even, two, one)
     end = columns - 1
-    low_tile, high_tile = pl.ds(0, TILE), pl.ds(columns - TILE, TILE)
     for k in range(7):
-        ends[k, 0:TILE] = statics[k, low_tile]
-        ends[k, TILE : 2 * TILE] = statics[k, high_tile]
-    ocean = statics[7, 0:1]
+        ends[k, 0:TILE] = coefficient(statics, k, 0)
+        ends[k, TILE : 2 * TILE] = coefficient(statics, k, columns - TILE)
+    ocean = coefficient(statics, 7, 0)[0:1]
     face_west = west_list[7:8] * west_list[8:9] * ocean
-    last_east = statics[1, end:] * east_list[8:9]
-    ends[0, 0:1] = statics[0, 0:1] + ocean * west_list[7:8]
+    last_east = ends[1, 2 * TILE - 1 :] * east_list[8:9]
+    ends[0, 0:1] = ends[0, 0:1] + ocean * west_list[7:8]
     ends[2, 0:1] = face_west
     ends[1, 2 * TILE - 1 : 2 * TILE] = last_east
     blank = jnp.zeros((6, lanes), jnp.float32)
@@ -408,7 +449,7 @@
     for at in range(0, columns, TILE):
         tile = pl.ds(at, TILE)
         second = apply_tile(levels, f, statics, ends, at)[1]
-        w = jnp.where(statics[7, tile] > 0.5, second, v[pl.ds(EDGE + at, TILE)])
+        w = jnp.where(coefficient(statics, 7, at) > 0.5, second, v[pl.ds(EDGE + at, TILE)])
         image[tile] = w
         for k in range(4):
             spread = weights[k, tile]
@@ -443,7 +484,10 @@
     sums[...] = jnp.concatenate([lane_sums(energy), lane_sums(curve), jnp.zeros((6, 128), jnp.float32)], axis=0)
 
 
-def second_kernel(levels, columns, rows, others, spread, early, image, statics, ends, far, rim, *rest):
+def second_kernel(
+    levels, columns, rows, others, spread, early, image, own_part, ghost_part, patches, ends, far, rim, *rest
+):
+    statics = own_part, ghost_part, patches
     received = rest[: 1 + others]
     v, f, sums = rest[1 + others :]
     v[...] = spread[...] + told(far, received)
@@ -453,7 +497,7 @@
         tile = pl.ds(at, TILE)
         q, b = apply_tile(levels, v, statics, ends, at)
         f[pl.ds(EDGE + at, TILE)] = b
-        q, b, ocean = q[:, own], b[:, own], statics[7, tile, own]
+        q, b, ocean = q[:, own], b[:, own], own_part[7, tile]
         mixed.append(image[tile, own] * q)
         still = jnp.where(ocean > 0.5, b, q)
         last.append(still * still)
@@ -461,13 +505,14 @@
     sums[...] = jnp.concatenate([early[0:2], lane_sums(mixed), lane_sums(last), early[4:8]], axis=0)
 
 
-def turn_kernel(rows, levels, columns, precond, image, again, f, statics, ends, *outs):
+def turn_kernel(rows, levels, columns, precond, image, again, f, own_part, ghost_part, patches, ends, *outs):
+    statics = own_part, ghost_part, patches
     z = outs[4]
     own = own_lanes(rows, levels)
     for at in range(0, columns, TILE):
         second = apply_tile(levels, f, statics, ends, at)[1]
         tile = pl.ds(at, TILE)
-        z[tile] = jnp.where(statics[7, tile] > 0.5, second, again[pl.ds(EDGE + at, TILE)])
+        z[tile] = jnp.where(coefficient(statics, 7, at) > 0.5, second, again[pl.ds(EDGE + at, TILE)])
     group = REACH * levels
     slab = pl.ds(EDGE, columns)
     for j in range(0, rows, REACH):
@@ -551,7 +596,7 @@
     to_band = lambda x, pairs: lax.ppermute(x, ("lon", "lat"), pairs)
     got_second, got_first = to_band(second, lat_b), to_band(first, lat_a)
 
-    own_field, own_statics, own_edge, to_first, to_second = call(
+    own_field, made, own_edge, to_first, to_second = call(
         functools.partial(own_kernel, rows, levels, columns),
         [(columns, flat), (5, columns, flat), (8, flat), (16, flat), (16, flat)],
         noise, kappa2, conduct, land, weights,
@@ -571,19 +616,21 @@
         ]
 
     lists = exchange(to_first, to_second)
-    (own_spread,) = call(near_kernel, [(tall, flat)], near, own_field)
+    own_spread, own_part = call(
+        functools.partial(near_kernel, levels), [(tall, flat), (8, columns, flat)], near, own_field, made
+    )
     heights = sum(x.shape[0] for x in lists)
     side_second, side_first = call(functools.partial(forward_kernel, group), [(heights, group)] * 2, *lists)
     side_second, side_first = to_band(side_second, lat_b), to_band(side_first, lat_a)
-    ghost_spread, statics, edge = call(
+    ghost_spread, ghost_part, patches, edge = call(
         functools.partial(ghost_kernel, levels, columns),
-        [(tall, 2 * group), (8, columns, lanes), (8, 2 * group)],
-        got_second, got_first, near, own_statics,
+        [(tall, 2 * group), (8, columns, 2 * group), (3, columns, group), (8, 2 * group)],
+        got_second, got_first, near, made, own_part,
     )
     precond, image, ends, rim, to_first, to_second = call(
         functools.partial(first_kernel, rows, levels, columns, others),
         [(tall, lanes), (columns, lanes), (7, 2 * TILE, lanes), (7, 8, lanes), (8, lanes), (8, lanes)],
-        own_spread, own_edge, ghost_spread, statics, edge, far, columns_of, side_second, side_first, *lists,
+        own_spread, own_edge, ghost_spread, own_part, ghost_part, patches, edge, far, columns_of, side_second, side_first, *lists,
         scratch=[(tall, lanes)],
     )
     lists = exchange(to_first, to_second)
@@ -595,13 +642,13 @@
     again, half, sums = call(
         functools.partial(second_kernel, levels, columns, rows, others),
         [(tall, lanes), (tall, lanes), (8, 128)],
-        spread, sums, image, statics, ends, far, rim, *lists,
+        spread, sums, image, own_part, ghost_part, patches, ends, far, rim, *lists,
     )
     sums = summed(sums)
     turned_back = call(
         functools.partial(turn_kernel, rows, levels, columns),
         [(flat, columns)] * 4 + [(columns, lanes)],
-        precond, image, again, half, statics, ends,
+        precond, image, again, half, own_part, ghost_part, patches, ends,
     )[:4]
     operands = [pltpu.with_memory_space_constraint(x, pltpu.VMEM) for x in (sums, noise, *turned_back)]
     answer, left = pl.pallas_call(

time: 35.9 us -> 35.9 us (level)
  waiting for transfers between devices: 12 us -> 13.5 us
  starting transfers between devices: 13.2 us -> 12.3 us
  Pallas kernels: 9.9 us -> 9.23 us
    ppermute x2, waiting for transfers between devices: 2.74 us -> 3.59 us  [summed(): x = x + lax.ppermute(x, ('lon', 'lat'), pairs)]
    ppermute x2, starting transfers between devices: 2.56 us -> 1.73 us  [summed(): x = x + lax.ppermute(x, ('lon', 'lat'), pairs)]
    pallas_call x10, Pallas kernels: 7.13 us -> 6.46 us  [call(): pl.pallas_call(kernel, out_shape=[pltpu.VMEM(s, jnp.float32) for s in out...]
    ppermute x4, waiting for transfers between devices: 0.49 us -> 1.14 us  [body(): to_band = lambda x, pairs: lax.ppermute(x, ('lon', 'lat'), pairs)]
  transfers between devices with their start and end apart: 12 -> 12, of which waited for: 10 -> 9; matrix products, arithmetic and copies ran while one was open for 0% -> 0% of each run, Pallas kernels for 14% -> 12%
where the time goes in v9:
time: 35.9 us; the launch traced here: 35.8 us
  waiting for transfers between devices  13.5 us (38%)
  starting transfers between devices  12.3 us (34%)
  Pallas kernels  9.23 us (26%)
  between operations  0.74 us (2%)
    pallas_call x10, Pallas kernels, call(): pl.pallas_call(kernel, out_shape=[pltpu.VMEM(s, jnp.float32) for s in out...  6.46 us
    ppermute x4, starting transfers between devices, body(): to_band = lambda x, pairs: lax.ppermute(x, ('lon', 'lat'), pairs)  6.35 us
    ppermute x2, waiting for transfers between devices, summed(): x = x + lax.ppermute(x, ('lon', 'lat'), pairs)  3.59 us
    ppermute x2, waiting for transfers between devices, exchange(): got_two = lax.ppermute(two, 'lon', lon_b)  3.57 us
    ppermute x2, starting transfers between devices, exchange(): got_two = lax.ppermute(two, 'lon', lon_b)  2.65 us
    ppermute x2, waiting for transfers between devices, exchange(): got_one = lax.ppermute(one, 'lon', lon_a)  2.38 us
    pallas_call x1, Pallas kernels, body(): pl.pallas_call(functools.partial(band_kernel, rows, levels), out_shape=[p...  1.78 us
    ppermute x1, waiting for transfers between devices, summed(): x = x + lax.ppermute(x, 'lon', [(i, i ^ step ^ 1) for i in range(count)])  1.77 us
  transfers between devices with their start and end apart: 12, of which 9 were waited for; matrix products, arithmetic and copies ran while one was open for 0% of the time, Pallas kernels for 12%

profile of v9, /device:TPU:0, one launch (start us, length us, event | category | flops | bytes accessed | tf_op | source)
XLA Modules:
  0.0 35.8 jit_solution(6791798275313641220)
XLA Ops:
  0.6 1.8 %band_kernel.1 = (f32[21,32,128]{2,1,0:T(8,128)S(1)}, f32[21,32,128]{2,1,0:T(8,128)S(1)}, f32[512,128]{1,0:T(8,128)S(1)}, f32[512,128]{1,0:T(8,128)S(1)}, f32[3,...) custom-call(f32[512,128]{1,0:T(8,128)} %bitcast.7, ...), custom_call_target="tpu_custom_call" | custom-call | tf_op jit(solution)/shard_map/band_kernel/pallas_call | solution.py:586
  2.4 0.6 %collective-permute-start = (f32[21,32,128]{2,1,0:T(8,128)S(1)}, f32[21,32,128]{2,1,0:T(8,128)S(1)}, u32[]{:S(2)}, u32[]{:S(2)}) collective-permute-start(f32[21,32,128]{2,1,0:T(8,128)S(1)} %get-tuple-element.52), channel_id=1, source_target_pairs={{0,4},{1,2},{2,1},{3,7},{4,0},{5,6},{6,5},{7,3},{8,12},{9,10},{10,... | collective-permute-start | bytes 1032200 | tf_op jit(solution)/shard_map/ppermute | solution.py:596
  3.0 4.1 %collective-permute-start.1 = (f32[21,32,128]{2,1,0:T(8,128)S(1)}, f32[21,32,128]{2,1,0:T(8,128)S(1)}, u32[]{:S(2)}, u32[]{:S(2)}) collective-permute-start(f32[21,32,128]{2,1,0:T(8,128)S(1)} %get-tuple-element.53), channel_id=1, source_target_pairs={{0,1},{1,0},{2,3},{3,2},{4,5},{5,4},{6,7},{7,6},{8,9},{9,8},{10,11... | collective-permute-start | bytes 1032200 | tf_op jit(solution)/shard_map/ppermute | solution.py:596
  7.1 0.9 %own_kernel.1 = (f32[128,512]{1,0:T(8,128)S(1)}, f32[5,128,512]{2,1,0:T(8,128)S(1)}, f32[8,512]{1,0:T(8,128)S(1)}, f32[16,512]{1,0:T(8,128)S(1)}, f32[16,512]{1,0:T(8,128)S(1)}) custom-call(f32[512,128]{1,0:T(8,128)S(1)} %get-tuple-element.43.noise, f32[512,128]{1,0:T(8,128)S(1)} %get-tuple-element.44.kappa2, f32[3,512,128]{2,1,0:T(8,128)S(1)} %get-tuple-element.45.conduct, ...), custom_call_target="tpu_custom_call" | custom-call | tf_op jit(solution)/shard_map/own_kernel/pallas_call | solution.py:130
  8.0 0.1 collective-permute-start.2
  8.1 1.2 %collective-permute-done.2.got.refs_0_.rest_0_ = f32[16,512]{1,0:T(8,128)S(1)} collective-permute-done((f32[16,512]{1,0:T(8,128)S(1)}, f32[16,512]{1,0:T(8,128)S(1)}, u32[]{:S(2)}, u32[]{:S(2)}) %collective-permute-start.2) | collective-permute-done | bytes 32800 | tf_op jit(solution)/shard_map/ppermute | solution.py:608
  9.3 1.3 %collective-permute-start.3 = (f32[16,512]{1,0:T(8,128)S(1)}, f32[16,512]{1,0:T(8,128)S(1)}, u32[]{:S(2)}, u32[]{:S(2)}) collective-permute-start(f32[16,512]{1,0:T(8,128)S(1)} %chip_kernel.2), channel_id=1, source_target_pairs={{0,12},{4,8},{8,4},{12,0},{1,13},{5,9},{9,5},{13,1},{2,14},{6,10},... | collective-permute-start | bytes 98312 | tf_op jit(solution)/shard_map/ppermute | solution.py:610
  10.6 2.1 %collective-permute-done.3.refs_1_.rest_1_ = f32[16,512]{1,0:T(8,128)S(1)} collective-permute-done((f32[16,512]{1,0:T(8,128)S(1)}, f32[16,512]{1,0:T(8,128)S(1)}, u32[]{:S(2)}, u32[]{:S(2)}) %collective-permute-start.3) | collective-permute-done | bytes 32800 | tf_op jit(solution)/shard_map/ppermute | solution.py:610
  12.7 0.5 %collective-permute-start.4 = (f32[32,128]{1,0:T(8,128)S(1)}, f32[32,128]{1,0:T(8,128)S(1)}, u32[]{:S(2)}, u32[]{:S(2)}) collective-permute-start(f32[32,128]{1,0:T(8,128)S(1)} %get-tuple-element.63), channel_id=1, source_target_pairs={{0,4},{1,2},{2,1},{3,7},{4,0},{5,6},{6,5},{7,3},{8,12},{9,10},{10,... | collective-permute-start | bytes 49160 | tf_op jit(solution)/shard_map/ppermute | solution.py:596
  13.2 1.2 %collective-permute-start.5 = (f32[32,128]{1,0:T(8,128)S(1)}, f32[32,128]{1,0:T(8,128)S(1)}, u32[]{:S(2)}, u32[]{:S(2)}) collective-permute-start(f32[32,128]{1,0:T(8,128)S(1)} %get-tuple-element.64), channel_id=1, source_target_pairs={{0,1},{1,0},{2,3},{3,2},{4,5},{5,4},{6,7},{7,6},{8,9},{9,8},{10,11... | collective-permute-start | bytes 49160 | tf_op jit(solution)/shard_map/ppermute | solution.py:596
  14.4 0.7 %near_kernel.1 = (f32[144,512]{1,0:T(8,128)S(1)}, f32[8,128,512]{2,1,0:T(8,128)S(1)}) custom-call(f32[144,128]{1,0:T(8,128)S(1)} %get-tuple-element.42.near, f32[128,512]{1,0:T(8,128)S(1)} %get-tuple-element.48.field, f32[5,128,512]{2,1,0:T(8,128)S(1)} %get-tuple-element.49.made), custom_call_target="tpu_custom_call" | custom-call | tf_op jit(solution)/shard_map/near_kernel/pallas_call | solution.py:130
  15.1 0.0 collective-permute-done.got_second
  15.1 0.0 collective-permute-done.1.got_first
  15.1 0.6 %ghost_kernel.1 = (f32[144,256]{1,0:T(8,128)S(1)}, f32[8,128,256]{2,1,0:T(8,128)S(1)}, f32[3,128,128]{2,1,0:T(8,128)S(1)}, f32[8,256]{1,0:T(8,128)S(1)}) custom-call(f32[21,32,128]{2,1,0:T(8,128)S(1)} %collective-permute-done.got_second, f32[21,32,128]{2,1,0:T(8,128)S(1)} %collective-permute-done.1.got_first, f32[144,128]{1,0:T(8,128)S(1)} %get-tuple-element.42.near, ...), custom_call_target="tpu_custom_call" | custom-call | tf_op jit(solution)/shard_map/ghost_kernel/pallas_call | solution.py:130
  15.8 0.0 collective-permute-done.4.side_second
  15.8 1.1 %collective-permute-done.5.side_first = f32[32,128]{1,0:T(8,128)S(1)} collective-permute-done((f32[32,128]{1,0:T(8,128)S(1)}, f32[32,128]{1,0:T(8,128)S(1)}, u32[]{:S(2)}, u32[]{:S(2)}) %collective-permute-start.5) | collective-permute-done | bytes 16416 | tf_op jit(solution)/shard_map/ppermute | solution.py:596
  16.9 1.3 %first_kernel.1 = (f32[144,768]{1,0:T(8,128)S(1)}, f32[128,768]{1,0:T(8,128)S(1)}, f32[7,16,768]{2,1,0:T(8,128)S(1)}, f32[7,8,768]{2,1,0:T(8,128)S(1)}, f32[8,768]{1,0:T(8,128)S(1)}, /*index=5*/f32[8,768]{1,0:T(8,128)S(1)}) custom-call(f32[144,512]{1,0:T(8,128)S(1)} %get-tuple-element.50.own_spread, f32[8,512]{1,0:T(8,128)S(1)} %get-tuple-element.51.own_edge, ...), custom_call_target="tpu_custom_call" | custom-call | tf_op jit(solution)/shard_map/first_kernel/pallas_call | solution.py:130
  18.2 0.1 collective-permute-start.6
  18.3 1.2 %collective-permute-done.6.got.rest_0_ = f32[8,768]{1,0:T(8,128)S(1)} collective-permute-done((f32[8,768]{1,0:T(8,128)S(1)}, f32[8,768]{1,0:T(8,128)S(1)}, u32[]{:S(2)}, u32[]{:S(2)}) %collective-permute-start.6) | collective-permute-done | bytes 24608 | tf_op jit(solution)/shard_map/ppermute | solution.py:608
  19.5 1.3 %collective-permute-start.7 = (f32[8,768]{1,0:T(8,128)S(1)}, f32[8,768]{1,0:T(8,128)S(1)}, u32[]{:S(2)}, u32[]{:S(2)}) collective-permute-start(f32[8,768]{1,0:T(8,128)S(1)} %chip_kernel.3), channel_id=1, source_target_pairs={{0,12},{4,8},{8,4},{12,0},{1,13},{5,9},{9,5},{13,1},{2,14},{6,10},... | collective-permute-start | bytes 73736 | tf_op jit(solution)/shard_map/ppermute | solution.py:610
  20.8 0.5 %between_kernel.1 = (f32[144,768]{1,0:T(8,128)S(1)}, f32[8,128]{1,0:T(8,128)S(1)}) custom-call(f32[144,128]{1,0:T(8,128)S(1)} %get-tuple-element.42.near, f32[128,512]{1,0:T(8,128)S(1)} %get-tuple-element.48.field, f32[144,768]{1,0:T(8,128)S(1)} %get-tuple-element.65.precond, f32[128,768]{1,0:T(8,128)S(1)} %get-tuple-element.66.image), custom_call_target="tpu_custom_call" | custom-call | tf_op jit(solution)/shard_map/between_kernel/pallas_call | solution.py:130
  21.3 1.5 %collective-permute-done.7.rest_1_ = f32[8,768]{1,0:T(8,128)S(1)} collective-permute-done((f32[8,768]{1,0:T(8,128)S(1)}, f32[8,768]{1,0:T(8,128)S(1)}, u32[]{:S(2)}, u32[]{:S(2)}) %collective-permute-start.7) | collective-permute-done | bytes 24608 | tf_op jit(solution)/shard_map/ppermute | solution.py:610
  22.8 0.7 %second_kernel.1 = (f32[144,768]{1,0:T(8,128)S(1)}, f32[144,768]{1,0:T(8,128)S(1)}, f32[8,128]{1,0:T(8,128)S(1)}) custom-call(f32[144,768]{1,0:T(8,128)S(1)} %get-tuple-element.67.spread, f32[8,128]{1,0:T(8,128)S(1)} %get-tuple-element.68.early, f32[128,768]{1,0:T(8,128)S(1)} %get-tuple-element.66.image, f32[8,128,512]{2,1,0:T(8,128)S(1)} %get-tuple-element.54.own.own_part, ...), custom_call_target="tpu_custom_call" | custom-call | tf_op jit(solution)/shard_map/second_kernel/pallas_call | solution.py:130
  23.6 0.2 collective-permute-start.8
  23.8 1.0 %collective-permute-done.8 = f32[8,128]{1,0:T(8,128)S(1)} collective-permute-done((f32[8,128]{1,0:T(8,128)S(1)}, f32[8,128]{1,0:T(8,128)S(1)}, u32[]{:S(2)}, u32[]{:S(2)}) %collective-permute-start.8) | collective-permute-done | bytes 4128 | tf_op jit(solution)/shard_map/ppermute | solution.py:561
  24.8 1.3 %collective-permute-start.9 = (f32[8,128]{1,0:T(8,128)S(1)}, f32[8,128]{1,0:T(8,128)S(1)}, u32[]{:S(2)}, u32[]{:S(2)}) collective-permute-start(f32[8,128]{1,0:T(8,128)S(1)} %add.12), channel_id=1, source_target_pairs={{0,12},{4,8},{8,4},{12,0},{1,13},{5,9},{9,5},{13,1},{2,14},{6,10},... | collective-permute-start | bytes 12296 | tf_op jit(solution)/shard_map/ppermute | solution.py:563
  26.0 1.8 %collective-permute-done.9 = f32[8,128]{1,0:T(8,128)S(1)} collective-permute-done((f32[8,128]{1,0:T(8,128)S(1)}, f32[8,128]{1,0:T(8,128)S(1)}, u32[]{:S(2)}, u32[]{:S(2)}) %collective-permute-start.9) | collective-permute-done | bytes 4128 | tf_op jit(solution)/shard_map/ppermute | solution.py:563
  27.8 1.0 %collective-permute-start.10 = (f32[8,128]{1,0:T(8,128)S(1)}, f32[8,128]{1,0:T(8,128)S(1)}, u32[]{:S(2)}, u32[]{:S(2)}) collective-permute-start(f32[8,128]{1,0:T(8,128)S(1)} %add.13), channel_id=1, source_target_pairs={{0,5},{1,4},{2,7},{3,6},{4,1},{5,0},{6,3},{7,2},{8,13},{9,12},{10,... | collective-permute-start | bytes 12296 | tf_op jit(solution)/shard_map/ppermute | solution.py:566
  28.8 2.1 %collective-permute-done.10 = f32[8,128]{1,0:T(8,128)S(1)} collective-permute-done((f32[8,128]{1,0:T(8,128)S(1)}, f32[8,128]{1,0:T(8,128)S(1)}, u32[]{:S(2)}, u32[]{:S(2)}) %collective-permute-start.10) | collective-permute-done | bytes 4128 | tf_op jit(solution)/shard_map/ppermute | solution.py:566
  30.9 0.8 %collective-permute-start.11 = (f32[8,128]{1,0:T(8,128)S(1)}, f32[8,128]{1,0:T(8,128)S(1)}, u32[]{:S(2)}, u32[]{:S(2)}) collective-permute-start(f32[8,128]{1,0:T(8,128)S(1)} %add.14), channel_id=1, source_target_pairs={{0,6},{1,7},{2,4},{3,5},{4,2},{5,3},{6,0},{7,1},{8,14},{9,15},{10,... | collective-permute-start | bytes 12296 | tf_op jit(solution)/shard_map/ppermute | solution.py:566
  31.6 1.7 %turn_kernel.1 = (f32[512,128]{1,0:T(8,128)S(1)}, f32[512,128]{1,0:T(8,128)S(1)}, f32[512,128]{1,0:T(8,128)S(1)}, f32[512,128]{1,0:T(8,128)S(1)}, f32[128,768]{1,0:T(8,128)}) custom-call(f32[144,768]{1,0:T(8,128)S(1)} %get-tuple-element.65.precond, f32[128,768]{1,0:T(8,128)S(1)} %get-tuple-element.66.image, f32[144,768]{1,0:T(8,128)S(1)} %get-tuple-element.74.again, ...), custom_call_target="tpu_custom_call" | custom-call | tf_op jit(solution)/shard_map/turn_kernel/pallas_call | solution.py:130
  33.3 1.5 %collective-permute-done.11 = f32[8,128]{1,0:T(8,128)S(1)} collective-permute-done((f32[8,128]{1,0:T(8,128)S(1)}, f32[8,128]{1,0:T(8,128)S(1)}, u32[]{:S(2)}, u32[]{:S(2)}) %collective-permute-start.11) | collective-permute-done | bytes 4128 | tf_op jit(solution)/shard_map/ppermute | solution.py:566
  34.8 1.0 %combine_kernel.1 = (f32[512,128]{1,0:T(8,128)}, f32[512,128]{1,0:T(8,128)}) custom-call(f32[8,128]{1,0:T(8,128)S(1)} %add.15.sums, f32[512,128]{1,0:T(8,128)S(1)} %get-tuple-element.43.noise, f32[512,128]{1,0:T(8,128)S(1)} %get-tuple-element.76.precond, f32[512,128]{1,0:T(8,128)S(1)} %get-tuple-element.77.image, f32[512,128]{1,0:T(8,128)S(1)} %get-tuple-element.78.again, ...), custom_call_target="tpu_custom_call" | custom-call | tf_op jit(solution)/shard_map/combine_kernel/pallas_call | solution.py:654
  (7 shorter events, 0.1 us)
Async XLA Ops:
  2.4 12.7 %collective-permute-start = (f32[21,32,128]{2,1,0:T(8,128)S(1)}, f32[21,32,128]{2,1,0:T(8,128)S(1)}, u32[]{:S(2)}, u32[]{:S(2)}) collective-permute-start(f32[21,32,128]{2,1,0:T(8,128)S(1)} %get-tuple-element.52), channel_id=1, source_target_pairs={{0,4},{1,2},{2,1},{3,7},{4,0},{5,6},{6,5},{7,3},{8,12},{9,10},{10,... | collective-permute-start | bytes 1032200 | tf_op jit(solution)/shard_map/ppermute | solution.py:596
  3.0 12.2 %collective-permute-start.1 = (f32[21,32,128]{2,1,0:T(8,128)S(1)}, f32[21,32,128]{2,1,0:T(8,128)S(1)}, u32[]{:S(2)}, u32[]{:S(2)}) collective-permute-start(f32[21,32,128]{2,1,0:T(8,128)S(1)} %get-tuple-element.53), channel_id=1, source_target_pairs={{0,1},{1,0},{2,3},{3,2},{4,5},{5,4},{6,7},{7,6},{8,9},{9,8},{10,11... | collective-permute-start | bytes 1032200 | tf_op jit(solution)/shard_map/ppermute | solution.py:596
  8.0 1.3 %collective-permute-start.2 = (f32[16,512]{1,0:T(8,128)S(1)}, f32[16,512]{1,0:T(8,128)S(1)}, u32[]{:S(2)}, u32[]{:S(2)}) collective-permute-start(f32[16,512]{1,0:T(8,128)S(1)} %get-tuple-element.61), channel_id=1, source_target_pairs={{0,4},{4,0},{8,12},{12,8},{1,5},{5,1},{9,13},{13,9},{2,6},{6,2},{1... | collective-permute-start | bytes 98312 | tf_op jit(solution)/shard_map/ppermute | solution.py:608
  9.3 3.4 %collective-permute-start.3 = (f32[16,512]{1,0:T(8,128)S(1)}, f32[16,512]{1,0:T(8,128)S(1)}, u32[]{:S(2)}, u32[]{:S(2)}) collective-permute-start(f32[16,512]{1,0:T(8,128)S(1)} %chip_kernel.2), channel_id=1, source_target_pairs={{0,12},{4,8},{8,4},{12,0},{1,13},{5,9},{9,5},{13,1},{2,14},{6,10},... | collective-permute-start | bytes 98312 | tf_op jit(solution)/shard_map/ppermute | solution.py:610
  12.7 3.1 %collective-permute-start.4 = (f32[32,128]{1,0:T(8,128)S(1)}, f32[32,128]{1,0:T(8,128)S(1)}, u32[]{:S(2)}, u32[]{:S(2)}) collective-permute-start(f32[32,128]{1,0:T(8,128)S(1)} %get-tuple-element.63), channel_id=1, source_target_pairs={{0,4},{1,2},{2,1},{3,7},{4,0},{5,6},{6,5},{7,3},{8,12},{9,10},{10,... | collective-permute-start | bytes 49160 | tf_op jit(solution)/shard_map/ppermute | solution.py:596
  13.2 3.7 %collective-permute-start.5 = (f32[32,128]{1,0:T(8,128)S(1)}, f32[32,128]{1,0:T(8,128)S(1)}, u32[]{:S(2)}, u32[]{:S(2)}) collective-permute-start(f32[32,128]{1,0:T(8,128)S(1)} %get-tuple-element.64), channel_id=1, source_target_pairs={{0,1},{1,0},{2,3},{3,2},{4,5},{5,4},{6,7},{7,6},{8,9},{9,8},{10,11... | collective-permute-start | bytes 49160 | tf_op jit(solution)/shard_map/ppermute | solution.py:596
  18.2 1.3 %collective-permute-start.6 = (f32[8,768]{1,0:T(8,128)S(1)}, f32[8,768]{1,0:T(8,128)S(1)}, u32[]{:S(2)}, u32[]{:S(2)}) collective-permute-start(f32[8,768]{1,0:T(8,128)S(1)} %get-tuple-element.71), channel_id=1, source_target_pairs={{0,4},{4,0},{8,12},{12,8},{1,5},{5,1},{9,13},{13,9},{2,6},{6,2},{1... | collective-permute-start | bytes 73736 | tf_op jit(solution)/shard_map/ppermute | solution.py:608
  19.5 3.3 %collective-permute-start.7 = (f32[8,768]{1,0:T(8,128)S(1)}, f32[8,768]{1,0:T(8,128)S(1)}, u32[]{:S(2)}, u32[]{:S(2)}) collective-permute-start(f32[8,768]{1,0:T(8,128)S(1)} %chip_kernel.3), channel_id=1, source_target_pairs={{0,12},{4,8},{8,4},{12,0},{1,13},{5,9},{9,5},{13,1},{2,14},{6,10},... | collective-permute-start | bytes 73736 | tf_op jit(solution)/shard_map/ppermute | solution.py:610
  23.6 1.2 %collective-permute-start.8 = (f32[8,128]{1,0:T(8,128)S(1)}, f32[8,128]{1,0:T(8,128)S(1)}, u32[]{:S(2)}, u32[]{:S(2)}) collective-permute-start(f32[8,128]{1,0:T(8,128)S(1)} %get-tuple-element.73), channel_id=1, source_target_pairs={{0,4},{4,0},{8,12},{12,8},{1,5},{5,1},{9,13},{13,9},{2,6},{6,2},{1... | collective-permute-start | bytes 12296 | tf_op jit(solution)/shard_map/ppermute | solution.py:561
  24.8 3.0 %collective-permute-start.9 = (f32[8,128]{1,0:T(8,128)S(1)}, f32[8,128]{1,0:T(8,128)S(1)}, u32[]{:S(2)}, u32[]{:S(2)}) collective-permute-start(f32[8,128]{1,0:T(8,128)S(1)} %add.12), channel_id=1, source_target_pairs={{0,12},{4,8},{8,4},{12,0},{1,13},{5,9},{9,5},{13,1},{2,14},{6,10},... | collective-permute-start | bytes 12296 | tf_op jit(solution)/shard_map/ppermute | solution.py:563
  27.8 3.0 %collective-permute-start.10 = (f32[8,128]{1,0:T(8,128)S(1)}, f32[8,128]{1,0:T(8,128)S(1)}, u32[]{:S(2)}, u32[]{:S(2)}) collective-permute-start(f32[8,128]{1,0:T(8,128)S(1)} %add.13), channel_id=1, source_target_pairs={{0,5},{1,4},{2,7},{3,6},{4,1},{5,0},{6,3},{7,2},{8,13},{9,12},{10,... | collective-permute-start | bytes 12296 | tf_op jit(solution)/shard_map/ppermute | solution.py:566
  30.9 3.9 %collective-permute-start.11 = (f32[8,128]{1,0:T(8,128)S(1)}, f32[8,128]{1,0:T(8,128)S(1)}, u32[]{:S(2)}, u32[]{:S(2)}) collective-permute-start(f32[8,128]{1,0:T(8,128)S(1)} %add.14), channel_id=1, source_target_pairs={{0,6},{1,7},{2,4},{3,5},{4,2},{5,3},{6,0},{7,1},{8,14},{9,15},{10,... | collective-permute-start | bytes 12296 | tf_op jit(solution)/shard_map/ppermute | solution.py:566

commit v10 on v9

--- a/solution.py
+++ b/solution.py
@@ -139,35 +139,50 @@
 
 
 FULL, PART = REACH, REACH - 1
-PLANES = 3 * FULL + 3 * PART
+PLANES = 2 * FULL + 3 * PART
 
 
 def band_kernel(rows, levels, *refs):
     sources, (second, first), copies, sems = refs[:8], refs[8:10], refs[10:18], refs[18]
-    moves = [pltpu.make_async_copy(x, y, sems.at[k]) for k, (x, y) in enumerate(zip(sources, copies))]
+    order = (0, 3, 2, 1, 4, 5, 6, 7)
+    moves = [pltpu.make_async_copy(sources[k], copies[k], sems.at[k]) for k in order]
     for move in moves:
         move.start()
-    for move in moves:
-        move.wait()
     noise, kappa2, conduct, land = copies[:4]
     odd = lax.axis_index("lat") % 2
-    top = rows - REACH
-    loads = (
-        lambda at: noise[at, :],
-        lambda at: land[at, :].astype(jnp.float32),
-        lambda at: conduct[1, at, :],
-        lambda at: kappa2[at, :],
-        lambda at: conduct[0, at, :],
-        lambda at: conduct[2, at, :],
-    )
-    for out, side in ((first, odd), (second, 1 - odd)):
-        k = 0
-        for kind, load in enumerate(loads):
-            count = FULL if kind < 3 else PART
-            start = (1 - side) * (rows - count)
-            for j in range(count):
-                out[k] = load(pl.ds(start + j, levels, stride=rows))
-                k += 1
+    sides = ((first, odd), (second, 1 - odd))
+    plane = lambda lat: pl.ds(lat, levels, stride=rows)
+    moves[0].wait()
+    for out, side in sides:
+        for j in range(FULL):
+            out[j] = noise[plane((1 - side) * (rows - FULL) + j), :]
+    for move in moves[1:4]:
+        move.wait()
+    columns = noise.shape[1]
+    lane = lax.broadcasted_iota(jnp.int32, (1, columns), 1)
+    level = lax.broadcasted_iota(jnp.int32, (levels, 1), 0)
+    for out, side in sides:
+        base = (1 - side) * (rows - FULL)
+        ocean = [land[plane(base + j), :].astype(jnp.float32) for j in range(FULL)]
+        north = [conduct[1, plane(base + j), :] for j in range(FULL)]
+        for j in range(PART):
+            out[FULL + 3 * PART + j] = north[j] * ocean[j] * ocean[j + 1]
+        out[FULL + 4 * PART] = north[PART]
+        near = lambda x, j: jnp.where(side == 0, x[j + 1], x[j])
+        for j in range(PART):
+            at = plane(base + 1 - side + j)
+            o, n = near(ocean, j), near(north, j)
+            below = north[j] if j == 0 else jnp.where(side == 0, north[j], north[j - 1])
+            south = jnp.where(side == 0, below, 0.0) if j == 0 else below
+            e, k = conduct[0, at, :], kappa2[at, :]
+            u = jnp.where(level == levels - 1, 0.0, conduct[2, at, :])
+            west = jnp.where(lane == 0, 0.0, pltpu.roll(e, 1, 1))
+            ocean_east = jnp.where(lane == columns - 1, 1.0, pltpu.roll(o, columns - 1, 1))
+            out[FULL + j] = o * (k + e + west + n + south + u + pltpu.roll(u, 1, 0))
+            out[FULL + PART + j] = e * o * ocean_east
+            out[FULL + 2 * PART + j] = u * o * pltpu.roll(o, levels - 1, 0)
+    for move in moves[4:]:
+        move.wait()
 
 
 def turned(planes, rows_of_planes):
@@ -187,10 +202,16 @@
     return diagonal, east * ocean * ocean_east, upper * ocean * lane_roll(ocean, -1)
 
 
+def field_kernel(rows, levels, noise, weights, field, sums):
+    r = turned([noise[pl.ds(j, levels, stride=rows), :] for j in range(rows)], rows)
+    field[...] = r
+    sums[...] = dot(weights[...], r)
+
+
 def own_kernel(
     rows, levels, columns,
-    noise, kappa2, conduct, land, weights,
-    field, statics, edge, to_first, to_second,
+    kappa2, conduct, land, field,
+    statics, edge, to_first, to_second,
 ):
     last_band = lax.axis_index("lat") == lax.axis_size("lat") - 1
     lon_odd = lax.axis_index("lon") % 2
@@ -199,8 +220,6 @@
     def own(load):
         return turned([load(pl.ds(j, levels, stride=rows)) for j in range(rows)], rows)
 
-    r = own(lambda at: noise[at, :])
-    field[...] = r
     ocean = own(lambda at: land[at, :].astype(jnp.float32))
     north = own(lambda at: conduct[1, at, :])
     kappa = own(lambda at: kappa2[at, :])
@@ -211,25 +230,29 @@
     diagonal, to_east, to_upper = coefficients(levels, lanes, kappa, east, north, upper, ocean)
     for k, x in enumerate((diagonal, to_east, north, to_upper, ocean)):
         statics[k] = x
-    edge[0:1] = east[columns - 1 :]
-    m = dot(weights[...], r)[:4]
     end = columns - 1
-    blank = jnp.zeros((5, lanes), jnp.float32)
-    for_east = [m, r[end:], diagonal[end:], to_east[end - 1 : end], east[end:], ocean[end:], north[end:], to_upper[end:], blank]
-    for_west = [m, r[:1], diagonal[:1], to_east[:1], east[:1], ocean[:1], north[:1], to_upper[:1], blank]
+    edge[...] = jnp.concatenate([east[end:], jnp.zeros((7, lanes), jnp.float32)], axis=0)
+    blank = jnp.zeros((1, lanes), jnp.float32)
+    for_east = [field[end:], diagonal[end:], to_east[end - 1 : end], east[end:], ocean[end:], north[end:], to_upper[end:], blank]
+    for_west = [field[:1], diagonal[:1], to_east[:1], east[:1], ocean[:1], north[:1], to_upper[:1], blank]
     for_east = jnp.concatenate(for_east, axis=0)
     for_west = jnp.concatenate(for_west, axis=0)
     to_first[...] = jnp.where(lon_odd == 0, for_east, for_west)
     to_second[...] = jnp.where(lon_odd == 0, for_west, for_east)
 
 
-def ghost_kernel(levels, columns, got_second, got_first, near, made, own, spread, ghosts, patches, edge):
+MOMENTS, LIST = 4, 11
+
+
+def list_kernel(moments, edges, out):
+    out[...] = jnp.concatenate([moments[0:MOMENTS], edges[...], jnp.zeros((4, edges.shape[1]), jnp.float32)], axis=0)
+
+
+def ghost_kernel(levels, columns, got_second, got_first, near, made, own, spread, ghosts, patches):
     lat_odd = lax.axis_index("lat") % 2
     group = REACH * levels
 
-    def ghost(kind, north):
-        count = FULL if kind < 3 else PART
-        k = kind * FULL if kind < 3 else 3 * FULL + (kind - 3) * PART
+    def ghost(k, count, north):
         a = got_first[pl.ds(k, count)].reshape(count * levels, columns)
         b = jnp.where(inner_band(), got_second[pl.ds(k, count)], 0.0).reshape(count * levels, columns)
         from_first = (lat_odd == 0) if north else (lat_odd == 1)
@@ -239,12 +262,12 @@
         blank = jnp.zeros((group - count * levels, columns), jnp.float32)
         return jnp.concatenate([planes, blank] if north else [blank, planes], axis=0).T
 
-    r, ocean, north, kappa, east, upper = (
-        jnp.concatenate([ghost(kind, False), ghost(kind, True)], axis=1) for kind in range(6)
+    pieces = ((0, FULL), (FULL, PART), (FULL + PART, PART), (FULL + 2 * PART, PART), (FULL + 3 * PART, FULL))
+    r, diagonal, to_east, to_upper, north = (
+        jnp.concatenate([ghost(k, count, False), ghost(k, count, True)], axis=1) for k, count in pieces
     )
     spread[...] = dot(near[...], r)
-    diagonal, to_east, to_upper = coefficients(levels, group, kappa, east, north, upper, ocean)
-    edge[0:1] = east[columns - 1 :]
+    ocean = jnp.where(diagonal > 0.0, 1.0, 0.0)
     last = made.shape[2] - group
     low, high = slice(0, group), slice(group, 2 * group)
     lane = lax.broadcasted_iota(jnp.int32, (1, group), 1)
@@ -255,9 +278,9 @@
     ocean_low, ocean_high = made[4, :, own_low], made[4, :, own_high]
     north_high = own[3, :, own_high]
     north_high = jnp.where(last_one, north_high * down(ocean[:, high]), north_high)
-    north_of = lambda x, o, above: x * o * jnp.where(last_one, down(above), down(o))
-    ghost_low = north_of(north[:, low], ocean[:, low], ocean_low)
-    ghost_high = north_of(north[:, high], ocean[:, high], ocean[:, high])
+    ghost_low = north[:, low]
+    ghost_low = jnp.where(last_one, ghost_low * ocean[:, low] * down(ocean_low), ghost_low)
+    ghost_high = north[:, high]
     patches[0] = own[0, :, own_low] + jnp.where(first_one, ocean_low * up(north[:, low]), 0.0)
     patches[1] = jnp.where(first_one, up(ghost_low), own[4, :, own_low])
     patches[2] = north_high
@@ -286,15 +309,13 @@
 
 
 def forward_kernel(group, *refs):
-    lists, (second, first) = refs[:-2], refs[-2:]
+    (one, two, edge), more, (second, first) = refs[:3], refs[3:-2], refs[-2:]
     odd = lax.axis_index("lat") % 2
-    k = 0
-    for x in lists:
-        count, lanes = x.shape
-        low, high = x[:, 0:group], x[:, lanes - group :]
-        first[pl.ds(k, count)] = jnp.where(odd == 0, high, low)
-        second[pl.ds(k, count)] = jnp.where(odd == 0, low, high)
-        k += count
+    whole_rows = [one[0:LIST], two[0:LIST], edge[0:2]] + [x[...] for x in more]
+    x = jnp.concatenate(whole_rows, axis=0)
+    low, high = x[:, 0:group], x[:, x.shape[1] - group :]
+    first[...] = jnp.where(odd == 0, high, low)
+    second[...] = jnp.where(odd == 0, low, high)
 
 
 def joint_moments(left, right, rho, width):
@@ -310,11 +331,19 @@
     )
 
 
-def chip_kernel(rho, columns, own, got, out):
+def chip_kernel(rho, columns, own, edges, got, out):
     even = lax.axis_index("lon") % 2 == 0
-    mine, its = own[0:4], got[0:4]
+    mine, its = own[0:MOMENTS], got[0:MOMENTS]
+    m = joint_moments(jnp.where(even, mine, its), jnp.where(even, its, mine), rho, columns)
+    blank = jnp.zeros((out.shape[0] - MOMENTS - edges.shape[0], m.shape[1]), jnp.float32)
+    out[...] = jnp.concatenate([m, edges[...], blank], axis=0)
+
+
+def again_kernel(rho, columns, own, got, out):
+    even = lax.axis_index("lon") % 2 == 0
+    mine, its = own[0:MOMENTS], got[0:MOMENTS]
     out[...] = own[...]
-    out[0:4] = joint_moments(jnp.where(even, mine, its), jnp.where(even, its, mine), rho, columns)
+    out[0:MOMENTS] = joint_moments(jnp.where(even, mine, its), jnp.where(even, its, mine), rho, columns)
 
 
 def quad_kernel(rho, columns, mine, got, out):
@@ -354,7 +383,22 @@
     return n * lane_roll(v, -levels) + s * lane_roll(v, levels) + u * lane_roll(v, -1) + low * lane_roll(v, 1)
 
 
-def apply_tile(levels, v, statics, ends, at):
+def shifts(v, at, kept):
+    def turned_rows(i):
+        if i not in kept:
+            x = v[pl.ds(i, TILE)]
+            kept[i] = x, pltpu.roll(x, TILE - 1, 0), pltpu.roll(x, 1, 0)
+        return kept[i]
+
+    i = at + EDGE
+    row = lax.broadcasted_iota(jnp.int32, (TILE, 1), 0)
+    x, east_v, west_v = turned_rows(i)
+    east_v = jnp.where(row == TILE - 1, turned_rows(i + TILE)[1], east_v)
+    west_v = jnp.where(row == 0, turned_rows(i - TILE)[2], west_v)
+    return x, east_v, west_v
+
+
+def apply_tile(levels, v, statics, ends, at, kept):
     own = statics[0]
     if at == 0:
         faces_of = lambda k: ends[k, 0:TILE]
@@ -363,10 +407,8 @@
     else:
         faces_of = lambda k: coefficient(statics, k, at)
     d, e, w, n, s, u, low = (faces_of(k) for k in range(7))
-    i = at + EDGE
-    here = v[pl.ds(i, TILE)]
-    out = d * here - e * v[pl.ds(i + 1, TILE)] - w * v[pl.ds(i - 1, TILE)]
-    return here, out - faces(here, n, s, u, low, levels)
+    here, east_v, west_v = shifts(v, at, kept)
+    return here, d * here - e * east_v - w * west_v - faces(here, n, s, u, low, levels)
 
 
 def apply_rim(levels, columns, v, f, rim):
@@ -394,7 +436,7 @@
 
 def first_kernel(
     rows, levels, columns, others,
-    own_spread, own_edge, ghost_spread, own_part, ghost_part, patches, edge, far, weights, side_second, side_first, *rest,
+    own_spread, own_edge, ghost_spread, own_part, ghost_part, patches, far, weights, side_second, side_first, *rest,
 ):
     statics = own_part, ghost_part, patches
     received = rest[: 1 + others]
@@ -403,13 +445,14 @@
     even = lax.axis_index("lon") % 2 == 0
     group = REACH * levels
     lanes = rows * levels + 2 * group
+    a, b = side_first[...], jnp.where(inner_band(), side_second[...], 0.0)
+    south, north = jnp.where(lat_odd == 1, a, b), jnp.where(lat_odd == 1, b, a)
     lists, k = [], 0
-    for x in received:
-        count = x.shape[0]
-        a = side_first[pl.ds(k, count)]
-        b = jnp.where(inner_band(), side_second[pl.ds(k, count)], 0.0)
-        lists.append(jnp.concatenate([jnp.where(lat_odd == 1, a, b), x[...], jnp.where(lat_odd == 1, b, a)], axis=1))
-        k += count
+    for x in (received[0][0:LIST], received[1][0:LIST], own_edge[0:2], *[x[...] for x in received[2:]]):
+        at = slice(k, k + x.shape[0])
+        lists.append(jnp.concatenate([south[at], x, north[at]], axis=1))
+        k += x.shape[0]
+    last_face = lists.pop(2)[0:1]
     v[...] = joined(own_spread[...], ghost_spread[...]) + told(far, lists)
 
     one, two = lists[0], lists[1]
@@ -426,7 +469,6 @@
     ends[1, 2 * TILE - 1 : 2 * TILE] = last_east
     blank = jnp.zeros((6, lanes), jnp.float32)
     stack = lambda p, q: jnp.concatenate([p, q, blank], axis=0)
-    last_face = joined(own_edge[0:1], edge[0:1])
     rim_diagonal, rim_north = completed(
         levels, group,
         stack(west_list[5:6], east_list[5:6] + east_list[8:9] * last_face),
@@ -442,13 +484,14 @@
     rim[5] = rim_upper
     rim[6] = lane_roll(rim_upper, 1)
 
+    kept = {}
     for at in range(0, columns, TILE):
-        f[pl.ds(EDGE + at, TILE)] = apply_tile(levels, v, statics, ends, at)[1]
+        f[pl.ds(EDGE + at, TILE)] = apply_tile(levels, v, statics, ends, at, kept)[1]
     apply_rim(levels, columns, v, f, rim)
-    m = [0.0] * 4
+    m, kept = [0.0] * 4, {}
     for at in range(0, columns, TILE):
         tile = pl.ds(at, TILE)
-        second = apply_tile(levels, f, statics, ends, at)[1]
+        second = apply_tile(levels, f, statics, ends, at, kept)[1]
         w = jnp.where(coefficient(statics, 7, at) > 0.5, second, v[pl.ds(EDGE + at, TILE)])
         image[tile] = w
         for k in range(4):
@@ -492,10 +535,10 @@
     v, f, sums = rest[1 + others :]
     v[...] = spread[...] + told(far, received)
     own = own_lanes(rows, levels)
-    mixed, last = [], []
+    mixed, last, kept = [], [], {}
     for at in range(0, columns, TILE):
         tile = pl.ds(at, TILE)
-        q, b = apply_tile(levels, v, statics, ends, at)
+        q, b = apply_tile(levels, v, statics, ends, at, kept)
         f[pl.ds(EDGE + at, TILE)] = b
         q, b, ocean = q[:, own], b[:, own], own_part[7, tile]
         mixed.append(image[tile, own] * q)
@@ -509,8 +552,9 @@
     statics = own_part, ghost_part, patches
     z = outs[4]
     own = own_lanes(rows, levels)
+    kept = {}
     for at in range(0, columns, TILE):
-        second = apply_tile(levels, f, statics, ends, at)[1]
+        second = apply_tile(levels, f, statics, ends, at, kept)[1]
         tile = pl.ds(at, TILE)
         z[tile] = jnp.where(coefficient(statics, 7, at) > 0.5, second, again[pl.ds(EDGE + at, TILE)])
     group = REACH * levels
@@ -596,44 +640,49 @@
     to_band = lambda x, pairs: lax.ppermute(x, ("lon", "lat"), pairs)
     got_second, got_first = to_band(second, lat_b), to_band(first, lat_a)
 
-    own_field, made, own_edge, to_first, to_second = call(
+    own_field, mine = call(
+        functools.partial(field_kernel, rows, levels), [(columns, flat), (8, flat)], noise, weights
+    )
+    made, own_edge, to_first, to_second = call(
         functools.partial(own_kernel, rows, levels, columns),
-        [(columns, flat), (5, columns, flat), (8, flat), (16, flat), (16, flat)],
-        noise, kappa2, conduct, land, weights,
+        [(5, columns, flat), (8, flat), (8, flat), (8, flat)],
+        kappa2, conduct, land, own_field,
     )
     lon_a, lon_b = lon_perms(count)
 
-    def exchange(one, two):
-        wide = two.shape[1]
-        got_one = lax.ppermute(one, "lon", lon_a)
-        (two,) = call(functools.partial(chip_kernel, rho, columns), [two.shape], two, got_one)
-        got_two = lax.ppermute(two, "lon", lon_b)
+    def farther(two, got_two):
         if count == 4:
-            return [got_one, got_two]
-        (four,) = call(functools.partial(quad_kernel, rho, columns), [(8, wide)], two, got_two)
-        return [got_one, got_two] + [
-            lax.ppermute(four, "lon", [(i, (i + d) % count) for i in range(count)]) for d in range(4, count, 4)
-        ]
-
-    lists = exchange(to_first, to_second)
+            return []
+        (four,) = call(functools.partial(quad_kernel, rho, columns), [(8, two.shape[1])], two, got_two)
+        return [lax.ppermute(four, "lon", [(i, (i + d) % count) for i in range(count)]) for d in range(4, count, 4)]
+
+    got = lax.ppermute(mine, "lon", lon_a)
+    (two,) = call(functools.partial(chip_kernel, rho, columns), [(16, flat)], mine, to_second, got)
+    got_two = lax.ppermute(two, "lon", lon_b)
+    (got_one,) = call(list_kernel, [(16, flat)], got, lax.ppermute(to_first, "lon", lon_a))
+    lists = [got_one, got_two] + farther(two, got_two)
     own_spread, own_part = call(
         functools.partial(near_kernel, levels), [(tall, flat), (8, columns, flat)], near, own_field, made
     )
-    heights = sum(x.shape[0] for x in lists)
-    side_second, side_first = call(functools.partial(forward_kernel, group), [(heights, group)] * 2, *lists)
+    sent = (*lists[:2], own_edge, *lists[2:])
+    heights = 2 * LIST + 2 + sum(x.shape[0] for x in lists[2:])
+    side_second, side_first = call(functools.partial(forward_kernel, group), [(heights, group)] * 2, *sent)
     side_second, side_first = to_band(side_second, lat_b), to_band(side_first, lat_a)
-    ghost_spread, ghost_part, patches, edge = call(
+    ghost_spread, ghost_part, patches = call(
         functools.partial(ghost_kernel, levels, columns),
-        [(tall, 2 * group), (8, columns, 2 * group), (3, columns, group), (8, 2 * group)],
+        [(tall, 2 * group), (8, columns, 2 * group), (3, columns, group)],
         got_second, got_first, near, made, own_part,
     )
     precond, image, ends, rim, to_first, to_second = call(
         functools.partial(first_kernel, rows, levels, columns, others),
         [(tall, lanes), (columns, lanes), (7, 2 * TILE, lanes), (7, 8, lanes), (8, lanes), (8, lanes)],
-        own_spread, own_edge, ghost_spread, own_part, ghost_part, patches, edge, far, columns_of, side_second, side_first, *lists,
+        own_spread, own_edge, ghost_spread, own_part, ghost_part, patches, far, columns_of, side_second, side_first, *lists,
         scratch=[(tall, lanes)],
     )
-    lists = exchange(to_first, to_second)
+    got_one = lax.ppermute(to_first, "lon", lon_a)
+    (two,) = call(functools.partial(again_kernel, rho, columns), [(8, lanes)], to_second, got_one)
+    got_two = lax.ppermute(two, "lon", lon_b)
+    lists = [got_one, got_two] + farther(two, got_two)
     spread, sums = call(
         functools.partial(between_kernel, rows, levels, columns),
         [(tall, lanes), (8, 128)],

time: 35.9 us -> 35.1 us (0.978)
  waiting for transfers between devices: 13.5 us -> 12.5 us
  starting transfers between devices: 12.3 us -> 12.7 us
    ppermute x4 -> x5, waiting for transfers between devices: 5.95 us -> 4.81 us  [the longest x2 2.38 us: body(): got_two = lax.ppermute(two, 'lon', lon_b)]
    ppermute x4 -> x5, starting transfers between devices: 2.79 us -> 3.07 us  [the longest x2 2.65 us: body(): got_two = lax.ppermute(two, 'lon', lon_b)]
    pallas_call x10 -> x12, Pallas kernels: 6.46 us -> 6.42 us  [call(): pl.pallas_call(kernel, out_shape=[pltpu.VMEM(s, jnp.float32) for s in out...]
  transfers between devices with their start and end apart: 12 -> 13, of which waited for: 9 -> 10; matrix products, arithmetic and copies ran while one was open for 0% -> 0% of each run, Pallas kernels for 12% -> 13%
where the time goes in v10:
time: 35.1 us; the launch traced here: 35 us
  starting transfers between devices  12.7 us (36%)
  waiting for transfers between devices  12.5 us (36%)
  Pallas kernels  9.07 us (26%)
  between operations  0.74 us (2%)
    ppermute x4, starting transfers between devices, body(): to_band = lambda x, pairs: lax.ppermute(x, ('lon', 'lat'), pairs)  6.42 us
    pallas_call x12, Pallas kernels, call(): pl.pallas_call(kernel, out_shape=[pltpu.VMEM(s, jnp.float32) for s in out...  6.42 us
    ppermute x2, waiting for transfers between devices, summed(): x = x + lax.ppermute(x, ('lon', 'lat'), pairs)  3.62 us
    ppermute x2, starting transfers between devices, body(): got_two = lax.ppermute(two, 'lon', lon_b)  2.65 us
    ppermute x2, waiting for transfers between devices, body(): got_two = lax.ppermute(two, 'lon', lon_b)  2.38 us
    ppermute x1, waiting for transfers between devices, summed(): x = x + lax.ppermute(x, 'lon', [(i, i ^ step ^ 1) for i in range(count)])  1.77 us
    ppermute x2, starting transfers between devices, summed(): x = x + lax.ppermute(x, ('lon', 'lat'), pairs)  1.73 us
    pallas_call x1, Pallas kernels, body(): pl.pallas_call(functools.partial(band_kernel, rows, levels), out_shape=[p...  1.65 us
  transfers between devices with their start and end apart: 13, of which 10 were waited for; matrix products, arithmetic and copies ran while one was open for 0% of the time, Pallas kernels for 13%

profile of v10, /device:TPU:0, one launch (start us, length us, event | category | flops | bytes accessed | tf_op | source)
XLA Modules:
  0.0 35.0 jit_solution(17124615125927246974)
XLA Ops:
  0.6 1.7 %band_kernel.1 = (f32[17,32,128]{2,1,0:T(8,128)S(1)}, f32[17,32,128]{2,1,0:T(8,128)S(1)}, f32[512,128]{1,0:T(8,128)S(1)}, f32[512,128]{1,0:T(8,128)S(1)}, f32[3,...) custom-call(f32[512,128]{1,0:T(8,128)} %bitcast.7, ...), custom_call_target="tpu_custom_call" | custom-call | tf_op jit(solution)/shard_map/band_kernel/pallas_call | solution.py:630
  2.3 0.6 %collective-permute-start = (f32[17,32,128]{2,1,0:T(8,128)S(1)}, f32[17,32,128]{2,1,0:T(8,128)S(1)}, u32[]{:S(2)}, u32[]{:S(2)}) collective-permute-start(f32[17,32,128]{2,1,0:T(8,128)S(1)} %get-tuple-element.52), channel_id=1, source_target_pairs={{0,4},{1,2},{2,1},{3,7},{4,0},{5,6},{6,5},{7,3},{8,12},{9,10},{10,... | collective-permute-start | bytes 835592 | tf_op jit(solution)/shard_map/ppermute | solution.py:640
  2.9 4.1 %collective-permute-start.1 = (f32[17,32,128]{2,1,0:T(8,128)S(1)}, f32[17,32,128]{2,1,0:T(8,128)S(1)}, u32[]{:S(2)}, u32[]{:S(2)}) collective-permute-start(f32[17,32,128]{2,1,0:T(8,128)S(1)} %get-tuple-element.53), channel_id=1, source_target_pairs={{0,1},{1,0},{2,3},{3,2},{4,5},{5,4},{6,7},{7,6},{8,9},{9,8},{10,11... | collective-permute-start | bytes 835592 | tf_op jit(solution)/shard_map/ppermute | solution.py:640
  7.0 0.3 field_kernel.1
  7.3 0.0 collective-permute-start.2
  7.3 0.8 %own_kernel.1 = (f32[5,128,512]{2,1,0:T(8,128)S(1)}, f32[8,512]{1,0:T(8,128)S(1)}, f32[8,512]{1,0:T(8,128)S(1)}, f32[8,512]{1,0:T(8,128)S(1)}) custom-call(f32[512,128]{1,0:T(8,128)S(1)} %get-tuple-element.46.kappa2, f32[3,512,128]{2,1,0:T(8,128)S(1)} %get-tuple-element.47.conduct, s32[512,128]{1,0:T(8,128)S(1)} %get-tuple-element.48.land, ...), custom_call_target="tpu_custom_call" | custom-call | tf_op jit(solution)/shard_map/own_kernel/pallas_call | solution.py:130
  8.1 0.4 %collective-permute-done.2.moments.got = f32[8,512]{1,0:T(8,128)S(1)} collective-permute-done((f32[8,512]{1,0:T(8,128)S(1)}, f32[8,512]{1,0:T(8,128)S(1)}, u32[]{:S(2)}, u32[]{:S(2)}) %collective-permute-start.2) | collective-permute-done | bytes 16416 | tf_op jit(solution)/shard_map/ppermute | solution.py:659
  8.5 1.3 %collective-permute-start.4 = (f32[16,512]{1,0:T(8,128)S(1)}, f32[16,512]{1,0:T(8,128)S(1)}, u32[]{:S(2)}, u32[]{:S(2)}) collective-permute-start(f32[16,512]{1,0:T(8,128)S(1)} %chip_kernel.1), channel_id=1, source_target_pairs={{0,12},{4,8},{8,4},{12,0},{1,13},{5,9},{9,5},{13,1},{2,14},{6,10},... | collective-permute-start | bytes 98312 | tf_op jit(solution)/shard_map/ppermute | solution.py:661
  9.9 0.3 collective-permute-start.3
  10.2 0.8 %collective-permute-done.3.edges = f32[8,512]{1,0:T(8,128)S(1)} collective-permute-done((f32[8,512]{1,0:T(8,128)S(1)}, f32[8,512]{1,0:T(8,128)S(1)}, u32[]{:S(2)}, u32[]{:S(2)}) %collective-permute-start.3) | collective-permute-done | bytes 16416 | tf_op jit(solution)/shard_map/ppermute | solution.py:662
  11.1 0.9 %collective-permute-done.4.refs_1_.rest_1_ = f32[16,512]{1,0:T(8,128)S(1)} collective-permute-done((f32[16,512]{1,0:T(8,128)S(1)}, f32[16,512]{1,0:T(8,128)S(1)}, u32[]{:S(2)}, u32[]{:S(2)}) %collective-permute-start.4) | collective-permute-done | bytes 32800 | tf_op jit(solution)/shard_map/ppermute | solution.py:661
  12.0 0.5 %collective-permute-start.5 = (f32[24,128]{1,0:T(8,128)S(1)}, f32[24,128]{1,0:T(8,128)S(1)}, u32[]{:S(2)}, u32[]{:S(2)}) collective-permute-start(f32[24,128]{1,0:T(8,128)S(1)} %get-tuple-element.63), channel_id=1, source_target_pairs={{0,4},{1,2},{2,1},{3,7},{4,0},{5,6},{6,5},{7,3},{8,12},{9,10},{10,... | collective-permute-start | bytes 36872 | tf_op jit(solution)/shard_map/ppermute | solution.py:640
  12.5 1.2 %collective-permute-start.6 = (f32[24,128]{1,0:T(8,128)S(1)}, f32[24,128]{1,0:T(8,128)S(1)}, u32[]{:S(2)}, u32[]{:S(2)}) collective-permute-start(f32[24,128]{1,0:T(8,128)S(1)} %get-tuple-element.64), channel_id=1, source_target_pairs={{0,1},{1,0},{2,3},{3,2},{4,5},{5,4},{6,7},{7,6},{8,9},{9,8},{10,11... | collective-permute-start | bytes 36872 | tf_op jit(solution)/shard_map/ppermute | solution.py:640
  13.7 0.7 %near_kernel.1 = (f32[144,512]{1,0:T(8,128)S(1)}, f32[8,128,512]{2,1,0:T(8,128)S(1)}) custom-call(f32[144,128]{1,0:T(8,128)S(1)} %get-tuple-element.42.near, f32[128,512]{1,0:T(8,128)S(1)} %get-tuple-element.45.field, f32[5,128,512]{2,1,0:T(8,128)S(1)} %get-tuple-element.49.made), custom_call_target="tpu_custom_call" | custom-call | tf_op jit(solution)/shard_map/near_kernel/pallas_call | solution.py:130
  14.4 0.0 collective-permute-done.got_second
  14.4 0.0 collective-permute-done.1.got_first
  14.5 0.5 %ghost_kernel.1 = (f32[144,256]{1,0:T(8,128)S(1)}, f32[8,128,256]{2,1,0:T(8,128)S(1)}, f32[3,128,128]{2,1,0:T(8,128)S(1)}) custom-call(f32[17,32,128]{2,1,0:T(8,128)S(1)} %collective-permute-done.got_second, f32[17,32,128]{2,1,0:T(8,128)S(1)} %collective-permute-done.1.got_first, f32[144,128]{1,0:T(8,128)S(1)} %get-tuple-element.42.near, ...), custom_call_target="tpu_custom_call" | custom-call | tf_op jit(solution)/shard_map/ghost_kernel/pallas_call | solution.py:130
  14.9 0.0 collective-permute-done.5.side_second
  14.9 1.2 %collective-permute-done.6.side_first = f32[24,128]{1,0:T(8,128)S(1)} collective-permute-done((f32[24,128]{1,0:T(8,128)S(1)}, f32[24,128]{1,0:T(8,128)S(1)}, u32[]{:S(2)}, u32[]{:S(2)}) %collective-permute-start.6) | collective-permute-done | bytes 12320 | tf_op jit(solution)/shard_map/ppermute | solution.py:640
  16.2 1.2 %first_kernel.1 = (f32[144,768]{1,0:T(8,128)S(1)}, f32[128,768]{1,0:T(8,128)S(1)}, f32[7,16,768]{2,1,0:T(8,128)S(1)}, f32[7,8,768]{2,1,0:T(8,128)S(1)}, f32[8,768]{1,0:T(8,128)S(1)}, /*index=5*/f32[8,768]{1,0:T(8,128)S(1)}) custom-call(f32[144,512]{1,0:T(8,128)S(1)} %get-tuple-element.50.own_spread, f32[8,512]{1,0:T(8,128)S(1)} %get-tuple-element.51.refs_2_.own_edge, ...), custom_call_target="tpu_custom_call" | custom-call | tf_op jit(solution)/shard_map/first_kernel/pallas_call | solution.py:130
  17.4 0.1 collective-permute-start.7
  17.5 1.2 %collective-permute-done.7.got.rest_0_ = f32[8,768]{1,0:T(8,128)S(1)} collective-permute-done((f32[8,768]{1,0:T(8,128)S(1)}, f32[8,768]{1,0:T(8,128)S(1)}, u32[]{:S(2)}, u32[]{:S(2)}) %collective-permute-start.7) | collective-permute-done | bytes 24608 | tf_op jit(solution)/shard_map/ppermute | solution.py:682
  18.7 1.3 %collective-permute-start.8 = (f32[8,768]{1,0:T(8,128)S(1)}, f32[8,768]{1,0:T(8,128)S(1)}, u32[]{:S(2)}, u32[]{:S(2)}) collective-permute-start(f32[8,768]{1,0:T(8,128)S(1)} %again_kernel.1), channel_id=1, source_target_pairs={{0,12},{4,8},{8,4},{12,0},{1,13},{5,9},{9,5},{13,1},{2,14},{6,10},... | collective-permute-start | bytes 73736 | tf_op jit(solution)/shard_map/ppermute | solution.py:684
  20.0 0.5 %between_kernel.1 = (f32[144,768]{1,0:T(8,128)S(1)}, f32[8,128]{1,0:T(8,128)S(1)}) custom-call(f32[144,128]{1,0:T(8,128)S(1)} %get-tuple-element.42.near, f32[128,512]{1,0:T(8,128)S(1)} %get-tuple-element.45.field, f32[144,768]{1,0:T(8,128)S(1)} %get-tuple-element.65.precond, f32[128,768]{1,0:T(8,128)S(1)} %get-tuple-element.66.image), custom_call_target="tpu_custom_call" | custom-call | tf_op jit(solution)/shard_map/between_kernel/pallas_call | solution.py:130
  20.5 1.5 %collective-permute-done.8.rest_1_ = f32[8,768]{1,0:T(8,128)S(1)} collective-permute-done((f32[8,768]{1,0:T(8,128)S(1)}, f32[8,768]{1,0:T(8,128)S(1)}, u32[]{:S(2)}, u32[]{:S(2)}) %collective-permute-start.8) | collective-permute-done | bytes 24608 | tf_op jit(solution)/shard_map/ppermute | solution.py:684
  22.0 0.7 %second_kernel.1 = (f32[144,768]{1,0:T(8,128)S(1)}, f32[144,768]{1,0:T(8,128)S(1)}, f32[8,128]{1,0:T(8,128)S(1)}) custom-call(f32[144,768]{1,0:T(8,128)S(1)} %get-tuple-element.67.spread, f32[8,128]{1,0:T(8,128)S(1)} %get-tuple-element.68.early, f32[128,768]{1,0:T(8,128)S(1)} %get-tuple-element.66.image, f32[8,128,512]{2,1,0:T(8,128)S(1)} %get-tuple-element.54.own.own_part, ...), custom_call_target="tpu_custom_call" | custom-call | tf_op jit(solution)/shard_map/second_kernel/pallas_call | solution.py:130
  22.7 0.2 collective-permute-start.9
  23.0 1.0 %collective-permute-done.9 = f32[8,128]{1,0:T(8,128)S(1)} collective-permute-done((f32[8,128]{1,0:T(8,128)S(1)}, f32[8,128]{1,0:T(8,128)S(1)}, u32[]{:S(2)}, u32[]{:S(2)}) %collective-permute-start.9) | collective-permute-done | bytes 4128 | tf_op jit(solution)/shard_map/ppermute | solution.py:605
  24.0 1.3 %collective-permute-start.10 = (f32[8,128]{1,0:T(8,128)S(1)}, f32[8,128]{1,0:T(8,128)S(1)}, u32[]{:S(2)}, u32[]{:S(2)}) collective-permute-start(f32[8,128]{1,0:T(8,128)S(1)} %add.12), channel_id=1, source_target_pairs={{0,12},{4,8},{8,4},{12,0},{1,13},{5,9},{9,5},{13,1},{2,14},{6,10},... | collective-permute-start | bytes 12296 | tf_op jit(solution)/shard_map/ppermute | solution.py:607
  25.2 1.8 %collective-permute-done.10 = f32[8,128]{1,0:T(8,128)S(1)} collective-permute-done((f32[8,128]{1,0:T(8,128)S(1)}, f32[8,128]{1,0:T(8,128)S(1)}, u32[]{:S(2)}, u32[]{:S(2)}) %collective-permute-start.10) | collective-permute-done | bytes 4128 | tf_op jit(solution)/shard_map/ppermute | solution.py:607
  27.0 1.0 %collective-permute-start.11 = (f32[8,128]{1,0:T(8,128)S(1)}, f32[8,128]{1,0:T(8,128)S(1)}, u32[]{:S(2)}, u32[]{:S(2)}) collective-permute-start(f32[8,128]{1,0:T(8,128)S(1)} %add.13), channel_id=1, source_target_pairs={{0,5},{1,4},{2,7},{3,6},{4,1},{5,0},{6,3},{7,2},{8,13},{9,12},{10,... | collective-permute-start | bytes 12296 | tf_op jit(solution)/shard_map/ppermute | solution.py:610
  28.0 2.1 %collective-permute-done.11 = f32[8,128]{1,0:T(8,128)S(1)} collective-permute-done((f32[8,128]{1,0:T(8,128)S(1)}, f32[8,128]{1,0:T(8,128)S(1)}, u32[]{:S(2)}, u32[]{:S(2)}) %collective-permute-start.11) | collective-permute-done | bytes 4128 | tf_op jit(solution)/shard_map/ppermute | solution.py:610
  30.1 0.8 %collective-permute-start.12 = (f32[8,128]{1,0:T(8,128)S(1)}, f32[8,128]{1,0:T(8,128)S(1)}, u32[]{:S(2)}, u32[]{:S(2)}) collective-permute-start(f32[8,128]{1,0:T(8,128)S(1)} %add.14), channel_id=1, source_target_pairs={{0,6},{1,7},{2,4},{3,5},{4,2},{5,3},{6,0},{7,1},{8,14},{9,15},{10,... | collective-permute-start | bytes 12296 | tf_op jit(solution)/shard_map/ppermute | solution.py:610
  30.8 1.6 %turn_kernel.1 = (f32[512,128]{1,0:T(8,128)S(1)}, f32[512,128]{1,0:T(8,128)S(1)}, f32[512,128]{1,0:T(8,128)S(1)}, f32[512,128]{1,0:T(8,128)S(1)}, f32[128,768]{1,0:T(8,128)}) custom-call(f32[144,768]{1,0:T(8,128)S(1)} %get-tuple-element.65.precond, f32[128,768]{1,0:T(8,128)S(1)} %get-tuple-element.66.image, f32[144,768]{1,0:T(8,128)S(1)} %get-tuple-element.74.again, ...), custom_call_target="tpu_custom_call" | custom-call | tf_op jit(solution)/shard_map/turn_kernel/pallas_call | solution.py:130
  32.4 1.6 %collective-permute-done.12 = f32[8,128]{1,0:T(8,128)S(1)} collective-permute-done((f32[8,128]{1,0:T(8,128)S(1)}, f32[8,128]{1,0:T(8,128)S(1)}, u32[]{:S(2)}, u32[]{:S(2)}) %collective-permute-start.12) | collective-permute-done | bytes 4128 | tf_op jit(solution)/shard_map/ppermute | solution.py:610
  34.0 1.0 %combine_kernel.1 = (f32[512,128]{1,0:T(8,128)}, f32[512,128]{1,0:T(8,128)}) custom-call(f32[8,128]{1,0:T(8,128)S(1)} %add.15.sums, f32[512,128]{1,0:T(8,128)S(1)} %get-tuple-element.43.noise, f32[512,128]{1,0:T(8,128)S(1)} %get-tuple-element.76.precond, f32[512,128]{1,0:T(8,128)S(1)} %get-tuple-element.77.image, f32[512,128]{1,0:T(8,128)S(1)} %get-tuple-element.78.again, ...), custom_call_target="tpu_custom_call" | custom-call | tf_op jit(solution)/shard_map/combine_kernel/pallas_call | solution.py:703
  (8 shorter events, 0.1 us)
Async XLA Ops:
  2.3 12.1 %collective-permute-start = (f32[17,32,128]{2,1,0:T(8,128)S(1)}, f32[17,32,128]{2,1,0:T(8,128)S(1)}, u32[]{:S(2)}, u32[]{:S(2)}) collective-permute-start(f32[17,32,128]{2,1,0:T(8,128)S(1)} %get-tuple-element.52), channel_id=1, source_target_pairs={{0,4},{1,2},{2,1},{3,7},{4,0},{5,6},{6,5},{7,3},{8,12},{9,10},{10,... | collective-permute-start | bytes 835592 | tf_op jit(solution)/shard_map/ppermute | solution.py:640
  2.9 11.6 %collective-permute-start.1 = (f32[17,32,128]{2,1,0:T(8,128)S(1)}, f32[17,32,128]{2,1,0:T(8,128)S(1)}, u32[]{:S(2)}, u32[]{:S(2)}) collective-permute-start(f32[17,32,128]{2,1,0:T(8,128)S(1)} %get-tuple-element.53), channel_id=1, source_target_pairs={{0,1},{1,0},{2,3},{3,2},{4,5},{5,4},{6,7},{7,6},{8,9},{9,8},{10,11... | collective-permute-start | bytes 835592 | tf_op jit(solution)/shard_map/ppermute | solution.py:640
  7.3 1.2 %collective-permute-start.2 = (f32[8,512]{1,0:T(8,128)S(1)}, f32[8,512]{1,0:T(8,128)S(1)}, u32[]{:S(2)}, u32[]{:S(2)}) collective-permute-start(f32[8,512]{1,0:T(8,128)S(1)} %get-tuple-element.60.own), channel_id=1, source_target_pairs={{0,4},{4,0},{8,12},{12,8},{1,5},{5,1},{9,13},{13,9},{2,6},{6,2},{1... | collective-permute-start | bytes 49160 | tf_op jit(solution)/shard_map/ppermute | solution.py:659
  8.5 3.4 %collective-permute-start.4 = (f32[16,512]{1,0:T(8,128)S(1)}, f32[16,512]{1,0:T(8,128)S(1)}, u32[]{:S(2)}, u32[]{:S(2)}) collective-permute-start(f32[16,512]{1,0:T(8,128)S(1)} %chip_kernel.1), channel_id=1, source_target_pairs={{0,12},{4,8},{8,4},{12,0},{1,13},{5,9},{9,5},{13,1},{2,14},{6,10},... | collective-permute-start | bytes 98312 | tf_op jit(solution)/shard_map/ppermute | solution.py:661
  9.9 1.2 %collective-permute-start.3 = (f32[8,512]{1,0:T(8,128)S(1)}, f32[8,512]{1,0:T(8,128)S(1)}, u32[]{:S(2)}, u32[]{:S(2)}) collective-permute-start(f32[8,512]{1,0:T(8,128)S(1)} %get-tuple-element.61), channel_id=1, source_target_pairs={{0,4},{4,0},{8,12},{12,8},{1,5},{5,1},{9,13},{13,9},{2,6},{6,2},{1... | collective-permute-start | bytes 49160 | tf_op jit(solution)/shard_map/ppermute | solution.py:662
  12.0 3.0 %collective-permute-start.5 = (f32[24,128]{1,0:T(8,128)S(1)}, f32[24,128]{1,0:T(8,128)S(1)}, u32[]{:S(2)}, u32[]{:S(2)}) collective-permute-start(f32[24,128]{1,0:T(8,128)S(1)} %get-tuple-element.63), channel_id=1, source_target_pairs={{0,4},{1,2},{2,1},{3,7},{4,0},{5,6},{6,5},{7,3},{8,12},{9,10},{10,... | collective-permute-start | bytes 36872 | tf_op jit(solution)/shard_map/ppermute | solution.py:640
  12.5 3.7 %collective-permute-start.6 = (f32[24,128]{1,0:T(8,128)S(1)}, f32[24,128]{1,0:T(8,128)S(1)}, u32[]{:S(2)}, u32[]{:S(2)}) collective-permute-start(f32[24,128]{1,0:T(8,128)S(1)} %get-tuple-element.64), channel_id=1, source_target_pairs={{0,1},{1,0},{2,3},{3,2},{4,5},{5,4},{6,7},{7,6},{8,9},{9,8},{10,11... | collective-permute-start | bytes 36872 | tf_op jit(solution)/shard_map/ppermute | solution.py:640
  17.4 1.3 %collective-permute-start.7 = (f32[8,768]{1,0:T(8,128)S(1)}, f32[8,768]{1,0:T(8,128)S(1)}, u32[]{:S(2)}, u32[]{:S(2)}) collective-permute-start(f32[8,768]{1,0:T(8,128)S(1)} %get-tuple-element.71), channel_id=1, source_target_pairs={{0,4},{4,0},{8,12},{12,8},{1,5},{5,1},{9,13},{13,9},{2,6},{6,2},{1... | collective-permute-start | bytes 73736 | tf_op jit(solution)/shard_map/ppermute | solution.py:682
  18.7 3.3 %collective-permute-start.8 = (f32[8,768]{1,0:T(8,128)S(1)}, f32[8,768]{1,0:T(8,128)S(1)}, u32[]{:S(2)}, u32[]{:S(2)}) collective-permute-start(f32[8,768]{1,0:T(8,128)S(1)} %again_kernel.1), channel_id=1, source_target_pairs={{0,12},{4,8},{8,4},{12,0},{1,13},{5,9},{9,5},{13,1},{2,14},{6,10},... | collective-permute-start | bytes 73736 | tf_op jit(solution)/shard_map/ppermute | solution.py:684
  22.7 1.2 %collective-permute-start.9 = (f32[8,128]{1,0:T(8,128)S(1)}, f32[8,128]{1,0:T(8,128)S(1)}, u32[]{:S(2)}, u32[]{:S(2)}) collective-permute-start(f32[8,128]{1,0:T(8,128)S(1)} %get-tuple-element.73), channel_id=1, source_target_pairs={{0,4},{4,0},{8,12},{12,8},{1,5},{5,1},{9,13},{13,9},{2,6},{6,2},{1... | collective-permute-start | bytes 12296 | tf_op jit(solution)/shard_map/ppermute | solution.py:605
  24.0 3.0 %collective-permute-start.10 = (f32[8,128]{1,0:T(8,128)S(1)}, f32[8,128]{1,0:T(8,128)S(1)}, u32[]{:S(2)}, u32[]{:S(2)}) collective-permute-start(f32[8,128]{1,0:T(8,128)S(1)} %add.12), channel_id=1, source_target_pairs={{0,12},{4,8},{8,4},{12,0},{1,13},{5,9},{9,5},{13,1},{2,14},{6,10},... | collective-permute-start | bytes 12296 | tf_op jit(solution)/shard_map/ppermute | solution.py:607
  27.0 3.0 %collective-permute-start.11 = (f32[8,128]{1,0:T(8,128)S(1)}, f32[8,128]{1,0:T(8,128)S(1)}, u32[]{:S(2)}, u32[]{:S(2)}) collective-permute-start(f32[8,128]{1,0:T(8,128)S(1)} %add.13), channel_id=1, source_target_pairs={{0,5},{1,4},{2,7},{3,6},{4,1},{5,0},{6,3},{7,2},{8,13},{9,12},{10,... | collective-permute-start | bytes 12296 | tf_op jit(solution)/shard_map/ppermute | solution.py:610
  30.1 3.9 %collective-permute-start.12 = (f32[8,128]{1,0:T(8,128)S(1)}, f32[8,128]{1,0:T(8,128)S(1)}, u32[]{:S(2)}, u32[]{:S(2)}) collective-permute-start(f32[8,128]{1,0:T(8,128)S(1)} %add.14), channel_id=1, source_target_pairs={{0,6},{1,7},{2,4},{3,5},{4,2},{5,3},{6,0},{7,1},{8,14},{9,15},{10,... | collective-permute-start | bytes 12296 | tf_op jit(solution)/shard_map/ppermute | solution.py:610

commit v11 on v10

--- a/solution.py
+++ b/solution.py
@@ -143,7 +143,7 @@
 
 
 def band_kernel(rows, levels, *refs):
-    sources, (second, first), copies, sems = refs[:8], refs[8:10], refs[10:18], refs[18]
+    sources, (first, second), copies, sems = refs[:8], refs[8:10], refs[10:18], refs[18]
     order = (0, 3, 2, 1, 4, 5, 6, 7)
     moves = [pltpu.make_async_copy(sources[k], copies[k], sems.at[k]) for k in order]
     for move in moves:
@@ -248,7 +248,7 @@
     out[...] = jnp.concatenate([moments[0:MOMENTS], edges[...], jnp.zeros((4, edges.shape[1]), jnp.float32)], axis=0)
 
 
-def ghost_kernel(levels, columns, got_second, got_first, near, made, own, spread, ghosts, patches):
+def ghost_kernel(levels, columns, got_first, got_second, near, made, own, spread, ghosts, patches):
     lat_odd = lax.axis_index("lat") % 2
     group = REACH * levels
 
@@ -309,7 +309,7 @@
 
 
 def forward_kernel(group, *refs):
-    (one, two, edge), more, (second, first) = refs[:3], refs[3:-2], refs[-2:]
+    (one, two, edge), more, (first, second) = refs[:3], refs[3:-2], refs[-2:]
     odd = lax.axis_index("lat") % 2
     whole_rows = [one[0:LIST], two[0:LIST], edge[0:2]] + [x[...] for x in more]
     x = jnp.concatenate(whole_rows, axis=0)
@@ -436,7 +436,7 @@
 
 def first_kernel(
     rows, levels, columns, others,
-    own_spread, own_edge, ghost_spread, own_part, ghost_part, patches, far, weights, side_second, side_first, *rest,
+    own_spread, own_edge, ghost_spread, own_part, ghost_part, patches, far, weights, side_first, side_second, *rest,
 ):
     statics = own_part, ghost_part, patches
     received = rest[: 1 + others]
@@ -627,7 +627,7 @@
 
     sources = (noise, kappa2, conduct, land, near, far, weights, columns_of)
     planes = (PLANES, levels, columns)
-    second, first, noise, kappa2, conduct, land, near, far, weights, columns_of = pl.pallas_call(
+    first, second, noise, kappa2, conduct, land, near, far, weights, columns_of = pl.pallas_call(
         functools.partial(band_kernel, rows, levels),
         out_shape=[pltpu.VMEM(planes, jnp.float32)] * 2 + [pltpu.VMEM(x.shape, x.dtype) for x in sources],
         in_specs=[pl.BlockSpec(memory_space=pltpu.HBM)] * len(sources),
@@ -666,17 +666,17 @@
     )
     sent = (*lists[:2], own_edge, *lists[2:])
     heights = 2 * LIST + 2 + sum(x.shape[0] for x in lists[2:])
-    side_second, side_first = call(functools.partial(forward_kernel, group), [(heights, group)] * 2, *sent)
+    side_first, side_second = call(functools.partial(forward_kernel, group), [(heights, group)] * 2, *sent)
     side_second, side_first = to_band(side_second, lat_b), to_band(side_first, lat_a)
     ghost_spread, ghost_part, patches = call(
         functools.partial(ghost_kernel, levels, columns),
         [(tall, 2 * group), (8, columns, 2 * group), (3, columns, group)],
-        got_second, got_first, near, made, own_part,
+        got_first, got_second, near, made, own_part,
     )
     precond, image, ends, rim, to_first, to_second = call(
         functools.partial(first_kernel, rows, levels, columns, others),
         [(tall, lanes), (columns, lanes), (7, 2 * TILE, lanes), (7, 8, lanes), (8, lanes), (8, lanes)],
-        own_spread, own_edge, ghost_spread, own_part, ghost_part, patches, far, columns_of, side_second, side_first, *lists,
+        own_spread, own_edge, ghost_spread, own_part, ghost_part, patches, far, columns_of, side_first, side_second, *lists,
         scratch=[(tall, lanes)],
     )
     got_one = lax.ppermute(to_first, "lon", lon_a)

time: 35.1 us -> 34.4 us (0.980)
  waiting for transfers between devices: 12.5 us -> 9.39 us
  starting transfers between devices: 12.7 us -> 15.1 us
    ppermute x2, starting transfers between devices: 1.73 us -> 3.53 us  [summed(): x = x + lax.ppermute(x, ('lon', 'lat'), pairs)]
    ppermute x2, waiting for transfers between devices: 3.62 us -> 1.99 us  [summed(): x = x + lax.ppermute(x, ('lon', 'lat'), pairs)]
    ppermute x4, waiting for transfers between devices: 1.24 us -> 0.26 us  [body(): to_band = lambda x, pairs: lax.ppermute(x, ('lon', 'lat'), pairs)]
    ppermute x1, starting transfers between devices: 0.01 us -> 0.51 us  [body(): got = lax.ppermute(mine, 'lon', lon_a)]
where the time goes in v11:
time: 34.4 us; the launch traced here: 34.2 us
  starting transfers between devices  15.1 us (44%)
  waiting for transfers between devices  9.39 us (27%)
  Pallas kernels  9.06 us (26%)
  between operations  0.72 us (2%)
    pallas_call x12, Pallas kernels, call(): pl.pallas_call(kernel, out_shape=[pltpu.VMEM(s, jnp.float32) for s in out...  6.42 us
    ppermute x4, starting transfers between devices, body(): to_band = lambda x, pairs: lax.ppermute(x, ('lon', 'lat'), pairs)  6.37 us
    ppermute x2, starting transfers between devices, summed(): x = x + lax.ppermute(x, ('lon', 'lat'), pairs)  3.53 us
    ppermute x2, starting transfers between devices, body(): got_two = lax.ppermute(two, 'lon', lon_b)  2.83 us
    ppermute x2, waiting for transfers between devices, body(): got_two = lax.ppermute(two, 'lon', lon_b)  2.19 us
    ppermute x2, waiting for transfers between devices, summed(): x = x + lax.ppermute(x, ('lon', 'lat'), pairs)  1.99 us
    ppermute x1, waiting for transfers between devices, summed(): x = x + lax.ppermute(x, 'lon', [(i, i ^ step ^ 1) for i in range(count)])  1.77 us
    pallas_call x1, Pallas kernels, body(): pl.pallas_call(functools.partial(band_kernel, rows, levels), out_shape=[p...  1.65 us
  transfers between devices with their start and end apart: 13, of which 10 were waited for; matrix products, arithmetic and copies ran while one was open for 0% of the time, Pallas kernels for 13%

profile of v11, /device:TPU:0, one launch (start us, length us, event | category | flops | bytes accessed | tf_op | source)
XLA Modules:
  0.0 34.2 jit_solution(14517358276967217051)
XLA Ops:
  0.6 1.7 %band_kernel.1 = (f32[17,32,128]{2,1,0:T(8,128)S(1)}, f32[17,32,128]{2,1,0:T(8,128)S(1)}, f32[512,128]{1,0:T(8,128)S(1)}, f32[512,128]{1,0:T(8,128)S(1)}, f32[3,...) custom-call(f32[512,128]{1,0:T(8,128)} %bitcast.7, ...), custom_call_target="tpu_custom_call" | custom-call | tf_op jit(solution)/shard_map/band_kernel/pallas_call | solution.py:630
  2.3 3.1 %collective-permute-start = (f32[17,32,128]{2,1,0:T(8,128)S(1)}, f32[17,32,128]{2,1,0:T(8,128)S(1)}, u32[]{:S(2)}, u32[]{:S(2)}) collective-permute-start(f32[17,32,128]{2,1,0:T(8,128)S(1)} %get-tuple-element.52), channel_id=1, source_target_pairs={{0,1},{1,0},{2,3},{3,2},{4,5},{5,4},{6,7},{7,6},{8,9},{9,8},{10,11... | collective-permute-start | bytes 835592 | tf_op jit(solution)/shard_map/ppermute | solution.py:640
  5.4 0.0 collective-permute-start.1
  5.4 0.3 field_kernel.1
  5.8 0.5 %collective-permute-start.2 = (f32[8,512]{1,0:T(8,128)S(1)}, f32[8,512]{1,0:T(8,128)S(1)}, u32[]{:S(2)}, u32[]{:S(2)}) collective-permute-start(f32[8,512]{1,0:T(8,128)S(1)} %get-tuple-element.60.own), channel_id=1, source_target_pairs={{0,4},{4,0},{8,12},{12,8},{1,5},{5,1},{9,13},{13,9},{2,6},{6,2},{1... | collective-permute-start | bytes 49160 | tf_op jit(solution)/shard_map/ppermute | solution.py:659
  6.3 0.8 %own_kernel.1 = (f32[5,128,512]{2,1,0:T(8,128)S(1)}, f32[8,512]{1,0:T(8,128)S(1)}, f32[8,512]{1,0:T(8,128)S(1)}, f32[8,512]{1,0:T(8,128)S(1)}) custom-call(f32[512,128]{1,0:T(8,128)S(1)} %get-tuple-element.46.kappa2, f32[3,512,128]{2,1,0:T(8,128)S(1)} %get-tuple-element.47.conduct, s32[512,128]{1,0:T(8,128)S(1)} %get-tuple-element.48.land, ...), custom_call_target="tpu_custom_call" | custom-call | tf_op jit(solution)/shard_map/own_kernel/pallas_call | solution.py:130
  7.0 0.1 collective-permute-done.2.moments.got
  7.1 1.5 %collective-permute-start.4 = (f32[16,512]{1,0:T(8,128)S(1)}, f32[16,512]{1,0:T(8,128)S(1)}, u32[]{:S(2)}, u32[]{:S(2)}) collective-permute-start(f32[16,512]{1,0:T(8,128)S(1)} %chip_kernel.1), channel_id=1, source_target_pairs={{0,12},{4,8},{8,4},{12,0},{1,13},{5,9},{9,5},{13,1},{2,14},{6,10},... | collective-permute-start | bytes 98312 | tf_op jit(solution)/shard_map/ppermute | solution.py:661
  8.6 0.2 collective-permute-start.3
  8.8 1.0 %collective-permute-done.3.edges = f32[8,512]{1,0:T(8,128)S(1)} collective-permute-done((f32[8,512]{1,0:T(8,128)S(1)}, f32[8,512]{1,0:T(8,128)S(1)}, u32[]{:S(2)}, u32[]{:S(2)}) %collective-permute-start.3) | collective-permute-done | bytes 16416 | tf_op jit(solution)/shard_map/ppermute | solution.py:662
  9.8 0.7 %collective-permute-done.4.refs_1_.rest_1_ = f32[16,512]{1,0:T(8,128)S(1)} collective-permute-done((f32[16,512]{1,0:T(8,128)S(1)}, f32[16,512]{1,0:T(8,128)S(1)}, u32[]{:S(2)}, u32[]{:S(2)}) %collective-permute-start.4) | collective-permute-done | bytes 32800 | tf_op jit(solution)/shard_map/ppermute | solution.py:661
  10.5 3.1 %collective-permute-start.5 = (f32[24,128]{1,0:T(8,128)S(1)}, f32[24,128]{1,0:T(8,128)S(1)}, u32[]{:S(2)}, u32[]{:S(2)}) collective-permute-start(f32[24,128]{1,0:T(8,128)S(1)} %get-tuple-element.63), channel_id=1, source_target_pairs={{0,1},{1,0},{2,3},{3,2},{4,5},{5,4},{6,7},{7,6},{8,9},{9,8},{10,11... | collective-permute-start | bytes 36872 | tf_op jit(solution)/shard_map/ppermute | solution.py:640
  13.6 0.2 collective-permute-start.6
  13.8 0.7 %near_kernel.1 = (f32[144,512]{1,0:T(8,128)S(1)}, f32[8,128,512]{2,1,0:T(8,128)S(1)}) custom-call(f32[144,128]{1,0:T(8,128)S(1)} %get-tuple-element.42.near, f32[128,512]{1,0:T(8,128)S(1)} %get-tuple-element.45.field, f32[5,128,512]{2,1,0:T(8,128)S(1)} %get-tuple-element.49.made), custom_call_target="tpu_custom_call" | custom-call | tf_op jit(solution)/shard_map/near_kernel/pallas_call | solution.py:130
  14.5 0.0 collective-permute-done.got_first
  14.6 0.0 collective-permute-done.1.got_second
  14.6 0.5 %ghost_kernel.1 = (f32[144,256]{1,0:T(8,128)S(1)}, f32[8,128,256]{2,1,0:T(8,128)S(1)}, f32[3,128,128]{2,1,0:T(8,128)S(1)}) custom-call(f32[17,32,128]{2,1,0:T(8,128)S(1)} %collective-permute-done.got_first, f32[17,32,128]{2,1,0:T(8,128)S(1)} %collective-permute-done.1.got_second, f32[144,128]{1,0:T(8,128)S(1)} %get-tuple-element.42.near, ...), custom_call_target="tpu_custom_call" | custom-call | tf_op jit(solution)/shard_map/ghost_kernel/pallas_call | solution.py:130
  15.0 0.2 collective-permute-done.5.side_first
  15.3 0.0 collective-permute-done.6.side_second
  15.3 1.2 %first_kernel.1 = (f32[144,768]{1,0:T(8,128)S(1)}, f32[128,768]{1,0:T(8,128)S(1)}, f32[7,16,768]{2,1,0:T(8,128)S(1)}, f32[7,8,768]{2,1,0:T(8,128)S(1)}, f32[8,768]{1,0:T(8,128)S(1)}, /*index=5*/f32[8,768]{1,0:T(8,128)S(1)}) custom-call(f32[144,512]{1,0:T(8,128)S(1)} %get-tuple-element.50.own_spread, f32[8,512]{1,0:T(8,128)S(1)} %get-tuple-element.51.refs_2_.own_edge, ...), custom_call_target="tpu_custom_call" | custom-call | tf_op jit(solution)/shard_map/first_kernel/pallas_call | solution.py:130
  16.5 0.2 collective-permute-start.7
  16.7 1.1 %collective-permute-done.7.got.rest_0_ = f32[8,768]{1,0:T(8,128)S(1)} collective-permute-done((f32[8,768]{1,0:T(8,128)S(1)}, f32[8,768]{1,0:T(8,128)S(1)}, u32[]{:S(2)}, u32[]{:S(2)}) %collective-permute-start.7) | collective-permute-done | bytes 24608 | tf_op jit(solution)/shard_map/ppermute | solution.py:682
  17.8 1.3 %collective-permute-start.8 = (f32[8,768]{1,0:T(8,128)S(1)}, f32[8,768]{1,0:T(8,128)S(1)}, u32[]{:S(2)}, u32[]{:S(2)}) collective-permute-start(f32[8,768]{1,0:T(8,128)S(1)} %again_kernel.1), channel_id=1, source_target_pairs={{0,12},{4,8},{8,4},{12,0},{1,13},{5,9},{9,5},{13,1},{2,14},{6,10},... | collective-permute-start | bytes 73736 | tf_op jit(solution)/shard_map/ppermute | solution.py:684
  19.1 0.5 %between_kernel.1 = (f32[144,768]{1,0:T(8,128)S(1)}, f32[8,128]{1,0:T(8,128)S(1)}) custom-call(f32[144,128]{1,0:T(8,128)S(1)} %get-tuple-element.42.near, f32[128,512]{1,0:T(8,128)S(1)} %get-tuple-element.45.field, f32[144,768]{1,0:T(8,128)S(1)} %get-tuple-element.65.precond, f32[128,768]{1,0:T(8,128)S(1)} %get-tuple-element.66.image), custom_call_target="tpu_custom_call" | custom-call | tf_op jit(solution)/shard_map/between_kernel/pallas_call | solution.py:130
  19.6 1.5 %collective-permute-done.8.rest_1_ = f32[8,768]{1,0:T(8,128)S(1)} collective-permute-done((f32[8,768]{1,0:T(8,128)S(1)}, f32[8,768]{1,0:T(8,128)S(1)}, u32[]{:S(2)}, u32[]{:S(2)}) %collective-permute-start.8) | collective-permute-done | bytes 24608 | tf_op jit(solution)/shard_map/ppermute | solution.py:684
  21.1 0.7 %second_kernel.1 = (f32[144,768]{1,0:T(8,128)S(1)}, f32[144,768]{1,0:T(8,128)S(1)}, f32[8,128]{1,0:T(8,128)S(1)}) custom-call(f32[144,768]{1,0:T(8,128)S(1)} %get-tuple-element.67.spread, f32[8,128]{1,0:T(8,128)S(1)} %get-tuple-element.68.early, f32[128,768]{1,0:T(8,128)S(1)} %get-tuple-element.66.image, f32[8,128,512]{2,1,0:T(8,128)S(1)} %get-tuple-element.54.own.own_part, ...), custom_call_target="tpu_custom_call" | custom-call | tf_op jit(solution)/shard_map/second_kernel/pallas_call | solution.py:130
  21.8 0.2 collective-permute-start.9
  22.1 1.0 %collective-permute-done.9 = f32[8,128]{1,0:T(8,128)S(1)} collective-permute-done((f32[8,128]{1,0:T(8,128)S(1)}, f32[8,128]{1,0:T(8,128)S(1)}, u32[]{:S(2)}, u32[]{:S(2)}) %collective-permute-start.9) | collective-permute-done | bytes 4128 | tf_op jit(solution)/shard_map/ppermute | solution.py:605
  23.1 1.3 %collective-permute-start.10 = (f32[8,128]{1,0:T(8,128)S(1)}, f32[8,128]{1,0:T(8,128)S(1)}, u32[]{:S(2)}, u32[]{:S(2)}) collective-permute-start(f32[8,128]{1,0:T(8,128)S(1)} %add.12), channel_id=1, source_target_pairs={{0,12},{4,8},{8,4},{12,0},{1,13},{5,9},{9,5},{13,1},{2,14},{6,10},... | collective-permute-start | bytes 12296 | tf_op jit(solution)/shard_map/ppermute | solution.py:607
  24.3 1.8 %collective-permute-done.10 = f32[8,128]{1,0:T(8,128)S(1)} collective-permute-done((f32[8,128]{1,0:T(8,128)S(1)}, f32[8,128]{1,0:T(8,128)S(1)}, u32[]{:S(2)}, u32[]{:S(2)}) %collective-permute-start.10) | collective-permute-done | bytes 4128 | tf_op jit(solution)/shard_map/ppermute | solution.py:607
  26.1 1.9 %collective-permute-start.11 = (f32[8,128]{1,0:T(8,128)S(1)}, f32[8,128]{1,0:T(8,128)S(1)}, u32[]{:S(2)}, u32[]{:S(2)}) collective-permute-start(f32[8,128]{1,0:T(8,128)S(1)} %add.13), channel_id=1, source_target_pairs={{0,5},{1,4},{2,7},{3,6},{4,1},{5,0},{6,3},{7,2},{8,13},{9,12},{10,... | collective-permute-start | bytes 12296 | tf_op jit(solution)/shard_map/ppermute | solution.py:610
  28.0 1.3 %collective-permute-done.11 = f32[8,128]{1,0:T(8,128)S(1)} collective-permute-done((f32[8,128]{1,0:T(8,128)S(1)}, f32[8,128]{1,0:T(8,128)S(1)}, u32[]{:S(2)}, u32[]{:S(2)}) %collective-permute-start.11) | collective-permute-done | bytes 4128 | tf_op jit(solution)/shard_map/ppermute | solution.py:610
  29.3 1.7 %collective-permute-start.12 = (f32[8,128]{1,0:T(8,128)S(1)}, f32[8,128]{1,0:T(8,128)S(1)}, u32[]{:S(2)}, u32[]{:S(2)}) collective-permute-start(f32[8,128]{1,0:T(8,128)S(1)} %add.14), channel_id=1, source_target_pairs={{0,6},{1,7},{2,4},{3,5},{4,2},{5,3},{6,0},{7,1},{8,14},{9,15},{10,... | collective-permute-start | bytes 12296 | tf_op jit(solution)/shard_map/ppermute | solution.py:610
  31.0 1.6 %turn_kernel.1 = (f32[512,128]{1,0:T(8,128)S(1)}, f32[512,128]{1,0:T(8,128)S(1)}, f32[512,128]{1,0:T(8,128)S(1)}, f32[512,128]{1,0:T(8,128)S(1)}, f32[128,768]{1,0:T(8,128)}) custom-call(f32[144,768]{1,0:T(8,128)S(1)} %get-tuple-element.65.precond, f32[128,768]{1,0:T(8,128)S(1)} %get-tuple-element.66.image, f32[144,768]{1,0:T(8,128)S(1)} %get-tuple-element.74.again, ...), custom_call_target="tpu_custom_call" | custom-call | tf_op jit(solution)/shard_map/turn_kernel/pallas_call | solution.py:130
  32.6 0.7 %collective-permute-done.12 = f32[8,128]{1,0:T(8,128)S(1)} collective-permute-done((f32[8,128]{1,0:T(8,128)S(1)}, f32[8,128]{1,0:T(8,128)S(1)}, u32[]{:S(2)}, u32[]{:S(2)}) %collective-permute-start.12) | collective-permute-done | bytes 4128 | tf_op jit(solution)/shard_map/ppermute | solution.py:610
  33.3 1.0 %combine_kernel.1 = (f32[512,128]{1,0:T(8,128)}, f32[512,128]{1,0:T(8,128)}) custom-call(f32[8,128]{1,0:T(8,128)S(1)} %add.15.sums, f32[512,128]{1,0:T(8,128)S(1)} %get-tuple-element.43.noise, f32[512,128]{1,0:T(8,128)S(1)} %get-tuple-element.76.precond, f32[512,128]{1,0:T(8,128)S(1)} %get-tuple-element.77.image, f32[512,128]{1,0:T(8,128)S(1)} %get-tuple-element.78.again, ...), custom_call_target="tpu_custom_call" | custom-call | tf_op jit(solution)/shard_map/combine_kernel/pallas_call | solution.py:703
  (8 shorter events, 0.1 us)
Async XLA Ops:
  2.3 12.3 %collective-permute-start = (f32[17,32,128]{2,1,0:T(8,128)S(1)}, f32[17,32,128]{2,1,0:T(8,128)S(1)}, u32[]{:S(2)}, u32[]{:S(2)}) collective-permute-start(f32[17,32,128]{2,1,0:T(8,128)S(1)} %get-tuple-element.52), channel_id=1, source_target_pairs={{0,1},{1,0},{2,3},{3,2},{4,5},{5,4},{6,7},{7,6},{8,9},{9,8},{10,11... | collective-permute-start | bytes 835592 | tf_op jit(solution)/shard_map/ppermute | solution.py:640
  5.4 9.1 %collective-permute-start.1 = (f32[17,32,128]{2,1,0:T(8,128)S(1)}, f32[17,32,128]{2,1,0:T(8,128)S(1)}, u32[]{:S(2)}, u32[]{:S(2)}) collective-permute-start(f32[17,32,128]{2,1,0:T(8,128)S(1)} %get-tuple-element.53), channel_id=1, source_target_pairs={{0,4},{1,2},{2,1},{3,7},{4,0},{5,6},{6,5},{7,3},{8,12},{9,10},{10,... | collective-permute-start | bytes 835592 | tf_op jit(solution)/shard_map/ppermute | solution.py:640
  5.8 1.3 %collective-permute-start.2 = (f32[8,512]{1,0:T(8,128)S(1)}, f32[8,512]{1,0:T(8,128)S(1)}, u32[]{:S(2)}, u32[]{:S(2)}) collective-permute-start(f32[8,512]{1,0:T(8,128)S(1)} %get-tuple-element.60.own), channel_id=1, source_target_pairs={{0,4},{4,0},{8,12},{12,8},{1,5},{5,1},{9,13},{13,9},{2,6},{6,2},{1... | collective-permute-start | bytes 49160 | tf_op jit(solution)/shard_map/ppermute | solution.py:659
  7.1 3.4 %collective-permute-start.4 = (f32[16,512]{1,0:T(8,128)S(1)}, f32[16,512]{1,0:T(8,128)S(1)}, u32[]{:S(2)}, u32[]{:S(2)}) collective-permute-start(f32[16,512]{1,0:T(8,128)S(1)} %chip_kernel.1), channel_id=1, source_target_pairs={{0,12},{4,8},{8,4},{12,0},{1,13},{5,9},{9,5},{13,1},{2,14},{6,10},... | collective-permute-start | bytes 98312 | tf_op jit(solution)/shard_map/ppermute | solution.py:661
  8.6 1.2 %collective-permute-start.3 = (f32[8,512]{1,0:T(8,128)S(1)}, f32[8,512]{1,0:T(8,128)S(1)}, u32[]{:S(2)}, u32[]{:S(2)}) collective-permute-start(f32[8,512]{1,0:T(8,128)S(1)} %get-tuple-element.61), channel_id=1, source_target_pairs={{0,4},{4,0},{8,12},{12,8},{1,5},{5,1},{9,13},{13,9},{2,6},{6,2},{1... | collective-permute-start | bytes 49160 | tf_op jit(solution)/shard_map/ppermute | solution.py:662
  10.5 4.7 %collective-permute-start.5 = (f32[24,128]{1,0:T(8,128)S(1)}, f32[24,128]{1,0:T(8,128)S(1)}, u32[]{:S(2)}, u32[]{:S(2)}) collective-permute-start(f32[24,128]{1,0:T(8,128)S(1)} %get-tuple-element.63), channel_id=1, source_target_pairs={{0,1},{1,0},{2,3},{3,2},{4,5},{5,4},{6,7},{7,6},{8,9},{9,8},{10,11... | collective-permute-start | bytes 36872 | tf_op jit(solution)/shard_map/ppermute | solution.py:640
  13.6 1.7 %collective-permute-start.6 = (f32[24,128]{1,0:T(8,128)S(1)}, f32[24,128]{1,0:T(8,128)S(1)}, u32[]{:S(2)}, u32[]{:S(2)}) collective-permute-start(f32[24,128]{1,0:T(8,128)S(1)} %get-tuple-element.64), channel_id=1, source_target_pairs={{0,4},{1,2},{2,1},{3,7},{4,0},{5,6},{6,5},{7,3},{8,12},{9,10},{10,... | collective-permute-start | bytes 36872 | tf_op jit(solution)/shard_map/ppermute | solution.py:640
  16.5 1.3 %collective-permute-start.7 = (f32[8,768]{1,0:T(8,128)S(1)}, f32[8,768]{1,0:T(8,128)S(1)}, u32[]{:S(2)}, u32[]{:S(2)}) collective-permute-start(f32[8,768]{1,0:T(8,128)S(1)} %get-tuple-element.71), channel_id=1, source_target_pairs={{0,4},{4,0},{8,12},{12,8},{1,5},{5,1},{9,13},{13,9},{2,6},{6,2},{1... | collective-permute-start | bytes 73736 | tf_op jit(solution)/shard_map/ppermute | solution.py:682
  17.8 3.3 %collective-permute-start.8 = (f32[8,768]{1,0:T(8,128)S(1)}, f32[8,768]{1,0:T(8,128)S(1)}, u32[]{:S(2)}, u32[]{:S(2)}) collective-permute-start(f32[8,768]{1,0:T(8,128)S(1)} %again_kernel.1), channel_id=1, source_target_pairs={{0,12},{4,8},{8,4},{12,0},{1,13},{5,9},{9,5},{13,1},{2,14},{6,10},... | collective-permute-start | bytes 73736 | tf_op jit(solution)/shard_map/ppermute | solution.py:684
  21.8 1.2 %collective-permute-start.9 = (f32[8,128]{1,0:T(8,128)S(1)}, f32[8,128]{1,0:T(8,128)S(1)}, u32[]{:S(2)}, u32[]{:S(2)}) collective-permute-start(f32[8,128]{1,0:T(8,128)S(1)} %get-tuple-element.73), channel_id=1, source_target_pairs={{0,4},{4,0},{8,12},{12,8},{1,5},{5,1},{9,13},{13,9},{2,6},{6,2},{1... | collective-permute-start | bytes 12296 | tf_op jit(solution)/shard_map/ppermute | solution.py:605
  23.1 3.0 %collective-permute-start.10 = (f32[8,128]{1,0:T(8,128)S(1)}, f32[8,128]{1,0:T(8,128)S(1)}, u32[]{:S(2)}, u32[]{:S(2)}) collective-permute-start(f32[8,128]{1,0:T(8,128)S(1)} %add.12), channel_id=1, source_target_pairs={{0,12},{4,8},{8,4},{12,0},{1,13},{5,9},{9,5},{13,1},{2,14},{6,10},... | collective-permute-start | bytes 12296 | tf_op jit(solution)/shard_map/ppermute | solution.py:607
  26.1 3.2 %collective-permute-start.11 = (f32[8,128]{1,0:T(8,128)S(1)}, f32[8,128]{1,0:T(8,128)S(1)}, u32[]{:S(2)}, u32[]{:S(2)}) collective-permute-start(f32[8,128]{1,0:T(8,128)S(1)} %add.13), channel_id=1, source_target_pairs={{0,5},{1,4},{2,7},{3,6},{4,1},{5,0},{6,3},{7,2},{8,13},{9,12},{10,... | collective-permute-start | bytes 12296 | tf_op jit(solution)/shard_map/ppermute | solution.py:610
  29.3 3.9 %collective-permute-start.12 = (f32[8,128]{1,0:T(8,128)S(1)}, f32[8,128]{1,0:T(8,128)S(1)}, u32[]{:S(2)}, u32[]{:S(2)}) collective-permute-start(f32[8,128]{1,0:T(8,128)S(1)} %add.14), channel_id=1, source_target_pairs={{0,6},{1,7},{2,4},{3,5},{4,2},{5,3},{6,0},{7,1},{8,14},{9,15},{10,... | collective-permute-start | bytes 12296 | tf_op jit(solution)/shard_map/ppermute | solution.py:610

commit v12 on v11

--- a/solution.py
+++ b/solution.py
@@ -144,23 +144,26 @@
 
 def band_kernel(rows, levels, *refs):
     sources, (first, second), copies, sems = refs[:8], refs[8:10], refs[10:18], refs[18]
-    order = (0, 3, 2, 1, 4, 5, 6, 7)
-    moves = [pltpu.make_async_copy(sources[k], copies[k], sems.at[k]) for k in order]
+    pairs = [(sources[0], copies[0]), (sources[3], copies[3])]
+    pairs += [(sources[2].at[k], copies[2].at[k]) for k in (1, 0, 2)]
+    pairs += [(sources[k], copies[k]) for k in (1, 6, 4, 5, 7)]
+    moves = [pltpu.make_async_copy(x, y, sems.at[k]) for k, (x, y) in enumerate(pairs)]
     for move in moves:
         move.start()
     noise, kappa2, conduct, land = copies[:4]
+    columns = noise.shape[1]
     odd = lax.axis_index("lat") % 2
+    lane = lax.broadcasted_iota(jnp.int32, (1, columns), 1)
+    level = lax.broadcasted_iota(jnp.int32, (levels, 1), 0)
+    plane = lambda lat: pl.ds(lat, levels, stride=rows)
     sides = ((first, odd), (second, 1 - odd))
-    plane = lambda lat: pl.ds(lat, levels, stride=rows)
     moves[0].wait()
     for out, side in sides:
         for j in range(FULL):
             out[j] = noise[plane((1 - side) * (rows - FULL) + j), :]
-    for move in moves[1:4]:
-        move.wait()
-    columns = noise.shape[1]
-    lane = lax.broadcasted_iota(jnp.int32, (1, columns), 1)
-    level = lax.broadcasted_iota(jnp.int32, (levels, 1), 0)
+    moves[1].wait()
+    moves[2].wait()
+    oceans, totals = [], []
     for out, side in sides:
         base = (1 - side) * (rows - FULL)
         ocean = [land[plane(base + j), :].astype(jnp.float32) for j in range(FULL)]
@@ -169,19 +172,29 @@
             out[FULL + 3 * PART + j] = north[j] * ocean[j] * ocean[j + 1]
         out[FULL + 4 * PART] = north[PART]
         near = lambda x, j: jnp.where(side == 0, x[j + 1], x[j])
+        below = [north[0]] + [near([north[j - 1], north[j]], 0) for j in range(1, PART)]
+        below[0] = jnp.where(side == 0, north[0], 0.0)
+        oceans.append([near(ocean, j) for j in range(PART)])
+        totals.append([near(north, j) + below[j] for j in range(PART)])
+    at = lambda side, j: plane((1 - side) * (rows - PART) + j)
+    moves[3].wait()
+    for (out, side), ocean, total in zip(sides, oceans, totals):
         for j in range(PART):
-            at = plane(base + 1 - side + j)
-            o, n = near(ocean, j), near(north, j)
-            below = north[j] if j == 0 else jnp.where(side == 0, north[j], north[j - 1])
-            south = jnp.where(side == 0, below, 0.0) if j == 0 else below
-            e, k = conduct[0, at, :], kappa2[at, :]
-            u = jnp.where(level == levels - 1, 0.0, conduct[2, at, :])
-            west = jnp.where(lane == 0, 0.0, pltpu.roll(e, 1, 1))
+            e, o = conduct[0, at(side, j), :], ocean[j]
             ocean_east = jnp.where(lane == columns - 1, 1.0, pltpu.roll(o, columns - 1, 1))
-            out[FULL + j] = o * (k + e + west + n + south + u + pltpu.roll(u, 1, 0))
             out[FULL + PART + j] = e * o * ocean_east
+            total[j] = total[j] + (e + jnp.where(lane == 0, 0.0, pltpu.roll(e, 1, 1)))
+    moves[4].wait()
+    for (out, side), ocean, total in zip(sides, oceans, totals):
+        for j in range(PART):
+            u, o = jnp.where(level == levels - 1, 0.0, conduct[2, at(side, j), :]), ocean[j]
             out[FULL + 2 * PART + j] = u * o * pltpu.roll(o, levels - 1, 0)
-    for move in moves[4:]:
+            total[j] = total[j] + (u + pltpu.roll(u, 1, 0))
+    moves[5].wait()
+    for (out, side), ocean, total in zip(sides, oceans, totals):
+        for j in range(PART):
+            out[FULL + j] = ocean[j] * (kappa2[at(side, j), :] + total[j])
+    for move in moves[6:]:
         move.wait()
 
 
@@ -309,7 +322,7 @@
 
 
 def forward_kernel(group, *refs):
-    (one, two, edge), more, (first, second) = refs[:3], refs[3:-2], refs[-2:]
+    (one, two, edge), more, (first, second) = refs[1:4], refs[4:-2], refs[-2:]
     odd = lax.axis_index("lat") % 2
     whole_rows = [one[0:LIST], two[0:LIST], edge[0:2]] + [x[...] for x in more]
     x = jnp.concatenate(whole_rows, axis=0)
@@ -603,11 +616,11 @@
 def summed(x):
     count, bands = lax.axis_size("lon"), lax.axis_size("lat")
     x = x + lax.ppermute(x, "lon", [(i, i ^ 1) for i in range(count)])
+    for step in doubling(bands)[::-1]:
+        pairs = [(i * bands + j, (i ^ 1) * bands + (j ^ step)) for i in range(count) for j in range(bands)]
+        x = x + lax.ppermute(x, ("lon", "lat"), pairs)
     for step in doubling(count)[1:]:
         x = x + lax.ppermute(x, "lon", [(i, i ^ step ^ 1) for i in range(count)])
-    for step in doubling(bands):
-        pairs = [(i * bands + j, (i ^ 1) * bands + (j ^ step)) for i in range(count) for j in range(bands)]
-        x = x + lax.ppermute(x, ("lon", "lat"), pairs)
     return x
 
 
@@ -632,7 +645,7 @@
         out_shape=[pltpu.VMEM(planes, jnp.float32)] * 2 + [pltpu.VMEM(x.shape, x.dtype) for x in sources],
         in_specs=[pl.BlockSpec(memory_space=pltpu.HBM)] * len(sources),
         out_specs=whole(2 + len(sources)),
-        scratch_shapes=[pltpu.SemaphoreType.DMA((len(sources),))],
+        scratch_shapes=[pltpu.SemaphoreType.DMA((len(sources) + 2,))],
         compiler_params=pltpu.CompilerParams(vmem_limit_bytes=8 << 20),
         name="band_kernel",
     )(*[pltpu.with_memory_space_constraint(x, pltpu.HBM) for x in sources])
@@ -666,7 +679,7 @@
     )
     sent = (*lists[:2], own_edge, *lists[2:])
     heights = 2 * LIST + 2 + sum(x.shape[0] for x in lists[2:])
-    side_first, side_second = call(functools.partial(forward_kernel, group), [(heights, group)] * 2, *sent)
+    side_first, side_second = call(functools.partial(forward_kernel, group), [(heights, group)] * 2, own_spread, *sent)
     side_second, side_first = to_band(side_second, lat_b), to_band(side_first, lat_a)
     ghost_spread, ghost_part, patches = call(
         functools.partial(ghost_kernel, levels, columns),

time: 34.4 us -> 34.3 us (level)
    ppermute x1, waiting for transfers between devices: 1.77 us -> 0.03 us  [summed(): x = x + lax.ppermute(x, 'lon', [(i, i ^ step ^ 1) for i in range(count)])]
    ppermute x2, waiting for transfers between devices: 1.99 us -> 3.43 us  [summed(): x = x + lax.ppermute(x, ('lon', 'lat'), pairs)]
    ppermute x4, waiting for transfers between devices: 0.26 us -> 1.02 us  [body(): to_band = lambda x, pairs: lax.ppermute(x, ('lon', 'lat'), pairs)]
    ppermute x1, waiting for transfers between devices: 1.02 us -> 0.26 us  [body(): lax.ppermute(to_first, 'lon', lon_a)]
  transfers between devices with their start and end apart: 13 -> 13, of which waited for: 10 -> 9; matrix products, arithmetic and copies ran while one was open for 0% -> 0% of each run, Pallas kernels for 13% -> 13%
where the time goes in v12:
time: 34.3 us; the launch traced here: 34.2 us
  starting transfers between devices  15.2 us (44%)
  waiting for transfers between devices  9.2 us (27%)
  Pallas kernels  8.98 us (26%)
  between operations  0.71 us (2%)
    pallas_call x12, Pallas kernels, call(): pl.pallas_call(kernel, out_shape=[pltpu.VMEM(s, jnp.float32) for s in out...  6.4 us
    ppermute x4, starting transfers between devices, body(): to_band = lambda x, pairs: lax.ppermute(x, ('lon', 'lat'), pairs)  6.36 us
    ppermute x2, starting transfers between devices, summed(): x = x + lax.ppermute(x, ('lon', 'lat'), pairs)  3.7 us
    ppermute x2, waiting for transfers between devices, summed(): x = x + lax.ppermute(x, ('lon', 'lat'), pairs)  3.43 us
    ppermute x2, starting transfers between devices, body(): got_two = lax.ppermute(two, 'lon', lon_b)  2.83 us
    ppermute x2, waiting for transfers between devices, body(): got_two = lax.ppermute(two, 'lon', lon_b)  2.2 us
    pallas_call x1, Pallas kernels, body(): pl.pallas_call(functools.partial(band_kernel, rows, levels), out_shape=[p...  1.58 us
    ppermute x1, starting transfers between devices, summed(): x = x + lax.ppermute(x, 'lon', [(i, i ^ step ^ 1) for i in range(count)])  1.4 us
  transfers between devices with their start and end apart: 13, of which 9 were waited for; matrix products, arithmetic and copies ran while one was open for 0% of the time, Pallas kernels for 13%

profile of v12, /device:TPU:0, one launch (start us, length us, event | category | flops | bytes accessed | tf_op | source)
XLA Modules:
  0.0 34.2 jit_solution(10467247648411394278)
XLA Ops:
  0.6 1.6 %band_kernel.1 = (f32[17,32,128]{2,1,0:T(8,128)S(1)}, f32[17,32,128]{2,1,0:T(8,128)S(1)}, f32[512,128]{1,0:T(8,128)S(1)}, f32[512,128]{1,0:T(8,128)S(1)}, f32[3,...) custom-call(f32[512,128]{1,0:T(8,128)} %bitcast.7, ...), custom_call_target="tpu_custom_call" | custom-call | tf_op jit(solution)/shard_map/band_kernel/pallas_call | solution.py:643
  2.2 3.1 %collective-permute-start = (f32[17,32,128]{2,1,0:T(8,128)S(1)}, f32[17,32,128]{2,1,0:T(8,128)S(1)}, u32[]{:S(2)}, u32[]{:S(2)}) collective-permute-start(f32[17,32,128]{2,1,0:T(8,128)S(1)} %get-tuple-element.52), channel_id=1, source_target_pairs={{0,1},{1,0},{2,3},{3,2},{4,5},{5,4},{6,7},{7,6},{8,9},{9,8},{10,11... | collective-permute-start | bytes 835592 | tf_op jit(solution)/shard_map/ppermute | solution.py:653
  5.3 0.0 collective-permute-start.1
  5.3 0.3 field_kernel.1
  5.7 0.5 %collective-permute-start.2 = (f32[8,512]{1,0:T(8,128)S(1)}, f32[8,512]{1,0:T(8,128)S(1)}, u32[]{:S(2)}, u32[]{:S(2)}) collective-permute-start(f32[8,512]{1,0:T(8,128)S(1)} %get-tuple-element.60.own), channel_id=1, source_target_pairs={{0,4},{4,0},{8,12},{12,8},{1,5},{5,1},{9,13},{13,9},{2,6},{6,2},{1... | collective-permute-start | bytes 49160 | tf_op jit(solution)/shard_map/ppermute | solution.py:672
  6.2 0.8 %own_kernel.1 = (f32[5,128,512]{2,1,0:T(8,128)S(1)}, f32[8,512]{1,0:T(8,128)S(1)}, f32[8,512]{1,0:T(8,128)S(1)}, f32[8,512]{1,0:T(8,128)S(1)}) custom-call(f32[512,128]{1,0:T(8,128)S(1)} %get-tuple-element.46.kappa2, f32[3,512,128]{2,1,0:T(8,128)S(1)} %get-tuple-element.47.conduct, s32[512,128]{1,0:T(8,128)S(1)} %get-tuple-element.48.land, ...), custom_call_target="tpu_custom_call" | custom-call | tf_op jit(solution)/shard_map/own_kernel/pallas_call | solution.py:130
  7.0 0.1 collective-permute-done.2.moments.got
  7.0 1.5 %collective-permute-start.4 = (f32[16,512]{1,0:T(8,128)S(1)}, f32[16,512]{1,0:T(8,128)S(1)}, u32[]{:S(2)}, u32[]{:S(2)}) collective-permute-start(f32[16,512]{1,0:T(8,128)S(1)} %chip_kernel.1), channel_id=1, source_target_pairs={{0,12},{4,8},{8,4},{12,0},{1,13},{5,9},{9,5},{13,1},{2,14},{6,10},... | collective-permute-start | bytes 98312 | tf_op jit(solution)/shard_map/ppermute | solution.py:674
  8.6 0.2 collective-permute-start.3
  8.7 0.7 %near_kernel.1 = (f32[144,512]{1,0:T(8,128)S(1)}, f32[8,128,512]{2,1,0:T(8,128)S(1)}) custom-call(f32[144,128]{1,0:T(8,128)S(1)} %get-tuple-element.42.near, f32[128,512]{1,0:T(8,128)S(1)} %get-tuple-element.45.field, f32[5,128,512]{2,1,0:T(8,128)S(1)} %get-tuple-element.49.made), custom_call_target="tpu_custom_call" | custom-call | tf_op jit(solution)/shard_map/near_kernel/pallas_call | solution.py:130
  9.5 0.3 collective-permute-done.3.edges
  9.7 0.7 %collective-permute-done.4.refs_2_.rest_1_ = f32[16,512]{1,0:T(8,128)S(1)} collective-permute-done((f32[16,512]{1,0:T(8,128)S(1)}, f32[16,512]{1,0:T(8,128)S(1)}, u32[]{:S(2)}, u32[]{:S(2)}) %collective-permute-start.4) | collective-permute-done | bytes 32800 | tf_op jit(solution)/shard_map/ppermute | solution.py:674
  10.5 3.1 %collective-permute-start.5 = (f32[24,128]{1,0:T(8,128)S(1)}, f32[24,128]{1,0:T(8,128)S(1)}, u32[]{:S(2)}, u32[]{:S(2)}) collective-permute-start(f32[24,128]{1,0:T(8,128)S(1)} %get-tuple-element.63), channel_id=1, source_target_pairs={{0,1},{1,0},{2,3},{3,2},{4,5},{5,4},{6,7},{7,6},{8,9},{9,8},{10,11... | collective-permute-start | bytes 36872 | tf_op jit(solution)/shard_map/ppermute | solution.py:653
  13.5 0.2 collective-permute-start.6
  13.7 0.0 collective-permute-done.got_first
  13.7 0.0 collective-permute-done.1.got_second
  13.7 0.5 %ghost_kernel.1 = (f32[144,256]{1,0:T(8,128)S(1)}, f32[8,128,256]{2,1,0:T(8,128)S(1)}, f32[3,128,128]{2,1,0:T(8,128)S(1)}) custom-call(f32[17,32,128]{2,1,0:T(8,128)S(1)} %collective-permute-done.got_first, f32[17,32,128]{2,1,0:T(8,128)S(1)} %collective-permute-done.1.got_second, f32[144,128]{1,0:T(8,128)S(1)} %get-tuple-element.42.near, ...), custom_call_target="tpu_custom_call" | custom-call | tf_op jit(solution)/shard_map/ghost_kernel/pallas_call | solution.py:130
  14.2 1.0 %collective-permute-done.5.side_first = f32[24,128]{1,0:T(8,128)S(1)} collective-permute-done((f32[24,128]{1,0:T(8,128)S(1)}, f32[24,128]{1,0:T(8,128)S(1)}, u32[]{:S(2)}, u32[]{:S(2)}) %collective-permute-start.5) | collective-permute-done | bytes 12320 | tf_op jit(solution)/shard_map/ppermute | solution.py:653
  15.2 0.0 collective-permute-done.6.side_second
  15.2 1.2 %first_kernel.1 = (f32[144,768]{1,0:T(8,128)S(1)}, f32[128,768]{1,0:T(8,128)S(1)}, f32[7,16,768]{2,1,0:T(8,128)S(1)}, f32[7,8,768]{2,1,0:T(8,128)S(1)}, f32[8,768]{1,0:T(8,128)S(1)}, /*index=5*/f32[8,768]{1,0:T(8,128)S(1)}) custom-call(f32[144,512]{1,0:T(8,128)S(1)} %get-tuple-element.50.refs_0_.own_spread, f32[8,512]{1,0:T(8,128)S(1)} %get-tuple-element.51.refs_3_.own_edge, ...), custom_call_target="tpu_custom_call" | custom-call | tf_op jit(solution)/shard_map/first_kernel/pallas_call | solution.py:130
  16.4 0.1 collective-permute-start.7
  16.5 1.2 %collective-permute-done.7.got.rest_0_ = f32[8,768]{1,0:T(8,128)S(1)} collective-permute-done((f32[8,768]{1,0:T(8,128)S(1)}, f32[8,768]{1,0:T(8,128)S(1)}, u32[]{:S(2)}, u32[]{:S(2)}) %collective-permute-start.7) | collective-permute-done | bytes 24608 | tf_op jit(solution)/shard_map/ppermute | solution.py:695
  17.7 1.3 %collective-permute-start.8 = (f32[8,768]{1,0:T(8,128)S(1)}, f32[8,768]{1,0:T(8,128)S(1)}, u32[]{:S(2)}, u32[]{:S(2)}) collective-permute-start(f32[8,768]{1,0:T(8,128)S(1)} %again_kernel.1), channel_id=1, source_target_pairs={{0,12},{4,8},{8,4},{12,0},{1,13},{5,9},{9,5},{13,1},{2,14},{6,10},... | collective-permute-start | bytes 73736 | tf_op jit(solution)/shard_map/ppermute | solution.py:697
  19.0 0.5 %between_kernel.1 = (f32[144,768]{1,0:T(8,128)S(1)}, f32[8,128]{1,0:T(8,128)S(1)}) custom-call(f32[144,128]{1,0:T(8,128)S(1)} %get-tuple-element.42.near, f32[128,512]{1,0:T(8,128)S(1)} %get-tuple-element.45.field, f32[144,768]{1,0:T(8,128)S(1)} %get-tuple-element.65.precond, f32[128,768]{1,0:T(8,128)S(1)} %get-tuple-element.66.image), custom_call_target="tpu_custom_call" | custom-call | tf_op jit(solution)/shard_map/between_kernel/pallas_call | solution.py:130
  19.5 1.5 %collective-permute-done.8.rest_1_ = f32[8,768]{1,0:T(8,128)S(1)} collective-permute-done((f32[8,768]{1,0:T(8,128)S(1)}, f32[8,768]{1,0:T(8,128)S(1)}, u32[]{:S(2)}, u32[]{:S(2)}) %collective-permute-start.8) | collective-permute-done | bytes 24608 | tf_op jit(solution)/shard_map/ppermute | solution.py:697
  21.0 0.7 %second_kernel.1 = (f32[144,768]{1,0:T(8,128)S(1)}, f32[144,768]{1,0:T(8,128)S(1)}, f32[8,128]{1,0:T(8,128)S(1)}) custom-call(f32[144,768]{1,0:T(8,128)S(1)} %get-tuple-element.67.spread, f32[8,128]{1,0:T(8,128)S(1)} %get-tuple-element.68.early, f32[128,768]{1,0:T(8,128)S(1)} %get-tuple-element.66.image, f32[8,128,512]{2,1,0:T(8,128)S(1)} %get-tuple-element.54.own.own_part, ...), custom_call_target="tpu_custom_call" | custom-call | tf_op jit(solution)/shard_map/second_kernel/pallas_call | solution.py:130
  21.8 0.2 collective-permute-start.9
  22.0 1.0 %collective-permute-done.9 = f32[8,128]{1,0:T(8,128)S(1)} collective-permute-done((f32[8,128]{1,0:T(8,128)S(1)}, f32[8,128]{1,0:T(8,128)S(1)}, u32[]{:S(2)}, u32[]{:S(2)}) %collective-permute-start.9) | collective-permute-done | bytes 4128 | tf_op jit(solution)/shard_map/ppermute | solution.py:618
  23.0 1.8 %collective-permute-start.10 = (f32[8,128]{1,0:T(8,128)S(1)}, f32[8,128]{1,0:T(8,128)S(1)}, u32[]{:S(2)}, u32[]{:S(2)}) collective-permute-start(f32[8,128]{1,0:T(8,128)S(1)} %add.12), channel_id=1, source_target_pairs={{0,6},{1,7},{2,4},{3,5},{4,2},{5,3},{6,0},{7,1},{8,14},{9,15},{10,... | collective-permute-start | bytes 12296 | tf_op jit(solution)/shard_map/ppermute | solution.py:621
  24.8 2.1 %collective-permute-done.10 = f32[8,128]{1,0:T(8,128)S(1)} collective-permute-done((f32[8,128]{1,0:T(8,128)S(1)}, f32[8,128]{1,0:T(8,128)S(1)}, u32[]{:S(2)}, u32[]{:S(2)}) %collective-permute-start.10) | collective-permute-done | bytes 4128 | tf_op jit(solution)/shard_map/ppermute | solution.py:621
  26.9 1.9 %collective-permute-start.11 = (f32[8,128]{1,0:T(8,128)S(1)}, f32[8,128]{1,0:T(8,128)S(1)}, u32[]{:S(2)}, u32[]{:S(2)}) collective-permute-start(f32[8,128]{1,0:T(8,128)S(1)} %add.13), channel_id=1, source_target_pairs={{0,5},{1,4},{2,7},{3,6},{4,1},{5,0},{6,3},{7,2},{8,13},{9,12},{10,... | collective-permute-start | bytes 12296 | tf_op jit(solution)/shard_map/ppermute | solution.py:621
  28.8 1.3 %collective-permute-done.11 = f32[8,128]{1,0:T(8,128)S(1)} collective-permute-done((f32[8,128]{1,0:T(8,128)S(1)}, f32[8,128]{1,0:T(8,128)S(1)}, u32[]{:S(2)}, u32[]{:S(2)}) %collective-permute-start.11) | collective-permute-done | bytes 4128 | tf_op jit(solution)/shard_map/ppermute | solution.py:621
  30.1 1.4 %collective-permute-start.12 = (f32[8,128]{1,0:T(8,128)S(1)}, f32[8,128]{1,0:T(8,128)S(1)}, u32[]{:S(2)}, u32[]{:S(2)}) collective-permute-start(f32[8,128]{1,0:T(8,128)S(1)} %add.14), channel_id=1, source_target_pairs={{0,12},{4,8},{8,4},{12,0},{1,13},{5,9},{9,5},{13,1},{2,14},{6,10},... | collective-permute-start | bytes 12296 | tf_op jit(solution)/shard_map/ppermute | solution.py:623
  31.5 1.6 %turn_kernel.1 = (f32[512,128]{1,0:T(8,128)S(1)}, f32[512,128]{1,0:T(8,128)S(1)}, f32[512,128]{1,0:T(8,128)S(1)}, f32[512,128]{1,0:T(8,128)S(1)}, f32[128,768]{1,0:T(8,128)}) custom-call(f32[144,768]{1,0:T(8,128)S(1)} %get-tuple-element.65.precond, f32[128,768]{1,0:T(8,128)S(1)} %get-tuple-element.66.image, f32[144,768]{1,0:T(8,128)S(1)} %get-tuple-element.74.again, ...), custom_call_target="tpu_custom_call" | custom-call | tf_op jit(solution)/shard_map/turn_kernel/pallas_call | solution.py:130
  33.1 0.0 collective-permute-done.12
  33.2 1.0 %combine_kernel.1 = (f32[512,128]{1,0:T(8,128)}, f32[512,128]{1,0:T(8,128)}) custom-call(f32[8,128]{1,0:T(8,128)S(1)} %add.15.sums, f32[512,128]{1,0:T(8,128)S(1)} %get-tuple-element.43.noise, f32[512,128]{1,0:T(8,128)S(1)} %get-tuple-element.76.precond, f32[512,128]{1,0:T(8,128)S(1)} %get-tuple-element.77.image, f32[512,128]{1,0:T(8,128)S(1)} %get-tuple-element.78.again, ...), custom_call_target="tpu_custom_call" | custom-call | tf_op jit(solution)/shard_map/combine_kernel/pallas_call | solution.py:716
  (8 shorter events, 0.1 us)
Async XLA Ops:
  2.2 11.5 %collective-permute-start = (f32[17,32,128]{2,1,0:T(8,128)S(1)}, f32[17,32,128]{2,1,0:T(8,128)S(1)}, u32[]{:S(2)}, u32[]{:S(2)}) collective-permute-start(f32[17,32,128]{2,1,0:T(8,128)S(1)} %get-tuple-element.52), channel_id=1, source_target_pairs={{0,1},{1,0},{2,3},{3,2},{4,5},{5,4},{6,7},{7,6},{8,9},{9,8},{10,11... | collective-permute-start | bytes 835592 | tf_op jit(solution)/shard_map/ppermute | solution.py:653
  5.3 8.4 %collective-permute-start.1 = (f32[17,32,128]{2,1,0:T(8,128)S(1)}, f32[17,32,128]{2,1,0:T(8,128)S(1)}, u32[]{:S(2)}, u32[]{:S(2)}) collective-permute-start(f32[17,32,128]{2,1,0:T(8,128)S(1)} %get-tuple-element.53), channel_id=1, source_target_pairs={{0,4},{1,2},{2,1},{3,7},{4,0},{5,6},{6,5},{7,3},{8,12},{9,10},{10,... | collective-permute-start | bytes 835592 | tf_op jit(solution)/shard_map/ppermute | solution.py:653
  5.7 1.3 %collective-permute-start.2 = (f32[8,512]{1,0:T(8,128)S(1)}, f32[8,512]{1,0:T(8,128)S(1)}, u32[]{:S(2)}, u32[]{:S(2)}) collective-permute-start(f32[8,512]{1,0:T(8,128)S(1)} %get-tuple-element.60.own), channel_id=1, source_target_pairs={{0,4},{4,0},{8,12},{12,8},{1,5},{5,1},{9,13},{13,9},{2,6},{6,2},{1... | collective-permute-start | bytes 49160 | tf_op jit(solution)/shard_map/ppermute | solution.py:672
  7.0 3.4 %collective-permute-start.4 = (f32[16,512]{1,0:T(8,128)S(1)}, f32[16,512]{1,0:T(8,128)S(1)}, u32[]{:S(2)}, u32[]{:S(2)}) collective-permute-start(f32[16,512]{1,0:T(8,128)S(1)} %chip_kernel.1), channel_id=1, source_target_pairs={{0,12},{4,8},{8,4},{12,0},{1,13},{5,9},{9,5},{13,1},{2,14},{6,10},... | collective-permute-start | bytes 98312 | tf_op jit(solution)/shard_map/ppermute | solution.py:674
  8.6 1.2 %collective-permute-start.3 = (f32[8,512]{1,0:T(8,128)S(1)}, f32[8,512]{1,0:T(8,128)S(1)}, u32[]{:S(2)}, u32[]{:S(2)}) collective-permute-start(f32[8,512]{1,0:T(8,128)S(1)} %get-tuple-element.61), channel_id=1, source_target_pairs={{0,4},{4,0},{8,12},{12,8},{1,5},{5,1},{9,13},{13,9},{2,6},{6,2},{1... | collective-permute-start | bytes 49160 | tf_op jit(solution)/shard_map/ppermute | solution.py:675
  10.5 4.7 %collective-permute-start.5 = (f32[24,128]{1,0:T(8,128)S(1)}, f32[24,128]{1,0:T(8,128)S(1)}, u32[]{:S(2)}, u32[]{:S(2)}) collective-permute-start(f32[24,128]{1,0:T(8,128)S(1)} %get-tuple-element.63), channel_id=1, source_target_pairs={{0,1},{1,0},{2,3},{3,2},{4,5},{5,4},{6,7},{7,6},{8,9},{9,8},{10,11... | collective-permute-start | bytes 36872 | tf_op jit(solution)/shard_map/ppermute | solution.py:653
  13.5 1.7 %collective-permute-start.6 = (f32[24,128]{1,0:T(8,128)S(1)}, f32[24,128]{1,0:T(8,128)S(1)}, u32[]{:S(2)}, u32[]{:S(2)}) collective-permute-start(f32[24,128]{1,0:T(8,128)S(1)} %get-tuple-element.64), channel_id=1, source_target_pairs={{0,4},{1,2},{2,1},{3,7},{4,0},{5,6},{6,5},{7,3},{8,12},{9,10},{10,... | collective-permute-start | bytes 36872 | tf_op jit(solution)/shard_map/ppermute | solution.py:653
  16.4 1.3 %collective-permute-start.7 = (f32[8,768]{1,0:T(8,128)S(1)}, f32[8,768]{1,0:T(8,128)S(1)}, u32[]{:S(2)}, u32[]{:S(2)}) collective-permute-start(f32[8,768]{1,0:T(8,128)S(1)} %get-tuple-element.71), channel_id=1, source_target_pairs={{0,4},{4,0},{8,12},{12,8},{1,5},{5,1},{9,13},{13,9},{2,6},{6,2},{1... | collective-permute-start | bytes 73736 | tf_op jit(solution)/shard_map/ppermute | solution.py:695
  17.7 3.3 %collective-permute-start.8 = (f32[8,768]{1,0:T(8,128)S(1)}, f32[8,768]{1,0:T(8,128)S(1)}, u32[]{:S(2)}, u32[]{:S(2)}) collective-permute-start(f32[8,768]{1,0:T(8,128)S(1)} %again_kernel.1), channel_id=1, source_target_pairs={{0,12},{4,8},{8,4},{12,0},{1,13},{5,9},{9,5},{13,1},{2,14},{6,10},... | collective-permute-start | bytes 73736 | tf_op jit(solution)/shard_map/ppermute | solution.py:697
  21.8 1.2 %collective-permute-start.9 = (f32[8,128]{1,0:T(8,128)S(1)}, f32[8,128]{1,0:T(8,128)S(1)}, u32[]{:S(2)}, u32[]{:S(2)}) collective-permute-start(f32[8,128]{1,0:T(8,128)S(1)} %get-tuple-element.73), channel_id=1, source_target_pairs={{0,4},{4,0},{8,12},{12,8},{1,5},{5,1},{9,13},{13,9},{2,6},{6,2},{1... | collective-permute-start | bytes 12296 | tf_op jit(solution)/shard_map/ppermute | solution.py:618
  23.0 3.9 %collective-permute-start.10 = (f32[8,128]{1,0:T(8,128)S(1)}, f32[8,128]{1,0:T(8,128)S(1)}, u32[]{:S(2)}, u32[]{:S(2)}) collective-permute-start(f32[8,128]{1,0:T(8,128)S(1)} %add.12), channel_id=1, source_target_pairs={{0,6},{1,7},{2,4},{3,5},{4,2},{5,3},{6,0},{7,1},{8,14},{9,15},{10,... | collective-permute-start | bytes 12296 | tf_op jit(solution)/shard_map/ppermute | solution.py:621
  26.9 3.2 %collective-permute-start.11 = (f32[8,128]{1,0:T(8,128)S(1)}, f32[8,128]{1,0:T(8,128)S(1)}, u32[]{:S(2)}, u32[]{:S(2)}) collective-permute-start(f32[8,128]{1,0:T(8,128)S(1)} %add.13), channel_id=1, source_target_pairs={{0,5},{1,4},{2,7},{3,6},{4,1},{5,0},{6,3},{7,2},{8,13},{9,12},{10,... | collective-permute-start | bytes 12296 | tf_op jit(solution)/shard_map/ppermute | solution.py:621
  30.1 3.0 %collective-permute-start.12 = (f32[8,128]{1,0:T(8,128)S(1)}, f32[8,128]{1,0:T(8,128)S(1)}, u32[]{:S(2)}, u32[]{:S(2)}) collective-permute-start(f32[8,128]{1,0:T(8,128)S(1)} %add.14), channel_id=1, source_target_pairs={{0,12},{4,8},{8,4},{12,0},{1,13},{5,9},{9,5},{13,1},{2,14},{6,10},... | collective-permute-start | bytes 12296 | tf_op jit(solution)/shard_map/ppermute | solution.py:623

commit v13 on v12

--- a/solution.py
+++ b/solution.py
@@ -580,7 +580,7 @@
                 out[pl.ds(j + i, levels, stride=rows), :] = t[i * levels : (i + 1) * levels]
 
 
-PIECES = 4
+PIECES = 2
 
 
 def combine_kernel(sums, noise, precond, image, again, along, answer, left, x, y, sems):

time: 34.3 us -> 34.3 us (level)
  no operation moved by 1% of the time
where the time goes in v13:
time: 34.3 us; the launch traced here: 34.1 us
  starting transfers between devices  15.2 us (44%)
  waiting for transfers between devices  9.2 us (27%)
  Pallas kernels  8.96 us (26%)
  between operations  0.71 us (2%)
    pallas_call x12, Pallas kernels, call(): pl.pallas_call(kernel, out_shape=[pltpu.VMEM(s, jnp.float32) for s in out...  6.4 us
    ppermute x4, starting transfers between devices, body(): to_band = lambda x, pairs: lax.ppermute(x, ('lon', 'lat'), pairs)  6.36 us
    ppermute x2, starting transfers between devices, summed(): x = x + lax.ppermute(x, ('lon', 'lat'), pairs)  3.7 us
    ppermute x2, waiting for transfers between devices, summed(): x = x + lax.ppermute(x, ('lon', 'lat'), pairs)  3.43 us
    ppermute x2, starting transfers between devices, body(): got_two = lax.ppermute(two, 'lon', lon_b)  2.83 us
    ppermute x2, waiting for transfers between devices, body(): got_two = lax.ppermute(two, 'lon', lon_b)  2.2 us
    pallas_call x1, Pallas kernels, body(): pl.pallas_call(functools.partial(band_kernel, rows, levels), out_shape=[p...  1.58 us
    ppermute x1, starting transfers between devices, summed(): x = x + lax.ppermute(x, 'lon', [(i, i ^ step ^ 1) for i in range(count)])  1.4 us
  transfers between devices with their start and end apart: 13, of which 9 were waited for; matrix products, arithmetic and copies ran while one was open for 0% of the time, Pallas kernels for 13%

profile of v13, /device:TPU:0, one launch (start us, length us, event | category | flops | bytes accessed | tf_op | source)
XLA Modules:
  0.0 34.1 jit_solution(3290336110326443764)
XLA Ops:
  0.6 1.6 %band_kernel.1 = (f32[17,32,128]{2,1,0:T(8,128)S(1)}, f32[17,32,128]{2,1,0:T(8,128)S(1)}, f32[512,128]{1,0:T(8,128)S(1)}, f32[512,128]{1,0:T(8,128)S(1)}, f32[3,...) custom-call(f32[512,128]{1,0:T(8,128)} %bitcast.7, ...), custom_call_target="tpu_custom_call" | custom-call | tf_op jit(solution)/shard_map/band_kernel/pallas_call | solution.py:643
  2.2 3.1 %collective-permute-start = (f32[17,32,128]{2,1,0:T(8,128)S(1)}, f32[17,32,128]{2,1,0:T(8,128)S(1)}, u32[]{:S(2)}, u32[]{:S(2)}) collective-permute-start(f32[17,32,128]{2,1,0:T(8,128)S(1)} %get-tuple-element.52), channel_id=1, source_target_pairs={{0,1},{1,0},{2,3},{3,2},{4,5},{5,4},{6,7},{7,6},{8,9},{9,8},{10,11... | collective-permute-start | bytes 835592 | tf_op jit(solution)/shard_map/ppermute | solution.py:653
  5.3 0.0 collective-permute-start.1
  5.3 0.3 field_kernel.1
  5.7 0.5 %collective-permute-start.2 = (f32[8,512]{1,0:T(8,128)S(1)}, f32[8,512]{1,0:T(8,128)S(1)}, u32[]{:S(2)}, u32[]{:S(2)}) collective-permute-start(f32[8,512]{1,0:T(8,128)S(1)} %get-tuple-element.60.own), channel_id=1, source_target_pairs={{0,4},{4,0},{8,12},{12,8},{1,5},{5,1},{9,13},{13,9},{2,6},{6,2},{1... | collective-permute-start | bytes 49160 | tf_op jit(solution)/shard_map/ppermute | solution.py:672
  6.2 0.8 %own_kernel.1 = (f32[5,128,512]{2,1,0:T(8,128)S(1)}, f32[8,512]{1,0:T(8,128)S(1)}, f32[8,512]{1,0:T(8,128)S(1)}, f32[8,512]{1,0:T(8,128)S(1)}) custom-call(f32[512,128]{1,0:T(8,128)S(1)} %get-tuple-element.46.kappa2, f32[3,512,128]{2,1,0:T(8,128)S(1)} %get-tuple-element.47.conduct, s32[512,128]{1,0:T(8,128)S(1)} %get-tuple-element.48.land, ...), custom_call_target="tpu_custom_call" | custom-call | tf_op jit(solution)/shard_map/own_kernel/pallas_call | solution.py:130
  7.0 0.1 collective-permute-done.2.moments.got
  7.0 1.5 %collective-permute-start.4 = (f32[16,512]{1,0:T(8,128)S(1)}, f32[16,512]{1,0:T(8,128)S(1)}, u32[]{:S(2)}, u32[]{:S(2)}) collective-permute-start(f32[16,512]{1,0:T(8,128)S(1)} %chip_kernel.1), channel_id=1, source_target_pairs={{0,12},{4,8},{8,4},{12,0},{1,13},{5,9},{9,5},{13,1},{2,14},{6,10},... | collective-permute-start | bytes 98312 | tf_op jit(solution)/shard_map/ppermute | solution.py:674
  8.6 0.2 collective-permute-start.3
  8.7 0.7 %near_kernel.1 = (f32[144,512]{1,0:T(8,128)S(1)}, f32[8,128,512]{2,1,0:T(8,128)S(1)}) custom-call(f32[144,128]{1,0:T(8,128)S(1)} %get-tuple-element.42.near, f32[128,512]{1,0:T(8,128)S(1)} %get-tuple-element.45.field, f32[5,128,512]{2,1,0:T(8,128)S(1)} %get-tuple-element.49.made), custom_call_target="tpu_custom_call" | custom-call | tf_op jit(solution)/shard_map/near_kernel/pallas_call | solution.py:130
  9.5 0.3 collective-permute-done.3.edges
  9.7 0.7 %collective-permute-done.4.refs_2_.rest_1_ = f32[16,512]{1,0:T(8,128)S(1)} collective-permute-done((f32[16,512]{1,0:T(8,128)S(1)}, f32[16,512]{1,0:T(8,128)S(1)}, u32[]{:S(2)}, u32[]{:S(2)}) %collective-permute-start.4) | collective-permute-done | bytes 32800 | tf_op jit(solution)/shard_map/ppermute | solution.py:674
  10.5 3.1 %collective-permute-start.5 = (f32[24,128]{1,0:T(8,128)S(1)}, f32[24,128]{1,0:T(8,128)S(1)}, u32[]{:S(2)}, u32[]{:S(2)}) collective-permute-start(f32[24,128]{1,0:T(8,128)S(1)} %get-tuple-element.63), channel_id=1, source_target_pairs={{0,1},{1,0},{2,3},{3,2},{4,5},{5,4},{6,7},{7,6},{8,9},{9,8},{10,11... | collective-permute-start | bytes 36872 | tf_op jit(solution)/shard_map/ppermute | solution.py:653
  13.5 0.2 collective-permute-start.6
  13.7 0.0 collective-permute-done.got_first
  13.7 0.0 collective-permute-done.1.got_second
  13.7 0.5 %ghost_kernel.1 = (f32[144,256]{1,0:T(8,128)S(1)}, f32[8,128,256]{2,1,0:T(8,128)S(1)}, f32[3,128,128]{2,1,0:T(8,128)S(1)}) custom-call(f32[17,32,128]{2,1,0:T(8,128)S(1)} %collective-permute-done.got_first, f32[17,32,128]{2,1,0:T(8,128)S(1)} %collective-permute-done.1.got_second, f32[144,128]{1,0:T(8,128)S(1)} %get-tuple-element.42.near, ...), custom_call_target="tpu_custom_call" | custom-call | tf_op jit(solution)/shard_map/ghost_kernel/pallas_call | solution.py:130
  14.2 1.0 %collective-permute-done.5.side_first = f32[24,128]{1,0:T(8,128)S(1)} collective-permute-done((f32[24,128]{1,0:T(8,128)S(1)}, f32[24,128]{1,0:T(8,128)S(1)}, u32[]{:S(2)}, u32[]{:S(2)}) %collective-permute-start.5) | collective-permute-done | bytes 12320 | tf_op jit(solution)/shard_map/ppermute | solution.py:653
  15.2 0.0 collective-permute-done.6.side_second
  15.2 1.2 %first_kernel.1 = (f32[144,768]{1,0:T(8,128)S(1)}, f32[128,768]{1,0:T(8,128)S(1)}, f32[7,16,768]{2,1,0:T(8,128)S(1)}, f32[7,8,768]{2,1,0:T(8,128)S(1)}, f32[8,768]{1,0:T(8,128)S(1)}, /*index=5*/f32[8,768]{1,0:T(8,128)S(1)}) custom-call(f32[144,512]{1,0:T(8,128)S(1)} %get-tuple-element.50.refs_0_.own_spread, f32[8,512]{1,0:T(8,128)S(1)} %get-tuple-element.51.refs_3_.own_edge, ...), custom_call_target="tpu_custom_call" | custom-call | tf_op jit(solution)/shard_map/first_kernel/pallas_call | solution.py:130
  16.4 0.1 collective-permute-start.7
  16.5 1.2 %collective-permute-done.7.got.rest_0_ = f32[8,768]{1,0:T(8,128)S(1)} collective-permute-done((f32[8,768]{1,0:T(8,128)S(1)}, f32[8,768]{1,0:T(8,128)S(1)}, u32[]{:S(2)}, u32[]{:S(2)}) %collective-permute-start.7) | collective-permute-done | bytes 24608 | tf_op jit(solution)/shard_map/ppermute | solution.py:695
  17.7 1.3 %collective-permute-start.8 = (f32[8,768]{1,0:T(8,128)S(1)}, f32[8,768]{1,0:T(8,128)S(1)}, u32[]{:S(2)}, u32[]{:S(2)}) collective-permute-start(f32[8,768]{1,0:T(8,128)S(1)} %again_kernel.1), channel_id=1, source_target_pairs={{0,12},{4,8},{8,4},{12,0},{1,13},{5,9},{9,5},{13,1},{2,14},{6,10},... | collective-permute-start | bytes 73736 | tf_op jit(solution)/shard_map/ppermute | solution.py:697
  19.0 0.5 %between_kernel.1 = (f32[144,768]{1,0:T(8,128)S(1)}, f32[8,128]{1,0:T(8,128)S(1)}) custom-call(f32[144,128]{1,0:T(8,128)S(1)} %get-tuple-element.42.near, f32[128,512]{1,0:T(8,128)S(1)} %get-tuple-element.45.field, f32[144,768]{1,0:T(8,128)S(1)} %get-tuple-element.65.precond, f32[128,768]{1,0:T(8,128)S(1)} %get-tuple-element.66.image), custom_call_target="tpu_custom_call" | custom-call | tf_op jit(solution)/shard_map/between_kernel/pallas_call | solution.py:130
  19.5 1.5 %collective-permute-done.8.rest_1_ = f32[8,768]{1,0:T(8,128)S(1)} collective-permute-done((f32[8,768]{1,0:T(8,128)S(1)}, f32[8,768]{1,0:T(8,128)S(1)}, u32[]{:S(2)}, u32[]{:S(2)}) %collective-permute-start.8) | collective-permute-done | bytes 24608 | tf_op jit(solution)/shard_map/ppermute | solution.py:697
  21.0 0.7 %second_kernel.1 = (f32[144,768]{1,0:T(8,128)S(1)}, f32[144,768]{1,0:T(8,128)S(1)}, f32[8,128]{1,0:T(8,128)S(1)}) custom-call(f32[144,768]{1,0:T(8,128)S(1)} %get-tuple-element.67.spread, f32[8,128]{1,0:T(8,128)S(1)} %get-tuple-element.68.early, f32[128,768]{1,0:T(8,128)S(1)} %get-tuple-element.66.image, f32[8,128,512]{2,1,0:T(8,128)S(1)} %get-tuple-element.54.own.own_part, ...), custom_call_target="tpu_custom_call" | custom-call | tf_op jit(solution)/shard_map/second_kernel/pallas_call | solution.py:130
  21.8 0.2 collective-permute-start.9
  22.0 1.0 %collective-permute-done.9 = f32[8,128]{1,0:T(8,128)S(1)} collective-permute-done((f32[8,128]{1,0:T(8,128)S(1)}, f32[8,128]{1,0:T(8,128)S(1)}, u32[]{:S(2)}, u32[]{:S(2)}) %collective-permute-start.9) | collective-permute-done | bytes 4128 | tf_op jit(solution)/shard_map/ppermute | solution.py:618
  23.0 1.8 %collective-permute-start.10 = (f32[8,128]{1,0:T(8,128)S(1)}, f32[8,128]{1,0:T(8,128)S(1)}, u32[]{:S(2)}, u32[]{:S(2)}) collective-permute-start(f32[8,128]{1,0:T(8,128)S(1)} %add.12), channel_id=1, source_target_pairs={{0,6},{1,7},{2,4},{3,5},{4,2},{5,3},{6,0},{7,1},{8,14},{9,15},{10,... | collective-permute-start | bytes 12296 | tf_op jit(solution)/shard_map/ppermute | solution.py:621
  24.8 2.1 %collective-permute-done.10 = f32[8,128]{1,0:T(8,128)S(1)} collective-permute-done((f32[8,128]{1,0:T(8,128)S(1)}, f32[8,128]{1,0:T(8,128)S(1)}, u32[]{:S(2)}, u32[]{:S(2)}) %collective-permute-start.10) | collective-permute-done | bytes 4128 | tf_op jit(solution)/shard_map/ppermute | solution.py:621
  26.9 1.9 %collective-permute-start.11 = (f32[8,128]{1,0:T(8,128)S(1)}, f32[8,128]{1,0:T(8,128)S(1)}, u32[]{:S(2)}, u32[]{:S(2)}) collective-permute-start(f32[8,128]{1,0:T(8,128)S(1)} %add.13), channel_id=1, source_target_pairs={{0,5},{1,4},{2,7},{3,6},{4,1},{5,0},{6,3},{7,2},{8,13},{9,12},{10,... | collective-permute-start | bytes 12296 | tf_op jit(solution)/shard_map/ppermute | solution.py:621
  28.8 1.3 %collective-permute-done.11 = f32[8,128]{1,0:T(8,128)S(1)} collective-permute-done((f32[8,128]{1,0:T(8,128)S(1)}, f32[8,128]{1,0:T(8,128)S(1)}, u32[]{:S(2)}, u32[]{:S(2)}) %collective-permute-start.11) | collective-permute-done | bytes 4128 | tf_op jit(solution)/shard_map/ppermute | solution.py:621
  30.1 1.4 %collective-permute-start.12 = (f32[8,128]{1,0:T(8,128)S(1)}, f32[8,128]{1,0:T(8,128)S(1)}, u32[]{:S(2)}, u32[]{:S(2)}) collective-permute-start(f32[8,128]{1,0:T(8,128)S(1)} %add.14), channel_id=1, source_target_pairs={{0,12},{4,8},{8,4},{12,0},{1,13},{5,9},{9,5},{13,1},{2,14},{6,10},... | collective-permute-start | bytes 12296 | tf_op jit(solution)/shard_map/ppermute | solution.py:623
  31.5 1.6 %turn_kernel.1 = (f32[512,128]{1,0:T(8,128)S(1)}, f32[512,128]{1,0:T(8,128)S(1)}, f32[512,128]{1,0:T(8,128)S(1)}, f32[512,128]{1,0:T(8,128)S(1)}, f32[128,768]{1,0:T(8,128)}) custom-call(f32[144,768]{1,0:T(8,128)S(1)} %get-tuple-element.65.precond, f32[128,768]{1,0:T(8,128)S(1)} %get-tuple-element.66.image, f32[144,768]{1,0:T(8,128)S(1)} %get-tuple-element.74.again, ...), custom_call_target="tpu_custom_call" | custom-call | tf_op jit(solution)/shard_map/turn_kernel/pallas_call | solution.py:130
  33.1 0.0 collective-permute-done.12
  33.2 1.0 %combine_kernel.1 = (f32[512,128]{1,0:T(8,128)}, f32[512,128]{1,0:T(8,128)}) custom-call(f32[8,128]{1,0:T(8,128)S(1)} %add.15.sums, f32[512,128]{1,0:T(8,128)S(1)} %get-tuple-element.43.noise, f32[512,128]{1,0:T(8,128)S(1)} %get-tuple-element.76.precond, f32[512,128]{1,0:T(8,128)S(1)} %get-tuple-element.77.image, f32[512,128]{1,0:T(8,128)S(1)} %get-tuple-element.78.again, ...), custom_call_target="tpu_custom_call" | custom-call | tf_op jit(solution)/shard_map/combine_kernel/pallas_call | solution.py:716
  (8 shorter events, 0.1 us)
Async XLA Ops:
  2.2 11.5 %collective-permute-start = (f32[17,32,128]{2,1,0:T(8,128)S(1)}, f32[17,32,128]{2,1,0:T(8,128)S(1)}, u32[]{:S(2)}, u32[]{:S(2)}) collective-permute-start(f32[17,32,128]{2,1,0:T(8,128)S(1)} %get-tuple-element.52), channel_id=1, source_target_pairs={{0,1},{1,0},{2,3},{3,2},{4,5},{5,4},{6,7},{7,6},{8,9},{9,8},{10,11... | collective-permute-start | bytes 835592 | tf_op jit(solution)/shard_map/ppermute | solution.py:653
  5.3 8.4 %collective-permute-start.1 = (f32[17,32,128]{2,1,0:T(8,128)S(1)}, f32[17,32,128]{2,1,0:T(8,128)S(1)}, u32[]{:S(2)}, u32[]{:S(2)}) collective-permute-start(f32[17,32,128]{2,1,0:T(8,128)S(1)} %get-tuple-element.53), channel_id=1, source_target_pairs={{0,4},{1,2},{2,1},{3,7},{4,0},{5,6},{6,5},{7,3},{8,12},{9,10},{10,... | collective-permute-start | bytes 835592 | tf_op jit(solution)/shard_map/ppermute | solution.py:653
  5.7 1.3 %collective-permute-start.2 = (f32[8,512]{1,0:T(8,128)S(1)}, f32[8,512]{1,0:T(8,128)S(1)}, u32[]{:S(2)}, u32[]{:S(2)}) collective-permute-start(f32[8,512]{1,0:T(8,128)S(1)} %get-tuple-element.60.own), channel_id=1, source_target_pairs={{0,4},{4,0},{8,12},{12,8},{1,5},{5,1},{9,13},{13,9},{2,6},{6,2},{1... | collective-permute-start | bytes 49160 | tf_op jit(solution)/shard_map/ppermute | solution.py:672
  7.0 3.4 %collective-permute-start.4 = (f32[16,512]{1,0:T(8,128)S(1)}, f32[16,512]{1,0:T(8,128)S(1)}, u32[]{:S(2)}, u32[]{:S(2)}) collective-permute-start(f32[16,512]{1,0:T(8,128)S(1)} %chip_kernel.1), channel_id=1, source_target_pairs={{0,12},{4,8},{8,4},{12,0},{1,13},{5,9},{9,5},{13,1},{2,14},{6,10},... | collective-permute-start | bytes 98312 | tf_op jit(solution)/shard_map/ppermute | solution.py:674
  8.6 1.2 %collective-permute-start.3 = (f32[8,512]{1,0:T(8,128)S(1)}, f32[8,512]{1,0:T(8,128)S(1)}, u32[]{:S(2)}, u32[]{:S(2)}) collective-permute-start(f32[8,512]{1,0:T(8,128)S(1)} %get-tuple-element.61), channel_id=1, source_target_pairs={{0,4},{4,0},{8,12},{12,8},{1,5},{5,1},{9,13},{13,9},{2,6},{6,2},{1... | collective-permute-start | bytes 49160 | tf_op jit(solution)/shard_map/ppermute | solution.py:675
  10.5 4.7 %collective-permute-start.5 = (f32[24,128]{1,0:T(8,128)S(1)}, f32[24,128]{1,0:T(8,128)S(1)}, u32[]{:S(2)}, u32[]{:S(2)}) collective-permute-start(f32[24,128]{1,0:T(8,128)S(1)} %get-tuple-element.63), channel_id=1, source_target_pairs={{0,1},{1,0},{2,3},{3,2},{4,5},{5,4},{6,7},{7,6},{8,9},{9,8},{10,11... | collective-permute-start | bytes 36872 | tf_op jit(solution)/shard_map/ppermute | solution.py:653
  13.5 1.7 %collective-permute-start.6 = (f32[24,128]{1,0:T(8,128)S(1)}, f32[24,128]{1,0:T(8,128)S(1)}, u32[]{:S(2)}, u32[]{:S(2)}) collective-permute-start(f32[24,128]{1,0:T(8,128)S(1)} %get-tuple-element.64), channel_id=1, source_target_pairs={{0,4},{1,2},{2,1},{3,7},{4,0},{5,6},{6,5},{7,3},{8,12},{9,10},{10,... | collective-permute-start | bytes 36872 | tf_op jit(solution)/shard_map/ppermute | solution.py:653
  16.4 1.3 %collective-permute-start.7 = (f32[8,768]{1,0:T(8,128)S(1)}, f32[8,768]{1,0:T(8,128)S(1)}, u32[]{:S(2)}, u32[]{:S(2)}) collective-permute-start(f32[8,768]{1,0:T(8,128)S(1)} %get-tuple-element.71), channel_id=1, source_target_pairs={{0,4},{4,0},{8,12},{12,8},{1,5},{5,1},{9,13},{13,9},{2,6},{6,2},{1... | collective-permute-start | bytes 73736 | tf_op jit(solution)/shard_map/ppermute | solution.py:695
  17.7 3.3 %collective-permute-start.8 = (f32[8,768]{1,0:T(8,128)S(1)}, f32[8,768]{1,0:T(8,128)S(1)}, u32[]{:S(2)}, u32[]{:S(2)}) collective-permute-start(f32[8,768]{1,0:T(8,128)S(1)} %again_kernel.1), channel_id=1, source_target_pairs={{0,12},{4,8},{8,4},{12,0},{1,13},{5,9},{9,5},{13,1},{2,14},{6,10},... | collective-permute-start | bytes 73736 | tf_op jit(solution)/shard_map/ppermute | solution.py:697
  21.8 1.2 %collective-permute-start.9 = (f32[8,128]{1,0:T(8,128)S(1)}, f32[8,128]{1,0:T(8,128)S(1)}, u32[]{:S(2)}, u32[]{:S(2)}) collective-permute-start(f32[8,128]{1,0:T(8,128)S(1)} %get-tuple-element.73), channel_id=1, source_target_pairs={{0,4},{4,0},{8,12},{12,8},{1,5},{5,1},{9,13},{13,9},{2,6},{6,2},{1... | collective-permute-start | bytes 12296 | tf_op jit(solution)/shard_map/ppermute | solution.py:618
  23.0 3.9 %collective-permute-start.10 = (f32[8,128]{1,0:T(8,128)S(1)}, f32[8,128]{1,0:T(8,128)S(1)}, u32[]{:S(2)}, u32[]{:S(2)}) collective-permute-start(f32[8,128]{1,0:T(8,128)S(1)} %add.12), channel_id=1, source_target_pairs={{0,6},{1,7},{2,4},{3,5},{4,2},{5,3},{6,0},{7,1},{8,14},{9,15},{10,... | collective-permute-start | bytes 12296 | tf_op jit(solution)/shard_map/ppermute | solution.py:621
  26.9 3.2 %collective-permute-start.11 = (f32[8,128]{1,0:T(8,128)S(1)}, f32[8,128]{1,0:T(8,128)S(1)}, u32[]{:S(2)}, u32[]{:S(2)}) collective-permute-start(f32[8,128]{1,0:T(8,128)S(1)} %add.13), channel_id=1, source_target_pairs={{0,5},{1,4},{2,7},{3,6},{4,1},{5,0},{6,3},{7,2},{8,13},{9,12},{10,... | collective-permute-start | bytes 12296 | tf_op jit(solution)/shard_map/ppermute | solution.py:621
  30.1 3.0 %collective-permute-start.12 = (f32[8,128]{1,0:T(8,128)S(1)}, f32[8,128]{1,0:T(8,128)S(1)}, u32[]{:S(2)}, u32[]{:S(2)}) collective-permute-start(f32[8,128]{1,0:T(8,128)S(1)} %add.14), channel_id=1, source_target_pairs={{0,12},{4,8},{8,4},{12,0},{1,13},{5,9},{9,5},{13,1},{2,14},{6,10},... | collective-permute-start | bytes 12296 | tf_op jit(solution)/shard_map/ppermute | solution.py:623
